TPU v7x, 32 devices: a whole 2x2x4 slice. The times are simulated.
32 devices in a mesh: dp: 16 (over z, y, core), tensor: 2 (over x).
Axes of the slice: x: 2, y: 2, z: 4, core: 2. Of those that a mesh axis runs over, the one named last changes fastest.
Arguments:
- tokens: bfloat16 [16384, 1536], P(('dp', 'tensor')), may hold values from -6 to 6
- parents: int32 [16, 8], P('dp'), may hold values from -1 to 6, as said below
- attn_gain: float32 [1536], replicated, may hold values from 0.5 to 1.5
- ffn_gain: float32 [1536], replicated, may hold values from 0.5 to 1.5
- query_weight: bfloat16 [1536, 1536], P('dp', 'tensor'), may hold values from -0.21875 to 0.21875
- key_weight: bfloat16 [1536, 1536], P('dp', 'tensor'), may hold values from -0.21875 to 0.21875
- value_weight: bfloat16 [1536, 1536], P('dp', 'tensor'), may hold values from -0.15625 to 0.15625
- output_weight: bfloat16 [1536, 1536], P('tensor', 'dp'), may hold values from -0.4375 to 0.4375
- gate_weight: bfloat16 [1536, 4096], P('dp', 'tensor'), may hold values from -0.15625 to 0.15625
- up_weight: bfloat16 [1536, 4096], P('dp', 'tensor'), may hold values from -0.15625 to 0.15625
- down_weight: bfloat16 [4096, 1536], P('tensor', 'dp'), may hold values from -0.09375 to 0.09375
- cotangent: bfloat16 [16384, 1536], P(('dp', 'tensor')), may hold values from -6 to 6
Outputs:
- block_out: bfloat16 [16384, 1536], P(('dp', 'tensor'))
- token_grad: bfloat16 [16384, 1536], P(('dp', 'tensor'))
- query_grad: float32 [1536, 1536], P('dp', 'tensor')
- key_grad: float32 [1536, 1536], P('dp', 'tensor')
- value_grad: float32 [1536, 1536], P('dp', 'tensor')
- output_grad: float32 [1536, 1536], P('tensor', 'dp')
- gate_grad: float32 [1536, 4096], P('dp', 'tensor')
- up_grad: float32 [1536, 4096], P('dp', 'tensor')
- down_grad: float32 [4096, 1536], P('tensor', 'dp')
- attn_gain_grad: float32 [1536], P(('dp', 'tensor'))
- ffn_gain_grad: float32 [1536], P(('dp', 'tensor'))
Inputs may be any that keep to these rules, and one draw needn't show every extreme that they name: parents[t, 0] is -1 (the root segment of tree t); for s >= 1, parents[t, s] is a segment before s of the same tree; in tree 0 the parent of the last segment is the segment before it.
All inputs are finite; a program needn't handle non-finite values.
Results may differ from a plain program's by a relative error of at most 0.02.
Values may be sent and summed in bfloat16 or wider, within the bound.
A program may use at most 256 MiB of HBM per device.

v0:
```python
import math

import jax
import jax.numpy as jnp
from jax import lax
from jax.sharding import PartitionSpec as P

HD = 64


epsilon = 1e-05


def tree_layout(parent_row):
    seg_count = parent_row.shape[0]
    seg_index = jnp.arange(seg_count, dtype=jnp.int32)
    step_up = (parent_row[:, None] == seg_index[None, :]).astype(jnp.int32)
    eye_ints = (seg_index[:, None] == seg_index[None, :]).astype(jnp.int32)
    reachable = eye_ints
    for sweep in range(seg_count):
        reachable = jnp.minimum(eye_ints + jnp.dot(step_up, reachable), 1)
    depths = jnp.sum(reachable, axis=1) - 1
    return (reachable, depths)


def row_tables(parent_row, seg_rows):
    reachable, depths = tree_layout(parent_row)
    seg_count = parent_row.shape[0]
    length = seg_count * seg_rows
    wide_mask = jnp.broadcast_to(
        reachable[:, None, :, None], (seg_count, seg_rows, seg_count, seg_rows)
    ).reshape(length, length)
    row_ids = jnp.arange(length, dtype=jnp.int32)
    allowed = (wide_mask > 0) & (row_ids[None, :] <= row_ids[:, None])
    positions = (
        jnp.broadcast_to((depths * seg_rows)[:, None], (seg_count, seg_rows)).reshape(length)
        + row_ids % seg_rows
    )
    return (allowed, positions.astype(jnp.float32))


def rotate(values, positions, direction):
    head_width = values.shape[-1]
    middle = head_width // 2
    freq_rates = jnp.exp(
        jnp.arange(middle, dtype=jnp.float32) * (-2.0 * math.log(10000.0) / head_width)
    )
    angles = positions[:, None, None] * freq_rates[None, None, :]
    cosine = jnp.cos(angles)
    sine_part = direction * jnp.sin(angles)
    first_half = values[..., :middle]
    second_half = values[..., middle:]
    return jnp.concatenate(
        [
            first_half * cosine - second_half * sine_part,
            second_half * cosine + first_half * sine_part,
        ],
        axis=-1,
    )


def rms_parts(values, gain_vec):
    inverse = lax.rsqrt(jnp.mean(values * values, axis=-1, keepdims=True) + epsilon)
    unit_rows = values * inverse
    return (unit_rows, inverse, (unit_rows * gain_vec).astype(jnp.bfloat16))


def rms_back(grad_out, unit_rows, inverse, gain_vec):
    scaled = grad_out * gain_vec
    inner_mean = jnp.mean(scaled * unit_rows, axis=-1, keepdims=True)
    return (inverse * (scaled - unit_rows * inner_mean), jnp.sum(grad_out * unit_rows, axis=0))


def contract_last(left, right):
    return lax.dot_general(
        left, right, (((1,), (1,)), ((), ())), preferred_element_type=jnp.float32
    )


def contract_first(left, right):
    return lax.dot_general(
        left, right, (((0,), (0,)), ((), ())), preferred_element_type=jnp.float32
    )


def feed_front(middle_all, ffn_vec, gate_mat, up_mat):
    unit_two, inverse_two, normed_two = rms_parts(middle_all.astype(jnp.float32), ffn_vec)
    gate_pre = jnp.dot(normed_two, gate_mat, preferred_element_type=jnp.float32)
    up_pre = jnp.dot(normed_two, up_mat, preferred_element_type=jnp.float32)
    sigmoid = jax.nn.sigmoid(gate_pre)
    hidden = (gate_pre * sigmoid * up_pre).astype(jnp.bfloat16)
    return (unit_two, inverse_two, normed_two, gate_pre, up_pre, sigmoid, hidden)


def attend_forward(queries, keys_rot, values_low, allowed, score_scale, block_rows):
    length, heads_local, head_width = queries.shape

    def one_block(offset):
        query_rows = lax.dynamic_slice_in_dim(queries, offset, block_rows, 0)
        mask_rows = lax.dynamic_slice_in_dim(allowed, offset, block_rows, 0)
        scores = (
            jnp.einsum("qhd,khd->hqk", query_rows, keys_rot, preferred_element_type=jnp.float32)
            * score_scale
        )
        scores = jnp.where(mask_rows[None], scores, -1e30)
        peak_score = jnp.max(scores, axis=-1, keepdims=True)
        exponent = jnp.exp(scores - peak_score)
        totals = jnp.sum(exponent, axis=-1, keepdims=True)
        probs_low = (exponent / totals).astype(jnp.bfloat16)
        attended = jnp.einsum(
            "hqk,khd->qhd", probs_low, values_low, preferred_element_type=jnp.float32
        )
        return (attended.astype(jnp.bfloat16), (peak_score + jnp.log(totals))[..., 0])

    offsets = jnp.arange(length // block_rows, dtype=jnp.int32) * block_rows
    blocks_out, logsum = lax.map(one_block, offsets)
    return (blocks_out.reshape(length, heads_local * head_width), logsum)


def attend_backward(
    queries, keys_rot, values_low, allowed, logsum, grad_attended, score_scale, block_rows
):
    length, heads_local, head_width = queries.shape

    def one_block(carry, packed):
        offset, block_lse = packed
        key_acc, value_acc = carry
        query_rows = lax.dynamic_slice_in_dim(queries, offset, block_rows, 0)
        mask_rows = lax.dynamic_slice_in_dim(allowed, offset, block_rows, 0)
        grad_rows = lax.dynamic_slice_in_dim(grad_attended, offset, block_rows, 0)
        scores = (
            jnp.einsum("qhd,khd->hqk", query_rows, keys_rot, preferred_element_type=jnp.float32)
            * score_scale
        )
        scores = jnp.where(mask_rows[None], scores, -1e30)
        attn_probs = jnp.exp(scores - block_lse[..., None])
        probs_low = attn_probs.astype(jnp.bfloat16)
        value_acc = value_acc + jnp.einsum(
            "hqk,qhd->khd", probs_low, grad_rows, preferred_element_type=jnp.float32
        )
        grad_probs = jnp.einsum(
            "qhd,khd->hqk", grad_rows, values_low, preferred_element_type=jnp.float32
        )
        inner_sum = jnp.sum(attn_probs * grad_probs, axis=-1, keepdims=True)
        grad_scores = (attn_probs * (grad_probs - inner_sum)).astype(jnp.bfloat16)
        query_part = (
            jnp.einsum("hqk,khd->qhd", grad_scores, keys_rot, preferred_element_type=jnp.float32)
            * score_scale
        )
        key_acc = (
            key_acc
            + jnp.einsum(
                "hqk,qhd->khd", grad_scores, query_rows, preferred_element_type=jnp.float32
            )
            * score_scale
        )
        return ((key_acc, value_acc), query_part)

    offsets = jnp.arange(length // block_rows, dtype=jnp.int32) * block_rows
    zeros_acc = jnp.zeros((length, heads_local, head_width), jnp.float32)
    (key_part, value_part), query_blocks = lax.scan(
        one_block, (zeros_acc, zeros_acc), (offsets, logsum)
    )
    return (query_blocks.reshape(length, heads_local, head_width), key_part, value_part)


def gather_rows(local_rows):
    return lax.all_gather(local_rows, "tensor", axis=0, tiled=True)


def reduce_rows(term_rows):
    return lax.psum_scatter(
        term_rows.astype(jnp.bfloat16), "tensor", scatter_dimension=0, tiled=True
    ).astype(jnp.float32)


def reduce_input(term_rows, gain_piece):
    return (
        lax.psum_scatter(
            term_rows.astype(jnp.bfloat16), "tensor", scatter_dimension=0, tiled=True
        ).astype(jnp.float32),
        lax.psum_scatter(
            gain_piece.astype(jnp.bfloat16), "tensor", scatter_dimension=0, tiled=True
        ).astype(jnp.float32),
    )


def body(
    tokens,
    parents,
    attn_gain,
    ffn_gain,
    query_weight,
    key_weight,
    value_weight,
    output_weight,
    gate_weight,
    up_weight,
    down_weight,
    cotangent,
):
    length = tokens.shape[0] * lax.axis_size("tensor")
    block_rows = min(512, length)
    score_scale = 1.0 / math.sqrt(HD)
    allowed, positions = row_tables(parents[0], length // parents.shape[1])
    query_full, key_full, value_full, output_full = (
        lax.all_gather(query_weight, "dp", axis=0, tiled=True),
        lax.all_gather(key_weight, "dp", axis=0, tiled=True),
        lax.all_gather(value_weight, "dp", axis=0, tiled=True),
        lax.all_gather(output_weight, "dp", axis=1, tiled=True),
    )
    heads_local = query_full.shape[1] // HD
    rows_all = gather_rows(tokens)
    unit_one, inverse_one, normed_one = rms_parts(rows_all.astype(jnp.float32), attn_gain)
    query_pre = jnp.dot(normed_one, query_full, preferred_element_type=jnp.float32)
    key_pre = jnp.dot(normed_one, key_full, preferred_element_type=jnp.float32)
    queries = rotate(query_pre.reshape(length, heads_local, HD), positions, 1.0).astype(
        jnp.bfloat16
    )
    keys_rot = rotate(key_pre.reshape(length, heads_local, HD), positions, 1.0).astype(jnp.bfloat16)
    values_low = (
        jnp.dot(normed_one, value_full, preferred_element_type=jnp.float32)
        .astype(jnp.bfloat16)
        .reshape(length, heads_local, HD)
    )
    attended, logsum = attend_forward(
        queries, keys_rot, values_low, allowed, score_scale, block_rows
    )
    middle_local = (
        tokens.astype(jnp.float32)
        + reduce_rows(jnp.dot(attended, output_full, preferred_element_type=jnp.float32))
    ).astype(jnp.bfloat16)
    gate_full, up_full, down_full = (
        lax.all_gather(gate_weight, "dp", axis=0, tiled=True),
        lax.all_gather(up_weight, "dp", axis=0, tiled=True),
        lax.all_gather(down_weight, "dp", axis=1, tiled=True),
    )
    middle_all = gather_rows(middle_local)
    unit_two, inverse_two, normed_two, gate_pre, up_pre, sigmoid, hidden = feed_front(
        middle_all, ffn_gain, gate_full, up_full
    )
    block_out = (
        middle_local.astype(jnp.float32)
        + reduce_rows(jnp.dot(hidden, down_full, preferred_element_type=jnp.float32))
    ).astype(jnp.bfloat16)
    gate_back, up_back, down_back = (
        lax.all_gather(gate_weight, "dp", axis=0, tiled=True),
        lax.all_gather(up_weight, "dp", axis=0, tiled=True),
        lax.all_gather(down_weight, "dp", axis=1, tiled=True),
    )
    middle_again = lax.all_gather(middle_local, "tensor", axis=0, tiled=True)
    unit_two, inverse_two, normed_two, gate_pre, up_pre, sigmoid, hidden = feed_front(
        middle_again, ffn_gain, gate_back, up_back
    )
    grad_all = gather_rows(cotangent)
    grad_hidden = contract_last(grad_all, down_back)
    down_grad = contract_first(hidden, grad_all)
    grad_gate = (grad_hidden * up_pre * sigmoid * (1.0 + gate_pre * (1.0 - sigmoid))).astype(
        jnp.bfloat16
    )
    grad_up = (grad_hidden * gate_pre * sigmoid).astype(jnp.bfloat16)
    grad_normed_two = contract_last(grad_gate, gate_back) + contract_last(grad_up, up_back)
    gate_grad = contract_first(normed_two, grad_gate)
    up_grad = contract_first(normed_two, grad_up)
    grad_middle_part, ffn_gain_part = rms_back(grad_normed_two, unit_two, inverse_two, ffn_gain)
    gate_grad, up_grad, down_grad, ffn_gain_piece = (
        lax.psum_scatter(gate_grad, "dp", scatter_dimension=0, tiled=True),
        lax.psum_scatter(up_grad, "dp", scatter_dimension=0, tiled=True),
        lax.psum_scatter(down_grad, "dp", scatter_dimension=1, tiled=True),
        lax.psum_scatter(ffn_gain_part, "dp", scatter_dimension=0, tiled=True),
    )
    grad_middle_local, ffn_gain_grad = reduce_input(grad_middle_part, ffn_gain_piece)
    grad_middle = (cotangent.astype(jnp.float32) + grad_middle_local).astype(jnp.bfloat16)
    query_back, key_back, value_back, output_back = (
        lax.all_gather(query_weight, "dp", axis=0, tiled=True),
        lax.all_gather(key_weight, "dp", axis=0, tiled=True),
        lax.all_gather(value_weight, "dp", axis=0, tiled=True),
        lax.all_gather(output_weight, "dp", axis=1, tiled=True),
    )
    grad_middle_all = gather_rows(grad_middle)
    grad_attended = contract_last(grad_middle_all, output_back).astype(jnp.bfloat16)
    output_grad = contract_first(attended, grad_middle_all)
    query_rot_grad, key_rot_grad, value_rows_grad = attend_backward(
        queries,
        keys_rot,
        values_low,
        allowed,
        logsum,
        grad_attended.reshape(length, heads_local, HD),
        score_scale,
        block_rows,
    )
    query_pre_grad = (
        rotate(query_rot_grad, positions, -1.0)
        .reshape(length, heads_local * HD)
        .astype(jnp.bfloat16)
    )
    key_pre_grad = (
        rotate(key_rot_grad, positions, -1.0).reshape(length, heads_local * HD).astype(jnp.bfloat16)
    )
    value_pre_grad = value_rows_grad.reshape(length, heads_local * HD).astype(jnp.bfloat16)
    grad_normed_one = (
        contract_last(query_pre_grad, query_back)
        + contract_last(key_pre_grad, key_back)
        + contract_last(value_pre_grad, value_back)
    )
    query_grad = contract_first(normed_one, query_pre_grad)
    key_grad = contract_first(normed_one, key_pre_grad)
    value_grad = contract_first(normed_one, value_pre_grad)
    grad_tokens_part, attn_gain_part = rms_back(grad_normed_one, unit_one, inverse_one, attn_gain)
    query_grad, key_grad, value_grad, output_grad, attn_gain_piece = (
        lax.psum_scatter(query_grad, "dp", scatter_dimension=0, tiled=True),
        lax.psum_scatter(key_grad, "dp", scatter_dimension=0, tiled=True),
        lax.psum_scatter(value_grad, "dp", scatter_dimension=0, tiled=True),
        lax.psum_scatter(output_grad, "dp", scatter_dimension=1, tiled=True),
        lax.psum_scatter(attn_gain_part, "dp", scatter_dimension=0, tiled=True),
    )
    grad_tokens_local, attn_gain_grad = reduce_input(grad_tokens_part, attn_gain_piece)
    token_grad = (grad_middle.astype(jnp.float32) + grad_tokens_local).astype(jnp.bfloat16)
    return (
        block_out,
        token_grad,
        query_grad,
        key_grad,
        value_grad,
        output_grad,
        gate_grad,
        up_grad,
        down_grad,
        attn_gain_grad,
        ffn_gain_grad,
    )


def solution(mesh):
    placed = (
        P(("dp", "tensor"), None),
        P("dp", None),
        P(),
        P(),
        P("dp", "tensor"),
        P("dp", "tensor"),
        P("dp", "tensor"),
        P("tensor", "dp"),
        P("dp", "tensor"),
        P("dp", "tensor"),
        P("tensor", "dp"),
        P(("dp", "tensor"), None),
    )
    return jax.shard_map(
        body,
        mesh=mesh,
        in_specs=placed,
        out_specs=(
            P(("dp", "tensor"), None),
            P(("dp", "tensor"), None),
            P("dp", "tensor"),
            P("dp", "tensor"),
            P("dp", "tensor"),
            P("tensor", "dp"),
            P("dp", "tensor"),
            P("dp", "tensor"),
            P("tensor", "dp"),
            P(("dp", "tensor")),
            P(("dp", "tensor")),
        ),
        check_vma=False,
    )
```

profile of v0, /device:TPU:0, one launch (start us, length us, event | category | flops | bytes accessed | tf_op | source)
XLA Modules:
  0.0 1812.9 jit_solution(1311223907688781169)
XLA Ops:
  18.1 39.2 %all-gather.12.cloned.1.call-done = bf16[1024,1536]{1,0:T(8,128)(2,1)} async-done(((bf16[512,1536]{1,0:T(8,128)(2,1)}), bf16[1024,1536]{1,0:T(8,128)(2,1)}) %all-gather.12.cloned.1.call-update) | async-done | bytes 3145744 | tf_op jit(solution)/shard_map/all_gather | solution.py:168
  60.0 41.8 %all-gather.16.cloned.1.call-done = bf16[1536,768]{1,0:T(8,128)(2,1)} async-done(((bf16[96,768]{1,0:T(8,128)(2,1)}), bf16[1536,768]{1,0:T(8,128)(2,1)}) %all-gather.16.cloned.1.call-update) | async-done | bytes 2359312 | tf_op jit(solution)/shard_map/all_gather | solution.py:208
  107.9 37.2 %all-gather.14.cloned.1.call-done = bf16[1536,768]{1,0:T(8,128)(2,1)} async-done(((bf16[96,768]{1,0:T(8,128)(2,1)}), bf16[1536,768]{1,0:T(8,128)(2,1)}) %all-gather.14.cloned.1.call-update) | async-done | bytes 2359312 | tf_op jit(solution)/shard_map/all_gather | solution.py:207
  152.4 35.8 %all-gather.18.cloned.1.call-done = bf16[1536,768]{1,0:T(8,128)(2,1)} async-done(((bf16[96,768]{1,0:T(8,128)(2,1)}), bf16[1536,768]{1,0:T(8,128)(2,1)}) %all-gather.18.cloned.1.call-update) | async-done | bytes 2359312 | tf_op jit(solution)/shard_map/all_gather | solution.py:209
  195.2 82.3 %while.27 = (s32[]{:T(128)}, bf16[2,512,12,64]{1,3,2,0:T(8,128)(2,1)S(1)}, f32[2,12,512]{2,1,0:T(8,128)S(1)}, s32[2]{0:T(128)S(1)}, pred[1024,1024]{1,0:T(8,128)...) while((s32[]{:T(128)}, ...), condition=%wide.region_5.6_spmd, body=%wide.region_2.5_spmd.sunk | while | flops 1686497280 | bytes 183738576 | solution.py:116
  286.5 42.2 %reduce-scatter.12.cloned.1.call-done = bf16[512,1536]{1,0:T(8,128)(2,1)} async-done(((bf16[1024,1536]{1,0:T(8,128)(2,1)}), bf16[512,1536]{1,0:T(8,128)(2,1)}) %reduce-scatter.12.cloned.1.call-update) | async-done | bytes 1572880 | tf_op jit(solution)/shard_map/reduce_scatter | solution.py:172
  335.0 41.8 %all-gather.22.cloned.1.call-done = bf16[1024,1536]{1,0:T(8,128)(2,1)} async-done(((bf16[512,1536]{1,0:T(8,128)(2,1)}), bf16[1024,1536]{1,0:T(8,128)(2,1)}) %all-gather.22.cloned.1.call-update) | async-done | bytes 3145744 | tf_op jit(solution)/shard_map/all_gather | solution.py:168
  379.4 61.8 %all-gather.24.cloned.1.call-done = bf16[1536,2048]{1,0:T(8,128)(2,1)} async-done(((bf16[96,2048]{1,0:T(8,128)(2,1)}), bf16[1536,2048]{1,0:T(8,128)(2,1)}) %all-gather.24.cloned.1.call-update) | async-done | bytes 6291472 | tf_op jit(solution)/shard_map/all_gather | solution.py:234
  453.6 50.7 %all-gather.26.cloned.1.call-done = bf16[1536,2048]{1,0:T(8,128)(2,1)} async-done(((bf16[96,2048]{1,0:T(8,128)(2,1)}), bf16[1536,2048]{1,0:T(8,128)(2,1)}) %all-gather.26.cloned.1.call-update) | async-done | bytes 6291472 | tf_op jit(solution)/shard_map/all_gather | solution.py:235
  516.5 32.8 %all-gather.30.cloned.1.call-done = bf16[1024,1536]{1,0:T(8,128)(2,1)} async-done(((bf16[512,1536]{1,0:T(8,128)(2,1)}), bf16[1024,1536]{1,0:T(8,128)(2,1)}) %all-gather.30.cloned.1.call-update) | async-done | bytes 3145744 | tf_op jit(solution)/shard_map/all_gather | solution.py:168
  549.3 64.4 %all-gather.28.cloned.1.call-done = bf16[2048,1536]{0,1:T(8,128)(2,1)} async-done(((bf16[2048,96]{0,1:T(8,128)(2,1)}), bf16[2048,1536]{0,1:T(8,128)(2,1)}) %all-gather.28.cloned.1.call-update) | async-done | bytes 6291472 | tf_op jit(solution)/shard_map/all_gather | solution.py:236
  659.1 42.0 %reduce-scatter.16.cloned.1.call-done = bf16[512,1536]{1,0:T(8,128)(2,1)} async-done(((bf16[1024,1536]{1,0:T(8,128)(2,1)}), bf16[512,1536]{1,0:T(8,128)(2,1)}) %reduce-scatter.16.cloned.1.call-update) | async-done | bytes 1572880 | tf_op jit(solution)/shard_map/reduce_scatter | solution.py:179
  715.5 33.7 %all-gather.32.cloned.1.call-done = bf16[1024,1536]{1,0:T(8,128)(2,1)} async-done(((bf16[512,1536]{1,0:T(8,128)(2,1)}), bf16[1024,1536]{1,0:T(8,128)(2,1)}) %all-gather.32.cloned.1.call-update) | async-done | bytes 3145744 | tf_op jit(solution)/shard_map/all_gather | solution.py:168
  755.6 242.8 %while.28 = (s32[]{:T(128)}, f32[1024,12,64]{0,2,1:T(8,128)}, f32[1024,12,64]{0,2,1:T(8,128)}, f32[2,512,12,64]{1,0,3,2:T(2,128)}, s32[2]{0:T(128)S(1)}, /*index...) while((s32[]{:T(128)}, f32[1024,12,64]{0,2,1:T(8,128)}, ...), condition=%wide.region_13.14_spmd.clone, body=%wide.region_11.13_spmd.clone.sunk | while | flops 4125222912 | bytes 251314496 | solution.py:161
  791.6 21.4 %multiply_convert_fusion.5 = bf16[12,512,1024]{2,1,0:T(8,128)(2,1)} fusion(f32[12,512,1024]{2,1,0:T(8,128)} %get-tuple-element.350, f32[12,512,1024]{2,1,0:T(8,128)} %fusion.180, f32[12,512]{1,0:T(8,128)S(1)} %get-tuple-element.351, f32[12,512]{1,0:T(8,128)S(1)} %dynamic-slice_bitcast_fusion.2, pred[512,1024]{1,0:T(8,128)(4,1)S(1)} %constant_dynamic-slice_fusion.5), kind=kLoop, calls=%fused_computation.16.clone.1 | loop fusion | flops 37748736 | bytes 63488000 | tf_op jit(solution)/shard_map/while/body/eval_jaxpr/convert_element_type | solution.py:145
  848.3 28.7 %dynamic_update_slice.20 = f32[2,512,12,64]{1,0,3,2:T(2,128)} dynamic-update-slice(f32[2,512,12,64]{1,0,3,2:T(2,128)} %get-tuple-element.402, f32[1,512,12,64]{1,0,3,2:T(1,128)S(1)} %copy.43, s32[]{:T(128)S(6)} %copy.60, s32[]{:T(128)} %constant.46.clone.1..sunk.1, s32[]{:T(128)} %constant.46.clone.1..sunk.1, s32[]{:T(128)} %constant.46.clone.1..sunk.1) | dynamic-update-slice | bytes 3145732 | tf_op jit(solution)/shard_map/while/body/jit(dynamic_update_index_in_dim)/dynamic_update_slice | solution.py:161
  969.6 28.7 %dynamic_update_slice.20 = f32[2,512,12,64]{1,0,3,2:T(2,128)} dynamic-update-slice(f32[2,512,12,64]{1,0,3,2:T(2,128)} %get-tuple-element.402, f32[1,512,12,64]{1,0,3,2:T(1,128)S(1)} %copy.43, s32[]{:T(128)S(6)} %copy.60, s32[]{:T(128)} %constant.46.clone.1..sunk.1, s32[]{:T(128)} %constant.46.clone.1..sunk.1, s32[]{:T(128)} %constant.46.clone.1..sunk.1) | dynamic-update-slice | bytes 3145732 | tf_op jit(solution)/shard_map/while/body/jit(dynamic_update_index_in_dim)/dynamic_update_slice | solution.py:161
  1101.2 62.6 %all-reduce.4 = (bf16[1536]{0:T(1024)(128)(2,1)S(1)}, bf16[1536]{0:T(1024)(128)(2,1)S(1)}) all-reduce(f32[1536]{0:T(1024)S(1)} %get-tuple-element.156, f32[1536]{0:T(1024)S(1)} %copy-done.31), channel_id=13, replica_groups=mesh['dp'=16,'tensor'=2] {'dp'}, use_global_device_ids=true, to_apply=%region_24.25.clone | all-reduce | flops 3072 | bytes 18432
  1173.1 58.6 %reduce-scatter.22.cloned.1.call-done = f32[96,768]{1,0:T(8,128)} async-done(((f32[1536,768]{1,0:T(8,128)}), f32[96,768]{1,0:T(8,128)}) %reduce-scatter.22.cloned.1.call-update) | async-done | bytes 294928 | tf_op jit(solution)/shard_map/reduce_scatter | solution.py:313
  1231.6 78.9 %reduce-scatter.24.cloned.1.call-done = f32[96,768]{1,0:T(8,128)} async-done(((f32[1536,768]{1,0:T(8,128)}), f32[96,768]{1,0:T(8,128)}) %reduce-scatter.24.cloned.1.call-update) | async-done | bytes 294928 | tf_op jit(solution)/shard_map/reduce_scatter | solution.py:314
  1310.6 79.5 %reduce-scatter.26.cloned.1.call-done = f32[768,96]{0,1:T(8,128)} async-done(((f32[768,1536]{0,1:T(8,128)}), f32[768,96]{0,1:T(8,128)}) %reduce-scatter.26.cloned.1.call-update) | async-done | bytes 294928 | tf_op jit(solution)/shard_map/reduce_scatter | solution.py:315
  1390.1 138.3 %reduce-scatter.28.cloned.1.call-done = f32[96,2048]{1,0:T(8,128)} async-done(((f32[1536,2048]{1,0:T(8,128)}), f32[96,2048]{1,0:T(8,128)}) %reduce-scatter.28.cloned.1.call-update) | async-done | bytes 786448 | tf_op jit(solution)/shard_map/reduce_scatter | solution.py:267
  1528.5 138.6 %reduce-scatter.30.cloned.1.call-done = f32[96,2048]{1,0:T(8,128)} async-done(((f32[1536,2048]{1,0:T(8,128)}), f32[96,2048]{1,0:T(8,128)}) %reduce-scatter.30.cloned.1.call-update) | async-done | bytes 786448 | tf_op jit(solution)/shard_map/reduce_scatter | solution.py:268
  1667.0 138.6 %reduce-scatter.32.cloned.1.call-done = f32[2048,96]{0,1:T(8,128)} async-done(((f32[2048,1536]{0,1:T(8,128)}), f32[2048,96]{0,1:T(8,128)}) %reduce-scatter.32.cloned.1.call-update) | async-done | bytes 786448 | tf_op jit(solution)/shard_map/reduce_scatter | solution.py:269
  (229 shorter events, 490.5 us)
Async XLA Ops:
  7.2 50.1 %all-gather.12.cloned.1.call-start = ((), (), s32[]{:S(2)}) async-start(), calls=%async_computation.11 | async-start | bytes 4718592 | tf_op jit(solution)/shard_map/all_gather | solution.py:168
  7.9 93.9 %all-gather.16.cloned.1.call-start = ((), (), s32[]{:S(2)}) async-start(), calls=%async_computation.13 | async-start | bytes 2506752 | tf_op jit(solution)/shard_map/all_gather | solution.py:208
  8.7 136.4 %all-gather.14.cloned.1.call-start = ((), (), s32[]{:S(2)}) async-start(), calls=%async_computation.12 | async-start | bytes 2506752 | tf_op jit(solution)/shard_map/all_gather | solution.py:207
  9.4 178.9 %all-gather.18.cloned.1.call-start = ((), (), s32[]{:S(2)}) async-start(), calls=%async_computation.14 | async-start | bytes 2506752 | tf_op jit(solution)/shard_map/all_gather | solution.py:209
  10.0 269.6 %all-gather.20.cloned.1.call-start = ((), (), s32[]{:S(2)}) async-start(), calls=%async_computation.15 | async-start | bytes 2506752 | tf_op jit(solution)/shard_map/all_gather | solution.py:210
  10.6 318.2 %reduce-scatter.12.cloned.1.call-start = ((), (), s32[]{:S(2)}) async-start(), calls=%async_computation.16 | async-start | bytes 4718592 | tf_op jit(solution)/shard_map/reduce_scatter | solution.py:172
  18.1 131.8 %copy-start.20 = (f32[1024,32]{0,1:T(8,128)}, f32[1024,32]{0,1:T(8,128)S(1)}, u32[]{:S(2)}) copy-start(f32[1024,32]{0,1:T(8,128)S(1)} %get-tuple-element.221) | copy-start | bytes 393220
  286.5 90.3 %all-gather.22.cloned.1.call-start = ((), (), s32[]{:S(2)}) async-start(), calls=%async_computation.17 | async-start | bytes 4718592 | tf_op jit(solution)/shard_map/all_gather | solution.py:168
  331.8 109.5 %all-gather.24.cloned.1.call-start = ((), (), s32[]{:S(2)}) async-start(), calls=%async_computation.18 | async-start | bytes 6684672 | tf_op jit(solution)/shard_map/all_gather | solution.py:234
  332.5 171.8 %all-gather.26.cloned.1.call-start = ((), (), s32[]{:S(2)}) async-start(), calls=%async_computation.19 | async-start | bytes 6684672 | tf_op jit(solution)/shard_map/all_gather | solution.py:235
  333.2 216.1 %all-gather.30.cloned.1.call-start = ((), (), s32[]{:S(2)}) async-start(), calls=%async_computation.22 | async-start | bytes 4718592 | tf_op jit(solution)/shard_map/all_gather | solution.py:168
  333.8 279.9 %all-gather.28.cloned.1.call-start = ((), (), s32[]{:S(2)}) async-start(), calls=%async_computation.20 | async-start | bytes 6684672 | tf_op jit(solution)/shard_map/all_gather | solution.py:236
  334.6 366.6 %reduce-scatter.16.cloned.1.call-start = ((), (), s32[]{:S(2)}) async-start(), calls=%async_computation.23 | async-start | bytes 4718592 | tf_op jit(solution)/shard_map/reduce_scatter | solution.py:179
  379.4 276.8 %copy-start.27 = (f32[1024]{0:T(1024)}, f32[1024]{0:T(1024)S(1)}, u32[]{:S(2)}) copy-start(f32[1024]{0:T(1024)S(1)} %add_rsqrt_fusion) | copy-start | bytes 12292
  659.0 90.2 %all-gather.32.cloned.1.call-start = ((), (), s32[]{:S(2)}) async-start(), calls=%async_computation.24 | async-start | bytes 4718592 | tf_op jit(solution)/shard_map/all_gather | solution.py:168
  704.1 394.1 %reduce-scatter.14.cloned.1.call-start = ((), (), s32[]{:S(2)}) async-start(), calls=%async_computation.21 | async-start | bytes 4718592 | tf_op jit(solution)/shard_map/reduce_scatter | solution.py:172
  715.5 454.6 %reduce-scatter.18.cloned.1.call-start = ((), (), s32[]{:S(2)}) async-start(), calls=%async_computation.25 | async-start | bytes 4718592 | tf_op jit(solution)/shard_map/reduce_scatter | solution.py:179
  1028.1 145.0 %reduce-scatter.20.cloned.1.call-start = ((), (), s32[]{:S(2)}) async-start(), calls=%async_computation.26 | async-start | bytes 5013504 | tf_op jit(solution)/shard_map/reduce_scatter | solution.py:312
  1034.7 197.0 %reduce-scatter.22.cloned.1.call-start = ((), (), s32[]{:S(2)}) async-start(), calls=%async_computation.27 | async-start | bytes 5013504 | tf_op jit(solution)/shard_map/reduce_scatter | solution.py:313
  1041.3 269.3 %reduce-scatter.24.cloned.1.call-start = ((), (), s32[]{:S(2)}) async-start(), calls=%async_computation.28 | async-start | bytes 5013504 | tf_op jit(solution)/shard_map/reduce_scatter | solution.py:314
  1047.6 342.5 %reduce-scatter.26.cloned.1.call-start = ((), (), s32[]{:S(2)}) async-start(), calls=%async_computation.29 | async-start | bytes 5013504 | tf_op jit(solution)/shard_map/reduce_scatter | solution.py:315
  1055.7 472.8 %reduce-scatter.28.cloned.1.call-start = ((), (), s32[]{:S(2)}) async-start(), calls=%async_computation.30 | async-start | bytes 13369344 | tf_op jit(solution)/shard_map/reduce_scatter | solution.py:267
  1069.3 597.7 %reduce-scatter.30.cloned.1.call-start = ((), (), s32[]{:S(2)}) async-start(), calls=%async_computation.31 | async-start | bytes 13369344 | tf_op jit(solution)/shard_map/reduce_scatter | solution.py:268
  1081.5 724.1 %reduce-scatter.32.cloned.1.call-start = ((), (), s32[]{:S(2)}) async-start(), calls=%async_computation.32 | async-start | bytes 13369344 | tf_op jit(solution)/shard_map/reduce_scatter | solution.py:269
  (40 other events, 738.6 us)
Sparse Core Ops, SparseCore 0:
  9.6 47.6 all-gather.11
  59.5 42.2 all-gather.15
  104.1 40.9 all-gather.13
  147.2 40.9 all-gather.17
  190.4 40.9 all-gather.19
  286.6 42.1 reduce-scatter.11
  331.9 44.9 all-gather.21
  379.4 61.8 all-gather.23
  443.8 60.4 all-gather.25
  505.7 43.5 all-gather.29
  551.9 61.8 all-gather.27
  659.1 41.9 reduce-scatter.15
  704.2 44.9 all-gather.31
  751.3 43.3 reduce-scatter.13
  1028.2 43.5 reduce-scatter.17
  1076.1 76.0 reduce-scatter.19
  1157.0 74.6 reduce-scatter.21
  1235.9 74.5 reduce-scatter.23
  1315.5 74.5 reduce-scatter.25
  1394.6 133.8 reduce-scatter.27
  1533.1 133.9 reduce-scatter.29
  1671.7 133.8 reduce-scatter.31
where the time goes:
time: 1830 us; the launch traced here: 1810 us
  waiting for transfers between devices  1160 us (63%)
  matrix products  354 us (19%)
  other arithmetic  103 us (6%)
  local copies, waits for them, and re-layouts  100 us (5%)
  blocking collectives  67.5 us (4%)
    all_gather x4, waiting for transfers between devices, gather_rows(): return lax.all_gather(local_rows, 'tensor', axis=0, tiled=True)  147 us
    reduce_scatter x1, waiting for transfers between devices, body(): lax.psum_scatter(up_grad, 'dp', scatter_dimension=0, tiled=True)  139 us
    reduce_scatter x1, waiting for transfers between devices, body(): lax.psum_scatter(down_grad, 'dp', scatter_dimension=1, tiled=True)  139 us
    reduce_scatter x1, waiting for transfers between devices, body(): lax.psum_scatter(gate_grad, 'dp', scatter_dimension=0, tiled=True)  138 us
    reduce_scatter x1, waiting for transfers between devices, body(): lax.psum_scatter(output_grad, 'dp', scatter_dimension=1, tiled=True)  79.5 us
    reduce_scatter x1, waiting for transfers between devices, body(): lax.psum_scatter(value_grad, 'dp', scatter_dimension=0, tiled=True)  78.9 us
    unnamed x2, blocking collectives  67.5 us
    all_gather x1, waiting for transfers between devices, body(): lax.all_gather(down_weight, 'dp', axis=1, tiled=True)  64.4 us
  transfers between devices with their start and end apart: 22, of which 18 were waited for; matrix products, arithmetic and copies ran while one was open for 27% of the time, Pallas kernels for 0%

commit v1 on v0

v1 whole, which is shorter than its diff:
```python
import functools
import math

import jax
import jax.numpy as jnp
from jax import lax
from jax.experimental import pallas as pl
from jax.experimental.pallas import tpu as pltpu
from jax.sharding import PartitionSpec as P

HD = 64
EPS = 1e-05
BF = jnp.bfloat16
F32 = jnp.float32
COLS = 256
LANES = 128
MASKED = -1e30


def settings(mib=48):
    return pltpu.CompilerParams(
        dimension_semantics=("arbitrary",), vmem_limit_bytes=mib * 1024 * 1024
    )


def cost(flops, bytes_accessed, transcendentals=0):
    return pl.CostEstimate(
        flops=int(flops), bytes_accessed=int(bytes_accessed), transcendentals=int(transcendentals)
    )


def nn(a, b):
    return jnp.dot(a, b, preferred_element_type=F32)


def nt(a, b):
    return lax.dot_general(a, b, (((1,), (1,)), ((), ())), preferred_element_type=F32)


def tree_tables(parent_row, seg_rows):
    segs = parent_row.shape[0]
    index = jnp.arange(segs, dtype=jnp.int32)
    step_up = (parent_row[:, None] == index[None, :]).astype(jnp.int32)
    eye = (index[:, None] == index[None, :]).astype(jnp.int32)
    reach = eye
    for _ in range(segs):
        up = jnp.sum(step_up[:, :, None] * reach[None, :, :], axis=1)
        reach = jnp.minimum(eye + up, 1)
    depths = jnp.sum(reach, axis=1) - 1
    bias = jnp.where(reach.T > 0, 0.0, MASKED).astype(F32)
    bias = jnp.repeat(bias, seg_rows, axis=1)
    rows = jnp.arange(segs * seg_rows, dtype=jnp.int32)
    positions = jnp.repeat(depths * seg_rows, seg_rows) + rows % seg_rows
    return bias, positions.astype(F32)


def turn_tables(positions, width):
    half = HD // 2
    rates = jnp.exp(jnp.arange(half, dtype=F32) * (-2.0 * math.log(10000.0) / HD))
    angles = positions[:, None] * rates[None, :]
    cosine, sine = jnp.cos(angles), jnp.sin(angles)
    heads = width // HD
    return (
        jnp.tile(jnp.concatenate([cosine, cosine], axis=1), (1, heads)),
        jnp.tile(jnp.concatenate([-sine, sine], axis=1), (1, heads)),
    )


def turn(x, cosine, sine):
    width = x.shape[1]
    lane = lax.broadcasted_iota(jnp.int32, x.shape, 1)
    first = (lane % HD) < HD // 2
    other = jnp.where(
        first, pltpu.roll(x, width - HD // 2, 1), pltpu.roll(x, HD // 2, 1)
    )
    return x * cosine + other * sine


def inverse_rms(x):
    return lax.rsqrt(jnp.mean(x * x, axis=1, keepdims=True) + EPS)


def project_kernel(parts, x_ref, gain_ref, cos_ref, sin_ref, w_ref, out_ref, normed_ref):
    j = pl.program_id(0)
    rows = x_ref.shape[0]
    chunk = 256

    @pl.when(j == 0)
    def _():
        for r in range(0, rows, chunk):
            x = x_ref[r : r + chunk, :].astype(F32)
            normed_ref[r : r + chunk, :] = (x * inverse_rms(x) * gain_ref[...]).astype(BF)

    @pl.when(j < 2 * parts)
    def _():
        scale = jnp.where(j < parts, 1.0 / math.sqrt(HD), 1.0).astype(F32)
        for r in range(0, rows, chunk):
            pre = nn(normed_ref[r : r + chunk, :], w_ref[...])
            rotated = turn(pre, cos_ref[r : r + chunk, :], sin_ref[r : r + chunk, :])
            out_ref[r : r + chunk, :] = rotated.astype(BF) * scale.astype(BF)

    @pl.when(j >= 2 * parts)
    def _():
        for r in range(0, rows, chunk):
            out_ref[r : r + chunk, :] = nn(normed_ref[r : r + chunk, :], w_ref[...]).astype(BF)


def project(x, gain, cosine, sine, w, width):
    rows, d = x.shape
    parts = width // COLS
    whole = lambda j: (0, 0)
    return pl.pallas_call(
        functools.partial(project_kernel, parts),
        grid=(3 * parts,),
        in_specs=[
            pl.BlockSpec((rows, d), whole),
            pl.BlockSpec((1, d), whole),
            pl.BlockSpec((rows, COLS), whole),
            pl.BlockSpec((rows, COLS), whole),
            pl.BlockSpec((d, COLS), lambda j: (0, j)),
        ],
        out_specs=[
            pl.BlockSpec((rows, COLS), lambda j: (0, j)),
            pl.BlockSpec((rows, d), whole),
        ],
        out_shape=[
            jax.ShapeDtypeStruct((rows, 3 * width), BF),
            jax.ShapeDtypeStruct((rows, d), BF),
        ],
        compiler_params=settings(),
        cost_estimate=cost(6 * rows * d * width, 2 * (2 * rows * d + 3 * d * width)),
        name="project",
    )(x, gain, cosine, sine, w)


def mask_block(block, seg_rows, bias_ref, m, u):
    cols = slice(m * block, (m + 1) * block)
    per = block // seg_rows
    return jnp.concatenate(
        [
            jnp.broadcast_to(bias_ref[u * per + i : u * per + i + 1, cols], (seg_rows, block))
            for i in range(per)
        ],
        axis=0,
    )


def causal(block):
    key = lax.broadcasted_iota(jnp.int32, (block, block), 0)
    query = lax.broadcasted_iota(jnp.int32, (block, block), 1)
    return key <= query


def attend_kernel(block, seg_rows, q_ref, k_ref, v_ref, bias_ref, out_ref, lse_ref):
    length = q_ref.shape[0]
    heads = q_ref.shape[1] // HD
    v_turned = v_ref[...].T
    for m in range(length // block):
        cols = slice(m * block, (m + 1) * block)
        outs = []
        for h in range(heads):
            lanes = slice(h * HD, (h + 1) * HD)
            q = q_ref[cols, lanes]
            scores = []
            for u in range(m + 1):
                s = nt(k_ref[u * block : (u + 1) * block, lanes], q)
                s = s + mask_block(block, seg_rows, bias_ref, m, u)
                if u == m:
                    s = jnp.where(causal(block), s, MASKED)
                scores.append(s)
            peak = scores[0].max(axis=0, keepdims=True)
            for s in scores[1:]:
                peak = jnp.maximum(peak, s.max(axis=0, keepdims=True))
            total = jnp.zeros_like(peak)
            acc = jnp.zeros((HD, block), F32)
            for u, s in enumerate(scores):
                e = jnp.exp(s - peak)
                total = total + e.sum(axis=0, keepdims=True)
                acc = acc + nn(v_turned[lanes, u * block : (u + 1) * block], e.astype(BF))
            outs.append(acc / total)
            lse_ref[0, h : h + 1, cols] = peak + jnp.log(total)
        out_ref[cols, :] = jnp.concatenate(outs, axis=0).T.astype(BF)


def attend(qkv, bias, width, seg_rows):
    length = qkv.shape[0]
    groups = width // LANES
    heads = LANES // HD
    block = 2 * seg_rows
    live = length * length // 2
    return pl.pallas_call(
        functools.partial(attend_kernel, block, seg_rows),
        grid=(groups,),
        in_specs=[
            pl.BlockSpec((length, LANES), lambda i: (0, i)),
            pl.BlockSpec((length, LANES), lambda i: (0, groups + i)),
            pl.BlockSpec((length, LANES), lambda i: (0, 2 * groups + i)),
            pl.BlockSpec(bias.shape, lambda i: (0, 0)),
        ],
        out_specs=[
            pl.BlockSpec((length, LANES), lambda i: (0, i)),
            pl.BlockSpec((1, heads, length), lambda i: (i, 0, 0)),
        ],
        out_shape=[
            jax.ShapeDtypeStruct((length, width), BF),
            jax.ShapeDtypeStruct((groups, heads, length), F32),
        ],
        compiler_params=settings(),
        cost_estimate=cost(16 * live * width, 8 * length * width, live * width // HD),
        name="attend",
    )(qkv, qkv, qkv, bias)


def attend_back_kernel(
    block,
    seg_rows,
    q_ref,
    k_ref,
    v_ref,
    o_ref,
    do_ref,
    lse_ref,
    bias_ref,
    cos_ref,
    sin_ref,
    out_ref,
    dk_ref,
    dv_ref,
):
    length = q_ref.shape[0]
    heads = q_ref.shape[1] // HD
    k_turned = k_ref[...].T
    product = (do_ref[...].astype(F32) * o_ref[...].astype(F32)).T
    deltas = [product[h * HD : (h + 1) * HD].sum(axis=0, keepdims=True) for h in range(heads)]
    for m in range(length // block):
        cols = slice(m * block, (m + 1) * block)
        grads = []
        for h in range(heads):
            lanes = slice(h * HD, (h + 1) * HD)
            q, do = q_ref[cols, lanes], do_ref[cols, lanes]
            lse = lse_ref[0, h : h + 1, cols]
            delta = deltas[h][:, cols]
            acc = jnp.zeros((HD, block), F32)
            for u in range(m + 1):
                keys = slice(u * block, (u + 1) * block)
                s = nt(k_ref[keys, lanes], q)
                p = jnp.exp(s + (mask_block(block, seg_rows, bias_ref, m, u) - lse))
                if u == m:
                    p = jnp.where(causal(block), p, 0.0)
                dp = nt(v_ref[keys, lanes], do)
                ds = (p * (dp - delta)).astype(BF)
                dv = nn(p.astype(BF), do)
                dk = nn(ds, q)
                if u == m:
                    dv_ref[h, keys, :] = dv
                    dk_ref[h, keys, :] = dk
                else:
                    dv_ref[h, keys, :] += dv
                    dk_ref[h, keys, :] += dk
                acc = acc + nn(k_turned[lanes, keys], ds)
            grads.append(acc)
        dq = jnp.concatenate(grads, axis=0).T * (1.0 / math.sqrt(HD))
        out_ref[0, cols, :] = turn(dq, cos_ref[cols, :], -sin_ref[cols, :]).astype(BF)
    for m in range(length // block):
        cols = slice(m * block, (m + 1) * block)
        dk = jnp.concatenate([dk_ref[h, cols, :] for h in range(heads)], axis=1)
        out_ref[1, cols, :] = turn(dk, cos_ref[cols, :], -sin_ref[cols, :]).astype(BF)
        out_ref[2, cols, :] = jnp.concatenate(
            [dv_ref[h, cols, :] for h in range(heads)], axis=1
        ).astype(BF)


def attend_back(qkv, attended, grad_attended, lse, bias, cosine, sine, seg_rows):
    length, width = attended.shape
    groups = width // LANES
    heads = LANES // HD
    block = 2 * seg_rows
    live = length * length // 2
    return pl.pallas_call(
        functools.partial(attend_back_kernel, block, seg_rows),
        grid=(groups,),
        in_specs=[
            pl.BlockSpec((length, LANES), lambda i: (0, i)),
            pl.BlockSpec((length, LANES), lambda i: (0, groups + i)),
            pl.BlockSpec((length, LANES), lambda i: (0, 2 * groups + i)),
            pl.BlockSpec((length, LANES), lambda i: (0, i)),
            pl.BlockSpec((length, LANES), lambda i: (0, i)),
            pl.BlockSpec((1, heads, length), lambda i: (i, 0, 0)),
            pl.BlockSpec(bias.shape, lambda i: (0, 0)),
            pl.BlockSpec((length, LANES), lambda i: (0, 0)),
            pl.BlockSpec((length, LANES), lambda i: (0, 0)),
        ],
        out_specs=pl.BlockSpec((3, length, LANES), lambda i: (0, 0, i)),
        out_shape=jax.ShapeDtypeStruct((3, length, width), BF),
        scratch_shapes=[
            pltpu.VMEM((heads, length, HD), F32),
            pltpu.VMEM((heads, length, HD), F32),
        ],
        compiler_params=settings(),
        cost_estimate=cost(40 * live * width, 16 * length * width, live * width // HD),
        name="attend_back",
    )(qkv, qkv, qkv, attended, grad_attended, lse, bias, cosine, sine)


def rms_back(grad, x, gain):
    inverse = inverse_rms(x)
    unit = x * inverse
    scaled = grad * gain
    inner = jnp.mean(scaled * unit, axis=1, keepdims=True)
    return inverse * (scaled - unit * inner), jnp.sum(grad * unit, axis=0, keepdims=True)


def ffn_kernel(
    x_ref,
    cot_ref,
    gain_ref,
    wg_ref,
    wu_ref,
    wd_ref,
    hidden_ref,
    grads_ref,
    normed_ref,
    part_ref,
    gain_part_ref,
    acc_ref,
):
    j = pl.program_id(0)
    rows = x_ref.shape[0]
    chunk = 256

    @pl.when(j == 0)
    def _():
        for r in range(0, rows, chunk):
            x = x_ref[r : r + chunk, :].astype(F32)
            normed_ref[r : r + chunk, :] = (x * inverse_rms(x) * gain_ref[...]).astype(BF)
        acc_ref[...] = jnp.zeros_like(acc_ref)

    for r in range(0, rows, chunk):
        span = slice(r, r + chunk)
        gate = nn(normed_ref[span, :], wg_ref[...])
        up = nn(normed_ref[span, :], wu_ref[...])
        grad_hidden = nn(cot_ref[span, :], wd_ref[...])
        sig = jax.nn.sigmoid(gate)
        silu = gate * sig
        hidden_ref[span, :] = (silu * up).astype(BF)
        grad_gate = (grad_hidden * up * sig * (1.0 + gate * (1.0 - sig))).astype(BF)
        grad_up = (grad_hidden * silu).astype(BF)
        grads_ref[0, span, :] = grad_gate
        grads_ref[1, span, :] = grad_up
        acc_ref[span, :] += nt(grad_gate, wg_ref[...]) + nt(grad_up, wu_ref[...])

    @pl.when(j == pl.num_programs(0) - 1)
    def _():
        gain_part = jnp.zeros_like(gain_part_ref)
        for r in range(0, rows, chunk):
            span = slice(r, r + chunk)
            part, piece = rms_back(acc_ref[span, :], x_ref[span, :].astype(F32), gain_ref[...])
            part_ref[span, :] = part.astype(BF)
            gain_part = gain_part + piece
        gain_part_ref[...] = gain_part


def ffn(x, cot, gain, w, start, hidden_width):
    rows, d = x.shape
    steps = hidden_width // COLS
    first = start // COLS
    whole = lambda j: (0, 0)
    return pl.pallas_call(
        ffn_kernel,
        grid=(steps,),
        in_specs=[
            pl.BlockSpec((rows, d), whole),
            pl.BlockSpec((rows, d), whole),
            pl.BlockSpec((1, d), whole),
            pl.BlockSpec((d, COLS), lambda j: (0, first + j)),
            pl.BlockSpec((d, COLS), lambda j: (0, first + steps + j)),
            pl.BlockSpec((d, COLS), lambda j: (0, first + 2 * steps + j)),
        ],
        out_specs=[
            pl.BlockSpec((rows, COLS), lambda j: (0, j)),
            pl.BlockSpec((2, rows, COLS), lambda j: (0, 0, j)),
            pl.BlockSpec((rows, d), whole),
            pl.BlockSpec((rows, d), whole),
            pl.BlockSpec((1, d), whole),
        ],
        out_shape=[
            jax.ShapeDtypeStruct((rows, hidden_width), BF),
            jax.ShapeDtypeStruct((2, rows, hidden_width), BF),
            jax.ShapeDtypeStruct((rows, d), BF),
            jax.ShapeDtypeStruct((rows, d), BF),
            jax.ShapeDtypeStruct((1, d), F32),
        ],
        scratch_shapes=[pltpu.VMEM((rows, d), F32)],
        compiler_params=settings(),
        cost_estimate=cost(
            10 * rows * d * hidden_width,
            6 * d * hidden_width + 8 * rows * d + 6 * rows * hidden_width,
            rows * hidden_width,
        ),
        name="ffn",
    )(x, cot, gain, w, w, w)


def input_grad_kernel(x_ref, gain_ref, g_ref, w_ref, part_ref, gain_part_ref, acc_ref):
    j = pl.program_id(0)
    rows = x_ref.shape[0]
    chunk = 256

    @pl.when(j == 0)
    def _():
        acc_ref[...] = jnp.zeros_like(acc_ref)

    for r in range(0, rows, chunk):
        acc_ref[r : r + chunk, :] += nt(g_ref[0, r : r + chunk, :], w_ref[...])

    @pl.when(j == pl.num_programs(0) - 1)
    def _():
        gain_part = jnp.zeros_like(gain_part_ref)
        for r in range(0, rows, chunk):
            span = slice(r, r + chunk)
            part, piece = rms_back(acc_ref[span, :], x_ref[span, :].astype(F32), gain_ref[...])
            part_ref[span, :] = part.astype(BF)
            gain_part = gain_part + piece
        gain_part_ref[...] = gain_part


def input_grad(x, gain, grads, w):
    rows, d = x.shape
    kinds, _, width = grads.shape
    per = width // COLS
    whole = lambda j: (0, 0)
    return pl.pallas_call(
        input_grad_kernel,
        grid=(kinds * per,),
        in_specs=[
            pl.BlockSpec((rows, d), whole),
            pl.BlockSpec((1, d), whole),
            pl.BlockSpec((1, rows, COLS), lambda j: (j // per, 0, j % per)),
            pl.BlockSpec((d, COLS), lambda j: (0, j)),
        ],
        out_specs=[pl.BlockSpec((rows, d), whole), pl.BlockSpec((1, d), whole)],
        out_shape=[jax.ShapeDtypeStruct((rows, d), BF), jax.ShapeDtypeStruct((1, d), F32)],
        scratch_shapes=[pltpu.VMEM((rows, d), F32)],
        compiler_params=settings(),
        cost_estimate=cost(2 * rows * d * kinds * width, 2 * kinds * width * (rows + d)),
        name="input_grad",
    )(x, gain, grads, w)


def weight_grad_kernel(count, *refs):
    lefts, rights = refs[:count], refs[count : 2 * count]
    out_ref, turned_ref = refs[-2], refs[-1]
    j = pl.program_id(0)
    chunk = 256

    @pl.when(j == 0)
    def _():
        start = 0
        for left in lefts:
            for r in range(0, left.shape[0], chunk):
                turned_ref[:, start + r : start + r + chunk] = left[r : r + chunk, :].T
            start += left.shape[0]

    d = out_ref.shape[0]
    for c in range(0, d, chunk):
        total, start = None, 0
        for right in rights:
            rows = right.shape[1]
            piece = nn(turned_ref[c : c + chunk, start : start + rows], right[0])
            total = piece if total is None else total + piece
            start += rows
        out_ref[c : c + chunk, :] = total.astype(BF)


def weight_grad(lefts, rights):
    d = lefts[0].shape[1]
    kinds, _, width = rights[0].shape
    rows = sum(left.shape[0] for left in lefts)
    per = width // COLS
    return pl.pallas_call(
        functools.partial(weight_grad_kernel, len(lefts)),
        grid=(kinds * per,),
        in_specs=[pl.BlockSpec(left.shape, lambda j: (0, 0)) for left in lefts]
        + [
            pl.BlockSpec((1, right.shape[1], COLS), lambda j: (j // per, 0, j % per))
            for right in rights
        ],
        out_specs=pl.BlockSpec((d, COLS), lambda j: (0, j)),
        out_shape=jax.ShapeDtypeStruct((d, kinds * width), BF),
        scratch_shapes=[pltpu.VMEM((d, rows), BF)],
        compiler_params=settings(),
        cost_estimate=cost(2 * rows * d * kinds * width, 2 * kinds * width * (rows + d)),
        name="weight_grad",
    )(*lefts, *rights)


def swap(x):
    return lax.ppermute(x, "tensor", [(0, 1), (1, 0)])


def body(
    tokens,
    parents,
    attn_gain,
    ffn_gain,
    query_weight,
    key_weight,
    value_weight,
    output_weight,
    gate_weight,
    up_weight,
    down_weight,
    cotangent,
):
    half, d = tokens.shape
    length = 2 * half
    width = query_weight.shape[1]
    hidden_width = gate_weight.shape[1]
    seg_rows = length // parents.shape[1]
    mine = lax.axis_index("tensor")
    own_start = mine * half
    other_start = (1 - mine) * half

    def place(own, other):
        full = jnp.zeros((length, own.shape[1]), own.dtype)
        full = lax.dynamic_update_slice(full, own, (own_start, 0))
        return lax.dynamic_update_slice(full, other, (other_start, 0))

    def own_rows(full):
        return lax.dynamic_slice_in_dim(full, own_start, half, 0)

    def other_rows(full):
        return lax.dynamic_slice_in_dim(full, other_start, half, 0)

    def gather(shard):
        return lax.all_gather(shard, "dp", axis=0, tiled=True)

    attn_row = attn_gain[None, :]
    ffn_row = ffn_gain[None, :]

    wqkv = gather(jnp.concatenate([query_weight, key_weight, value_weight], axis=1))
    wrest = gather(
        jnp.concatenate([output_weight.T, gate_weight, up_weight, down_weight.T], axis=1)
    )

    bias, positions = tree_tables(parents[0], seg_rows)
    cosine, sine = turn_tables(positions, COLS)
    rows_all = place(tokens, swap(tokens))
    cot_other = swap(cotangent)

    qkv, normed_one = project(rows_all, attn_row, cosine, sine, wqkv, width)
    attended, lse = attend(qkv, bias, width, seg_rows)
    out_turned = wrest[:, :width]
    send = nt(other_rows(attended), out_turned).astype(BF)
    received = swap(send)
    middle = (
        tokens.astype(F32) + nt(own_rows(attended), out_turned) + received.astype(F32)
    ).astype(BF)
    middle_other = swap(middle)

    hid_own, gg_own, normed_own, part_own, gp_own = ffn(
        middle, cotangent, ffn_row, wrest, width, hidden_width
    )
    hid_other, gg_other, normed_other, part_other, gp_other = ffn(
        middle_other, cot_other, ffn_row, wrest, width, hidden_width
    )
    gp = gp_own + gp_other
    part_received = swap(part_other)
    gp_received = swap(gp)
    down_turned_grad = weight_grad([cotangent, cot_other], [hid_own[None], hid_other[None]])
    gate_up_grad = weight_grad([normed_own, normed_other], [gg_own, gg_other])
    grad_middle = (
        cotangent.astype(F32) + part_own.astype(F32) + part_received.astype(F32)
    ).astype(BF)
    grad_middle_other = swap(grad_middle)

    down_turned = wrest[:, width + 2 * hidden_width :]
    out_received = swap(nt(hid_other, down_turned).astype(BF))
    block_out = (
        middle.astype(F32) + nt(hid_own, down_turned) + out_received.astype(F32)
    ).astype(BF)

    def scatter(grad):
        return lax.psum_scatter(grad, "dp", scatter_dimension=0, tiled=True).astype(F32)

    def gain_block(gain_sum):
        return jnp.broadcast_to(gain_sum.astype(BF).T, (d, LANES))

    down_grad = scatter(down_turned_grad).T
    gate_up = scatter(jnp.concatenate([gate_up_grad, gain_block(gp + gp_received)], axis=1))
    gate_grad = gate_up[:, :hidden_width]
    up_grad = gate_up[:, hidden_width : 2 * hidden_width]

    grad_attended = place(
        nn(grad_middle, out_turned).astype(BF), nn(grad_middle_other, out_turned).astype(BF)
    )
    grads = attend_back(
        qkv, attended, grad_attended, lse, bias, cosine[:, :LANES], sine[:, :LANES], seg_rows
    )
    part, gain_part = input_grad(rows_all, attn_row, grads, wqkv)
    tokens_received = swap(other_rows(part))
    gain_received = swap(gain_part)
    qkv_grad = weight_grad([normed_one], [grads])
    out_turned_grad = weight_grad(
        [grad_middle, grad_middle_other], [own_rows(attended)[None], other_rows(attended)[None]]
    )
    token_grad = (
        grad_middle.astype(F32) + own_rows(part).astype(F32) + tokens_received.astype(F32)
    ).astype(BF)
    last = scatter(
        jnp.concatenate(
            [qkv_grad, out_turned_grad, gain_block(gain_part + gain_received)], axis=1
        )
    )
    gain_rows = d // lax.axis_size("dp") // 2

    def gain_piece(column):
        return lax.dynamic_slice_in_dim(column[:, 0], mine * gain_rows, gain_rows, 0)

    return (
        block_out,
        token_grad,
        last[:, :width],
        last[:, width : 2 * width],
        last[:, 2 * width : 3 * width],
        last[:, 3 * width : 4 * width].T,
        gate_grad,
        up_grad,
        down_grad,
        gain_piece(last[:, 4 * width :]),
        gain_piece(gate_up[:, 2 * hidden_width :]),
    )


def solution(mesh):
    rows = P(("dp", "tensor"), None)
    tall = P("dp", "tensor")
    wide = P("tensor", "dp")
    return jax.shard_map(
        body,
        mesh=mesh,
        in_specs=(
            rows, P("dp", None), P(), P(), tall, tall, tall, wide, tall, tall, wide, rows,
        ),
        out_specs=(
            rows, rows, tall, tall, tall, wide, tall, tall, wide,
            P(("dp", "tensor")), P(("dp", "tensor")),
        ),
        check_vma=False,
    )
```

time: 1830 us -> 777 us (0.42)
  waiting for transfers between devices: 1160 us -> 448 us
  matrix products: 354 us -> 26.5 us
  Pallas kernels: 0 us -> 196 us
  local copies, waits for them, and re-layouts: 100 us -> 30.8 us
  blocking collectives: 67.5 us -> 0 us
  other arithmetic: 103 us -> 36.6 us
    reduce_scatter x11 -> x3, waiting for transfers between devices: 717 us -> 136 us  [scatter(): lax.psum_scatter(grad, 'dp', scatter_dimension=0, tiled=True).astype(F32)]
    all_gather x11 -> x2, waiting for transfers between devices: 439 us -> 100 us  [gather(): return lax.all_gather(shard, 'dp', axis=0, tiled=True)]
    dot_general x39 -> x6, matrix products: 354 us -> 26.5 us  [the longest x4 20.3 us: nt(): lax.dot_general(a, b, (((1,), (1,)), ((), ())), preferred_element_type=F32)]
    ppermute x0 -> x10, waiting for transfers between devices: none -> 212 us  [swap(): return lax.ppermute(x, 'tensor', [(0, 1), (1, 0)])]
    pallas_call x0 -> x10, Pallas kernels: none -> 196 us  [the longest x2 56.6 us: ffn(): pl.pallas_call(ffn_kernel, grid=(steps,), in_specs=[pl.BlockSpec((rows, d...]
    unnamed x2 -> x0, blocking collectives: 67.5 us -> none
    dynamic_update_slice x4 -> x2, local copies, waits for them, and re-layouts: 63.5 us -> 5.55 us  [the longest x1 2.79 us: place(): full = lax.dynamic_update_slice(full, own, (own_start, 0))]
    convert_element_type x12 -> x8, other arithmetic: 64.7 us -> 9.03 us  [the longest x1 3.23 us: body(): block_out = (middle.astype(F32) + nt(hid_own, down_turned) + out_received...]
  transfers between devices with their start and end apart: 22 -> 15, of which waited for: 18 -> 10; matrix products, arithmetic and copies ran while one was open for 27% -> 9% of each run, Pallas kernels for 0% -> 20%
where the time goes in v1:
time: 777 us; the launch traced here: 767 us
  waiting for transfers between devices  448 us (58%)
  Pallas kernels  196 us (25%)
  other arithmetic  36.6 us (5%)
  local copies, waits for them, and re-layouts  30.8 us (4%)
  matrix products  26.5 us (3%)
  between operations  14.6 us (2%)
  starting transfers between devices  14 us (2%)
    ppermute x10, waiting for transfers between devices, swap(): return lax.ppermute(x, 'tensor', [(0, 1), (1, 0)])  212 us
    reduce_scatter x3, waiting for transfers between devices, scatter(): lax.psum_scatter(grad, 'dp', scatter_dimension=0, tiled=True).astype(F32)  136 us
    all_gather x2, waiting for transfers between devices, gather(): return lax.all_gather(shard, 'dp', axis=0, tiled=True)  100 us
    pallas_call x2, Pallas kernels, ffn(): pl.pallas_call(ffn_kernel, grid=(steps,), in_specs=[pl.BlockSpec((rows, d...  56.6 us
    pallas_call x4, Pallas kernels, weight_grad(): pl.pallas_call(functools.partial(weight_grad_kernel, len(lefts)), grid=(k...  52.6 us
    pallas_call x1, Pallas kernels, attend_back(): pl.pallas_call(functools.partial(attend_back_kernel, block, seg_rows), gr...  33.9 us
    pallas_call x1, Pallas kernels, attend(): pl.pallas_call(functools.partial(attend_kernel, block, seg_rows), grid=(g...  21.6 us
    dot_general x4, matrix products, nt(): lax.dot_general(a, b, (((1,), (1,)), ((), ())), preferred_element_type=F32)  20.3 us
  transfers between devices with their start and end apart: 15, of which 10 were waited for; matrix products, arithmetic and copies ran while one was open for 9% of the time, Pallas kernels for 20%

profile of v1, /device:TPU:0, one launch (start us, length us, event | category | flops | bytes accessed | tf_op | source)
XLA Modules:
  0.0 767.3 jit_solution(4807936790959637529)
XLA Ops:
  22.2 27.1 %collective-permute-done = bf16[512,1536]{1,0:T(8,128)(2,1)} collective-permute-done((bf16[512,1536]{1,0:T(8,128)(2,1)}, bf16[512,1536]{1,0:T(8,128)(2,1)}, u32[]{:S(2)}, u32[]{:S(2)}) %collective-permute-start) | collective-permute-done | bytes 1572896 | tf_op jit(solution)/shard_map/ppermute | solution.py:498
  52.1 28.1 %all-gather.3.cloned.1.call-done.w_ref = bf16[1536,2304]{1,0:T(8,128)(2,1)} async-done(((bf16[96,2304]{1,0:T(8,128)(2,1)}), bf16[1536,2304]{1,0:T(8,128)(2,1)}) %all-gather.3.cloned.1.call-update) | async-done | bytes 7077904 | tf_op jit(solution)/shard_map/all_gather | solution.py:536
  80.2 15.4 %project.1 = (bf16[1024,2304]{1,0:T(8,128)(2,1)}, bf16[1024,1536]{1,0:T(8,128)(2,1)S(1)}) custom-call(bf16[1024,1536]{1,0:T(8,128)(2,1)} %constant_dynamic-update-slice_fusion.x_ref, f32[1,1536]{1,0:T(1,128)S(1)} %broadcast_in_dim.37.gain_ref, f32[1024,256]{1,0:T(8,128)S(1)} %copy.45.cos_ref, f32[1024,256]{1,0:T(8,128)S(1)} %copy.46.sin_ref, ...), custom_call_target="tpu_custom_call" | custom-call | flops 7247757312 | bytes 13369344 | tf_op jit(solution)/shard_map/project/pallas_call | solution.py:112
  97.3 21.6 %attend.1 = (bf16[1024,768]{1,0:T(8,128)(2,1)S(1)}, f32[6,2,1024]{2,1,0:T(2,128)S(1)}) custom-call(bf16[1024,2304]{1,0:T(8,128)(2,1)} %get-tuple-element.27.q_ref.k_ref.v_ref, bf16[1024,2304]{1,0:T(8,128)(2,1)} %get-tuple-element.27.q_ref.k_ref.v_ref, bf16[1024,2304]{1,0:T(8,128)(2,1)} %get-tuple-element.27.q_ref.k_ref.v_ref, ...), custom_call_target="tpu_custom_call" | custom-call | flops 6442450944 | bytes 6291456 | tf_op jit(solution)/shard_map/attend/pallas_call | solution.py:191
  118.9 72.1 %all-gather.5.cloned.1.call-done.wg_ref.wu_ref.wd_ref = bf16[1536,6912]{1,0:T(8,128)(2,1)} async-done(((bf16[96,6912]{1,0:T(8,128)(2,1)}), bf16[1536,6912]{1,0:T(8,128)(2,1)}) %all-gather.5.cloned.1.call-update) | async-done | bytes 21233680 | tf_op jit(solution)/shard_map/all_gather | solution.py:536
  196.2 35.2 %collective-permute-done.1 = bf16[512,1536]{1,0:T(8,128)(2,1)S(1)} collective-permute-done((bf16[512,1536]{1,0:T(8,128)(2,1)S(1)}, bf16[512,1536]{1,0:T(8,128)(2,1)S(1)}, u32[]{:S(2)}, u32[]{:S(2)}) %collective-permute-start.1) | collective-permute-done | bytes 1572896 | tf_op jit(solution)/shard_map/ppermute | solution.py:498
  236.6 28.4 %ffn.2 = (bf16[512,2048]{1,0:T(8,128)(2,1)}, bf16[2,512,2048]{2,1,0:T(8,128)(2,1)}, bf16[512,1536]{1,0:T(8,128)(2,1)S(1)}, bf16[512,1536]{1,0:T(8,128)(2,1)S(1)}, f32[1,1536]{1,0:T(1,128)S(1)}) custom-call(bf16[512,1536]{1,0:T(8,128)(2,1)S(1)} %add_convert_fusion.3.x_ref, bf16[512,1536]{1,0:T(8,128)(2,1)} %refs_0_.1, ...), custom_call_target="tpu_custom_call" | custom-call | flops 16106127360 | bytes 31457280 | tf_op jit(solution)/shard_map/ffn/pallas_call | solution.py:368
  267.3 30.8 %collective-permute-done.2.x_ref = bf16[512,1536]{1,0:T(8,128)(2,1)S(1)} collective-permute-done((bf16[512,1536]{1,0:T(8,128)(2,1)S(1)}, bf16[512,1536]{1,0:T(8,128)(2,1)S(1)}, u32[]{:S(2)}, u32[]{:S(2)}) %collective-permute-start.2) | collective-permute-done | bytes 1572896 | tf_op jit(solution)/shard_map/ppermute | solution.py:498
  298.2 28.2 %ffn.3 = (bf16[512,2048]{1,0:T(8,128)(2,1)}, bf16[2,512,2048]{2,1,0:T(8,128)(2,1)}, bf16[512,1536]{1,0:T(8,128)(2,1)S(1)}, bf16[512,1536]{1,0:T(8,128)(2,1)S(1)}, f32[1,1536]{1,0:T(1,128)S(1)}) custom-call(bf16[512,1536]{1,0:T(8,128)(2,1)S(1)} %collective-permute-done.2.x_ref, bf16[512,1536]{1,0:T(8,128)(2,1)} %copy-done.9, ...), custom_call_target="tpu_custom_call" | custom-call | flops 16106127360 | bytes 31457280 | tf_op jit(solution)/shard_map/ffn/pallas_call | solution.py:368
  329.5 12.1 %weight_grad.7 = bf16[1536,2048]{1,0:T(8,128)(2,1)} custom-call(bf16[512,1536]{1,0:T(8,128)(2,1)} %refs_0_.1, bf16[512,1536]{1,0:T(8,128)(2,1)S(1)} %copy-done.10, bf16[1,512,2048]{2,1,0:T(8,128)(2,1)S(1)} %bitcast.31, bf16[1,512,2048]{2,1,0:T(8,128)(2,1)} %bitcast.37), custom_call_target="tpu_custom_call" | custom-call | flops 6442450944 | bytes 10485760 | tf_op jit(solution)/shard_map/weight_grad/pallas_call | solution.py:480
  344.5 34.3 %collective-permute-done.5 = bf16[512,1536]{1,0:T(8,128)(2,1)S(1)} collective-permute-done((bf16[512,1536]{1,0:T(8,128)(2,1)S(1)}, bf16[512,1536]{1,0:T(8,128)(2,1)S(1)}, u32[]{:S(2)}, u32[]{:S(2)}) %collective-permute-start.5) | collective-permute-done | bytes 1572896 | tf_op jit(solution)/shard_map/ppermute | solution.py:498
  386.4 30.0 %collective-permute-done.6.refs_1_ = bf16[512,1536]{1,0:T(8,128)(2,1)S(1)} collective-permute-done((bf16[512,1536]{1,0:T(8,128)(2,1)S(1)}, bf16[512,1536]{1,0:T(8,128)(2,1)S(1)}, u32[]{:S(2)}, u32[]{:S(2)}) %collective-permute-start.6) | collective-permute-done | bytes 1572896 | tf_op jit(solution)/shard_map/ppermute | solution.py:498
  419.5 33.9 %attend_back.1.g_ref.refs_1_ = bf16[3,1024,768]{2,1,0:T(8,128)(2,1)} custom-call(bf16[1024,2304]{1,0:T(8,128)(2,1)} %get-tuple-element.27.q_ref.k_ref.v_ref, bf16[1024,2304]{1,0:T(8,128)(2,1)} %get-tuple-element.27.q_ref.k_ref.v_ref, bf16[1024,2304]{1,0:T(8,128)(2,1)} %get-tuple-element.27.q_ref.k_ref.v_ref, bf16[1024,768]{1,0:T(8,128)(2,1)S(1)} %copy-done.7, ...), custom_call_target="tpu_custom_call" | custom-call | flops 16106127360 | bytes 12582912 | tf_op jit(solution)/shard_map/attend_back/pallas_call | solution.py:279
  453.4 16.3 %input_grad.1 = (bf16[1024,1536]{1,0:T(8,128)(2,1)S(1)}, f32[1,1536]{1,0:T(1,128)S(1)}) custom-call(bf16[1024,1536]{1,0:T(8,128)(2,1)} %constant_dynamic-update-slice_fusion.x_ref, f32[1,1536]{1,0:T(1,128)S(1)} %broadcast_in_dim.37.gain_ref, bf16[3,1024,768]{2,1,0:T(8,128)(2,1)} %attend_back.1.g_ref.refs_1_, ...), custom_call_target="tpu_custom_call" | custom-call | flops 7247757312 | bytes 11796480 | tf_op jit(solution)/shard_map/input_grad/pallas_call | solution.py:432
  472.8 13.3 %weight_grad.4 = bf16[1536,2304]{1,0:T(8,128)(2,1)} custom-call(bf16[1024,1536]{1,0:T(8,128)(2,1)S(1)} %copy-done.20, bf16[3,1024,768]{2,1,0:T(8,128)(2,1)} %attend_back.1.g_ref.refs_1_), custom_call_target="tpu_custom_call" | custom-call | flops 7247757312 | bytes 11796480 | tf_op jit(solution)/shard_map/weight_grad/pallas_call | solution.py:480
  486.1 5.3 weight_grad.5
  491.7 9.2 %pad_maximum_fusion.1 = bf16[1536,3200]{1,0:T(8,128)(2,1)} fusion(bf16[1536,128]{1,0:T(8,128)(2,1)S(1)} %broadcast_in_dim.84, bf16[1536,768]{1,0:T(8,128)(2,1)} %weight_grad.5, bf16[1536,2304]{1,0:T(8,128)(2,1)} %weight_grad.4), kind=kLoop, calls=%fused_computation.1 | loop fusion | flops 29491200 | bytes 19660800 | tf_op jit(solution)/shard_map/concatenate | solution.py:611
  504.5 21.8 %weight_grad.6 = bf16[1536,4096]{1,0:T(8,128)(2,1)} custom-call(bf16[512,1536]{1,0:T(8,128)(2,1)S(1)} %copy-done.14, bf16[512,1536]{1,0:T(8,128)(2,1)S(1)} %copy-done.16, bf16[2,512,2048]{2,1,0:T(8,128)(2,1)} %get-tuple-element.39.refs_2_, bf16[2,512,2048]{2,1,0:T(8,128)(2,1)} %get-tuple-element.40.refs_3_), custom_call_target="tpu_custom_call" | custom-call | flops 12884901888 | bytes 20971520 | tf_op jit(solution)/shard_map/weight_grad/pallas_call | solution.py:480
  526.6 10.7 %pad_maximum_fusion = bf16[1536,4224]{1,0:T(8,128)(2,1)} fusion(bf16[1536,128]{1,0:T(8,128)(2,1)S(1)} %broadcast_in_dim.86, bf16[1536,4096]{1,0:T(8,128)(2,1)} %weight_grad.6), kind=kLoop, calls=%fused_computation | loop fusion | flops 25952256 | bytes 25952256 | tf_op jit(solution)/shard_map/concatenate | solution.py:590
  537.4 8.0 %fusion.4 = bf16[512,1536]{1,0:T(8,128)(2,1)} fusion(bf16[512,2048]{1,0:T(8,128)(2,1)} %get-tuple-element.30, bf16[1536,6912]{1,0:T(8,128)(2,1)} %all-gather.5.cloned.1.call-done.wg_ref.wu_ref.wd_ref), kind=kOutput, calls=%fused_computation.11 | convolution fusion | flops 3222011904 | bytes 9961472 | tf_op jit(solution)/shard_map/dot_general | solution.py:37
  549.1 5.6 fusion.2
  554.7 28.3 %collective-permute-done.4 = bf16[512,1536]{1,0:T(8,128)(2,1)} collective-permute-done((bf16[512,1536]{1,0:T(8,128)(2,1)}, bf16[512,1536]{1,0:T(8,128)(2,1)}, u32[]{:S(2)}, u32[]{:S(2)}) %collective-permute-start.4) | collective-permute-done | bytes 1572896 | tf_op jit(solution)/shard_map/ppermute | solution.py:498
  586.2 26.6 %collective-permute-done.7 = bf16[512,1536]{1,0:T(8,128)(2,1)S(1)} collective-permute-done((bf16[512,1536]{1,0:T(8,128)(2,1)S(1)}, bf16[512,1536]{1,0:T(8,128)(2,1)S(1)}, u32[]{:S(2)}, u32[]{:S(2)}) %collective-permute-start.7) | collective-permute-done | bytes 1572896 | tf_op jit(solution)/shard_map/ppermute | solution.py:498
  620.8 135.8 %reduce-scatter.6.cloned.1.call-done = bf16[96,4224]{1,0:T(8,128)(2,1)} async-done(((bf16[1536,4224]{1,0:T(8,128)(2,1)}), bf16[96,4224]{1,0:T(8,128)(2,1)}) %reduce-scatter.6.cloned.1.call-update) | async-done | bytes 811024 | tf_op jit(solution)/shard_map/reduce_scatter | solution.py:584
  (139 shorter events, 74.4 us)
Async XLA Ops:
  7.2 73.0 %all-gather.3.cloned.1.call-start = ((), (), s32[]{:S(2)}) async-start(), calls=%async_computation.3 | async-start | bytes 7520256 | tf_op jit(solution)/shard_map/all_gather | solution.py:536
  9.1 181.9 %all-gather.5.cloned.1.call-start = ((), (), s32[]{:S(2)}) async-start(), calls=%async_computation.4 | async-start | bytes 22560768 | tf_op jit(solution)/shard_map/all_gather | solution.py:536
  11.6 603.0 %reduce-scatter.8.cloned.1.call-start = ((), (), s32[]{:S(2)}) async-start(), calls=%async_computation.7 | async-start | bytes 6684672 | tf_op jit(solution)/shard_map/reduce_scatter | solution.py:584
  11.6 37.7 %collective-permute-start = (bf16[512,1536]{1,0:T(8,128)(2,1)}, bf16[512,1536]{1,0:T(8,128)(2,1)}, u32[]{:S(2)}, u32[]{:S(2)}) collective-permute-start(bf16[512,1536]{1,0:T(8,128)(2,1)} %param.12), channel_id=1, source_target_pairs={{0,1},{1,0},{2,3},{3,2},{4,5},{5,4},{6,7},{7,6},{8,9},{9,8},{10,11... | collective-permute-start | bytes 4718600 | tf_op jit(solution)/shard_map/ppermute | solution.py:498
  16.9 63.4 %copy-start.2 = (f32[1024,256]{1,0:T(8,128)}, f32[1024,256]{1,0:T(8,128)S(1)}, u32[]{:S(2)}) copy-start(f32[1024,256]{1,0:T(8,128)S(1)} %copy.45.cos_ref) | copy-start | bytes 3145732
  17.4 62.9 %copy-start.4 = (f32[1024,256]{1,0:T(8,128)}, f32[1024,256]{1,0:T(8,128)S(1)}, u32[]{:S(2)}) copy-start(f32[1024,256]{1,0:T(8,128)S(1)} %copy.46.sin_ref) | copy-start | bytes 3145732
  118.9 112.5 %copy-start.6 = (bf16[1024,768]{1,0:T(8,128)(2,1)}, bf16[1024,768]{1,0:T(8,128)(2,1)S(1)}, u32[]{:S(2)}) copy-start(bf16[1024,768]{1,0:T(8,128)(2,1)S(1)} %get-tuple-element.28.o_ref) | copy-start | bytes 4718596
  194.1 42.5 %copy-start.23 = (f32[1536]{0:T(1024)S(1)}, f32[1536]{0:T(1024)}, u32[]{:S(2)}) copy-start(f32[1536]{0:T(1024)} %param.15) | copy-start | bytes 18436
  194.1 37.3 %collective-permute-start.1 = (bf16[512,1536]{1,0:T(8,128)(2,1)S(1)}, bf16[512,1536]{1,0:T(8,128)(2,1)S(1)}, u32[]{:S(2)}, u32[]{:S(2)}) collective-permute-start(bf16[512,1536]{1,0:T(8,128)(2,1)S(1)} %convolution_convert_fusion), channel_id=1, source_target_pairs={{0,1},{1,0},{2,3},{3,2},{4,5},{5,4},{6,7},{7,6},{8,9},{9,8},{10,11... | collective-permute-start | bytes 4718600 | tf_op jit(solution)/shard_map/ppermute | solution.py:498
  195.7 71.7 %collective-permute-start.3 = (bf16[512,1536]{1,0:T(8,128)(2,1)}, bf16[512,1536]{1,0:T(8,128)(2,1)S(1)}, u32[]{:S(2)}, u32[]{:S(2)}) collective-permute-start(bf16[512,1536]{1,0:T(8,128)(2,1)} %refs_0_.1), channel_id=1, source_target_pairs={{0,1},{1,0},{2,3},{3,2},{4,5},{5,4},{6,7},{7,6},{8,9},{9,8},{10,11... | collective-permute-start | bytes 4718600 | tf_op jit(solution)/shard_map/ppermute | solution.py:498
  235.1 63.1 %collective-permute-start.2 = (bf16[512,1536]{1,0:T(8,128)(2,1)S(1)}, bf16[512,1536]{1,0:T(8,128)(2,1)S(1)}, u32[]{:S(2)}, u32[]{:S(2)}) collective-permute-start(bf16[512,1536]{1,0:T(8,128)(2,1)S(1)} %add_convert_fusion.3.x_ref), channel_id=1, source_target_pairs={{0,1},{1,0},{2,3},{3,2},{4,5},{5,4},{6,7},{7,6},{8,9},{9,8},{10,11... | collective-permute-start | bytes 4718600 | tf_op jit(solution)/shard_map/ppermute | solution.py:498
  267.3 60.2 %copy-start.11 = (bf16[512,2048]{1,0:T(8,128)(2,1)S(1)}, bf16[512,2048]{1,0:T(8,128)(2,1)}, u32[]{:S(2)}) copy-start(bf16[512,2048]{1,0:T(8,128)(2,1)} %get-tuple-element.29) | copy-start | bytes 6291460
  267.3 30.8 %copy-start.9 = (bf16[512,1536]{1,0:T(8,128)(2,1)}, bf16[512,1536]{1,0:T(8,128)(2,1)S(1)}, u32[]{:S(2)}) copy-start(bf16[512,1536]{1,0:T(8,128)(2,1)S(1)} %collective-permute-done.3.cot_ref.refs_1_) | copy-start | bytes 4718596
  327.5 14.1 %copy-start.15 = (bf16[512,1536]{1,0:T(8,128)(2,1)}, bf16[512,1536]{1,0:T(8,128)(2,1)S(1)}, u32[]{:S(2)}) copy-start(bf16[512,1536]{1,0:T(8,128)(2,1)S(1)} %get-tuple-element.38.refs_1_) | copy-start | bytes 4718596
  341.6 274.8 %reduce-scatter.4.cloned.1.call-start = ((), (), s32[]{:S(2)}) async-start(), calls=%async_computation.5 | async-start | bytes 10444800 | tf_op jit(solution)/shard_map/reduce_scatter | solution.py:584
  343.0 35.8 %collective-permute-start.5 = (bf16[512,1536]{1,0:T(8,128)(2,1)S(1)}, bf16[512,1536]{1,0:T(8,128)(2,1)S(1)}, u32[]{:S(2)}, u32[]{:S(2)}) collective-permute-start(bf16[512,1536]{1,0:T(8,128)(2,1)S(1)} %copy-done.18), channel_id=1, source_target_pairs={{0,1},{1,0},{2,3},{3,2},{4,5},{5,4},{6,7},{7,6},{8,9},{9,8},{10,11... | collective-permute-start | bytes 4718600 | tf_op jit(solution)/shard_map/ppermute | solution.py:498
  381.4 35.0 %collective-permute-start.6 = (bf16[512,1536]{1,0:T(8,128)(2,1)S(1)}, bf16[512,1536]{1,0:T(8,128)(2,1)S(1)}, u32[]{:S(2)}, u32[]{:S(2)}) collective-permute-start(bf16[512,1536]{1,0:T(8,128)(2,1)S(1)} %add_convert_fusion.1.refs_0_), channel_id=1, source_target_pairs={{0,1},{1,0},{2,3},{3,2},{4,5},{5,4},{6,7},{7,6},{8,9},{9,8},{10,11... | collective-permute-start | bytes 4718600 | tf_op jit(solution)/shard_map/ppermute | solution.py:498
  453.4 19.4 %copy-start.20 = (bf16[1024,1536]{1,0:T(8,128)(2,1)S(1)}, bf16[1024,1536]{1,0:T(8,128)(2,1)}, u32[]{:S(2)}) copy-start(bf16[1024,1536]{1,0:T(8,128)(2,1)} %copy-done.19) | copy-start | bytes 9437188
  471.3 20.1 %collective-permute-start.8 = (f32[1,1536]{1,0:T(1,128)S(1)}, f32[1,1536]{1,0:T(1,128)S(1)}, u32[]{:S(2)}, u32[]{:S(2)}) collective-permute-start(f32[1,1536]{1,0:T(1,128)S(1)} %get-tuple-element.36), channel_id=1, source_target_pairs={{0,1},{1,0},{2,3},{3,2},{4,5},{5,4},{6,7},{7,6},{8,9},{9,8},{10,11... | collective-permute-start | bytes 18440 | tf_op jit(solution)/shard_map/ppermute | solution.py:498
  501.0 255.6 %reduce-scatter.6.cloned.1.call-start = ((), (), s32[]{:S(2)}) async-start(), calls=%async_computation.6 | async-start | bytes 13787136 | tf_op jit(solution)/shard_map/reduce_scatter | solution.py:584
  501.0 25.3 %collective-permute-start.9 = (f32[1,1536]{1,0:T(1,128)S(1)}, f32[1,1536]{1,0:T(1,128)S(1)}, u32[]{:S(2)}, u32[]{:S(2)}) collective-permute-start(f32[1,1536]{1,0:T(1,128)S(1)} %add.152), channel_id=1, source_target_pairs={{0,1},{1,0},{2,3},{3,2},{4,5},{5,4},{6,7},{7,6},{8,9},{9,8},{10,11... | collective-permute-start | bytes 18440 | tf_op jit(solution)/shard_map/ppermute | solution.py:498
  545.4 37.6 %collective-permute-start.4 = (bf16[512,1536]{1,0:T(8,128)(2,1)}, bf16[512,1536]{1,0:T(8,128)(2,1)}, u32[]{:S(2)}, u32[]{:S(2)}) collective-permute-start(bf16[512,1536]{1,0:T(8,128)(2,1)} %fusion.4), channel_id=1, source_target_pairs={{0,1},{1,0},{2,3},{3,2},{4,5},{5,4},{6,7},{7,6},{8,9},{9,8},{10,11... | collective-permute-start | bytes 4718600 | tf_op jit(solution)/shard_map/ppermute | solution.py:498
  548.5 64.3 %collective-permute-start.7 = (bf16[512,1536]{1,0:T(8,128)(2,1)S(1)}, bf16[512,1536]{1,0:T(8,128)(2,1)S(1)}, u32[]{:S(2)}, u32[]{:S(2)}) collective-permute-start(bf16[512,1536]{1,0:T(8,128)(2,1)S(1)} %constant_dynamic-slice_fusion), channel_id=1, source_target_pairs={{0,1},{1,0},{2,3},{3,2},{4,5},{5,4},{6,7},{7,6},{8,9},{9,8},{10,11... | collective-permute-start | bytes 4718600 | tf_op jit(solution)/shard_map/ppermute | solution.py:498
  554.7 58.1 %copy-start.1 = (bf16[1024,1536]{1,0:T(8,128)(2,1)S(1)}, bf16[1024,1536]{1,0:T(8,128)(2,1)}, u32[]{:S(2)}) copy-start(bf16[1024,1536]{1,0:T(8,128)(2,1)} %copy-done) | copy-start | bytes 9437188
  (16 other events, 40.9 us)
Sparse Core Ops, SparseCore 0:
  10.9 69.3 all-gather.2
  82.4 108.5 all-gather.4
  341.8 85.1 reduce-scatter.7
  501.1 113.3 reduce-scatter.3
  619.0 137.4 reduce-scatter.5

commit v2 on v1

--- a/solution.py
+++ b/solution.py
@@ -317,7 +317,6 @@
     wg_ref,
     wu_ref,
     wd_ref,
-    hidden_ref,
     grads_ref,
     normed_ref,
     part_ref,
@@ -326,7 +325,7 @@
 ):
     j = pl.program_id(0)
     rows = x_ref.shape[0]
-    chunk = 256
+    chunk = rows
 
     @pl.when(j == 0)
     def _():
@@ -342,7 +341,7 @@
         grad_hidden = nn(cot_ref[span, :], wd_ref[...])
         sig = jax.nn.sigmoid(gate)
         silu = gate * sig
-        hidden_ref[span, :] = (silu * up).astype(BF)
+        grads_ref[2, span, :] = (silu * up).astype(BF)
         grad_gate = (grad_hidden * up * sig * (1.0 + gate * (1.0 - sig))).astype(BF)
         grad_up = (grad_hidden * silu).astype(BF)
         grads_ref[0, span, :] = grad_gate
@@ -377,15 +376,13 @@
             pl.BlockSpec((d, COLS), lambda j: (0, first + 2 * steps + j)),
         ],
         out_specs=[
-            pl.BlockSpec((rows, COLS), lambda j: (0, j)),
-            pl.BlockSpec((2, rows, COLS), lambda j: (0, 0, j)),
+            pl.BlockSpec((3, rows, COLS), lambda j: (0, 0, j)),
             pl.BlockSpec((rows, d), whole),
             pl.BlockSpec((rows, d), whole),
             pl.BlockSpec((1, d), whole),
         ],
         out_shape=[
-            jax.ShapeDtypeStruct((rows, hidden_width), BF),
-            jax.ShapeDtypeStruct((2, rows, hidden_width), BF),
+            jax.ShapeDtypeStruct((3, rows, hidden_width), BF),
             jax.ShapeDtypeStruct((rows, d), BF),
             jax.ShapeDtypeStruct((rows, d), BF),
             jax.ShapeDtypeStruct((1, d), F32),
@@ -419,7 +416,8 @@
         for r in range(0, rows, chunk):
             span = slice(r, r + chunk)
             part, piece = rms_back(acc_ref[span, :], x_ref[span, :].astype(F32), gain_ref[...])
-            part_ref[span, :] = part.astype(BF)
+            half = part_ref.shape[1]
+            part_ref[r // half, r % half : r % half + chunk, :] = part.astype(BF)
             gain_part = gain_part + piece
         gain_part_ref[...] = gain_part
 
@@ -438,8 +436,11 @@
             pl.BlockSpec((1, rows, COLS), lambda j: (j // per, 0, j % per)),
             pl.BlockSpec((d, COLS), lambda j: (0, j)),
         ],
-        out_specs=[pl.BlockSpec((rows, d), whole), pl.BlockSpec((1, d), whole)],
-        out_shape=[jax.ShapeDtypeStruct((rows, d), BF), jax.ShapeDtypeStruct((1, d), F32)],
+        out_specs=[pl.BlockSpec((2, rows // 2, d), lambda j: (0, 0, 0)), pl.BlockSpec((1, d), whole)],
+        out_shape=[
+            jax.ShapeDtypeStruct((2, rows // 2, d), BF),
+            jax.ShapeDtypeStruct((1, d), F32),
+        ],
         scratch_shapes=[pltpu.VMEM((rows, d), F32)],
         compiler_params=settings(),
         cost_estimate=cost(2 * rows * d * kinds * width, 2 * kinds * width * (rows + d)),
@@ -447,51 +448,356 @@
     )(x, gain, grads, w)
 
 
-def weight_grad_kernel(count, *refs):
-    lefts, rights = refs[:count], refs[count : 2 * count]
-    out_ref, turned_ref = refs[-2], refs[-1]
-    j = pl.program_id(0)
-    chunk = 256
-
-    @pl.when(j == 0)
-    def _():
-        start = 0
-        for left in lefts:
-            for r in range(0, left.shape[0], chunk):
-                turned_ref[:, start + r : start + r + chunk] = left[r : r + chunk, :].T
-            start += left.shape[0]
-
-    d = out_ref.shape[0]
-    for c in range(0, d, chunk):
-        total, start = None, 0
-        for right in rights:
-            rows = right.shape[1]
-            piece = nn(turned_ref[c : c + chunk, start : start + rows], right[0])
-            total = piece if total is None else total + piece
-            start += rows
-        out_ref[c : c + chunk, :] = total.astype(BF)
-
-
-def weight_grad(lefts, rights):
-    d = lefts[0].shape[1]
-    kinds, _, width = rights[0].shape
-    rows = sum(left.shape[0] for left in lefts)
-    per = width // COLS
+MESH = pl.DeviceIdType.MESH
+QUARTERS = 4
+
+
+class Scatter:
+    def __init__(self, devices, rows, count):
+        self.devices, self.rows, self.count = devices, rows, count
+        self.stages = devices.bit_length() - 1
+        self.lags = [2 if s == 1 else 1 for s in range(self.stages)]
+        self.starts = [sum(self.lags[:s]) for s in range(self.stages + 1)]
+        self.steps = count + self.starts[-1]
+
+    def scratch(self):
+        shapes = []
+        for s in range(self.stages):
+            slots, left = 2 * self.lags[s], self.devices >> (s + 1)
+            shapes.append(pltpu.VMEM((slots, 2, left, self.rows, COLS), BF))
+            shapes.append(pltpu.VMEM((slots, left, self.rows, COLS), BF))
+            shapes.append(pltpu.SemaphoreType.DMA((slots,)))
+            shapes.append(pltpu.SemaphoreType.DMA((slots,)))
+        return shapes
+
+    def bind(self, refs):
+        self.held, self.got = refs[0::4], refs[1::4]
+        self.sent_sem, self.got_sem = refs[2::4], refs[3::4]
+        self.me, self.side = lax.axis_index("dp"), lax.axis_index("tensor")
+
+    def bit(self, s):
+        return (self.me // (1 << s)) % 2
+
+    def partner(self, s):
+        return (self.me + (1 - 2 * self.bit(s)) * (1 << s), self.side)
+
+    def barrier(self):
+        arrived = pltpu.get_barrier_semaphore()
+        for s in range(self.stages):
+            pl.semaphore_signal(arrived, inc=1, device_id=self.partner(s), device_id_type=MESH)
+        pl.semaphore_signal(
+            arrived, inc=1, device_id=(self.me, 1 - self.side), device_id_type=MESH
+        )
+        pl.semaphore_wait(arrived, self.stages + 1)
+
+    def copy(self, s, slot):
+        return pltpu.make_async_remote_copy(
+            src_ref=self.held[s].at[slot, 1 - self.bit(s)],
+            dst_ref=self.got[s].at[slot],
+            send_sem=self.sent_sem[s].at[slot],
+            recv_sem=self.got_sem[s].at[slot],
+            device_id=self.partner(s),
+            device_id_type=MESH,
+        )
+
+    def advance(self, step, out_ref):
+        for s in range(self.stages, 0, -1):
+            block = step - self.starts[s]
+
+            @pl.when((block >= 0) & (block < self.count))
+            def _():
+                slot = block % (2 * self.lags[s - 1])
+                keep = self.bit(s - 1)
+                self.copy(s - 1, slot).wait()
+                held, got = self.held[s - 1], self.got[s - 1]
+                if s == self.stages:
+                    out_ref[...] = held[slot, keep, 0].astype(F32) + got[slot, 0].astype(F32)
+                else:
+                    later = block % (2 * self.lags[s])
+                    for k in range(self.devices >> s):
+                        total = held[slot, keep, k].astype(F32) + got[slot, k].astype(F32)
+                        self.held[s][later, k % 2, k // 2] = total.astype(BF)
+                    self.copy(s, later).start()
+
+    def put(self, slot, start, piece):
+        for r in range(0, piece.shape[0], self.rows):
+            k = (start + r) // self.rows
+            self.held[0][slot, k % 2, k // 2] = piece[r : r + self.rows].astype(BF)
+
+    def put_gain(self, slot, mine_ref, other_ref):
+        for k in range(self.devices):
+            span = slice(k * self.rows, (k + 1) * self.rows)
+            total = mine_ref[span, :].astype(F32) + other_ref[span, :].astype(F32)
+            total = jnp.concatenate([total] * (COLS // LANES), axis=1)
+            self.held[0][slot, k % 2, k // 2] = total.astype(BF)
+
+
+def turn_into(turned_ref, lefts):
+    start = 0
+    for left in lefts:
+        for r in range(0, left.shape[0], 256):
+            turned_ref[:, start + r : start + r + 256] = left[r : r + 256, :].T
+        start += left.shape[0]
+
+
+def gain_copy(scatter, gain_ref, got_ref, sems):
+    return pltpu.make_async_remote_copy(
+        src_ref=gain_ref,
+        dst_ref=got_ref,
+        send_sem=sems.at[0],
+        recv_sem=sems.at[1],
+        device_id=(scatter.me, 1 - scatter.side),
+        device_id_type=MESH,
+    )
+
+
+def ffn_scatter_kernel(scatter, per, *refs):
+    (
+        norm_own, norm_other, cot_own, cot_other, right_own, right_other,
+        part_own, part_other, gain_ref,
+    ) = refs[:9]
+    out_ref, gm_ref = refs[9:11]
+    turned_ref, got_part, gm_own, gain_got, gain_sems, x_sems, local_sem = refs[11:18]
+    scatter.bind(refs[18:])
+    step = pl.program_id(0)
+    side = scatter.side
+    quarter = part_own.shape[0] // QUARTERS
+
+    def part_copy(r):
+        span = pl.ds(r * quarter, quarter)
+        return pltpu.make_async_remote_copy(
+            src_ref=part_other.at[span],
+            dst_ref=got_part.at[span],
+            send_sem=x_sems.at[0, r],
+            recv_sem=x_sems.at[1, r],
+            device_id=(scatter.me, 1 - side),
+            device_id_type=MESH,
+        )
+
+    def gm_copy(r):
+        span = pl.ds(r * quarter, quarter)
+        return pltpu.make_async_remote_copy(
+            src_ref=gm_own.at[span],
+            dst_ref=gm_ref.at[side, span],
+            send_sem=x_sems.at[2, r],
+            recv_sem=x_sems.at[3, r],
+            device_id=(scatter.me, 1 - side),
+            device_id_type=MESH,
+        )
+
+    def gm_keep():
+        return pltpu.make_async_copy(gm_own, gm_ref.at[side], local_sem)
+
+    @pl.when(step == 0)
+    def _():
+        scatter.barrier()
+        for r in range(QUARTERS):
+            part_copy(r).start()
+        gain_copy(scatter, gain_ref, gain_got, gain_sems).start()
+        turn_into(turned_ref, [norm_own, norm_other])
+
+    @pl.when(step == 2 * per)
+    def _():
+        turn_into(turned_ref, [cot_own, cot_other])
+
+    scatter.advance(step, out_ref)
+
+    @pl.when(step < 3 * per)
+    def _():
+        slot = step % 2
+        piece_rows = 384
+        half = right_own.shape[1]
+        for r in range(0, turned_ref.shape[0], piece_rows):
+            span = slice(r, r + piece_rows)
+            piece = nn(turned_ref[span, :half], right_own[0])
+            piece = piece + nn(turned_ref[span, half:], right_other[0])
+            scatter.put(slot, r, piece)
+        scatter.copy(0, slot).start()
+
+    @pl.when(step == 3 * per)
+    def _():
+        slot = step % 2
+        gain_copy(scatter, gain_ref, gain_got, gain_sems).wait()
+        scatter.put_gain(slot, gain_ref, gain_got)
+        scatter.copy(0, slot).start()
+
+    for r in range(QUARTERS):
+
+        @pl.when(step == 3 + 2 * r)
+        def _():
+            span = slice(r * quarter, (r + 1) * quarter)
+            part_copy(r).wait()
+            total = cot_own[span, :].astype(F32) + part_own[span, :].astype(F32)
+            gm_own[span, :] = (total + got_part[span, :].astype(F32)).astype(BF)
+            gm_copy(r).start()
+            if r == QUARTERS - 1:
+                gm_keep().start()
+
+    @pl.when(step == scatter.steps - 1)
+    def _():
+        for r in range(QUARTERS):
+            gm_copy(r).wait()
+        gm_keep().wait()
+
+
+def resident(shape):
+    zeros = (0,) * len(shape)
+    return pl.BlockSpec(shape, lambda j: zeros, pipeline_mode=pl.Buffered(1))
+
+
+def remote_settings(identity, mib=56):
+    return pltpu.CompilerParams(
+        dimension_semantics=("arbitrary",),
+        vmem_limit_bytes=mib * 1024 * 1024,
+        collective_id=identity,
+        has_side_effects=True,
+    )
+
+
+def ffn_scatter(devices, normed, cots, rights, parts, gain_block):
+    half, d = normed[0].shape
+    per = rights[0].shape[2] // COLS
+    scatter = Scatter(devices, d // devices, 3 * per + 1)
+    last = 3 * per - 1
+
+    def right_map(j):
+        c = jnp.minimum(j, last)
+        return (c // per, 0, c % per)
+
+    first = scatter.starts[-1]
     return pl.pallas_call(
-        functools.partial(weight_grad_kernel, len(lefts)),
-        grid=(kinds * per,),
-        in_specs=[pl.BlockSpec(left.shape, lambda j: (0, 0)) for left in lefts]
+        functools.partial(ffn_scatter_kernel, scatter, per),
+        grid=(scatter.steps,),
+        in_specs=[resident((half, d))] * 4
+        + [pl.BlockSpec((1, half, COLS), right_map)] * 2
         + [
-            pl.BlockSpec((1, right.shape[1], COLS), lambda j: (j // per, 0, j % per))
-            for right in rights
-        ],
-        out_specs=pl.BlockSpec((d, COLS), lambda j: (0, j)),
-        out_shape=jax.ShapeDtypeStruct((d, kinds * width), BF),
-        scratch_shapes=[pltpu.VMEM((d, rows), BF)],
-        compiler_params=settings(),
-        cost_estimate=cost(2 * rows * d * kinds * width, 2 * kinds * width * (rows + d)),
-        name="weight_grad",
-    )(*lefts, *rights)
+            resident((half, d)),
+            pl.BlockSpec(memory_space=pl.ANY),
+            resident((d, LANES)),
+        ],
+        out_specs=[
+            pl.BlockSpec((scatter.rows, COLS), lambda j: (0, jnp.maximum(j - first, 0))),
+            pl.BlockSpec(memory_space=pl.ANY),
+        ],
+        out_shape=[
+            jax.ShapeDtypeStruct((scatter.rows, scatter.count * COLS), F32),
+            jax.ShapeDtypeStruct((2, half, d), BF),
+        ],
+        scratch_shapes=[
+            pltpu.VMEM((d, 2 * half), BF),
+            pltpu.VMEM((half, d), BF),
+            pltpu.VMEM((half, d), BF),
+            pltpu.VMEM((d, LANES), BF),
+            pltpu.SemaphoreType.DMA((2,)),
+            pltpu.SemaphoreType.DMA((4, QUARTERS)),
+            pltpu.SemaphoreType.DMA,
+        ]
+        + scatter.scratch(),
+        compiler_params=remote_settings(0),
+        cost_estimate=cost(12 * half * d * per * COLS, 20 * half * d),
+        name="ffn_scatter",
+    )(*normed, *cots, *rights, *parts, gain_block)
+
+
+def attention_scatter_kernel(scatter, per, *refs):
+    normed_ref, gm_ref, right_ref, attended_ref, part_ref, gain_ref = refs[:6]
+    out_ref, got_part = refs[6:8]
+    turned_ref, gain_got, gain_sems, x_sems = refs[8:12]
+    scatter.bind(refs[12:])
+    step = pl.program_id(0)
+    side = scatter.side
+    piece_rows = 384
+
+    def part_copy():
+        return pltpu.make_async_remote_copy(
+            src_ref=part_ref.at[1 - side],
+            dst_ref=got_part,
+            send_sem=x_sems.at[0],
+            recv_sem=x_sems.at[1],
+            device_id=(scatter.me, 1 - side),
+            device_id_type=MESH,
+        )
+
+    @pl.when(step == 0)
+    def _():
+        scatter.barrier()
+        part_copy().start()
+        gain_copy(scatter, gain_ref, gain_got, gain_sems).start()
+        turn_into(turned_ref, [normed_ref])
+
+    @pl.when(step == 3 * per)
+    def _():
+        turn_into(turned_ref, [gm_ref])
+
+    scatter.advance(step, out_ref)
+    slot = step % 2
+
+    @pl.when(step < 3 * per)
+    def _():
+        for r in range(0, turned_ref.shape[0], piece_rows):
+            scatter.put(slot, r, nn(turned_ref[r : r + piece_rows, :], right_ref[0]))
+        scatter.copy(0, slot).start()
+
+    @pl.when((step >= 3 * per) & (step < 4 * per))
+    def _():
+        for r in range(0, turned_ref.shape[0], piece_rows):
+            scatter.put(slot, r, nn(turned_ref[r : r + piece_rows, :], attended_ref[...]))
+        scatter.copy(0, slot).start()
+
+    @pl.when(step == 4 * per)
+    def _():
+        gain_copy(scatter, gain_ref, gain_got, gain_sems).wait()
+        scatter.put_gain(slot, gain_ref, gain_got)
+        scatter.copy(0, slot).start()
+
+    @pl.when(step == scatter.steps - 1)
+    def _():
+        part_copy().wait()
+
+
+def attention_scatter(devices, normed, gm, grads, attended, part, gain_block):
+    length, d = normed.shape
+    per = grads.shape[2] // COLS
+    scatter = Scatter(devices, d // devices, 4 * per + 1)
+
+    def right_map(j):
+        c = jnp.minimum(j, 3 * per - 1)
+        return (c // per, 0, c % per)
+
+    def attended_map(j):
+        return (0, jnp.clip(j - 3 * per, 0, per - 1))
+
+    first = scatter.starts[-1]
+    return pl.pallas_call(
+        functools.partial(attention_scatter_kernel, scatter, per),
+        grid=(scatter.steps,),
+        in_specs=[
+            resident((length, d)),
+            resident((length, d)),
+            pl.BlockSpec((1, length, COLS), right_map),
+            pl.BlockSpec((length, COLS), attended_map),
+            pl.BlockSpec(memory_space=pl.ANY),
+            resident((d, LANES)),
+        ],
+        out_specs=[
+            pl.BlockSpec((scatter.rows, COLS), lambda j: (0, jnp.maximum(j - first, 0))),
+            pl.BlockSpec(memory_space=pl.ANY),
+        ],
+        out_shape=[
+            jax.ShapeDtypeStruct((scatter.rows, scatter.count * COLS), F32),
+            jax.ShapeDtypeStruct((length // 2, d), BF),
+        ],
+        scratch_shapes=[
+            pltpu.VMEM((d, length), BF),
+            pltpu.VMEM((d, LANES), BF),
+            pltpu.SemaphoreType.DMA((2,)),
+            pltpu.SemaphoreType.DMA((2,)),
+        ]
+        + scatter.scratch(),
+        compiler_params=remote_settings(1),
+        cost_estimate=cost(8 * length * d * per * COLS, 20 * length * d),
+        name="attention_scatter",
+    )(normed, gm, grads, attended, part, gain_block)
 
 
 def swap(x):
@@ -538,19 +844,20 @@
     attn_row = attn_gain[None, :]
     ffn_row = ffn_gain[None, :]
 
-    wqkv = gather(jnp.concatenate([query_weight, key_weight, value_weight], axis=1))
-    wrest = gather(
-        jnp.concatenate([output_weight.T, gate_weight, up_weight, down_weight.T], axis=1)
-    )
+    first = gather(
+        jnp.concatenate([query_weight, key_weight, value_weight, output_weight.T], axis=1)
+    )
+    second = gather(jnp.concatenate([gate_weight, up_weight, down_weight.T], axis=1))
+    devices = lax.axis_size("dp")
 
     bias, positions = tree_tables(parents[0], seg_rows)
     cosine, sine = turn_tables(positions, COLS)
     rows_all = place(tokens, swap(tokens))
     cot_other = swap(cotangent)
 
-    qkv, normed_one = project(rows_all, attn_row, cosine, sine, wqkv, width)
+    qkv, normed_one = project(rows_all, attn_row, cosine, sine, first, width)
     attended, lse = attend(qkv, bias, width, seg_rows)
-    out_turned = wrest[:, :width]
+    out_turned = first[:, 3 * width :]
     send = nt(other_rows(attended), out_turned).astype(BF)
     received = swap(send)
     middle = (
@@ -558,77 +865,65 @@
     ).astype(BF)
     middle_other = swap(middle)
 
-    hid_own, gg_own, normed_own, part_own, gp_own = ffn(
-        middle, cotangent, ffn_row, wrest, width, hidden_width
-    )
-    hid_other, gg_other, normed_other, part_other, gp_other = ffn(
-        middle_other, cot_other, ffn_row, wrest, width, hidden_width
-    )
-    gp = gp_own + gp_other
-    part_received = swap(part_other)
-    gp_received = swap(gp)
-    down_turned_grad = weight_grad([cotangent, cot_other], [hid_own[None], hid_other[None]])
-    gate_up_grad = weight_grad([normed_own, normed_other], [gg_own, gg_other])
-    grad_middle = (
-        cotangent.astype(F32) + part_own.astype(F32) + part_received.astype(F32)
-    ).astype(BF)
-    grad_middle_other = swap(grad_middle)
-
-    down_turned = wrest[:, width + 2 * hidden_width :]
-    out_received = swap(nt(hid_other, down_turned).astype(BF))
-    block_out = (
-        middle.astype(F32) + nt(hid_own, down_turned) + out_received.astype(F32)
-    ).astype(BF)
-
-    def scatter(grad):
-        return lax.psum_scatter(grad, "dp", scatter_dimension=0, tiled=True).astype(F32)
+    gg_own, normed_own, part_own, gp_own = ffn(
+        middle, cotangent, ffn_row, second, 0, hidden_width
+    )
+    gg_other, normed_other, part_other, gp_other = ffn(
+        middle_other, cot_other, ffn_row, second, 0, hidden_width
+    )
 
     def gain_block(gain_sum):
         return jnp.broadcast_to(gain_sum.astype(BF).T, (d, LANES))
 
-    down_grad = scatter(down_turned_grad).T
-    gate_up = scatter(jnp.concatenate([gate_up_grad, gain_block(gp + gp_received)], axis=1))
-    gate_grad = gate_up[:, :hidden_width]
-    up_grad = gate_up[:, hidden_width : 2 * hidden_width]
-
-    grad_attended = place(
-        nn(grad_middle, out_turned).astype(BF), nn(grad_middle_other, out_turned).astype(BF)
-    )
+    ffn_grads, grad_middle = ffn_scatter(
+        devices,
+        (normed_own, normed_other),
+        (cotangent, cot_other),
+        (gg_own, gg_other),
+        (part_own, part_other),
+        gain_block(gp_own + gp_other),
+    )
+    grad_middle_all = grad_middle.reshape(length, d)
+
+    down_turned = second[:, 2 * hidden_width :]
+    out_received = swap(nt(gg_other[2], down_turned).astype(BF))
+    block_out = (
+        middle.astype(F32) + nt(gg_own[2], down_turned) + out_received.astype(F32)
+    ).astype(BF)
+
+    grad_attended = nn(grad_middle_all, out_turned).astype(BF)
     grads = attend_back(
         qkv, attended, grad_attended, lse, bias, cosine[:, :LANES], sine[:, :LANES], seg_rows
     )
-    part, gain_part = input_grad(rows_all, attn_row, grads, wqkv)
-    tokens_received = swap(other_rows(part))
-    gain_received = swap(gain_part)
-    qkv_grad = weight_grad([normed_one], [grads])
-    out_turned_grad = weight_grad(
-        [grad_middle, grad_middle_other], [own_rows(attended)[None], other_rows(attended)[None]]
+    part, gain_part = input_grad(rows_all, attn_row, grads, first)
+    attn_grads, tokens_received = attention_scatter(
+        devices, normed_one, grad_middle_all, grads, attended, part, gain_block(gain_part)
     )
     token_grad = (
-        grad_middle.astype(F32) + own_rows(part).astype(F32) + tokens_received.astype(F32)
+        lax.dynamic_index_in_dim(grad_middle, mine, 0, False).astype(F32)
+        + lax.dynamic_index_in_dim(part, mine, 0, False).astype(F32)
+        + tokens_received.astype(F32)
     ).astype(BF)
-    last = scatter(
-        jnp.concatenate(
-            [qkv_grad, out_turned_grad, gain_block(gain_part + gain_received)], axis=1
-        )
-    )
-    gain_rows = d // lax.axis_size("dp") // 2
-
-    def gain_piece(column):
-        return lax.dynamic_slice_in_dim(column[:, 0], mine * gain_rows, gain_rows, 0)
+    gain_rows = d // devices // 2
+
+    def gain_piece(columns):
+        return lax.dynamic_slice_in_dim(columns[:, 0], mine * gain_rows, gain_rows, 0)
+
+    def column(grads_out, kind, size):
+        return grads_out[:, kind * size : (kind + 1) * size]
 
     return (
         block_out,
         token_grad,
-        last[:, :width],
-        last[:, width : 2 * width],
-        last[:, 2 * width : 3 * width],
-        last[:, 3 * width : 4 * width].T,
-        gate_grad,
-        up_grad,
-        down_grad,
-        gain_piece(last[:, 4 * width :]),
-        gain_piece(gate_up[:, 2 * hidden_width :]),
+        column(attn_grads, 0, width),
+        column(attn_grads, 1, width),
+        column(attn_grads, 2, width),
+        column(attn_grads, 3, width).T,
+        column(ffn_grads, 0, hidden_width),
+        column(ffn_grads, 1, hidden_width),
+        column(ffn_grads, 2, hidden_width).T,
+        gain_piece(attn_grads[:, 4 * width :]),
+        gain_piece(ffn_grads[:, 3 * hidden_width :]),
     )
 
 

time: 777 us -> 637 us (0.82)
  waiting for transfers between devices: 448 us -> 166 us
  Pallas kernels: 196 us -> 375 us
  other arithmetic: 36.6 us -> 12.5 us
    pallas_call x4 -> x2, Pallas kernels: 52.6 us -> 213 us  [the longest x1 135 us: ffn_scatter(): pl.pallas_call(functools.partial(ffn_scatter_kernel, scatter, per), grid=...]
    reduce_scatter x3 -> x0, waiting for transfers between devices: 136 us -> none  [scatter(): lax.psum_scatter(grad, 'dp', scatter_dimension=0, tiled=True).astype(F32)]
    ppermute x10 -> x5, waiting for transfers between devices: 212 us -> 124 us  [swap(): return lax.ppermute(x, 'tensor', [(0, 1), (1, 0)])]
    all_gather x2, waiting for transfers between devices: 100 us -> 42.6 us  [gather(): return lax.all_gather(shard, 'dp', axis=0, tiled=True)]
    concatenate x4 -> x2, other arithmetic: 24.2 us -> 4.32 us  [the longest x1 2.33 us: body(): jnp.concatenate([gate_weight, up_weight, down_weight.T], axis=1)]
    pallas_call x2, Pallas kernels: 56.6 us -> 74.5 us  [ffn(): pl.pallas_call(ffn_kernel, grid=(steps,), in_specs=[pl.BlockSpec((rows, d...]
  transfers between devices with their start and end apart: 15 -> 7, of which waited for: 10 -> 5; matrix products, arithmetic and copies ran while one was open for 9% -> 7% of each run, Pallas kernels for 20% -> 54%
where the time goes in v2:
time: 637 us; the launch traced here: 627 us
  Pallas kernels  375 us (59%)
  waiting for transfers between devices  166 us (26%)
  local copies, waits for them, and re-layouts  26.2 us (4%)
  matrix products  24.1 us (4%)
  between operations  14.6 us (2%)
  other arithmetic  12.5 us (2%)
  starting transfers between devices  8.16 us (1%)
    pallas_call x1, Pallas kernels, ffn_scatter(): pl.pallas_call(functools.partial(ffn_scatter_kernel, scatter, per), grid=...  135 us
    ppermute x5, waiting for transfers between devices, swap(): return lax.ppermute(x, 'tensor', [(0, 1), (1, 0)])  124 us
    pallas_call x1, Pallas kernels, attention_scatter(): pl.pallas_call(functools.partial(attention_scatter_kernel, scatter, per),...  78.4 us
    pallas_call x2, Pallas kernels, ffn(): pl.pallas_call(ffn_kernel, grid=(steps,), in_specs=[pl.BlockSpec((rows, d...  74.5 us
    all_gather x2, waiting for transfers between devices, gather(): return lax.all_gather(shard, 'dp', axis=0, tiled=True)  42.6 us
    pallas_call x1, Pallas kernels, attend_back(): pl.pallas_call(functools.partial(attend_back_kernel, block, seg_rows), gr...  34.1 us
    pallas_call x1, Pallas kernels, attend(): pl.pallas_call(functools.partial(attend_kernel, block, seg_rows), grid=(g...  21.6 us
    dot_general x4, matrix products, nt(): lax.dot_general(a, b, (((1,), (1,)), ((), ())), preferred_element_type=F32)  19.8 us
  transfers between devices with their start and end apart: 7, of which 5 were waited for; matrix products, arithmetic and copies ran while one was open for 7% of the time, Pallas kernels for 54%

profile of v2, /device:TPU:0, one launch (start us, length us, event | category | flops | bytes accessed | tf_op | source)
XLA Modules:
  0.0 627.1 jit_solution(3452278029953118149)
XLA Ops:
  11.6 3.0 collective-permute-start
  19.5 2.7 constant_dynamic-update-slice_fusion.1
  22.2 27.2 %collective-permute-done = bf16[512,1536]{1,0:T(8,128)(2,1)} collective-permute-done((bf16[512,1536]{1,0:T(8,128)(2,1)}, bf16[512,1536]{1,0:T(8,128)(2,1)}, u32[]{:S(2)}, u32[]{:S(2)}) %collective-permute-start) | collective-permute-done | bytes 1572896 | tf_op jit(solution)/shard_map/ppermute | solution.py:804
  49.4 3.1 constant_dynamic-update-slice_fusion.x_ref
  52.5 42.6 %all-gather.3.cloned.1.call-done.w_ref = bf16[1536,3072]{1,0:T(8,128)(2,1)} async-done(((bf16[96,3072]{1,0:T(8,128)(2,1)}), bf16[1536,3072]{1,0:T(8,128)(2,1)}) %all-gather.3.cloned.1.call-update) | async-done | bytes 9437200 | tf_op jit(solution)/shard_map/all_gather | solution.py:842
  95.1 15.8 %project.1 = (bf16[1024,2304]{1,0:T(8,128)(2,1)}, bf16[1024,1536]{1,0:T(8,128)(2,1)S(1)}) custom-call(bf16[1024,1536]{1,0:T(8,128)(2,1)} %constant_dynamic-update-slice_fusion.x_ref, f32[1,1536]{1,0:T(1,128)S(1)} %broadcast_in_dim.27.gain_ref, f32[1024,256]{1,0:T(8,128)S(1)} %copy.45.cos_ref, f32[1024,256]{1,0:T(8,128)S(1)} %copy.46.sin_ref, ...), custom_call_target="tpu_custom_call" | custom-call | flops 7247757312 | bytes 13369344 | tf_op jit(solution)/shard_map/project/pallas_call | solution.py:112
  112.5 21.6 %attend.1 = (bf16[1024,768]{1,0:T(8,128)(2,1)S(1)}, f32[6,2,1024]{2,1,0:T(2,128)S(1)}) custom-call(bf16[1024,2304]{1,0:T(8,128)(2,1)} %get-tuple-element.29.q_ref.k_ref.v_ref, bf16[1024,2304]{1,0:T(8,128)(2,1)} %get-tuple-element.29.q_ref.k_ref.v_ref, bf16[1024,2304]{1,0:T(8,128)(2,1)} %get-tuple-element.29.q_ref.k_ref.v_ref, ...), custom_call_target="tpu_custom_call" | custom-call | flops 6442450944 | bytes 6291456 | tf_op jit(solution)/shard_map/attend/pallas_call | solution.py:191
  137.8 35.2 %collective-permute-done.1 = bf16[512,1536]{1,0:T(8,128)(2,1)S(1)} collective-permute-done((bf16[512,1536]{1,0:T(8,128)(2,1)S(1)}, bf16[512,1536]{1,0:T(8,128)(2,1)S(1)}, u32[]{:S(2)}, u32[]{:S(2)}) %collective-permute-start.1) | collective-permute-done | bytes 1572896 | tf_op jit(solution)/shard_map/ppermute | solution.py:804
  173.0 2.9 add_convert_fusion.1.x_ref
  178.6 28.2 %collective-permute-done.3.cot_ref.refs_3_ = bf16[512,1536]{1,0:T(8,128)(2,1)} collective-permute-done((bf16[512,1536]{1,0:T(8,128)(2,1)}, bf16[512,1536]{1,0:T(8,128)(2,1)}, u32[]{:S(2)}, u32[]{:S(2)}) %collective-permute-start.3) | collective-permute-done | bytes 1572896 | tf_op jit(solution)/shard_map/ppermute | solution.py:804
  206.8 33.0 %collective-permute-done.2.x_ref = bf16[512,1536]{1,0:T(8,128)(2,1)} collective-permute-done((bf16[512,1536]{1,0:T(8,128)(2,1)S(1)}, bf16[512,1536]{1,0:T(8,128)(2,1)}, u32[]{:S(2)}, u32[]{:S(2)}) %collective-permute-start.2) | collective-permute-done | bytes 1572896 | tf_op jit(solution)/shard_map/ppermute | solution.py:804
  239.8 37.4 %ffn.3 = (bf16[3,512,2048]{2,1,0:T(8,128)(2,1)}, bf16[512,1536]{1,0:T(8,128)(2,1)S(1)}, bf16[512,1536]{1,0:T(8,128)(2,1)S(1)}, f32[1,1536]{1,0:T(1,128)S(1)}) custom-call(bf16[512,1536]{1,0:T(8,128)(2,1)} %collective-permute-done.2.x_ref, bf16[512,1536]{1,0:T(8,128)(2,1)} %collective-permute-done.3.cot_ref.refs_3_, f32[1,1536]{1,0:T(1,128)S(1)} %broadcast_in_dim.32.gain_ref, ...), custom_call_target="tpu_custom_call" | custom-call | flops 16106127360 | bytes 31457280 | tf_op jit(solution)/shard_map/ffn/pallas_call | solution.py:367
  277.2 9.1 %fusion.5 = bf16[512,1536]{1,0:T(8,128)(2,1)} fusion(bf16[1536,6144]{1,0:T(8,128)(2,1)} %all-gather.5.cloned.1.call-done.wg_ref.wu_ref.wd_ref, bf16[3,512,2048]{2,1,0:T(8,128)(2,1)} %get-tuple-element.32.refs_5_), kind=kOutput, calls=%fused_computation.9 | convolution fusion | flops 3222011904 | bytes 9961472 | tf_op jit(solution)/shard_map/dot_general | solution.py:37
  287.8 37.1 %ffn.2 = (bf16[3,512,2048]{2,1,0:T(8,128)(2,1)}, bf16[512,1536]{1,0:T(8,128)(2,1)S(1)}, bf16[512,1536]{1,0:T(8,128)(2,1)S(1)}, f32[1,1536]{1,0:T(1,128)S(1)}) custom-call(bf16[512,1536]{1,0:T(8,128)(2,1)S(1)} %add_convert_fusion.1.x_ref, bf16[512,1536]{1,0:T(8,128)(2,1)} %refs_2_.1, f32[1,1536]{1,0:T(1,128)S(1)} %broadcast_in_dim.32.gain_ref, ...), custom_call_target="tpu_custom_call" | custom-call | flops 16106127360 | bytes 31457280 | tf_op jit(solution)/shard_map/ffn/pallas_call | solution.py:367
  328.2 134.8 %ffn_scatter.1 = (f32[96,6400]{1,0:T(8,128)}, bf16[2,512,1536]{2,1,0:T(8,128)(2,1)}) custom-call(bf16[512,1536]{1,0:T(8,128)(2,1)} %copy-done.5, bf16[512,1536]{1,0:T(8,128)(2,1)} %copy-done.3, bf16[512,1536]{1,0:T(8,128)(2,1)} %refs_2_.1, bf16[512,1536]{1,0:T(8,128)(2,1)} %collective-permute-done.3.cot_ref.refs_3_, ...), custom_call_target="tpu_custom_call" | custom-call | flops 19327352832 | bytes 15728640 | tf_op jit(solution)/shard_map/ffn_scatter/pallas_call | solution.py:668
  463.0 3.2 slice_bitcast_fusion
  466.2 4.4 fusion.16.do_ref
  470.6 34.1 %attend_back.1.g_ref.refs_2_ = bf16[3,1024,768]{2,1,0:T(8,128)(2,1)} custom-call(bf16[1024,2304]{1,0:T(8,128)(2,1)} %get-tuple-element.29.q_ref.k_ref.v_ref, bf16[1024,2304]{1,0:T(8,128)(2,1)} %get-tuple-element.29.q_ref.k_ref.v_ref, bf16[1024,2304]{1,0:T(8,128)(2,1)} %get-tuple-element.29.q_ref.k_ref.v_ref, bf16[1024,768]{1,0:T(8,128)(2,1)S(1)} %copy-done.8, ...), custom_call_target="tpu_custom_call" | custom-call | flops 16106127360 | bytes 12582912 | tf_op jit(solution)/shard_map/attend_back/pallas_call | solution.py:279
  504.7 16.2 %input_grad.1 = (bf16[2,512,1536]{2,1,0:T(8,128)(2,1)S(1)}, f32[1,1536]{1,0:T(1,128)S(1)}) custom-call(bf16[1024,1536]{1,0:T(8,128)(2,1)} %constant_dynamic-update-slice_fusion.x_ref, f32[1,1536]{1,0:T(1,128)S(1)} %broadcast_in_dim.27.gain_ref, bf16[3,1024,768]{2,1,0:T(8,128)(2,1)} %attend_back.1.g_ref.refs_2_, ...), custom_call_target="tpu_custom_call" | custom-call | flops 7247757312 | bytes 11796480 | tf_op jit(solution)/shard_map/input_grad/pallas_call | solution.py:430
  523.6 78.4 %attention_scatter.1 = (f32[96,3328]{1,0:T(8,128)}, bf16[512,1536]{1,0:T(8,128)(2,1)}) custom-call(bf16[1024,1536]{1,0:T(8,128)(2,1)} %copy-done.9, bf16[1024,1536]{1,0:T(8,128)(2,1)} %bitcast.35, bf16[3,1024,768]{2,1,0:T(8,128)(2,1)} %attend_back.1.g_ref.refs_2_, bf16[1024,768]{1,0:T(8,128)(2,1)} %copy-done.7, bf16[2,512,1536]{2,1,0:T(8,128)(2,1)} %copy-done.1, ...), custom_call_target="tpu_custom_call" | custom-call | flops 9663676416 | bytes 31457280 | tf_op jit(solution)/shard_map/attention_scatter/pallas_call | solution.py:771
  602.0 2.4 slice_bitcast_fusion.1
  607.3 3.1 fusion.4
  610.4 6.2 fusion.2
  616.7 3.4 add_convert_fusion
  (94 shorter events, 27.4 us)
Async XLA Ops:
  7.2 87.9 %all-gather.3.cloned.1.call-start = ((), (), s32[]{:S(2)}) async-start(), calls=%async_computation | async-start | bytes 10027008 | tf_op jit(solution)/shard_map/all_gather | solution.py:842
  9.2 5.4 copy-start.14
  9.2 6.4 %copy-start.12 = (f32[1536]{0:T(1024)S(1)}, f32[1536]{0:T(1024)}, u32[]{:S(2)}) copy-start(f32[1536]{0:T(1024)} %param.14) | copy-start | bytes 18436
  9.2 230.5 %all-gather.5.cloned.1.call-start = ((), (), s32[]{:S(2)}) async-start(), calls=%async_computation.1 | async-start | bytes 20054016 | tf_op jit(solution)/shard_map/all_gather | solution.py:842
  11.6 37.7 %collective-permute-start = (bf16[512,1536]{1,0:T(8,128)(2,1)}, bf16[512,1536]{1,0:T(8,128)(2,1)}, u32[]{:S(2)}, u32[]{:S(2)}) collective-permute-start(bf16[512,1536]{1,0:T(8,128)(2,1)} %param.12), channel_id=1, source_target_pairs={{0,1},{1,0},{2,3},{3,2},{4,5},{5,4},{6,7},{7,6},{8,9},{9,8},{10,11... | collective-permute-start | bytes 4718600 | tf_op jit(solution)/shard_map/ppermute | solution.py:804
  17.4 77.6 %copy-start = (f32[1024,256]{1,0:T(8,128)}, f32[1024,256]{1,0:T(8,128)S(1)}, u32[]{:S(2)}) copy-start(f32[1024,256]{1,0:T(8,128)S(1)} %copy.46.sin_ref) | copy-start | bytes 3145732
  95.0 39.2 %slice-start = ((s8[9437184]{0:T(1024)(128)(4,1)}), s8[1048576]{0:T(1024)(128)(4,1)S(1)}, s32[]{:S(2)}) async-start(s8[9437184]{0:T(1024)(128)(4,1)} %bitcast.40), calls=%async_computation.2 | async-start | bytes 2097152
  95.1 39.2 %slice-start.1 = ((s8[9437184]{0:T(1024)(128)(4,1)}), s8[4194304]{0:T(1024)(128)(4,1)S(1)}, s32[]{:S(2)}) async-start(s8[9437184]{0:T(1024)(128)(4,1)} %bitcast.40), calls=%async_computation.3 | async-start | bytes 8388608
  110.9 1.7 copy-start.9
  112.5 21.7 %slice-start.2 = ((s8[9437184]{0:T(1024)(128)(4,1)}), s8[4194304]{0:T(1024)(128)(4,1)S(1)}, s32[]{:S(2)}) async-start(s8[9437184]{0:T(1024)(128)(4,1)} %bitcast.40), calls=%async_computation.4 | async-start | bytes 8388608
  134.2 38.8 %copy-start.7 = (bf16[1024,768]{1,0:T(8,128)(2,1)}, bf16[1024,768]{1,0:T(8,128)(2,1)S(1)}, u32[]{:S(2)}) copy-start(bf16[1024,768]{1,0:T(8,128)(2,1)S(1)} %get-tuple-element.30.o_ref.refs_3_) | copy-start | bytes 4718596
  135.7 42.9 %copy-start.13 = (f32[1536]{0:T(1024)S(1)}, f32[1536]{0:T(1024)}, u32[]{:S(2)}) copy-start(f32[1536]{0:T(1024)} %param.15) | copy-start | bytes 18436
  135.7 37.3 %collective-permute-start.1 = (bf16[512,1536]{1,0:T(8,128)(2,1)S(1)}, bf16[512,1536]{1,0:T(8,128)(2,1)S(1)}, u32[]{:S(2)}, u32[]{:S(2)}) collective-permute-start(bf16[512,1536]{1,0:T(8,128)(2,1)S(1)} %convolution_convert_fusion), channel_id=1, source_target_pairs={{0,1},{1,0},{2,3},{3,2},{4,5},{5,4},{6,7},{7,6},{8,9},{9,8},{10,11... | collective-permute-start | bytes 4718600 | tf_op jit(solution)/shard_map/ppermute | solution.py:804
  137.2 69.6 %collective-permute-start.3 = (bf16[512,1536]{1,0:T(8,128)(2,1)}, bf16[512,1536]{1,0:T(8,128)(2,1)}, u32[]{:S(2)}, u32[]{:S(2)}) collective-permute-start(bf16[512,1536]{1,0:T(8,128)(2,1)} %refs_2_.1), channel_id=1, source_target_pairs={{0,1},{1,0},{2,3},{3,2},{4,5},{5,4},{6,7},{7,6},{8,9},{9,8},{10,11... | collective-permute-start | bytes 4718600 | tf_op jit(solution)/shard_map/ppermute | solution.py:804
  175.9 63.9 %collective-permute-start.2 = (bf16[512,1536]{1,0:T(8,128)(2,1)S(1)}, bf16[512,1536]{1,0:T(8,128)(2,1)}, u32[]{:S(2)}, u32[]{:S(2)}) collective-permute-start(bf16[512,1536]{1,0:T(8,128)(2,1)S(1)} %add_convert_fusion.1.x_ref), channel_id=1, source_target_pairs={{0,1},{1,0},{2,3},{3,2},{4,5},{5,4},{6,7},{7,6},{8,9},{9,8},{10,11... | collective-permute-start | bytes 4718600 | tf_op jit(solution)/shard_map/ppermute | solution.py:804
  277.2 9.1 %copy-start.3 = (bf16[512,1536]{1,0:T(8,128)(2,1)}, bf16[512,1536]{1,0:T(8,128)(2,1)S(1)}, u32[]{:S(2)}) copy-start(bf16[512,1536]{1,0:T(8,128)(2,1)S(1)} %get-tuple-element.34.refs_1_) | copy-start | bytes 4718596
  277.2 9.1 %copy-start.4 = (bf16[512,1536]{1,0:T(8,128)(2,1)}, bf16[512,1536]{1,0:T(8,128)(2,1)S(1)}, u32[]{:S(2)}) copy-start(bf16[512,1536]{1,0:T(8,128)(2,1)S(1)} %get-tuple-element.36.refs_7_) | copy-start | bytes 4718596
  286.3 330.4 %collective-permute-start.4 = (bf16[512,1536]{1,0:T(8,128)(2,1)}, bf16[512,1536]{1,0:T(8,128)(2,1)}, u32[]{:S(2)}, u32[]{:S(2)}) collective-permute-start(bf16[512,1536]{1,0:T(8,128)(2,1)} %fusion.5), channel_id=1, source_target_pairs={{0,1},{1,0},{2,3},{3,2},{4,5},{5,4},{6,7},{7,6},{8,9},{9,8},{10,11... | collective-permute-start | bytes 4718600 | tf_op jit(solution)/shard_map/ppermute | solution.py:804
  326.0 1.2 copy-start.6
  463.0 3.2 copy-start.11
  466.2 4.4 copy-start.8
  520.9 1.7 copy-start.1
  523.6 83.6 %copy-start.2 = (bf16[2,512,1536]{2,1,0:T(8,128)(2,1)S(1)}, bf16[2,512,1536]{2,1,0:T(8,128)(2,1)}, u32[]{:S(2)}) copy-start(bf16[2,512,1536]{2,1,0:T(8,128)(2,1)} %copy-done.1) | copy-start | bytes 9437188
  602.0 5.2 copy-start.10
  (1 other events, 1.1 us)
Sparse Core Ops, SparseCore 0:
  10.9 84.1 all-gather.2
  97.2 97.0 all-gather.4

commit v3 on v2

--- a/solution.py
+++ b/solution.py
@@ -80,6 +80,16 @@
     return lax.rsqrt(jnp.mean(x * x, axis=1, keepdims=True) + EPS)
 
 
+def norm_rows(x_ref, gain_ref, normed_ref):
+    chunk = 128
+
+    @pl.loop(0, x_ref.shape[0] // chunk)
+    def _(i):
+        span = pl.ds(i * chunk, chunk)
+        x = x_ref[span, :].astype(F32)
+        normed_ref[span, :] = (x * inverse_rms(x) * gain_ref[...]).astype(BF)
+
+
 def project_kernel(parts, x_ref, gain_ref, cos_ref, sin_ref, w_ref, out_ref, normed_ref):
     j = pl.program_id(0)
     rows = x_ref.shape[0]
@@ -87,17 +97,15 @@
 
     @pl.when(j == 0)
     def _():
-        for r in range(0, rows, chunk):
-            x = x_ref[r : r + chunk, :].astype(F32)
-            normed_ref[r : r + chunk, :] = (x * inverse_rms(x) * gain_ref[...]).astype(BF)
+        norm_rows(x_ref, gain_ref, normed_ref)
 
     @pl.when(j < 2 * parts)
     def _():
-        scale = jnp.where(j < parts, 1.0 / math.sqrt(HD), 1.0).astype(F32)
+        scale = jnp.where(j < parts, 1.0 / math.sqrt(HD), 1.0).astype(BF)
         for r in range(0, rows, chunk):
             pre = nn(normed_ref[r : r + chunk, :], w_ref[...])
             rotated = turn(pre, cos_ref[r : r + chunk, :], sin_ref[r : r + chunk, :])
-            out_ref[r : r + chunk, :] = rotated.astype(BF) * scale.astype(BF)
+            out_ref[r : r + chunk, :] = rotated.astype(BF) * scale
 
     @pl.when(j >= 2 * parts)
     def _():
@@ -310,6 +318,18 @@
     return inverse * (scaled - unit * inner), jnp.sum(grad * unit, axis=0, keepdims=True)
 
 
+def back_rows(acc_ref, x_ref, gain_ref, gain_part_ref, part_ref):
+    chunk = 128
+    gain_part_ref[...] = jnp.zeros_like(gain_part_ref)
+
+    @pl.loop(0, x_ref.shape[0] // chunk)
+    def _(i):
+        span = pl.ds(i * chunk, chunk)
+        part, piece = rms_back(acc_ref[span, :], x_ref[span, :].astype(F32), gain_ref[...])
+        part_ref[span, :] = part.astype(BF)
+        gain_part_ref[...] += piece
+
+
 def ffn_kernel(
     x_ref,
     cot_ref,
@@ -325,17 +345,16 @@
 ):
     j = pl.program_id(0)
     rows = x_ref.shape[0]
-    chunk = rows
+    chunk = 256
 
     @pl.when(j == 0)
     def _():
-        for r in range(0, rows, chunk):
-            x = x_ref[r : r + chunk, :].astype(F32)
-            normed_ref[r : r + chunk, :] = (x * inverse_rms(x) * gain_ref[...]).astype(BF)
+        norm_rows(x_ref, gain_ref, normed_ref)
         acc_ref[...] = jnp.zeros_like(acc_ref)
 
-    for r in range(0, rows, chunk):
-        span = slice(r, r + chunk)
+    @pl.loop(0, rows // chunk)
+    def _(i):
+        span = pl.ds(i * chunk, chunk)
         gate = nn(normed_ref[span, :], wg_ref[...])
         up = nn(normed_ref[span, :], wu_ref[...])
         grad_hidden = nn(cot_ref[span, :], wd_ref[...])
@@ -350,13 +369,7 @@
 
     @pl.when(j == pl.num_programs(0) - 1)
     def _():
-        gain_part = jnp.zeros_like(gain_part_ref)
-        for r in range(0, rows, chunk):
-            span = slice(r, r + chunk)
-            part, piece = rms_back(acc_ref[span, :], x_ref[span, :].astype(F32), gain_ref[...])
-            part_ref[span, :] = part.astype(BF)
-            gain_part = gain_part + piece
-        gain_part_ref[...] = gain_part
+        back_rows(acc_ref, x_ref, gain_ref, gain_part_ref, part_ref)
 
 
 def ffn(x, cot, gain, w, start, hidden_width):
@@ -400,26 +413,20 @@
 
 def input_grad_kernel(x_ref, gain_ref, g_ref, w_ref, part_ref, gain_part_ref, acc_ref):
     j = pl.program_id(0)
-    rows = x_ref.shape[0]
     chunk = 256
 
     @pl.when(j == 0)
     def _():
         acc_ref[...] = jnp.zeros_like(acc_ref)
 
-    for r in range(0, rows, chunk):
-        acc_ref[r : r + chunk, :] += nt(g_ref[0, r : r + chunk, :], w_ref[...])
+    @pl.loop(0, x_ref.shape[0] // chunk)
+    def _(i):
+        span = pl.ds(i * chunk, chunk)
+        acc_ref[span, :] += nt(g_ref[0, span, :], w_ref[...])
 
     @pl.when(j == pl.num_programs(0) - 1)
     def _():
-        gain_part = jnp.zeros_like(gain_part_ref)
-        for r in range(0, rows, chunk):
-            span = slice(r, r + chunk)
-            part, piece = rms_back(acc_ref[span, :], x_ref[span, :].astype(F32), gain_ref[...])
-            half = part_ref.shape[1]
-            part_ref[r // half, r % half : r % half + chunk, :] = part.astype(BF)
-            gain_part = gain_part + piece
-        gain_part_ref[...] = gain_part
+        back_rows(acc_ref, x_ref, gain_ref, gain_part_ref, part_ref)
 
 
 def input_grad(x, gain, grads, w):
@@ -436,9 +443,9 @@
             pl.BlockSpec((1, rows, COLS), lambda j: (j // per, 0, j % per)),
             pl.BlockSpec((d, COLS), lambda j: (0, j)),
         ],
-        out_specs=[pl.BlockSpec((2, rows // 2, d), lambda j: (0, 0, 0)), pl.BlockSpec((1, d), whole)],
+        out_specs=[pl.BlockSpec((rows, d), whole), pl.BlockSpec((1, d), whole)],
         out_shape=[
-            jax.ShapeDtypeStruct((2, rows // 2, d), BF),
+            jax.ShapeDtypeStruct((rows, d), BF),
             jax.ShapeDtypeStruct((1, d), F32),
         ],
         scratch_shapes=[pltpu.VMEM((rows, d), F32)],
@@ -456,14 +463,17 @@
     def __init__(self, devices, rows, count):
         self.devices, self.rows, self.count = devices, rows, count
         self.stages = devices.bit_length() - 1
-        self.lags = [2 if s == 1 else 1 for s in range(self.stages)]
+        self.lags = [min(s + 1, 2) for s in range(self.stages)]
+        self.slots = [2 * lag for lag in self.lags]
+        if self.stages >= 3:
+            self.slots[1] = self.slots[2] = 8
         self.starts = [sum(self.lags[:s]) for s in range(self.stages + 1)]
         self.steps = count + self.starts[-1]
 
     def scratch(self):
         shapes = []
         for s in range(self.stages):
-            slots, left = 2 * self.lags[s], self.devices >> (s + 1)
+            slots, left = self.slots[s], self.devices >> (s + 1)
             shapes.append(pltpu.VMEM((slots, 2, left, self.rows, COLS), BF))
             shapes.append(pltpu.VMEM((slots, left, self.rows, COLS), BF))
             shapes.append(pltpu.SemaphoreType.DMA((slots,)))
@@ -475,68 +485,115 @@
         self.sent_sem, self.got_sem = refs[2::4], refs[3::4]
         self.me, self.side = lax.axis_index("dp"), lax.axis_index("tensor")
 
-    def bit(self, s):
-        return (self.me // (1 << s)) % 2
-
-    def partner(self, s):
-        return (self.me + (1 - 2 * self.bit(s)) * (1 << s), self.side)
+    def late(self, block):
+        return (block % 4) // 3
+
+    def own_bit(self, b):
+        return (self.me // (1 << b)) % 2
+
+    def partner(self, b):
+        return self.me + (1 - 2 * self.own_bit(b)) * (1 << b)
+
+    def turned(self, s, block):
+        if s not in (1, 2) or self.stages < 3:
+            return self.own_bit(s), self.partner(s)
+        late = self.late(block)
+        return (
+            self.own_bit(s) * (1 - late) + self.own_bit(3 - s) * late,
+            self.partner(s) * (1 - late) + self.partner(3 - s) * late,
+        )
 
     def barrier(self):
         arrived = pltpu.get_barrier_semaphore()
-        for s in range(self.stages):
-            pl.semaphore_signal(arrived, inc=1, device_id=self.partner(s), device_id_type=MESH)
+        for b in range(self.stages):
+            pl.semaphore_signal(
+                arrived, inc=1, device_id=(self.partner(b), self.side), device_id_type=MESH
+            )
         pl.semaphore_signal(
             arrived, inc=1, device_id=(self.me, 1 - self.side), device_id_type=MESH
         )
         pl.semaphore_wait(arrived, self.stages + 1)
 
-    def copy(self, s, slot):
+    def copy(self, s, block):
+        slot = block % self.slots[s]
+        bit, partner = self.turned(s, block)
         return pltpu.make_async_remote_copy(
-            src_ref=self.held[s].at[slot, 1 - self.bit(s)],
+            src_ref=self.held[s].at[slot, 1 - bit],
             dst_ref=self.got[s].at[slot],
             send_sem=self.sent_sem[s].at[slot],
             recv_sem=self.got_sem[s].at[slot],
-            device_id=self.partner(s),
+            device_id=(partner, self.side),
             device_id_type=MESH,
         )
 
-    def advance(self, step, out_ref):
+    def advance(self, step, emit):
         for s in range(self.stages, 0, -1):
             block = step - self.starts[s]
 
             @pl.when((block >= 0) & (block < self.count))
             def _():
-                slot = block % (2 * self.lags[s - 1])
-                keep = self.bit(s - 1)
-                self.copy(s - 1, slot).wait()
+                slot = block % self.slots[s - 1]
+                self.copy(s - 1, block).wait()
+                keep, _ = self.turned(s - 1, block)
                 held, got = self.held[s - 1], self.got[s - 1]
                 if s == self.stages:
-                    out_ref[...] = held[slot, keep, 0].astype(F32) + got[slot, 0].astype(F32)
+                    emit(block, held[slot, keep, 0].astype(F32) + got[slot, 0].astype(F32))
                 else:
-                    later = block % (2 * self.lags[s])
-                    for k in range(self.devices >> s):
+                    later = block % self.slots[s]
+                    late = self.late(block)
+
+                    def add(k, carry):
                         total = held[slot, keep, k].astype(F32) + got[slot, k].astype(F32)
-                        self.held[s][later, k % 2, k // 2] = total.astype(BF)
-                    self.copy(s, later).start()
-
-    def put(self, slot, start, piece):
-        for r in range(0, piece.shape[0], self.rows):
-            k = (start + r) // self.rows
-            self.held[0][slot, k % 2, k // 2] = piece[r : r + self.rows].astype(BF)
-
-    def put_gain(self, slot, mine_ref, other_ref):
+                        bit, rest = k % 2, k // 2
+                        if s == 1 and self.stages >= 3:
+                            bit = bit * (1 - late) + (k // 2) % 2 * late
+                            rest = rest * (1 - late) + (k // 4 * 2 + k % 2) * late
+                        self.held[s][later, bit, rest] = total.astype(BF)
+                        return carry
+
+                    lax.fori_loop(0, self.devices >> s, add, 0)
+                    self.copy(s, block).start()
+
+    def multiply(self, block, turned_ref, rights):
+        slot = block % self.slots[0]
+        pieces = 4
+        size = self.devices // pieces
+
+        def piece(i, carry):
+            span = pl.ds(i * size * self.rows, size * self.rows)
+            total, start = None, 0
+            for right in rights:
+                part = nn(turned_ref[span, start : start + right.shape[0]], right)
+                total = part if total is None else total + part
+                start += right.shape[0]
+            for r in range(size):
+                block_rows = total[r * self.rows : (r + 1) * self.rows].astype(BF)
+                self.held[0][slot, r % 2, i * (size // 2) + r // 2] = block_rows
+            return carry
+
+        lax.fori_loop(0, pieces, piece, 0)
+        self.copy(0, block).start()
+
+    def put_gain(self, block, mine_ref, other_ref):
+        slot = block % self.slots[0]
         for k in range(self.devices):
             span = slice(k * self.rows, (k + 1) * self.rows)
             total = mine_ref[span, :].astype(F32) + other_ref[span, :].astype(F32)
             total = jnp.concatenate([total] * (COLS // LANES), axis=1)
             self.held[0][slot, k % 2, k // 2] = total.astype(BF)
+        self.copy(0, block).start()
 
 
 def turn_into(turned_ref, lefts):
     start = 0
     for left in lefts:
         for r in range(0, left.shape[0], 256):
-            turned_ref[:, start + r : start + r + 256] = left[r : r + 256, :].T
+
+            @pl.loop(0, left.shape[1] // 256)
+            def _(i):
+                span = pl.ds(pl.multiple_of(i * 256, 256), 256)
+                turned_ref[span, start + r : start + r + 256] = left[r : r + 256, span].T
+
         start += left.shape[0]
 
 
@@ -551,17 +608,50 @@
     )
 
 
+def emit_into(outs, per, turned, block, value):
+    for kind, out in enumerate(outs):
+        first, last = kind * per, (kind + 1) * per
+
+        @pl.when((block >= first) & (block < last))
+        def _():
+            out[...] = value.T if kind in turned else value
+
+
+def emit_specs(scatter, kinds, per, width, turned):
+    lead = scatter.starts[-1]
+    specs, shapes = [], []
+    for kind in range(kinds + 1):
+        most = per - 1 if kind < kinds else 0
+
+        def where(j, kind=kind, most=most):
+            return jnp.clip(j - lead - kind * per, 0, most)
+
+        if kind in turned:
+            specs.append(pl.BlockSpec((COLS, scatter.rows), lambda j, f=where: (f(j), 0)))
+            shapes.append(jax.ShapeDtypeStruct((width, scatter.rows), F32))
+        else:
+            specs.append(pl.BlockSpec((scatter.rows, COLS), lambda j, f=where: (0, f(j))))
+            size = width if kind < kinds else COLS
+            shapes.append(jax.ShapeDtypeStruct((scatter.rows, size), F32))
+    return specs, shapes
+
+
 def ffn_scatter_kernel(scatter, per, *refs):
     (
         norm_own, norm_other, cot_own, cot_other, right_own, right_other,
-        part_own, part_other, gain_ref,
-    ) = refs[:9]
-    out_ref, gm_ref = refs[9:11]
-    turned_ref, got_part, gm_own, gain_got, gain_sems, x_sems, local_sem = refs[11:18]
-    scatter.bind(refs[18:])
+        part_own, part_other, gain_ref, middle_own, wd_ref,
+    ) = refs[:11]
+    outs, gm_ref, block_out_ref = refs[11:15], refs[15], refs[16]
+    (
+        turned_ref, got_part, gm_own, gain_got, acc_own, acc_other, block_send, block_got,
+        gain_sems, x_sems, block_sems, local_sem,
+    ) = refs[17:29]
+    scatter.bind(refs[29:])
     step = pl.program_id(0)
     side = scatter.side
-    quarter = part_own.shape[0] // QUARTERS
+    half = part_own.shape[0]
+    quarter = half // QUARTERS
+    row_chunk = 128
 
     def part_copy(r):
         span = pl.ds(r * quarter, quarter)
@@ -585,6 +675,16 @@
             device_id_type=MESH,
         )
 
+    def block_copy():
+        return pltpu.make_async_remote_copy(
+            src_ref=block_send,
+            dst_ref=block_got,
+            send_sem=block_sems.at[0],
+            recv_sem=block_sems.at[1],
+            device_id=(scatter.me, 1 - side),
+            device_id_type=MESH,
+        )
+
     def gm_keep():
         return pltpu.make_async_copy(gm_own, gm_ref.at[side], local_sem)
 
@@ -594,50 +694,66 @@
         for r in range(QUARTERS):
             part_copy(r).start()
         gain_copy(scatter, gain_ref, gain_got, gain_sems).start()
+        turn_into(turned_ref, [cot_own, cot_other])
+        acc_own[...] = jnp.zeros_like(acc_own)
+        acc_other[...] = jnp.zeros_like(acc_other)
+
+    @pl.when(step == per)
+    def _():
         turn_into(turned_ref, [norm_own, norm_other])
 
-    @pl.when(step == 2 * per)
-    def _():
-        turn_into(turned_ref, [cot_own, cot_other])
-
-    scatter.advance(step, out_ref)
+    scatter.advance(step, functools.partial(emit_into, outs, per, (0,)))
 
     @pl.when(step < 3 * per)
     def _():
-        slot = step % 2
-        piece_rows = 384
-        half = right_own.shape[1]
-        for r in range(0, turned_ref.shape[0], piece_rows):
-            span = slice(r, r + piece_rows)
-            piece = nn(turned_ref[span, :half], right_own[0])
-            piece = piece + nn(turned_ref[span, half:], right_other[0])
-            scatter.put(slot, r, piece)
-        scatter.copy(0, slot).start()
+        scatter.multiply(step, turned_ref, (right_own[0], right_other[0]))
 
     @pl.when(step == 3 * per)
     def _():
-        slot = step % 2
         gain_copy(scatter, gain_ref, gain_got, gain_sems).wait()
-        scatter.put_gain(slot, gain_ref, gain_got)
-        scatter.copy(0, slot).start()
+        scatter.put_gain(step, gain_ref, gain_got)
+
+    @pl.when(step < per)
+    def _():
+        @pl.loop(0, half // 256)
+        def _(i):
+            span = pl.ds(i * 256, 256)
+            acc_own[span, :] += nt(right_own[0, span, :], wd_ref[...])
+            acc_other[span, :] += nt(right_other[0, span, :], wd_ref[...])
 
     for r in range(QUARTERS):
 
         @pl.when(step == 3 + 2 * r)
         def _():
-            span = slice(r * quarter, (r + 1) * quarter)
             part_copy(r).wait()
-            total = cot_own[span, :].astype(F32) + part_own[span, :].astype(F32)
-            gm_own[span, :] = (total + got_part[span, :].astype(F32)).astype(BF)
+
+            @pl.loop(r * quarter // row_chunk, (r + 1) * quarter // row_chunk)
+            def _(i):
+                span = pl.ds(i * row_chunk, row_chunk)
+                total = cot_own[span, :].astype(F32) + part_own[span, :].astype(F32)
+                gm_own[span, :] = (total + got_part[span, :].astype(F32)).astype(BF)
+
             gm_copy(r).start()
             if r == QUARTERS - 1:
                 gm_keep().start()
 
+    @pl.when(step == 3 + 2 * QUARTERS)
+    def _():
+        block_send[...] = acc_other[...].astype(BF)
+        block_copy().start()
+
     @pl.when(step == scatter.steps - 1)
     def _():
         for r in range(QUARTERS):
             gm_copy(r).wait()
         gm_keep().wait()
+        block_copy().wait()
+
+        @pl.loop(0, half // row_chunk)
+        def _(i):
+            span = pl.ds(i * row_chunk, row_chunk)
+            total = middle_own[span, :].astype(F32) + acc_own[span, :]
+            block_out_ref[span, :] = (total + block_got[span, :].astype(F32)).astype(BF)
 
 
 def resident(shape):
@@ -654,17 +770,19 @@
     )
 
 
-def ffn_scatter(devices, normed, cots, rights, parts, gain_block):
-    half, d = normed[0].shape
-    per = rights[0].shape[2] // COLS
+def ffn_scatter(devices, normed, cots, rights, parts, gain_block, middle, w):
+    half, d = middle.shape
+    width = rights[0].shape[2]
+    per = width // COLS
     scatter = Scatter(devices, d // devices, 3 * per + 1)
-    last = 3 * per - 1
+    assert per >= 3 + 2 * QUARTERS - 3 and scatter.rows * devices == d
 
     def right_map(j):
-        c = jnp.minimum(j, last)
-        return (c // per, 0, c % per)
-
-    first = scatter.starts[-1]
+        c = jnp.minimum(j, 3 * per - 1)
+        return ((c // per + 2) % 3, 0, c % per)
+
+    specs, shapes = emit_specs(scatter, 3, per, width, (0,))
+    whole = lambda j: (0, 0)
     return pl.pallas_call(
         functools.partial(ffn_scatter_kernel, scatter, per),
         grid=(scatter.steps,),
@@ -674,39 +792,40 @@
             resident((half, d)),
             pl.BlockSpec(memory_space=pl.ANY),
             resident((d, LANES)),
-        ],
-        out_specs=[
-            pl.BlockSpec((scatter.rows, COLS), lambda j: (0, jnp.maximum(j - first, 0))),
-            pl.BlockSpec(memory_space=pl.ANY),
-        ],
-        out_shape=[
-            jax.ShapeDtypeStruct((scatter.rows, scatter.count * COLS), F32),
-            jax.ShapeDtypeStruct((2, half, d), BF),
-        ],
+            resident((half, d)),
+            pl.BlockSpec((d, COLS), lambda j: (0, 2 * per + jnp.minimum(j, per - 1))),
+        ],
+        out_specs=specs + [pl.BlockSpec(memory_space=pl.ANY), pl.BlockSpec((half, d), whole)],
+        out_shape=shapes
+        + [jax.ShapeDtypeStruct((2, half, d), BF), jax.ShapeDtypeStruct((half, d), BF)],
         scratch_shapes=[
             pltpu.VMEM((d, 2 * half), BF),
             pltpu.VMEM((half, d), BF),
             pltpu.VMEM((half, d), BF),
             pltpu.VMEM((d, LANES), BF),
+            pltpu.VMEM((half, d), F32),
+            pltpu.VMEM((half, d), F32),
+            pltpu.VMEM((half, d), BF),
+            pltpu.VMEM((half, d), BF),
             pltpu.SemaphoreType.DMA((2,)),
             pltpu.SemaphoreType.DMA((4, QUARTERS)),
+            pltpu.SemaphoreType.DMA((2,)),
             pltpu.SemaphoreType.DMA,
         ]
         + scatter.scratch(),
         compiler_params=remote_settings(0),
-        cost_estimate=cost(12 * half * d * per * COLS, 20 * half * d),
+        cost_estimate=cost(16 * half * d * per * COLS, 20 * half * d),
         name="ffn_scatter",
-    )(*normed, *cots, *rights, *parts, gain_block)
+    )(*normed, *cots, *rights, *parts, gain_block, middle, w)
 
 
 def attention_scatter_kernel(scatter, per, *refs):
     normed_ref, gm_ref, right_ref, attended_ref, part_ref, gain_ref = refs[:6]
-    out_ref, got_part = refs[6:8]
-    turned_ref, gain_got, gain_sems, x_sems = refs[8:12]
-    scatter.bind(refs[12:])
+    outs, got_part = refs[6:11], refs[11]
+    turned_ref, gain_got, gain_sems, x_sems = refs[12:16]
+    scatter.bind(refs[16:])
     step = pl.program_id(0)
     side = scatter.side
-    piece_rows = 384
 
     def part_copy():
         return pltpu.make_async_remote_copy(
@@ -729,26 +848,20 @@
     def _():
         turn_into(turned_ref, [gm_ref])
 
-    scatter.advance(step, out_ref)
-    slot = step % 2
+    scatter.advance(step, functools.partial(emit_into, outs, per, (3,)))
 
     @pl.when(step < 3 * per)
     def _():
-        for r in range(0, turned_ref.shape[0], piece_rows):
-            scatter.put(slot, r, nn(turned_ref[r : r + piece_rows, :], right_ref[0]))
-        scatter.copy(0, slot).start()
+        scatter.multiply(step, turned_ref, (right_ref[0],))
 
     @pl.when((step >= 3 * per) & (step < 4 * per))
     def _():
-        for r in range(0, turned_ref.shape[0], piece_rows):
-            scatter.put(slot, r, nn(turned_ref[r : r + piece_rows, :], attended_ref[...]))
-        scatter.copy(0, slot).start()
+        scatter.multiply(step, turned_ref, (attended_ref[...],))
 
     @pl.when(step == 4 * per)
     def _():
         gain_copy(scatter, gain_ref, gain_got, gain_sems).wait()
-        scatter.put_gain(slot, gain_ref, gain_got)
-        scatter.copy(0, slot).start()
+        scatter.put_gain(step, gain_ref, gain_got)
 
     @pl.when(step == scatter.steps - 1)
     def _():
@@ -757,7 +870,8 @@
 
 def attention_scatter(devices, normed, gm, grads, attended, part, gain_block):
     length, d = normed.shape
-    per = grads.shape[2] // COLS
+    width = grads.shape[2]
+    per = width // COLS
     scatter = Scatter(devices, d // devices, 4 * per + 1)
 
     def right_map(j):
@@ -767,7 +881,7 @@
     def attended_map(j):
         return (0, jnp.clip(j - 3 * per, 0, per - 1))
 
-    first = scatter.starts[-1]
+    specs, shapes = emit_specs(scatter, 4, per, width, (3,))
     return pl.pallas_call(
         functools.partial(attention_scatter_kernel, scatter, per),
         grid=(scatter.steps,),
@@ -779,14 +893,8 @@
             pl.BlockSpec(memory_space=pl.ANY),
             resident((d, LANES)),
         ],
-        out_specs=[
-            pl.BlockSpec((scatter.rows, COLS), lambda j: (0, jnp.maximum(j - first, 0))),
-            pl.BlockSpec(memory_space=pl.ANY),
-        ],
-        out_shape=[
-            jax.ShapeDtypeStruct((scatter.rows, scatter.count * COLS), F32),
-            jax.ShapeDtypeStruct((length // 2, d), BF),
-        ],
+        out_specs=specs + [pl.BlockSpec(memory_space=pl.ANY)],
+        out_shape=shapes + [jax.ShapeDtypeStruct((length // 2, d), BF)],
         scratch_shapes=[
             pltpu.VMEM((d, length), BF),
             pltpu.VMEM((d, LANES), BF),
@@ -852,8 +960,9 @@
 
     bias, positions = tree_tables(parents[0], seg_rows)
     cosine, sine = turn_tables(positions, COLS)
-    rows_all = place(tokens, swap(tokens))
-    cot_other = swap(cotangent)
+    rows_all, cot_other = lax.optimization_barrier(
+        (place(tokens, swap(tokens)), swap(cotangent))
+    )
 
     qkv, normed_one = project(rows_all, attn_row, cosine, sine, first, width)
     attended, lse = attend(qkv, bias, width, seg_rows)
@@ -875,55 +984,49 @@
     def gain_block(gain_sum):
         return jnp.broadcast_to(gain_sum.astype(BF).T, (d, LANES))
 
-    ffn_grads, grad_middle = ffn_scatter(
+    down_grad, gate_grad, up_grad, ffn_gain_grad, grad_middle, block_out = ffn_scatter(
         devices,
         (normed_own, normed_other),
         (cotangent, cot_other),
         (gg_own, gg_other),
         (part_own, part_other),
         gain_block(gp_own + gp_other),
+        middle,
+        second,
     )
     grad_middle_all = grad_middle.reshape(length, d)
-
-    down_turned = second[:, 2 * hidden_width :]
-    out_received = swap(nt(gg_other[2], down_turned).astype(BF))
-    block_out = (
-        middle.astype(F32) + nt(gg_own[2], down_turned) + out_received.astype(F32)
-    ).astype(BF)
 
     grad_attended = nn(grad_middle_all, out_turned).astype(BF)
     grads = attend_back(
         qkv, attended, grad_attended, lse, bias, cosine[:, :LANES], sine[:, :LANES], seg_rows
     )
     part, gain_part = input_grad(rows_all, attn_row, grads, first)
-    attn_grads, tokens_received = attention_scatter(
+    part = part.reshape(2, half, d)
+    query_grad, key_grad, value_grad, output_grad, attn_gain_grad, received = attention_scatter(
         devices, normed_one, grad_middle_all, grads, attended, part, gain_block(gain_part)
     )
     token_grad = (
         lax.dynamic_index_in_dim(grad_middle, mine, 0, False).astype(F32)
         + lax.dynamic_index_in_dim(part, mine, 0, False).astype(F32)
-        + tokens_received.astype(F32)
+        + received.astype(F32)
     ).astype(BF)
     gain_rows = d // devices // 2
 
     def gain_piece(columns):
         return lax.dynamic_slice_in_dim(columns[:, 0], mine * gain_rows, gain_rows, 0)
-
-    def column(grads_out, kind, size):
-        return grads_out[:, kind * size : (kind + 1) * size]
 
     return (
         block_out,
         token_grad,
-        column(attn_grads, 0, width),
-        column(attn_grads, 1, width),
-        column(attn_grads, 2, width),
-        column(attn_grads, 3, width).T,
-        column(ffn_grads, 0, hidden_width),
-        column(ffn_grads, 1, hidden_width),
-        column(ffn_grads, 2, hidden_width).T,
-        gain_piece(attn_grads[:, 4 * width :]),
-        gain_piece(ffn_grads[:, 3 * hidden_width :]),
+        query_grad,
+        key_grad,
+        value_grad,
+        output_grad,
+        gate_grad,
+        up_grad,
+        down_grad,
+        gain_piece(attn_gain_grad),
+        gain_piece(ffn_gain_grad),
     )
 
 

time: 637 us -> 581 us (0.912); the launches traced: 627 us -> 580 us
  waiting for transfers between devices: 166 us -> 119 us
  matrix products: 24.1 us -> 10.9 us
  Pallas kernels: 375 us -> 387 us
  local copies, waits for them, and re-layouts: 26.2 us -> 32.9 us
    ppermute x5 -> x4, waiting for transfers between devices: 124 us -> 91 us  [swap(): return lax.ppermute(x, 'tensor', [(0, 1), (1, 0)])]
    all_gather x2, waiting for transfers between devices: 42.6 us -> 28.1 us  [gather(): return lax.all_gather(shard, 'dp', axis=0, tiled=True)]
    dot_general x4 -> x2, matrix products: 19.8 us -> 5.53 us  [nt(): lax.dot_general(a, b, (((1,), (1,)), ((), ())), preferred_element_type=F32)]
    unnamed x36 -> x50, local copies, waits for them, and re-layouts: 5.71 us -> 17.3 us
  transfers between devices with their start and end apart: 7 -> 6, of which waited for: 5 -> 5; matrix products, arithmetic and copies ran while one was open for 7% -> 3% of each run, Pallas kernels for 54% -> 13%
where the time goes in v3:
time: 581 us; the launch traced here: 580 us
  Pallas kernels  387 us (67%)
  waiting for transfers between devices  119 us (20%)
  local copies, waits for them, and re-layouts  32.9 us (6%)
  between operations  14.4 us (2%)
  matrix products  10.9 us (2%)
  other arithmetic  9.72 us (2%)
  starting transfers between devices  6.33 us (1%)
    pallas_call x1, Pallas kernels, ffn_scatter(): pl.pallas_call(functools.partial(ffn_scatter_kernel, scatter, per), grid=...  136 us
    ppermute x4, waiting for transfers between devices, swap(): return lax.ppermute(x, 'tensor', [(0, 1), (1, 0)])  91 us
    pallas_call x2, Pallas kernels, ffn(): pl.pallas_call(ffn_kernel, grid=(steps,), in_specs=[pl.BlockSpec((rows, d...  79.1 us
    pallas_call x1, Pallas kernels, attention_scatter(): pl.pallas_call(functools.partial(attention_scatter_kernel, scatter, per),...  78.8 us
    pallas_call x1, Pallas kernels, attend_back(): pl.pallas_call(functools.partial(attend_back_kernel, block, seg_rows), gr...  33.9 us
    all_gather x2, waiting for transfers between devices, gather(): return lax.all_gather(shard, 'dp', axis=0, tiled=True)  28.1 us
    pallas_call x1, Pallas kernels, attend(): pl.pallas_call(functools.partial(attend_kernel, block, seg_rows), grid=(g...  21.6 us
    pallas_call x1, Pallas kernels, input_grad(): pl.pallas_call(input_grad_kernel, grid=(kinds * per,), in_specs=[pl.Block...  20.7 us
  transfers between devices with their start and end apart: 6, of which 5 were waited for; matrix products, arithmetic and copies ran while one was open for 3% of the time, Pallas kernels for 13%

profile of v3, /device:TPU:0, one launch (start us, length us, event | category | flops | bytes accessed | tf_op | source)
XLA Modules:
  0.0 579.9 jit_solution(2828437488254083801)
XLA Ops:
  7.2 2.0 pad_maximum_fusion.1
  9.3 2.3 pad_maximum_fusion
  11.6 3.0 collective-permute-start
  19.8 1.9 broadcast_in_dim.26
  21.7 2.7 constant_dynamic-update-slice_fusion.1
  24.4 25.8 %collective-permute-done = bf16[512,1536]{1,0:T(8,128)(2,1)} collective-permute-done((bf16[512,1536]{1,0:T(8,128)(2,1)}, bf16[512,1536]{1,0:T(8,128)(2,1)}, u32[]{:S(2)}, u32[]{:S(2)}) %collective-permute-start) | collective-permute-done | bytes 1572896 | tf_op jit(solution)/shard_map/ppermute | solution.py:912
  50.2 2.7 constant_dynamic-update-slice_fusion.x_ref
  52.9 30.2 %collective-permute-done.1.cot_ref.refs_3_ = bf16[512,1536]{1,0:T(8,128)(2,1)} collective-permute-done((bf16[512,1536]{1,0:T(8,128)(2,1)}, bf16[512,1536]{1,0:T(8,128)(2,1)}, u32[]{:S(2)}, u32[]{:S(2)}) %collective-permute-start.1) | collective-permute-done | bytes 1572896 | tf_op jit(solution)/shard_map/ppermute | solution.py:912
  83.1 12.0 %all-gather.3.cloned.1.call-done.w_ref = bf16[1536,3072]{1,0:T(8,128)(2,1)} async-done(((bf16[96,3072]{1,0:T(8,128)(2,1)}), bf16[1536,3072]{1,0:T(8,128)(2,1)}) %all-gather.3.cloned.1.call-update) | async-done | bytes 9437200 | tf_op jit(solution)/shard_map/all_gather | solution.py:950
  95.1 16.0 %project.1 = (bf16[1024,2304]{1,0:T(8,128)(2,1)}, bf16[1024,1536]{1,0:T(8,128)(2,1)S(1)}) custom-call(bf16[1024,1536]{1,0:T(8,128)(2,1)} %constant_dynamic-update-slice_fusion.x_ref, f32[1,1536]{1,0:T(1,128)S(1)} %broadcast_in_dim.27.gain_ref, f32[1024,256]{1,0:T(8,128)S(1)} %copy.49.cos_ref, f32[1024,256]{1,0:T(8,128)S(1)} %copy.50.sin_ref, ...), custom_call_target="tpu_custom_call" | custom-call | flops 7247757312 | bytes 13369344 | tf_op jit(solution)/shard_map/project/pallas_call | solution.py:120
  112.7 21.6 %attend.1 = (bf16[1024,768]{1,0:T(8,128)(2,1)S(1)}, f32[6,2,1024]{2,1,0:T(2,128)S(1)}) custom-call(bf16[1024,2304]{1,0:T(8,128)(2,1)} %get-tuple-element.40.q_ref.k_ref.v_ref, bf16[1024,2304]{1,0:T(8,128)(2,1)} %get-tuple-element.40.q_ref.k_ref.v_ref, bf16[1024,2304]{1,0:T(8,128)(2,1)} %get-tuple-element.40.q_ref.k_ref.v_ref, ...), custom_call_target="tpu_custom_call" | custom-call | flops 6442450944 | bytes 6291456 | tf_op jit(solution)/shard_map/attend/pallas_call | solution.py:199
  137.5 35.1 %collective-permute-done.2 = bf16[512,1536]{1,0:T(8,128)(2,1)S(1)} collective-permute-done((bf16[512,1536]{1,0:T(8,128)(2,1)S(1)}, bf16[512,1536]{1,0:T(8,128)(2,1)S(1)}, u32[]{:S(2)}, u32[]{:S(2)}) %collective-permute-start.2) | collective-permute-done | bytes 1572896 | tf_op jit(solution)/shard_map/ppermute | solution.py:912
  172.5 4.1 add_convert_fusion.x_ref.refs_9_
  178.3 16.1 %all-gather.5.cloned.1.call-done.wg_ref.wu_ref.wd_ref.refs_10_ = bf16[1536,6144]{1,0:T(8,128)(2,1)} async-done(((bf16[96,6144]{1,0:T(8,128)(2,1)}), bf16[1536,6144]{1,0:T(8,128)(2,1)}) %all-gather.5.cloned.1.call-update) | async-done | bytes 18874384 | tf_op jit(solution)/shard_map/all_gather | solution.py:950
  194.3 39.6 %ffn.2 = (bf16[3,512,2048]{2,1,0:T(8,128)(2,1)}, bf16[512,1536]{1,0:T(8,128)(2,1)S(1)}, bf16[512,1536]{1,0:T(8,128)(2,1)S(1)}, f32[1,1536]{1,0:T(1,128)S(1)}) custom-call(bf16[512,1536]{1,0:T(8,128)(2,1)} %add_convert_fusion.x_ref.refs_9_, bf16[512,1536]{1,0:T(8,128)(2,1)} %refs_2_.1, f32[1,1536]{1,0:T(1,128)S(1)} %broadcast_in_dim.32.gain_ref, ...), custom_call_target="tpu_custom_call" | custom-call | flops 16106127360 | bytes 31457280 | tf_op jit(solution)/shard_map/ffn/pallas_call | solution.py:380
  236.3 39.5 %ffn.3 = (bf16[3,512,2048]{2,1,0:T(8,128)(2,1)}, bf16[512,1536]{1,0:T(8,128)(2,1)S(1)}, bf16[512,1536]{1,0:T(8,128)(2,1)S(1)}, f32[1,1536]{1,0:T(1,128)S(1)}) custom-call(bf16[512,1536]{1,0:T(8,128)(2,1)} %collective-permute-done.3.x_ref, bf16[512,1536]{1,0:T(8,128)(2,1)} %collective-permute-done.1.cot_ref.refs_3_, f32[1,1536]{1,0:T(1,128)S(1)} %broadcast_in_dim.32.gain_ref, ...), custom_call_target="tpu_custom_call" | custom-call | flops 16106127360 | bytes 31457280 | tf_op jit(solution)/shard_map/ffn/pallas_call | solution.py:380
  279.2 136.4 %ffn_scatter.1 = (f32[2048,96]{1,0:T(8,128)}, f32[96,2048]{1,0:T(8,128)}, f32[96,2048]{1,0:T(8,128)}, f32[96,256]{1,0:T(8,128)}, bf16[2,512,1536]{2,1,0:T(8,128)(2,1)}, /*index=5*/bf16[512,1536]{1,0:T(8,128)(2,1)}) custom-call(bf16[512,1536]{1,0:T(8,128)(2,1)} %copy-done.2, bf16[512,1536]{1,0:T(8,128)(2,1)} %copy-done.4, bf16[512,1536]{1,0:T(8,128)(2,1)} %refs_2_.1, ...), custom_call_target="tpu_custom_call" | custom-call | flops 25769803776 | bytes 15728640 | tf_op jit(solution)/shard_map/ffn_scatter/pallas_call | solution.py:786
  416.4 2.4 copy.56
  418.8 5.3 fusion.5.do_ref
  424.2 33.9 %attend_back.1.g_ref.refs_2_ = bf16[3,1024,768]{2,1,0:T(8,128)(2,1)} custom-call(bf16[1024,2304]{1,0:T(8,128)(2,1)} %get-tuple-element.40.q_ref.k_ref.v_ref, bf16[1024,2304]{1,0:T(8,128)(2,1)} %get-tuple-element.40.q_ref.k_ref.v_ref, bf16[1024,2304]{1,0:T(8,128)(2,1)} %get-tuple-element.40.q_ref.k_ref.v_ref, bf16[1024,768]{1,0:T(8,128)(2,1)S(1)} %copy-done.7, ...), custom_call_target="tpu_custom_call" | custom-call | flops 16106127360 | bytes 12582912 | tf_op jit(solution)/shard_map/attend_back/pallas_call | solution.py:287
  458.1 20.7 %input_grad.1 = (bf16[1024,1536]{1,0:T(8,128)(2,1)S(1)}, f32[1,1536]{1,0:T(1,128)S(1)}) custom-call(bf16[1024,1536]{1,0:T(8,128)(2,1)} %constant_dynamic-update-slice_fusion.x_ref, f32[1,1536]{1,0:T(1,128)S(1)} %broadcast_in_dim.27.gain_ref, bf16[3,1024,768]{2,1,0:T(8,128)(2,1)} %attend_back.1.g_ref.refs_2_, ...), custom_call_target="tpu_custom_call" | custom-call | flops 7247757312 | bytes 11796480 | tf_op jit(solution)/shard_map/input_grad/pallas_call | solution.py:437
  481.5 78.8 %attention_scatter.1 = (f32[96,768]{1,0:T(8,128)}, f32[96,768]{1,0:T(8,128)}, f32[96,768]{1,0:T(8,128)}, f32[768,96]{1,0:T(8,128)}, f32[96,256]{1,0:T(8,128)}, /*index=5*/bf16[512,1536]{1,0:T(8,128)(2,1)}) custom-call(bf16[1024,1536]{1,0:T(8,128)(2,1)} %copy-done.8, bf16[1024,1536]{1,0:T(8,128)(2,1)} %bitcast.29, ...), custom_call_target="tpu_custom_call" | custom-call | flops 9663676416 | bytes 31457280 | tf_op jit(solution)/shard_map/attention_scatter/pallas_call | solution.py:885
  562.3 1.9 copy.55
  564.2 3.7 fusion
  (101 shorter events, 27.8 us)
Async XLA Ops:
  7.2 87.9 %all-gather.3.cloned.1.call-start = ((), (), s32[]{:S(2)}) async-start(), calls=%async_computation | async-start | bytes 10027008 | tf_op jit(solution)/shard_map/all_gather | solution.py:950
  9.2 5.5 copy-start.17
  9.2 6.6 %copy-start.15 = (f32[1536]{0:T(1024)S(1)}, f32[1536]{0:T(1024)}, u32[]{:S(2)}) copy-start(f32[1536]{0:T(1024)} %param.14) | copy-start | bytes 18436
  9.2 185.1 %all-gather.5.cloned.1.call-start = ((), (), s32[]{:S(2)}) async-start(), calls=%async_computation.1 | async-start | bytes 20054016 | tf_op jit(solution)/shard_map/all_gather | solution.py:950
  11.6 38.5 %collective-permute-start = (bf16[512,1536]{1,0:T(8,128)(2,1)}, bf16[512,1536]{1,0:T(8,128)(2,1)}, u32[]{:S(2)}, u32[]{:S(2)}) collective-permute-start(bf16[512,1536]{1,0:T(8,128)(2,1)} %param.12), channel_id=1, source_target_pairs={{0,1},{1,0},{2,3},{3,2},{4,5},{5,4},{6,7},{7,6},{8,9},{9,8},{10,11... | collective-permute-start | bytes 4718600 | tf_op jit(solution)/shard_map/ppermute | solution.py:912
  14.6 68.4 %collective-permute-start.1 = (bf16[512,1536]{1,0:T(8,128)(2,1)}, bf16[512,1536]{1,0:T(8,128)(2,1)}, u32[]{:S(2)}, u32[]{:S(2)}) collective-permute-start(bf16[512,1536]{1,0:T(8,128)(2,1)} %refs_2_.1), channel_id=1, source_target_pairs={{0,1},{1,0},{2,3},{3,2},{4,5},{5,4},{6,7},{7,6},{8,9},{9,8},{10,11... | collective-permute-start | bytes 4718600 | tf_op jit(solution)/shard_map/ppermute | solution.py:912
  95.0 39.3 %slice-start = ((s8[9437184]{0:T(1024)(128)(4,1)}), s8[1048576]{0:T(1024)(128)(4,1)S(1)}, s32[]{:S(2)}) async-start(s8[9437184]{0:T(1024)(128)(4,1)} %bitcast.33), calls=%async_computation.2 | async-start | bytes 2097152
  95.0 39.3 %slice-start.1 = ((s8[9437184]{0:T(1024)(128)(4,1)}), s8[4194304]{0:T(1024)(128)(4,1)S(1)}, s32[]{:S(2)}) async-start(s8[9437184]{0:T(1024)(128)(4,1)} %bitcast.33), calls=%async_computation.3 | async-start | bytes 8388608
  111.0 1.7 copy-start.8
  112.7 21.7 %slice-start.2 = ((s8[9437184]{0:T(1024)(128)(4,1)}), s8[4194304]{0:T(1024)(128)(4,1)S(1)}, s32[]{:S(2)}) async-start(s8[9437184]{0:T(1024)(128)(4,1)} %bitcast.33), calls=%async_computation.4 | async-start | bytes 8388608
  134.3 38.2 %copy-start.6 = (bf16[1024,768]{1,0:T(8,128)(2,1)}, bf16[1024,768]{1,0:T(8,128)(2,1)S(1)}, u32[]{:S(2)}) copy-start(bf16[1024,768]{1,0:T(8,128)(2,1)S(1)} %get-tuple-element.41.o_ref.refs_3_) | copy-start | bytes 4718596
  135.8 42.4 %copy-start.16 = (f32[1536]{0:T(1024)S(1)}, f32[1536]{0:T(1024)}, u32[]{:S(2)}) copy-start(f32[1536]{0:T(1024)} %param.15) | copy-start | bytes 18436
  135.8 36.7 %collective-permute-start.2 = (bf16[512,1536]{1,0:T(8,128)(2,1)S(1)}, bf16[512,1536]{1,0:T(8,128)(2,1)S(1)}, u32[]{:S(2)}, u32[]{:S(2)}) collective-permute-start(bf16[512,1536]{1,0:T(8,128)(2,1)S(1)} %convolution_convert_fusion), channel_id=1, source_target_pairs={{0,1},{1,0},{2,3},{3,2},{4,5},{5,4},{6,7},{7,6},{8,9},{9,8},{10,11... | collective-permute-start | bytes 4718600 | tf_op jit(solution)/shard_map/ppermute | solution.py:912
  176.6 59.6 %collective-permute-start.3 = (bf16[512,1536]{1,0:T(8,128)(2,1)}, bf16[512,1536]{1,0:T(8,128)(2,1)}, u32[]{:S(2)}, u32[]{:S(2)}) collective-permute-start(bf16[512,1536]{1,0:T(8,128)(2,1)} %add_convert_fusion.x_ref.refs_9_), channel_id=1, source_target_pairs={{0,1},{1,0},{2,3},{3,2},{4,5},{5,4},{6,7},{7,6},{8,9},{9,8},{10,11... | collective-permute-start | bytes 4718600 | tf_op jit(solution)/shard_map/ppermute | solution.py:912
  235.1 1.2 copy-start.3
  276.9 1.2 copy-start.5
  418.8 5.3 copy-start.7
  478.8 1.6 copy-start
  481.5 82.7 %copy-start.1 = (bf16[1024,1536]{1,0:T(8,128)(2,1)S(1)}, bf16[1024,1536]{1,0:T(8,128)(2,1)}, u32[]{:S(2)}) copy-start(bf16[1024,1536]{1,0:T(8,128)(2,1)} %copy-done) | copy-start | bytes 9437188
  564.2 3.7 copy-start.9
  567.9 1.9 copy-start.13
  567.9 2.6 copy-start.12
  567.9 3.3 copy-start.11
  569.1 3.0 copy-start.10
  (3 other events, 3.4 us)
Sparse Core Ops, SparseCore 0:
  10.9 84.1 all-gather.2
  97.2 97.0 all-gather.4

commit v4 on v3

--- a/solution.py
+++ b/solution.py
@@ -320,19 +320,20 @@
 
 def back_rows(acc_ref, x_ref, gain_ref, gain_part_ref, part_ref):
     chunk = 128
-    gain_part_ref[...] = jnp.zeros_like(gain_part_ref)
 
     @pl.loop(0, x_ref.shape[0] // chunk)
     def _(i):
         span = pl.ds(i * chunk, chunk)
         part, piece = rms_back(acc_ref[span, :], x_ref[span, :].astype(F32), gain_ref[...])
-        part_ref[span, :] = part.astype(BF)
-        gain_part_ref[...] += piece
+        part_ref[span, :] = part.astype(part_ref.dtype)
+        gain_part_ref[...] += jnp.broadcast_to(piece, gain_part_ref.shape)
 
 
 def ffn_kernel(
-    x_ref,
-    cot_ref,
+    x_own,
+    x_other,
+    cot_own,
+    cot_other,
     gain_ref,
     wg_ref,
     wu_ref,
@@ -341,118 +342,90 @@
     normed_ref,
     part_ref,
     gain_part_ref,
+    cot_ref,
     acc_ref,
 ):
-    j = pl.program_id(0)
-    rows = x_ref.shape[0]
+    h, j = pl.program_id(0), pl.program_id(1)
     chunk = 256
 
+    @pl.when((h == 0) & (j == 0))
+    def _():
+        gain_part_ref[...] = jnp.zeros_like(gain_part_ref)
+
+    for side, (x_ref, c_ref) in enumerate(((x_own, cot_own), (x_other, cot_other))):
+
+        @pl.when((h == side) & (j == 0))
+        def _():
+            norm_rows(x_ref, gain_ref, normed_ref)
+            cot_ref[...] = c_ref[...]
+
     @pl.when(j == 0)
     def _():
-        norm_rows(x_ref, gain_ref, normed_ref)
         acc_ref[...] = jnp.zeros_like(acc_ref)
 
-    @pl.loop(0, rows // chunk)
-    def _(i):
-        span = pl.ds(i * chunk, chunk)
+    for r in range(0, cot_ref.shape[0], chunk):
+        span = slice(r, r + chunk)
         gate = nn(normed_ref[span, :], wg_ref[...])
         up = nn(normed_ref[span, :], wu_ref[...])
         grad_hidden = nn(cot_ref[span, :], wd_ref[...])
         sig = jax.nn.sigmoid(gate)
         silu = gate * sig
         grads_ref[2, span, :] = (silu * up).astype(BF)
-        grad_gate = (grad_hidden * up * sig * (1.0 + gate * (1.0 - sig))).astype(BF)
+        grad_gate = (grad_hidden * up * (sig + silu * (1.0 - sig))).astype(BF)
         grad_up = (grad_hidden * silu).astype(BF)
         grads_ref[0, span, :] = grad_gate
         grads_ref[1, span, :] = grad_up
         acc_ref[span, :] += nt(grad_gate, wg_ref[...]) + nt(grad_up, wu_ref[...])
 
-    @pl.when(j == pl.num_programs(0) - 1)
-    def _():
-        back_rows(acc_ref, x_ref, gain_ref, gain_part_ref, part_ref)
-
-
-def ffn(x, cot, gain, w, start, hidden_width):
-    rows, d = x.shape
-    steps = hidden_width // COLS
-    first = start // COLS
-    whole = lambda j: (0, 0)
+    for side, x_ref in enumerate((x_own, x_other)):
+
+        @pl.when((h == side) & (j == pl.num_programs(1) - 1))
+        def _():
+            back_rows(acc_ref, x_ref, gain_ref, gain_part_ref, part_ref)
+
+
+def resident(shape):
+    zeros = (0,) * len(shape)
+    return pl.BlockSpec(shape, lambda *grid: zeros, pipeline_mode=pl.Buffered(1))
+
+
+def ffn(xs, cots, gain, w, hidden_width, cols=512):
+    rows, d = xs[0].shape
+    steps = hidden_width // cols
+    per_half = lambda h, j: (h, 0, 0)
     return pl.pallas_call(
         ffn_kernel,
-        grid=(steps,),
-        in_specs=[
-            pl.BlockSpec((rows, d), whole),
-            pl.BlockSpec((rows, d), whole),
-            pl.BlockSpec((1, d), whole),
-            pl.BlockSpec((d, COLS), lambda j: (0, first + j)),
-            pl.BlockSpec((d, COLS), lambda j: (0, first + steps + j)),
-            pl.BlockSpec((d, COLS), lambda j: (0, first + 2 * steps + j)),
+        grid=(2, steps),
+        in_specs=[resident((rows, d))] * 4
+        + [
+            resident((1, d)),
+            pl.BlockSpec((d, cols), lambda h, j: (0, j)),
+            pl.BlockSpec((d, cols), lambda h, j: (0, steps + j)),
+            pl.BlockSpec((d, cols), lambda h, j: (0, 2 * steps + j)),
         ],
         out_specs=[
-            pl.BlockSpec((3, rows, COLS), lambda j: (0, 0, j)),
-            pl.BlockSpec((rows, d), whole),
-            pl.BlockSpec((rows, d), whole),
-            pl.BlockSpec((1, d), whole),
+            pl.BlockSpec((None, 3, rows, cols), lambda h, j: (h, 0, 0, j)),
+            pl.BlockSpec((None, rows, d), per_half),
+            pl.BlockSpec((None, rows, d), per_half),
+            pl.BlockSpec((8, d), lambda h, j: (0, 0)),
         ],
         out_shape=[
-            jax.ShapeDtypeStruct((3, rows, hidden_width), BF),
-            jax.ShapeDtypeStruct((rows, d), BF),
-            jax.ShapeDtypeStruct((rows, d), BF),
-            jax.ShapeDtypeStruct((1, d), F32),
-        ],
-        scratch_shapes=[pltpu.VMEM((rows, d), F32)],
-        compiler_params=settings(),
+            jax.ShapeDtypeStruct((2, 3, rows, hidden_width), BF),
+            jax.ShapeDtypeStruct((2, rows, d), BF),
+            jax.ShapeDtypeStruct((2, rows, d), BF),
+            jax.ShapeDtypeStruct((8, d), F32),
+        ],
+        scratch_shapes=[pltpu.VMEM((rows, d), BF), pltpu.VMEM((rows, d), F32)],
+        compiler_params=pltpu.CompilerParams(
+            dimension_semantics=("arbitrary", "arbitrary"), vmem_limit_bytes=56 * 1024 * 1024
+        ),
         cost_estimate=cost(
-            10 * rows * d * hidden_width,
-            6 * d * hidden_width + 8 * rows * d + 6 * rows * hidden_width,
-            rows * hidden_width,
+            20 * rows * d * hidden_width,
+            12 * d * hidden_width + 16 * rows * d + 12 * rows * hidden_width,
+            2 * rows * hidden_width,
         ),
         name="ffn",
-    )(x, cot, gain, w, w, w)
-
-
-def input_grad_kernel(x_ref, gain_ref, g_ref, w_ref, part_ref, gain_part_ref, acc_ref):
-    j = pl.program_id(0)
-    chunk = 256
-
-    @pl.when(j == 0)
-    def _():
-        acc_ref[...] = jnp.zeros_like(acc_ref)
-
-    @pl.loop(0, x_ref.shape[0] // chunk)
-    def _(i):
-        span = pl.ds(i * chunk, chunk)
-        acc_ref[span, :] += nt(g_ref[0, span, :], w_ref[...])
-
-    @pl.when(j == pl.num_programs(0) - 1)
-    def _():
-        back_rows(acc_ref, x_ref, gain_ref, gain_part_ref, part_ref)
-
-
-def input_grad(x, gain, grads, w):
-    rows, d = x.shape
-    kinds, _, width = grads.shape
-    per = width // COLS
-    whole = lambda j: (0, 0)
-    return pl.pallas_call(
-        input_grad_kernel,
-        grid=(kinds * per,),
-        in_specs=[
-            pl.BlockSpec((rows, d), whole),
-            pl.BlockSpec((1, d), whole),
-            pl.BlockSpec((1, rows, COLS), lambda j: (j // per, 0, j % per)),
-            pl.BlockSpec((d, COLS), lambda j: (0, j)),
-        ],
-        out_specs=[pl.BlockSpec((rows, d), whole), pl.BlockSpec((1, d), whole)],
-        out_shape=[
-            jax.ShapeDtypeStruct((rows, d), BF),
-            jax.ShapeDtypeStruct((1, d), F32),
-        ],
-        scratch_shapes=[pltpu.VMEM((rows, d), F32)],
-        compiler_params=settings(),
-        cost_estimate=cost(2 * rows * d * kinds * width, 2 * kinds * width * (rows + d)),
-        name="input_grad",
-    )(x, gain, grads, w)
+    )(*xs, *cots, gain, w, w, w)
 
 
 MESH = pl.DeviceIdType.MESH
@@ -543,12 +516,12 @@
                     late = self.late(block)
 
                     def add(k, carry):
-                        total = held[slot, keep, k].astype(F32) + got[slot, k].astype(F32)
+                        total = held[slot, keep, k] + got[slot, k]
                         bit, rest = k % 2, k // 2
                         if s == 1 and self.stages >= 3:
                             bit = bit * (1 - late) + (k // 2) % 2 * late
                             rest = rest * (1 - late) + (k // 4 * 2 + k % 2) * late
-                        self.held[s][later, bit, rest] = total.astype(BF)
+                        self.held[s][later, bit, rest] = total
                         return carry
 
                     lax.fori_loop(0, self.devices >> s, add, 0)
@@ -563,7 +536,7 @@
             span = pl.ds(i * size * self.rows, size * self.rows)
             total, start = None, 0
             for right in rights:
-                part = nn(turned_ref[span, start : start + right.shape[0]], right)
+                part = nn(turned_ref[span, start : start + right.shape[0]], right[...])
                 total = part if total is None else total + part
                 start += right.shape[0]
             for r in range(size):
@@ -574,13 +547,13 @@
         lax.fori_loop(0, pieces, piece, 0)
         self.copy(0, block).start()
 
-    def put_gain(self, block, mine_ref, other_ref):
+    def put_gain(self, block, mine, other):
         slot = block % self.slots[0]
+        column = jnp.broadcast_to(mine + other, (LANES, mine.shape[1])).T.astype(BF)
         for k in range(self.devices):
-            span = slice(k * self.rows, (k + 1) * self.rows)
-            total = mine_ref[span, :].astype(F32) + other_ref[span, :].astype(F32)
-            total = jnp.concatenate([total] * (COLS // LANES), axis=1)
-            self.held[0][slot, k % 2, k // 2] = total.astype(BF)
+            rows = column[k * self.rows : (k + 1) * self.rows, :]
+            wide = jnp.concatenate([rows] * (COLS // LANES), axis=1)
+            self.held[0][slot, k % 2, k // 2] = wide
         self.copy(0, block).start()
 
 
@@ -608,82 +581,68 @@
     )
 
 
-def emit_into(outs, per, turned, block, value):
+def emit_into(outs, per, block, value):
     for kind, out in enumerate(outs):
-        first, last = kind * per, (kind + 1) * per
-
-        @pl.when((block >= first) & (block < last))
+
+        @pl.when((block >= kind * per) & (block < (kind + 1) * per))
         def _():
-            out[...] = value.T if kind in turned else value
-
-
-def emit_specs(scatter, kinds, per, width, turned):
+            out[...] = value
+
+
+def emit_specs(scatter, kinds, per, width):
     lead = scatter.starts[-1]
     specs, shapes = [], []
     for kind in range(kinds + 1):
-        most = per - 1 if kind < kinds else 0
-
-        def where(j, kind=kind, most=most):
-            return jnp.clip(j - lead - kind * per, 0, most)
-
-        if kind in turned:
-            specs.append(pl.BlockSpec((COLS, scatter.rows), lambda j, f=where: (f(j), 0)))
-            shapes.append(jax.ShapeDtypeStruct((width, scatter.rows), F32))
-        else:
-            specs.append(pl.BlockSpec((scatter.rows, COLS), lambda j, f=where: (0, f(j))))
-            size = width if kind < kinds else COLS
-            shapes.append(jax.ShapeDtypeStruct((scatter.rows, size), F32))
+        most, size = (per - 1, width) if kind < kinds else (0, COLS)
+
+        def where(j, first=lead + kind * per, most=most):
+            return (0, jnp.clip(j - first, 0, most))
+
+        specs.append(pl.BlockSpec((scatter.rows, COLS), where))
+        shapes.append(jax.ShapeDtypeStruct((scatter.rows, size), F32))
     return specs, shapes
+
+
+def remote(src, dst, sems, device):
+    return pltpu.make_async_remote_copy(
+        src_ref=src,
+        dst_ref=dst,
+        send_sem=sems.at[0],
+        recv_sem=sems.at[1],
+        device_id=device,
+        device_id_type=MESH,
+    )
 
 
 def ffn_scatter_kernel(scatter, per, *refs):
     (
-        norm_own, norm_other, cot_own, cot_other, right_own, right_other,
+        norm_own, norm_other, cot_own, cot_other, right_own, right_other, gate_own, gate_other,
         part_own, part_other, gain_ref, middle_own, wd_ref,
-    ) = refs[:11]
-    outs, gm_ref, block_out_ref = refs[11:15], refs[15], refs[16]
+    ) = refs[:13]
+    outs = refs[13:16]
+    gate_ref, gm_ref, block_own, block_send = refs[16:20]
     (
-        turned_ref, got_part, gm_own, gain_got, acc_own, acc_other, block_send, block_got,
-        gain_sems, x_sems, block_sems, local_sem,
-    ) = refs[17:29]
-    scatter.bind(refs[29:])
+        cot_turned, norm_turned, got_part, gm_own, gain_got, acc_other,
+        gain_sems, part_sems, gm_sems, local_sem,
+    ) = refs[20:30]
+    scatter.bind(refs[30:])
     step = pl.program_id(0)
     side = scatter.side
+    across = (scatter.me, 1 - side)
     half = part_own.shape[0]
     quarter = half // QUARTERS
     row_chunk = 128
 
     def part_copy(r):
         span = pl.ds(r * quarter, quarter)
-        return pltpu.make_async_remote_copy(
-            src_ref=part_other.at[span],
-            dst_ref=got_part.at[span],
-            send_sem=x_sems.at[0, r],
-            recv_sem=x_sems.at[1, r],
-            device_id=(scatter.me, 1 - side),
-            device_id_type=MESH,
-        )
+        return remote(part_other.at[1, span], got_part.at[span], part_sems.at[r], across)
 
     def gm_copy(r):
         span = pl.ds(r * quarter, quarter)
-        return pltpu.make_async_remote_copy(
-            src_ref=gm_own.at[span],
-            dst_ref=gm_ref.at[side, span],
-            send_sem=x_sems.at[2, r],
-            recv_sem=x_sems.at[3, r],
-            device_id=(scatter.me, 1 - side),
-            device_id_type=MESH,
-        )
-
-    def block_copy():
-        return pltpu.make_async_remote_copy(
-            src_ref=block_send,
-            dst_ref=block_got,
-            send_sem=block_sems.at[0],
-            recv_sem=block_sems.at[1],
-            device_id=(scatter.me, 1 - side),
-            device_id_type=MESH,
-        )
+        return remote(gm_own.at[span], gm_ref.at[side, span], gm_sems.at[r], across)
+
+    def gain_copy():
+        return remote(gain_ref, gain_got, gain_sems, across)
 
     def gm_keep():
         return pltpu.make_async_copy(gm_own, gm_ref.at[side], local_sem)
@@ -693,33 +652,45 @@
         scatter.barrier()
         for r in range(QUARTERS):
             part_copy(r).start()
-        gain_copy(scatter, gain_ref, gain_got, gain_sems).start()
-        turn_into(turned_ref, [cot_own, cot_other])
-        acc_own[...] = jnp.zeros_like(acc_own)
+        gain_copy().start()
+        turn_into(cot_turned, [cot_own, cot_other])
+        block_own[...] = jnp.zeros_like(block_own)
         acc_other[...] = jnp.zeros_like(acc_other)
 
-    @pl.when(step == per)
-    def _():
-        turn_into(turned_ref, [norm_own, norm_other])
-
-    scatter.advance(step, functools.partial(emit_into, outs, per, (0,)))
-
-    @pl.when(step < 3 * per)
-    def _():
-        scatter.multiply(step, turned_ref, (right_own[0], right_other[0]))
-
-    @pl.when(step == 3 * per)
-    def _():
-        gain_copy(scatter, gain_ref, gain_got, gain_sems).wait()
-        scatter.put_gain(step, gain_ref, gain_got)
+    @pl.when(step == 1)
+    def _():
+        turn_into(norm_turned, [norm_own, norm_other])
+
+    scatter.advance(step, functools.partial(emit_into, outs, per))
 
     @pl.when(step < per)
     def _():
+        scatter.multiply(step, cot_turned, (right_own, right_other))
+
         @pl.loop(0, half // 256)
         def _(i):
             span = pl.ds(i * 256, 256)
-            acc_own[span, :] += nt(right_own[0, span, :], wd_ref[...])
-            acc_other[span, :] += nt(right_other[0, span, :], wd_ref[...])
+            block_own[span, :] += nt(right_own[span, :], wd_ref[...])
+            acc_other[span, :] += nt(right_other[span, :], wd_ref[...])
+
+    @pl.when((step >= per) & (step < 2 * per))
+    def _():
+        scatter.multiply(step, norm_turned, (right_own, right_other))
+
+    @pl.when(step == 2 * per)
+    def _():
+        gain_copy().wait()
+        scatter.put_gain(step, gain_ref[0:1, :], gain_got[0:1, :])
+
+    @pl.when((step % 2 == 1) & (step < 2 * per))
+    def _():
+        rows = gate_ref.shape[0] // 4
+
+        @pl.loop(0, 4)
+        def _(i):
+            span = pl.ds(i * rows, rows)
+            total = nn(norm_turned[span, :half], gate_own[...])
+            gate_ref[span, :] = (total + nn(norm_turned[span, half:], gate_other[...])).astype(BF)
 
     for r in range(QUARTERS):
 
@@ -737,31 +708,22 @@
             if r == QUARTERS - 1:
                 gm_keep().start()
 
-    @pl.when(step == 3 + 2 * QUARTERS)
-    def _():
-        block_send[...] = acc_other[...].astype(BF)
-        block_copy().start()
+    @pl.when(step == per)
+    def _():
+        @pl.loop(0, half // row_chunk)
+        def _(i):
+            span = pl.ds(i * row_chunk, row_chunk)
+            block_own[span, :] += middle_own[span, :].astype(F32)
+            block_send[span, :] = acc_other[span, :].astype(BF)
 
     @pl.when(step == scatter.steps - 1)
     def _():
         for r in range(QUARTERS):
             gm_copy(r).wait()
         gm_keep().wait()
-        block_copy().wait()
-
-        @pl.loop(0, half // row_chunk)
-        def _(i):
-            span = pl.ds(i * row_chunk, row_chunk)
-            total = middle_own[span, :].astype(F32) + acc_own[span, :]
-            block_out_ref[span, :] = (total + block_got[span, :].astype(F32)).astype(BF)
-
-
-def resident(shape):
-    zeros = (0,) * len(shape)
-    return pl.BlockSpec(shape, lambda j: zeros, pipeline_mode=pl.Buffered(1))
-
-
-def remote_settings(identity, mib=56):
+
+
+def remote_settings(identity, mib=60):
     return pltpu.CompilerParams(
         dimension_semantics=("arbitrary",),
         vmem_limit_bytes=mib * 1024 * 1024,
@@ -770,142 +732,265 @@
     )
 
 
-def ffn_scatter(devices, normed, cots, rights, parts, gain_block, middle, w):
+def ffn_scatter(devices, normed, cots, grads, parts, gain_part, middle, w):
     half, d = middle.shape
-    width = rights[0].shape[2]
+    width = grads.shape[3]
     per = width // COLS
-    scatter = Scatter(devices, d // devices, 3 * per + 1)
-    assert per >= 3 + 2 * QUARTERS - 3 and scatter.rows * devices == d
-
-    def right_map(j):
-        c = jnp.minimum(j, 3 * per - 1)
-        return ((c // per + 2) % 3, 0, c % per)
-
-    specs, shapes = emit_specs(scatter, 3, per, width, (0,))
+    scatter = Scatter(devices, d // devices, 2 * per + 1)
+    assert 2 * per > 3 + 2 * QUARTERS and scatter.rows * devices == d
+
+    def right(side):
+        def where(j):
+            c = jnp.minimum(j, 2 * per - 1)
+            return (side, 2 - c // per, 0, c % per)
+
+        return pl.BlockSpec((None, None, half, COLS), where)
+
+    def gate_block(j):
+        return jnp.clip((j - 1) // 2, 0, per - 1)
+
+    def gate(side):
+        return pl.BlockSpec((None, None, half, COLS), lambda j: (side, 0, 0, gate_block(j)))
+
+    def rows_of(side):
+        return pl.BlockSpec(
+            (None, half, d), lambda j: (side, 0, 0), pipeline_mode=pl.Buffered(1)
+        )
+
+    specs, shapes = emit_specs(scatter, 2, per, width)
     whole = lambda j: (0, 0)
     return pl.pallas_call(
         functools.partial(ffn_scatter_kernel, scatter, per),
         grid=(scatter.steps,),
-        in_specs=[resident((half, d))] * 4
-        + [pl.BlockSpec((1, half, COLS), right_map)] * 2
-        + [
+        in_specs=[
+            rows_of(0),
+            rows_of(1),
             resident((half, d)),
+            resident((half, d)),
+            right(0),
+            right(1),
+            gate(0),
+            gate(1),
+            rows_of(0),
             pl.BlockSpec(memory_space=pl.ANY),
-            resident((d, LANES)),
+            resident((8, d)),
             resident((half, d)),
             pl.BlockSpec((d, COLS), lambda j: (0, 2 * per + jnp.minimum(j, per - 1))),
         ],
-        out_specs=specs + [pl.BlockSpec(memory_space=pl.ANY), pl.BlockSpec((half, d), whole)],
+        out_specs=specs
+        + [
+            pl.BlockSpec((d, COLS), lambda j: (0, gate_block(j))),
+            pl.BlockSpec(memory_space=pl.ANY),
+            pl.BlockSpec((half, d), whole),
+            pl.BlockSpec((half, d), whole),
+        ],
         out_shape=shapes
-        + [jax.ShapeDtypeStruct((2, half, d), BF), jax.ShapeDtypeStruct((half, d), BF)],
+        + [
+            jax.ShapeDtypeStruct((d, width), BF),
+            jax.ShapeDtypeStruct((2, half, d), BF),
+            jax.ShapeDtypeStruct((half, d), F32),
+            jax.ShapeDtypeStruct((half, d), BF),
+        ],
         scratch_shapes=[
+            pltpu.VMEM((d, 2 * half), BF),
             pltpu.VMEM((d, 2 * half), BF),
             pltpu.VMEM((half, d), BF),
             pltpu.VMEM((half, d), BF),
-            pltpu.VMEM((d, LANES), BF),
+            pltpu.VMEM((8, d), F32),
             pltpu.VMEM((half, d), F32),
-            pltpu.VMEM((half, d), F32),
-            pltpu.VMEM((half, d), BF),
-            pltpu.VMEM((half, d), BF),
             pltpu.SemaphoreType.DMA((2,)),
-            pltpu.SemaphoreType.DMA((4, QUARTERS)),
-            pltpu.SemaphoreType.DMA((2,)),
+            pltpu.SemaphoreType.DMA((QUARTERS, 2)),
+            pltpu.SemaphoreType.DMA((QUARTERS, 2)),
             pltpu.SemaphoreType.DMA,
         ]
         + scatter.scratch(),
         compiler_params=remote_settings(0),
         cost_estimate=cost(16 * half * d * per * COLS, 20 * half * d),
         name="ffn_scatter",
-    )(*normed, *cots, *rights, *parts, gain_block, middle, w)
+    )(
+        normed, normed, *cots, grads, grads, grads, grads, parts, parts, gain_part, middle, w,
+    )
 
 
 def attention_scatter_kernel(scatter, per, *refs):
-    normed_ref, gm_ref, right_ref, attended_ref, part_ref, gain_ref = refs[:6]
-    outs, got_part = refs[6:11], refs[11]
-    turned_ref, gain_got, gain_sems, x_sems = refs[12:16]
-    scatter.bind(refs[16:])
+    (
+        normed_ref, gm_ref, x_ref, gain_ref, right_ref, attended_ref, block_own, block_send,
+        first_ref, second_ref, w_first, w_second,
+    ) = refs[:12]
+    outs = refs[12:17]
+    token_grad_ref, block_out_ref = refs[17:19]
+    (
+        turned_ref, acc_ref, part_send, part_got, block_got, gain_part, gain_got,
+        gain_sems, part_sems, block_sems,
+    ) = refs[19:29]
+    scatter.bind(refs[29:])
     step = pl.program_id(0)
     side = scatter.side
-
-    def part_copy():
-        return pltpu.make_async_remote_copy(
-            src_ref=part_ref.at[1 - side],
-            dst_ref=got_part,
-            send_sem=x_sems.at[0],
-            recv_sem=x_sems.at[1],
-            device_id=(scatter.me, 1 - side),
-            device_id_type=MESH,
-        )
+    across = (scatter.me, 1 - side)
+    length = x_ref.shape[0]
+    half = length // 2
+    quarter = half // QUARTERS
+    chunk = 128
+    kinds = 3 * per
+    ready = (kinds + 1) // 2
+    own, other = side * half, (1 - side) * half
+
+    def part_copy(r):
+        span = pl.ds(r * quarter, quarter)
+        return remote(part_send.at[span], part_got.at[span], part_sems.at[r], across)
+
+    def block_copy():
+        return remote(block_send, block_got, block_sems, across)
+
+    def gain_copy():
+        return remote(gain_part, gain_got, gain_sems, across)
+
+    def back(row):
+        span = pl.ds(row, chunk)
+        part, piece = rms_back(acc_ref[span, :], x_ref[span, :].astype(F32), gain_ref[...])
+        gain_part[...] += jnp.broadcast_to(piece, gain_part.shape)
+        return part
 
     @pl.when(step == 0)
     def _():
         scatter.barrier()
-        part_copy().start()
-        gain_copy(scatter, gain_ref, gain_got, gain_sems).start()
         turn_into(turned_ref, [normed_ref])
-
-    @pl.when(step == 3 * per)
+        acc_ref[...] = jnp.zeros_like(acc_ref)
+        gain_part[...] = jnp.zeros_like(gain_part)
+
+    @pl.when(step == kinds)
     def _():
         turn_into(turned_ref, [gm_ref])
 
-    scatter.advance(step, functools.partial(emit_into, outs, per, (3,)))
-
-    @pl.when(step < 3 * per)
-    def _():
-        scatter.multiply(step, turned_ref, (right_ref[0],))
-
-    @pl.when((step >= 3 * per) & (step < 4 * per))
-    def _():
-        scatter.multiply(step, turned_ref, (attended_ref[...],))
+    scatter.advance(step, functools.partial(emit_into, outs, per))
+
+    @pl.when(step < kinds)
+    def _():
+        scatter.multiply(step, turned_ref, (right_ref,))
+
+    @pl.when((step >= kinds) & (step < 4 * per))
+    def _():
+        scatter.multiply(step, turned_ref, (attended_ref,))
+
+    for nth, (g_ref, w_ref) in enumerate(((first_ref, w_first), (second_ref, w_second))):
+
+        @pl.when(2 * step + nth < kinds)
+        def _():
+            @pl.loop(0, length // 256)
+            def _(i):
+                span = pl.ds(i * 256, 256)
+                acc_ref[span, :] += nt(g_ref[span, :], w_ref[...])
+
+    @pl.when(step == ready)
+    def _():
+        for r in range(QUARTERS):
+
+            @pl.loop(r * quarter // chunk, (r + 1) * quarter // chunk)
+            def _(i):
+                part_send[pl.ds(i * chunk, chunk), :] = back(other + i * chunk).astype(BF)
+
+            part_copy(r).start()
+
+    @pl.when(step == ready + 1)
+    def _():
+        @pl.loop(0, half // chunk)
+        def _(i):
+            span = pl.ds(own + i * chunk, chunk)
+            acc_ref[span, :] = back(own + i * chunk) + gm_ref[span, :].astype(F32)
+
+        gain_copy().start()
+        block_copy().start()
 
     @pl.when(step == 4 * per)
     def _():
-        gain_copy(scatter, gain_ref, gain_got, gain_sems).wait()
-        scatter.put_gain(step, gain_ref, gain_got)
+        gain_copy().wait()
+        scatter.put_gain(step, gain_part[0:1, :], gain_got[0:1, :])
+
+    for r in range(QUARTERS):
+
+        @pl.when(step == scatter.steps - 1 - QUARTERS + r)
+        def _():
+            part_copy(r).wait()
+
+            @pl.loop(r * quarter // chunk, (r + 1) * quarter // chunk)
+            def _(i):
+                span = pl.ds(i * chunk, chunk)
+                total = acc_ref[pl.ds(own + i * chunk, chunk), :]
+                token_grad_ref[span, :] = (total + part_got[span, :].astype(F32)).astype(BF)
 
     @pl.when(step == scatter.steps - 1)
     def _():
-        part_copy().wait()
-
-
-def attention_scatter(devices, normed, gm, grads, attended, part, gain_block):
+        block_copy().wait()
+
+        @pl.loop(0, half // chunk)
+        def _(i):
+            span = pl.ds(i * chunk, chunk)
+            total = block_own[span, :] + block_got[span, :].astype(F32)
+            block_out_ref[span, :] = total.astype(BF)
+
+
+def attention_scatter(
+    devices, normed, gm, x, gain, grads, attended, block_own, block_send, w
+):
     length, d = normed.shape
+    half = length // 2
     width = grads.shape[2]
     per = width // COLS
+    kinds = 3 * per
     scatter = Scatter(devices, d // devices, 4 * per + 1)
-
-    def right_map(j):
-        c = jnp.minimum(j, 3 * per - 1)
-        return (c // per, 0, c % per)
+    assert (kinds + 1) // 2 + 1 < 4 * per and scatter.rows * devices == d
+
+    def grads_spec(pick):
+        def where(j):
+            c = jnp.minimum(pick(j), kinds - 1)
+            return (c // per, 0, c % per)
+
+        return pl.BlockSpec((None, length, COLS), where)
+
+    def weight_spec(pick):
+        return pl.BlockSpec((d, COLS), lambda j: (0, jnp.minimum(pick(j), kinds - 1)))
 
     def attended_map(j):
-        return (0, jnp.clip(j - 3 * per, 0, per - 1))
-
-    specs, shapes = emit_specs(scatter, 4, per, width, (3,))
+        return (0, jnp.clip(j - kinds, 0, per - 1))
+
+    specs, shapes = emit_specs(scatter, 4, per, width)
+    whole = lambda j: (0, 0)
+    even, odd = (lambda j: 2 * j), (lambda j: 2 * j + 1)
     return pl.pallas_call(
         functools.partial(attention_scatter_kernel, scatter, per),
         grid=(scatter.steps,),
-        in_specs=[
-            resident((length, d)),
-            resident((length, d)),
-            pl.BlockSpec((1, length, COLS), right_map),
+        in_specs=[resident((length, d))] * 3
+        + [
+            resident((1, d)),
+            grads_spec(lambda j: j),
             pl.BlockSpec((length, COLS), attended_map),
+            resident((half, d)),
             pl.BlockSpec(memory_space=pl.ANY),
-            resident((d, LANES)),
-        ],
-        out_specs=specs + [pl.BlockSpec(memory_space=pl.ANY)],
-        out_shape=shapes + [jax.ShapeDtypeStruct((length // 2, d), BF)],
+            grads_spec(even),
+            grads_spec(odd),
+            weight_spec(even),
+            weight_spec(odd),
+        ],
+        out_specs=specs + [pl.BlockSpec((half, d), whole), pl.BlockSpec((half, d), whole)],
+        out_shape=shapes
+        + [jax.ShapeDtypeStruct((half, d), BF), jax.ShapeDtypeStruct((half, d), BF)],
         scratch_shapes=[
             pltpu.VMEM((d, length), BF),
-            pltpu.VMEM((d, LANES), BF),
+            pltpu.VMEM((length, d), F32),
+            pltpu.VMEM((half, d), BF),
+            pltpu.VMEM((half, d), BF),
+            pltpu.VMEM((half, d), BF),
+            pltpu.VMEM((8, d), F32),
+            pltpu.VMEM((8, d), F32),
             pltpu.SemaphoreType.DMA((2,)),
+            pltpu.SemaphoreType.DMA((QUARTERS, 2)),
             pltpu.SemaphoreType.DMA((2,)),
         ]
         + scatter.scratch(),
         compiler_params=remote_settings(1),
-        cost_estimate=cost(8 * length * d * per * COLS, 20 * length * d),
+        cost_estimate=cost(14 * length * d * per * COLS, 20 * length * d),
         name="attention_scatter",
-    )(normed, gm, grads, attended, part, gain_block)
+    )(normed, gm, x, gain, grads, attended, block_own, block_send, grads, grads, w, w)
 
 
 def swap(x):
@@ -974,42 +1059,40 @@
     ).astype(BF)
     middle_other = swap(middle)
 
-    gg_own, normed_own, part_own, gp_own = ffn(
-        middle, cotangent, ffn_row, second, 0, hidden_width
-    )
-    gg_other, normed_other, part_other, gp_other = ffn(
-        middle_other, cot_other, ffn_row, second, 0, hidden_width
-    )
-
-    def gain_block(gain_sum):
-        return jnp.broadcast_to(gain_sum.astype(BF).T, (d, LANES))
-
-    down_grad, gate_grad, up_grad, ffn_gain_grad, grad_middle, block_out = ffn_scatter(
+    ffn_grads, normed_two, parts, gain_part = ffn(
+        (middle, middle_other), (cotangent, cot_other), ffn_row, second, hidden_width
+    )
+    down_grad, up_grad, ffn_gain_grad, gate_whole, grad_middle, block_own, block_send = ffn_scatter(
         devices,
-        (normed_own, normed_other),
+        normed_two,
         (cotangent, cot_other),
-        (gg_own, gg_other),
-        (part_own, part_other),
-        gain_block(gp_own + gp_other),
+        ffn_grads,
+        parts,
+        gain_part,
         middle,
         second,
     )
-    grad_middle_all = grad_middle.reshape(length, d)
-
-    grad_attended = nn(grad_middle_all, out_turned).astype(BF)
+    gate_grad = lax.psum_scatter(gate_whole, "dp", scatter_dimension=0, tiled=True).astype(F32)
+    grad_middle = grad_middle.reshape(length, d)
+
+    grad_attended = nn(grad_middle, out_turned).astype(BF)
     grads = attend_back(
         qkv, attended, grad_attended, lse, bias, cosine[:, :LANES], sine[:, :LANES], seg_rows
     )
-    part, gain_part = input_grad(rows_all, attn_row, grads, first)
-    part = part.reshape(2, half, d)
-    query_grad, key_grad, value_grad, output_grad, attn_gain_grad, received = attention_scatter(
-        devices, normed_one, grad_middle_all, grads, attended, part, gain_block(gain_part)
-    )
-    token_grad = (
-        lax.dynamic_index_in_dim(grad_middle, mine, 0, False).astype(F32)
-        + lax.dynamic_index_in_dim(part, mine, 0, False).astype(F32)
-        + received.astype(F32)
-    ).astype(BF)
+    (
+        query_grad, key_grad, value_grad, output_grad, attn_gain_grad, token_grad, block_out,
+    ) = attention_scatter(
+        devices,
+        normed_one,
+        grad_middle,
+        rows_all,
+        attn_row,
+        grads,
+        attended,
+        block_own,
+        block_send,
+        first,
+    )
     gain_rows = d // devices // 2
 
     def gain_piece(columns):
@@ -1021,10 +1104,10 @@
         query_grad,
         key_grad,
         value_grad,
-        output_grad,
+        output_grad.T,
         gate_grad,
         up_grad,
-        down_grad,
+        down_grad.T,
         gain_piece(attn_gain_grad),
         gain_piece(ffn_gain_grad),
     )

time: 581 us -> 538 us (0.926)
  Pallas kernels: 387 us -> 338 us
  waiting for transfers between devices: 119 us -> 139 us
  local copies, waits for them, and re-layouts: 32.9 us -> 22.2 us
    pallas_call x3 -> x1, Pallas kernels: 99.8 us -> 49.7 us  [ffn(): pl.pallas_call(ffn_kernel, grid=(2, steps), in_specs=[resident((rows, d))...]
    ppermute x4, waiting for transfers between devices: 91 us -> 127 us  [swap(): return lax.ppermute(x, 'tensor', [(0, 1), (1, 0)])]
    pallas_call x1, Pallas kernels: 78.8 us -> 111 us  [attention_scatter(): pl.pallas_call(functools.partial(attention_scatter_kernel, scatter, per),...]
    pallas_call x1, Pallas kernels: 136 us -> 105 us  [ffn_scatter(): pl.pallas_call(functools.partial(ffn_scatter_kernel, scatter, per), grid=...]
    all_gather x2, waiting for transfers between devices: 28.1 us -> 11.9 us  [gather(): return lax.all_gather(shard, 'dp', axis=0, tiled=True)]
    unnamed x50 -> x46, local copies, waits for them, and re-layouts: 17.3 us -> 10.9 us
  transfers between devices with their start and end apart: 6 -> 7, of which waited for: 5 -> 5; matrix products, arithmetic and copies ran while one was open for 3% -> 5% of each run, Pallas kernels for 13% -> 34%
where the time goes in v4:
time: 538 us; the launch traced here: 537 us
  Pallas kernels  338 us (63%)
  waiting for transfers between devices  139 us (26%)
  local copies, waits for them, and re-layouts  22.2 us (4%)
  between operations  14.1 us (3%)
  matrix products  9.7 us (2%)
  other arithmetic  7.92 us (1%)
  starting transfers between devices  6.22 us (1%)
    ppermute x4, waiting for transfers between devices, swap(): return lax.ppermute(x, 'tensor', [(0, 1), (1, 0)])  127 us
    pallas_call x1, Pallas kernels, attention_scatter(): pl.pallas_call(functools.partial(attention_scatter_kernel, scatter, per),...  111 us
    pallas_call x1, Pallas kernels, ffn_scatter(): pl.pallas_call(functools.partial(ffn_scatter_kernel, scatter, per), grid=...  105 us
    pallas_call x1, Pallas kernels, ffn(): pl.pallas_call(ffn_kernel, grid=(2, steps), in_specs=[resident((rows, d))...  49.7 us
    pallas_call x1, Pallas kernels, attend_back(): pl.pallas_call(functools.partial(attend_back_kernel, block, seg_rows), gr...  34 us
    pallas_call x1, Pallas kernels, attend(): pl.pallas_call(functools.partial(attend_kernel, block, seg_rows), grid=(g...  21.6 us
    pallas_call x1, Pallas kernels, project(): pl.pallas_call(functools.partial(project_kernel, parts), grid=(3 * parts,...  15.9 us
    all_gather x2, waiting for transfers between devices, gather(): return lax.all_gather(shard, 'dp', axis=0, tiled=True)  11.9 us
  transfers between devices with their start and end apart: 7, of which 5 were waited for; matrix products, arithmetic and copies ran while one was open for 5% of the time, Pallas kernels for 34%

profile of v4, /device:TPU:0, one launch (start us, length us, event | category | flops | bytes accessed | tf_op | source)
XLA Modules:
  0.0 537.0 jit_solution(6269208445635538705)
XLA Ops:
  7.2 2.0 pad_maximum_fusion.1
  9.3 2.4 pad_maximum_fusion
  11.7 3.0 collective-permute-start
  17.7 1.9 broadcast_in_dim.16
  19.6 2.8 constant_dynamic-update-slice_fusion.1
  22.3 28.0 %collective-permute-done = bf16[512,1536]{1,0:T(8,128)(2,1)} collective-permute-done((bf16[512,1536]{1,0:T(8,128)(2,1)}, bf16[512,1536]{1,0:T(8,128)(2,1)}, u32[]{:S(2)}, u32[]{:S(2)}) %collective-permute-start) | collective-permute-done | bytes 1572896 | tf_op jit(solution)/shard_map/ppermute | solution.py:997
  50.3 2.7 constant_dynamic-update-slice_fusion.x_ref.refs_2_
  52.9 30.2 %collective-permute-done.1.cot_other.refs_3_ = bf16[512,1536]{1,0:T(8,128)(2,1)} collective-permute-done((bf16[512,1536]{1,0:T(8,128)(2,1)}, bf16[512,1536]{1,0:T(8,128)(2,1)}, u32[]{:S(2)}, u32[]{:S(2)}) %collective-permute-start.1) | collective-permute-done | bytes 1572896 | tf_op jit(solution)/shard_map/ppermute | solution.py:997
  83.2 11.9 %all-gather.3.cloned.1.call-done.w_ref.refs_10_.refs_11_ = bf16[1536,3072]{1,0:T(8,128)(2,1)} async-done(((bf16[96,3072]{1,0:T(8,128)(2,1)}), bf16[1536,3072]{1,0:T(8,128)(2,1)}) %all-gather.3.cloned.1.call-update) | async-done | bytes 9437200 | tf_op jit(solution)/shard_map/all_gather | solution.py:1035
  95.1 15.9 %project.1 = (bf16[1024,2304]{1,0:T(8,128)(2,1)}, bf16[1024,1536]{1,0:T(8,128)(2,1)S(1)}) custom-call(bf16[1024,1536]{1,0:T(8,128)(2,1)} %constant_dynamic-update-slice_fusion.x_ref.refs_2_, f32[1,1536]{1,0:T(1,128)S(1)} %broadcast_in_dim.17.gain_ref.refs_3_, f32[1024,256]{1,0:T(8,128)S(1)} %copy.45.cos_ref, f32[1024,256]{1,0:T(8,128)S(1)} %copy.46.sin_ref, ...), custom_call_target="tpu_custom_call" | custom-call | flops 7247757312 | bytes 13369344 | tf_op jit(solution)/shard_map/project/pallas_call | solution.py:120
  111.0 1.7 copy-done.3
  112.7 21.6 %attend.1 = (bf16[1024,768]{1,0:T(8,128)(2,1)S(1)}, f32[6,2,1024]{2,1,0:T(2,128)S(1)}) custom-call(bf16[1024,2304]{1,0:T(8,128)(2,1)} %get-tuple-element.37.q_ref.k_ref.v_ref, bf16[1024,2304]{1,0:T(8,128)(2,1)} %get-tuple-element.37.q_ref.k_ref.v_ref, bf16[1024,2304]{1,0:T(8,128)(2,1)} %get-tuple-element.37.q_ref.k_ref.v_ref, ...), custom_call_target="tpu_custom_call" | custom-call | flops 6442450944 | bytes 6291456 | tf_op jit(solution)/shard_map/attend/pallas_call | solution.py:199
  135.8 1.5 collective-permute-start.2
  137.3 35.2 %collective-permute-done.2 = bf16[512,1536]{1,0:T(8,128)(2,1)S(1)} collective-permute-done((bf16[512,1536]{1,0:T(8,128)(2,1)S(1)}, bf16[512,1536]{1,0:T(8,128)(2,1)S(1)}, u32[]{:S(2)}, u32[]{:S(2)}) %collective-permute-start.2) | collective-permute-done | bytes 1572896 | tf_op jit(solution)/shard_map/ppermute | solution.py:997
  172.5 2.9 add_convert_fusion.x_own.refs_11_
  175.5 1.5 collective-permute-start.3
  177.6 34.0 %collective-permute-done.3.x_other = bf16[512,1536]{1,0:T(8,128)(2,1)} collective-permute-done((bf16[512,1536]{1,0:T(8,128)(2,1)S(1)}, bf16[512,1536]{1,0:T(8,128)(2,1)}, u32[]{:S(2)}, u32[]{:S(2)}) %collective-permute-start.3) | collective-permute-done | bytes 1572896 | tf_op jit(solution)/shard_map/ppermute | solution.py:997
  211.6 49.7 %ffn.1 = (bf16[2,3,512,2048]{3,2,1,0:T(8,128)(2,1)}, bf16[2,512,1536]{2,1,0:T(8,128)(2,1)}, bf16[2,512,1536]{2,1,0:T(8,128)(2,1)}, f32[8,1536]{1,0:T(8,128)}) custom-call(bf16[512,1536]{1,0:T(8,128)(2,1)} %copy-done.15, bf16[512,1536]{1,0:T(8,128)(2,1)} %collective-permute-done.3.x_other, bf16[512,1536]{1,0:T(8,128)(2,1)} %refs_2_.1, ...), custom_call_target="tpu_custom_call" | custom-call | flops 32212254720 | bytes 62914560 | tf_op jit(solution)/shard_map/ffn/pallas_call | solution.py:396
  261.3 105.0 %ffn_scatter.1 = (f32[96,2048]{1,0:T(8,128)}, f32[96,2048]{1,0:T(8,128)}, f32[96,256]{1,0:T(8,128)}, bf16[1536,2048]{1,0:T(8,128)(2,1)}, bf16[2,512,1536]{2,1,0:...) custom-call(bf16[2,512,1536]{2,1,0:T(8,128)(2,1)} %get-tuple-element.40.refs_0_.refs_1_, ...), custom_call_target="tpu_custom_call" | custom-call | flops 25769803776 | bytes 15728640 | tf_op jit(solution)/shard_map/ffn_scatter/pallas_call | solution.py:762
  367.3 5.3 fusion.4.do_ref
  372.6 34.0 %attend_back.1.refs_4_.refs_8_.refs_9_ = bf16[3,1024,768]{2,1,0:T(8,128)(2,1)} custom-call(bf16[1024,2304]{1,0:T(8,128)(2,1)} %get-tuple-element.37.q_ref.k_ref.v_ref, bf16[1024,2304]{1,0:T(8,128)(2,1)} %get-tuple-element.37.q_ref.k_ref.v_ref, bf16[1024,2304]{1,0:T(8,128)(2,1)} %get-tuple-element.37.q_ref.k_ref.v_ref, bf16[1024,768]{1,0:T(8,128)(2,1)S(1)} %copy-done.2, ...), custom_call_target="tpu_custom_call" | custom-call | flops 16106127360 | bytes 12582912 | tf_op jit(solution)/shard_map/attend_back/pallas_call | solution.py:287
  406.6 111.3 %attention_scatter.1 = (f32[96,768]{1,0:T(8,128)}, f32[96,768]{1,0:T(8,128)}, f32[96,768]{1,0:T(8,128)}, f32[96,768]{1,0:T(8,128)}, f32[96,256]{1,0:T(8,128)}, /...) custom-call(bf16[1024,1536]{1,0:T(8,128)(2,1)} %copy-done.3, bf16[1024,1536]{1,0:T(8,128)(2,1)} %bitcast.31, ...), custom_call_target="tpu_custom_call" | custom-call | flops 16911433728 | bytes 31457280 | tf_op jit(solution)/shard_map/attention_scatter/pallas_call | solution.py:959
  520.1 1.9 convert_element_type.88
  522.0 2.7 copy.61
  (94 shorter events, 13.9 us)
Async XLA Ops:
  7.2 87.9 %all-gather.3.cloned.1.call-start = ((), (), s32[]{:S(2)}) async-start(), calls=%async_computation.1 | async-start | bytes 10027008 | tf_op jit(solution)/shard_map/all_gather | solution.py:1035
  9.2 5.6 %copy-start.14 = (s32[1,8]{1,0:T(1,128)S(1)}, s32[1,8]{1,0:T(1,128)}, u32[]{:S(2)}) copy-start(s32[1,8]{1,0:T(1,128)} %param.13) | copy-start | bytes 100
  9.2 6.7 %copy-start.12 = (f32[1536]{0:T(1024)S(1)}, f32[1536]{0:T(1024)}, u32[]{:S(2)}) copy-start(f32[1536]{0:T(1024)} %param.14) | copy-start | bytes 18436
  9.2 202.3 %all-gather.5.cloned.1.call-start = ((), (), s32[]{:S(2)}) async-start(), calls=%async_computation.2 | async-start | bytes 20054016 | tf_op jit(solution)/shard_map/all_gather | solution.py:1035
  11.7 508.4 %reduce-scatter.2.cloned.1.call-start = ((), (), s32[]{:S(2)}) async-start(), calls=%async_computation.3 | async-start | bytes 6684672 | tf_op jit(solution)/shard_map/reduce_scatter | solution.py:1075
  11.7 38.5 %collective-permute-start = (bf16[512,1536]{1,0:T(8,128)(2,1)}, bf16[512,1536]{1,0:T(8,128)(2,1)}, u32[]{:S(2)}, u32[]{:S(2)}) collective-permute-start(bf16[512,1536]{1,0:T(8,128)(2,1)} %param.12), channel_id=1, source_target_pairs={{0,1},{1,0},{2,3},{3,2},{4,5},{5,4},{6,7},{7,6},{8,9},{9,8},{10,11... | collective-permute-start | bytes 4718600 | tf_op jit(solution)/shard_map/ppermute | solution.py:997
  14.7 68.4 %collective-permute-start.1 = (bf16[512,1536]{1,0:T(8,128)(2,1)}, bf16[512,1536]{1,0:T(8,128)(2,1)}, u32[]{:S(2)}, u32[]{:S(2)}) collective-permute-start(bf16[512,1536]{1,0:T(8,128)(2,1)} %refs_2_.1), channel_id=1, source_target_pairs={{0,1},{1,0},{2,3},{3,2},{4,5},{5,4},{6,7},{7,6},{8,9},{9,8},{10,11... | collective-permute-start | bytes 4718600 | tf_op jit(solution)/shard_map/ppermute | solution.py:997
  15.9 79.1 %copy-start = (f32[1,1536]{1,0:T(1,128)}, f32[1,1536]{1,0:T(1,128)S(1)}, u32[]{:S(2)}) copy-start(f32[1,1536]{1,0:T(1,128)S(1)} %broadcast_in_dim.17.gain_ref.refs_3_) | copy-start | bytes 18436
  95.0 39.3 %slice-start = ((s8[9437184]{0:T(1024)(128)(4,1)}), s8[4194304]{0:T(1024)(128)(4,1)S(1)}, s32[]{:S(2)}) async-start(s8[9437184]{0:T(1024)(128)(4,1)} %bitcast.28), calls=%async_computation.4 | async-start | bytes 8388608
  95.1 39.3 %slice-start.1 = ((s8[9437184]{0:T(1024)(128)(4,1)}), s8[1048576]{0:T(1024)(128)(4,1)S(1)}, s32[]{:S(2)}) async-start(s8[9437184]{0:T(1024)(128)(4,1)} %bitcast.28), calls=%async_computation.5 | async-start | bytes 2097152
  111.0 1.7 copy-start.3
  112.7 21.7 %slice-start.2 = ((s8[9437184]{0:T(1024)(128)(4,1)}), s8[4194304]{0:T(1024)(128)(4,1)S(1)}, s32[]{:S(2)}) async-start(s8[9437184]{0:T(1024)(128)(4,1)} %bitcast.28), calls=%async_computation.6 | async-start | bytes 8388608
  134.3 38.2 %copy-start.1 = (bf16[1024,768]{1,0:T(8,128)(2,1)}, bf16[1024,768]{1,0:T(8,128)(2,1)S(1)}, u32[]{:S(2)}) copy-start(bf16[1024,768]{1,0:T(8,128)(2,1)S(1)} %get-tuple-element.38.o_ref.refs_5_) | copy-start | bytes 4718596
  135.8 41.2 %copy-start.13 = (f32[1536]{0:T(1024)S(1)}, f32[1536]{0:T(1024)}, u32[]{:S(2)}) copy-start(f32[1536]{0:T(1024)} %param.15) | copy-start | bytes 18436
  135.8 36.7 %collective-permute-start.2 = (bf16[512,1536]{1,0:T(8,128)(2,1)S(1)}, bf16[512,1536]{1,0:T(8,128)(2,1)S(1)}, u32[]{:S(2)}, u32[]{:S(2)}) collective-permute-start(bf16[512,1536]{1,0:T(8,128)(2,1)S(1)} %convolution_convert_fusion), channel_id=1, source_target_pairs={{0,1},{1,0},{2,3},{3,2},{4,5},{5,4},{6,7},{7,6},{8,9},{9,8},{10,11... | collective-permute-start | bytes 4718600 | tf_op jit(solution)/shard_map/ppermute | solution.py:997
  175.5 2.1 copy-start.15
  175.5 36.1 %collective-permute-start.3 = (bf16[512,1536]{1,0:T(8,128)(2,1)S(1)}, bf16[512,1536]{1,0:T(8,128)(2,1)}, u32[]{:S(2)}, u32[]{:S(2)}) collective-permute-start(bf16[512,1536]{1,0:T(8,128)(2,1)S(1)} %add_convert_fusion.x_own.refs_11_), channel_id=1, source_target_pairs={{0,1},{1,0},{2,3},{3,2},{4,5},{5,4},{6,7},{7,6},{8,9},{9,8},{10,11... | collective-permute-start | bytes 4718600 | tf_op jit(solution)/shard_map/ppermute | solution.py:997
  367.3 5.3 copy-start.2
  517.9 6.8 %copy-start.4 = (bf16[512,1536]{1,0:T(8,128)(2,1)S(1)}, bf16[512,1536]{1,0:T(8,128)(2,1)}, u32[]{:S(2)}) copy-start(bf16[512,1536]{1,0:T(8,128)(2,1)} %get-tuple-element.76) | copy-start | bytes 4718596
  524.7 1.9 copy-start.9
  524.7 2.6 copy-start.8
  524.7 3.3 copy-start.7
  524.7 4.0 copy-start.6
  525.9 3.8 copy-start.5
  (2 other events, 2.1 us)
Sparse Core Ops, SparseCore 0:
  10.9 84.1 all-gather.2
  96.6 97.0 all-gather.4
  366.5 92.2 reduce-scatter.1

commit v5 on v4

--- a/solution.py
+++ b/solution.py
@@ -547,9 +547,9 @@
         lax.fori_loop(0, pieces, piece, 0)
         self.copy(0, block).start()
 
-    def put_gain(self, block, mine, other):
+    def put_gain(self, block, row):
         slot = block % self.slots[0]
-        column = jnp.broadcast_to(mine + other, (LANES, mine.shape[1])).T.astype(BF)
+        column = jnp.broadcast_to(row, (LANES, row.shape[1])).T.astype(BF)
         for k in range(self.devices):
             rows = column[k * self.rows : (k + 1) * self.rows, :]
             wide = jnp.concatenate([rows] * (COLS // LANES), axis=1)
@@ -557,28 +557,11 @@
         self.copy(0, block).start()
 
 
-def turn_into(turned_ref, lefts):
-    start = 0
-    for left in lefts:
-        for r in range(0, left.shape[0], 256):
-
-            @pl.loop(0, left.shape[1] // 256)
-            def _(i):
-                span = pl.ds(pl.multiple_of(i * 256, 256), 256)
-                turned_ref[span, start + r : start + r + 256] = left[r : r + 256, span].T
-
-        start += left.shape[0]
-
-
-def gain_copy(scatter, gain_ref, got_ref, sems):
-    return pltpu.make_async_remote_copy(
-        src_ref=gain_ref,
-        dst_ref=got_ref,
-        send_sem=sems.at[0],
-        recv_sem=sems.at[1],
-        device_id=(scatter.me, 1 - scatter.side),
-        device_id_type=MESH,
-    )
+def turn_piece(turned_ref, left, start, row):
+    @pl.loop(0, left.shape[1] // 256)
+    def _(i):
+        span = pl.ds(pl.multiple_of(i * 256, 256), 256)
+        turned_ref[span, start + row : start + row + 256] = left[row : row + 256, span].T
 
 
 def emit_into(outs, per, block, value):
@@ -616,16 +599,16 @@
 
 def ffn_scatter_kernel(scatter, per, *refs):
     (
-        norm_own, norm_other, cot_own, cot_other, right_own, right_other, gate_own, gate_other,
-        part_own, part_other, gain_ref, middle_own, wd_ref,
-    ) = refs[:13]
-    outs = refs[13:16]
-    gate_ref, gm_ref, block_own, block_send = refs[16:20]
+        cot_turned, norm_own, norm_other, right_own, right_other, gate_own, gate_other,
+        cot_hbm, middle_hbm, parts_hbm, gain_ref, wd_ref,
+    ) = refs[:12]
+    outs = refs[12:15]
+    gate_ref, gm_ref, block_own, block_send = refs[15:19]
     (
-        cot_turned, norm_turned, got_part, gm_own, gain_got, acc_other,
-        gain_sems, part_sems, gm_sems, local_sem,
-    ) = refs[20:30]
-    scatter.bind(refs[30:])
+        norm_turned, cot_own, middle_own, part_own, got_part, gm_own, gain_got, acc_other,
+        gain_sems, part_sems, gm_sems, local_sems,
+    ) = refs[19:31]
+    scatter.bind(refs[31:])
     step = pl.program_id(0)
     side = scatter.side
     across = (scatter.me, 1 - side)
@@ -635,7 +618,7 @@
 
     def part_copy(r):
         span = pl.ds(r * quarter, quarter)
-        return remote(part_other.at[1, span], got_part.at[span], part_sems.at[r], across)
+        return remote(parts_hbm.at[1, span], got_part.at[span], part_sems.at[r], across)
 
     def gm_copy(r):
         span = pl.ds(r * quarter, quarter)
@@ -644,28 +627,34 @@
     def gain_copy():
         return remote(gain_ref, gain_got, gain_sems, across)
 
+    loads = [
+        pltpu.make_async_copy(cot_hbm, cot_own, local_sems.at[0]),
+        pltpu.make_async_copy(parts_hbm.at[0], part_own, local_sems.at[1]),
+        pltpu.make_async_copy(middle_hbm, middle_own, local_sems.at[2]),
+    ]
+
     def gm_keep():
-        return pltpu.make_async_copy(gm_own, gm_ref.at[side], local_sem)
+        return pltpu.make_async_copy(gm_own, gm_ref.at[side], local_sems.at[3])
 
     @pl.when(step == 0)
     def _():
+        for load in loads:
+            load.start()
         scatter.barrier()
         for r in range(QUARTERS):
             part_copy(r).start()
         gain_copy().start()
-        turn_into(cot_turned, [cot_own, cot_other])
-        block_own[...] = jnp.zeros_like(block_own)
-        acc_other[...] = jnp.zeros_like(acc_other)
-
-    @pl.when(step == 1)
-    def _():
-        turn_into(norm_turned, [norm_own, norm_other])
 
     scatter.advance(step, functools.partial(emit_into, outs, per))
 
     @pl.when(step < per)
     def _():
         scatter.multiply(step, cot_turned, (right_own, right_other))
+
+        @pl.when(step == 0)
+        def _():
+            block_own[...] = jnp.zeros_like(block_own)
+            acc_other[...] = jnp.zeros_like(acc_other)
 
         @pl.loop(0, half // 256)
         def _(i):
@@ -673,17 +662,17 @@
             block_own[span, :] += nt(right_own[span, :], wd_ref[...])
             acc_other[span, :] += nt(right_other[span, :], wd_ref[...])
 
+    pieces = [(norm_own, 0, r) for r in range(0, half, 256)]
+    pieces += [(norm_other, half, r) for r in range(0, half, 256)]
+    for nth, (left, start, row) in enumerate(pieces):
+
+        @pl.when(step == per - len(pieces) + nth)
+        def _():
+            turn_piece(norm_turned, left, start, row)
+
     @pl.when((step >= per) & (step < 2 * per))
     def _():
         scatter.multiply(step, norm_turned, (right_own, right_other))
-
-    @pl.when(step == 2 * per)
-    def _():
-        gain_copy().wait()
-        scatter.put_gain(step, gain_ref[0:1, :], gain_got[0:1, :])
-
-    @pl.when((step % 2 == 1) & (step < 2 * per))
-    def _():
         rows = gate_ref.shape[0] // 4
 
         @pl.loop(0, 4)
@@ -692,10 +681,18 @@
             total = nn(norm_turned[span, :half], gate_own[...])
             gate_ref[span, :] = (total + nn(norm_turned[span, half:], gate_other[...])).astype(BF)
 
+    @pl.when(step == 2 * per)
+    def _():
+        gain_copy().wait()
+        scatter.put_gain(step, gain_ref[0:1, :] + gain_got[0:1, :])
+
     for r in range(QUARTERS):
 
         @pl.when(step == 3 + 2 * r)
         def _():
+            if r == 0:
+                for load in loads:
+                    load.wait()
             part_copy(r).wait()
 
             @pl.loop(r * quarter // row_chunk, (r + 1) * quarter // row_chunk)
@@ -708,7 +705,7 @@
             if r == QUARTERS - 1:
                 gm_keep().start()
 
-    @pl.when(step == per)
+    @pl.when(step == 2 * per + 1)
     def _():
         @pl.loop(0, half // row_chunk)
         def _(i):
@@ -732,12 +729,12 @@
     )
 
 
-def ffn_scatter(devices, normed, cots, grads, parts, gain_part, middle, w):
+def ffn_scatter(devices, cot_turned, normed, grads, cot, middle, parts, gain_part, w):
     half, d = middle.shape
     width = grads.shape[3]
     per = width // COLS
     scatter = Scatter(devices, d // devices, 2 * per + 1)
-    assert 2 * per > 3 + 2 * QUARTERS and scatter.rows * devices == d
+    assert 2 * per > 3 + 2 * QUARTERS and scatter.rows * devices == d and per >= 2 * half // 256
 
     def right(side):
         def where(j):
@@ -747,7 +744,7 @@
         return pl.BlockSpec((None, None, half, COLS), where)
 
     def gate_block(j):
-        return jnp.clip((j - 1) // 2, 0, per - 1)
+        return jnp.clip(j - per, 0, per - 1)
 
     def gate(side):
         return pl.BlockSpec((None, None, half, COLS), lambda j: (side, 0, 0, gate_block(j)))
@@ -759,28 +756,28 @@
 
     specs, shapes = emit_specs(scatter, 2, per, width)
     whole = lambda j: (0, 0)
+    left_there = pl.BlockSpec(memory_space=pl.ANY)
     return pl.pallas_call(
         functools.partial(ffn_scatter_kernel, scatter, per),
         grid=(scatter.steps,),
         in_specs=[
+            resident((d, 2 * half)),
             rows_of(0),
             rows_of(1),
-            resident((half, d)),
-            resident((half, d)),
             right(0),
             right(1),
             gate(0),
             gate(1),
-            rows_of(0),
-            pl.BlockSpec(memory_space=pl.ANY),
+            left_there,
+            left_there,
+            left_there,
             resident((8, d)),
-            resident((half, d)),
             pl.BlockSpec((d, COLS), lambda j: (0, 2 * per + jnp.minimum(j, per - 1))),
         ],
         out_specs=specs
         + [
             pl.BlockSpec((d, COLS), lambda j: (0, gate_block(j))),
-            pl.BlockSpec(memory_space=pl.ANY),
+            left_there,
             pl.BlockSpec((half, d), whole),
             pl.BlockSpec((half, d), whole),
         ],
@@ -793,7 +790,9 @@
         ],
         scratch_shapes=[
             pltpu.VMEM((d, 2 * half), BF),
-            pltpu.VMEM((d, 2 * half), BF),
+            pltpu.VMEM((half, d), BF),
+            pltpu.VMEM((half, d), BF),
+            pltpu.VMEM((half, d), BF),
             pltpu.VMEM((half, d), BF),
             pltpu.VMEM((half, d), BF),
             pltpu.VMEM((8, d), F32),
@@ -801,29 +800,28 @@
             pltpu.SemaphoreType.DMA((2,)),
             pltpu.SemaphoreType.DMA((QUARTERS, 2)),
             pltpu.SemaphoreType.DMA((QUARTERS, 2)),
-            pltpu.SemaphoreType.DMA,
+            pltpu.SemaphoreType.DMA((4,)),
         ]
         + scatter.scratch(),
         compiler_params=remote_settings(0),
         cost_estimate=cost(16 * half * d * per * COLS, 20 * half * d),
         name="ffn_scatter",
     )(
-        normed, normed, *cots, grads, grads, grads, grads, parts, parts, gain_part, middle, w,
+        cot_turned, normed, normed, grads, grads, grads, grads, cot, middle, parts, gain_part, w,
     )
 
 
 def attention_scatter_kernel(scatter, per, *refs):
     (
-        normed_ref, gm_ref, x_ref, gain_ref, right_ref, attended_ref, block_own, block_send,
-        first_ref, second_ref, w_first, w_second,
-    ) = refs[:12]
-    outs = refs[12:17]
-    token_grad_ref, block_out_ref = refs[17:19]
+        norm_turned, gain_ref, right_ref, w_ref, attended_ref, gm_hbm, x_hbm, block_hbm, block_send,
+    ) = refs[:9]
+    outs = refs[9:14]
+    token_grad_ref, block_out_ref = refs[14:16]
     (
-        turned_ref, acc_ref, part_send, part_got, block_got, gain_part, gain_got,
-        gain_sems, part_sems, block_sems,
-    ) = refs[19:29]
-    scatter.bind(refs[29:])
+        gm_turned, gm_ref, x_ref, block_own, acc_ref, part_send, part_got, block_got,
+        gain_part, part_sems, block_sems, local_sems,
+    ) = refs[16:28]
+    scatter.bind(refs[28:])
     step = pl.program_id(0)
     side = scatter.side
     across = (scatter.me, 1 - side)
@@ -832,7 +830,6 @@
     quarter = half // QUARTERS
     chunk = 128
     kinds = 3 * per
-    ready = (kinds + 1) // 2
     own, other = side * half, (1 - side) * half
 
     def part_copy(r):
@@ -842,8 +839,11 @@
     def block_copy():
         return remote(block_send, block_got, block_sems, across)
 
-    def gain_copy():
-        return remote(gain_part, gain_got, gain_sems, across)
+    loads = [
+        pltpu.make_async_copy(x_hbm, x_ref, local_sems.at[0]),
+        pltpu.make_async_copy(gm_hbm, gm_ref, local_sems.at[1]),
+        pltpu.make_async_copy(block_hbm, block_own, local_sems.at[2]),
+    ]
 
     def back(row):
         span = pl.ds(row, chunk)
@@ -853,62 +853,74 @@
 
     @pl.when(step == 0)
     def _():
+        for load in loads:
+            load.start()
         scatter.barrier()
-        turn_into(turned_ref, [normed_ref])
+        block_copy().start()
+
+    scatter.advance(step, functools.partial(emit_into, outs, per))
+
+    @pl.when(step == 0)
+    def _():
         acc_ref[...] = jnp.zeros_like(acc_ref)
         gain_part[...] = jnp.zeros_like(gain_part)
 
-    @pl.when(step == kinds)
-    def _():
-        turn_into(turned_ref, [gm_ref])
-
-    scatter.advance(step, functools.partial(emit_into, outs, per))
-
     @pl.when(step < kinds)
     def _():
-        scatter.multiply(step, turned_ref, (right_ref,))
+        scatter.multiply(step, norm_turned, (right_ref,))
+
+        @pl.loop(0, length // 256)
+        def _(i):
+            span = pl.ds(i * 256, 256)
+            acc_ref[span, :] += nt(right_ref[span, :], w_ref[...])
+
+    @pl.when(step == 1)
+    def _():
+        for load in loads:
+            load.wait()
+
+    for nth, row in enumerate(range(0, length, 256)):
+
+        @pl.when(step == kinds - length // 256 + nth)
+        def _():
+            turn_piece(gm_turned, gm_ref, 0, row)
 
     @pl.when((step >= kinds) & (step < 4 * per))
     def _():
-        scatter.multiply(step, turned_ref, (attended_ref,))
-
-    for nth, (g_ref, w_ref) in enumerate(((first_ref, w_first), (second_ref, w_second))):
-
-        @pl.when(2 * step + nth < kinds)
+        scatter.multiply(step, gm_turned, (attended_ref,))
+
+    for r in range(QUARTERS):
+
+        @pl.when(step == kinds + min(r, per - 1))
         def _():
-            @pl.loop(0, length // 256)
-            def _(i):
-                span = pl.ds(i * 256, 256)
-                acc_ref[span, :] += nt(g_ref[span, :], w_ref[...])
-
-    @pl.when(step == ready)
-    def _():
-        for r in range(QUARTERS):
-
             @pl.loop(r * quarter // chunk, (r + 1) * quarter // chunk)
             def _(i):
                 part_send[pl.ds(i * chunk, chunk), :] = back(other + i * chunk).astype(BF)
 
             part_copy(r).start()
 
-    @pl.when(step == ready + 1)
-    def _():
+            @pl.loop(r * quarter // chunk, (r + 1) * quarter // chunk)
+            def _(i):
+                span = pl.ds(own + i * chunk, chunk)
+                acc_ref[span, :] = back(own + i * chunk) + gm_ref[span, :].astype(F32)
+
+    @pl.when(step == 4 * per)
+    def _():
+        scatter.put_gain(step, gain_part[0:1, :])
+
+    @pl.when(step == 4 * per + 1)
+    def _():
+        block_copy().wait()
+
         @pl.loop(0, half // chunk)
         def _(i):
-            span = pl.ds(own + i * chunk, chunk)
-            acc_ref[span, :] = back(own + i * chunk) + gm_ref[span, :].astype(F32)
-
-        gain_copy().start()
-        block_copy().start()
-
-    @pl.when(step == 4 * per)
-    def _():
-        gain_copy().wait()
-        scatter.put_gain(step, gain_part[0:1, :], gain_got[0:1, :])
+            span = pl.ds(i * chunk, chunk)
+            total = block_own[span, :] + block_got[span, :].astype(F32)
+            block_out_ref[span, :] = total.astype(BF)
 
     for r in range(QUARTERS):
 
-        @pl.when(step == scatter.steps - 1 - QUARTERS + r)
+        @pl.when(step == scatter.steps - QUARTERS + r)
         def _():
             part_copy(r).wait()
 
@@ -918,79 +930,65 @@
                 total = acc_ref[pl.ds(own + i * chunk, chunk), :]
                 token_grad_ref[span, :] = (total + part_got[span, :].astype(F32)).astype(BF)
 
-    @pl.when(step == scatter.steps - 1)
-    def _():
-        block_copy().wait()
-
-        @pl.loop(0, half // chunk)
-        def _(i):
-            span = pl.ds(i * chunk, chunk)
-            total = block_own[span, :] + block_got[span, :].astype(F32)
-            block_out_ref[span, :] = total.astype(BF)
-
 
 def attention_scatter(
-    devices, normed, gm, x, gain, grads, attended, block_own, block_send, w
+    devices, norm_turned, gm, x, gain, grads, attended, block_own, block_send, w
 ):
-    length, d = normed.shape
+    length, d = gm.shape
     half = length // 2
     width = grads.shape[2]
     per = width // COLS
     kinds = 3 * per
     scatter = Scatter(devices, d // devices, 4 * per + 1)
-    assert (kinds + 1) // 2 + 1 < 4 * per and scatter.rows * devices == d
-
-    def grads_spec(pick):
-        def where(j):
-            c = jnp.minimum(pick(j), kinds - 1)
-            return (c // per, 0, c % per)
-
-        return pl.BlockSpec((None, length, COLS), where)
-
-    def weight_spec(pick):
-        return pl.BlockSpec((d, COLS), lambda j: (0, jnp.minimum(pick(j), kinds - 1)))
+    assert kinds >= length // 256 and scatter.rows * devices == d
+    assert scatter.starts[-1] > QUARTERS
+
+    def grads_map(j):
+        c = jnp.minimum(j, kinds - 1)
+        return (c // per, 0, c % per)
 
     def attended_map(j):
         return (0, jnp.clip(j - kinds, 0, per - 1))
 
     specs, shapes = emit_specs(scatter, 4, per, width)
     whole = lambda j: (0, 0)
-    even, odd = (lambda j: 2 * j), (lambda j: 2 * j + 1)
+    left_there = pl.BlockSpec(memory_space=pl.ANY)
     return pl.pallas_call(
         functools.partial(attention_scatter_kernel, scatter, per),
         grid=(scatter.steps,),
-        in_specs=[resident((length, d))] * 3
-        + [
+        in_specs=[
+            resident((d, length)),
             resident((1, d)),
-            grads_spec(lambda j: j),
+            pl.BlockSpec((None, length, COLS), grads_map),
+            pl.BlockSpec((d, COLS), lambda j: (0, jnp.minimum(j, kinds - 1))),
             pl.BlockSpec((length, COLS), attended_map),
-            resident((half, d)),
-            pl.BlockSpec(memory_space=pl.ANY),
-            grads_spec(even),
-            grads_spec(odd),
-            weight_spec(even),
-            weight_spec(odd),
+            left_there,
+            left_there,
+            left_there,
+            left_there,
         ],
         out_specs=specs + [pl.BlockSpec((half, d), whole), pl.BlockSpec((half, d), whole)],
         out_shape=shapes
         + [jax.ShapeDtypeStruct((half, d), BF), jax.ShapeDtypeStruct((half, d), BF)],
         scratch_shapes=[
             pltpu.VMEM((d, length), BF),
+            pltpu.VMEM((length, d), BF),
+            pltpu.VMEM((length, d), BF),
+            pltpu.VMEM((half, d), F32),
             pltpu.VMEM((length, d), F32),
             pltpu.VMEM((half, d), BF),
             pltpu.VMEM((half, d), BF),
             pltpu.VMEM((half, d), BF),
             pltpu.VMEM((8, d), F32),
-            pltpu.VMEM((8, d), F32),
-            pltpu.SemaphoreType.DMA((2,)),
             pltpu.SemaphoreType.DMA((QUARTERS, 2)),
             pltpu.SemaphoreType.DMA((2,)),
+            pltpu.SemaphoreType.DMA((3,)),
         ]
         + scatter.scratch(),
         compiler_params=remote_settings(1),
         cost_estimate=cost(14 * length * d * per * COLS, 20 * length * d),
         name="attention_scatter",
-    )(normed, gm, x, gain, grads, attended, block_own, block_send, grads, grads, w, w)
+    )(norm_turned, gain, grads, w, attended, gm, x, block_own, block_send)
 
 
 def swap(x):
@@ -1045,15 +1043,22 @@
 
     bias, positions = tree_tables(parents[0], seg_rows)
     cosine, sine = turn_tables(positions, COLS)
-    rows_all, cot_other = lax.optimization_barrier(
-        (place(tokens, swap(tokens)), swap(cotangent))
+    cot_other = swap(cotangent)
+    rows_all, cot_other, cot_turned = lax.optimization_barrier(
+        (
+            place(tokens, swap(tokens)),
+            cot_other,
+            jnp.concatenate([cotangent.T, cot_other.T], axis=1),
+        )
     )
 
     qkv, normed_one = project(rows_all, attn_row, cosine, sine, first, width)
     attended, lse = attend(qkv, bias, width, seg_rows)
     out_turned = first[:, 3 * width :]
     send = nt(other_rows(attended), out_turned).astype(BF)
+    send, norm_source = lax.optimization_barrier((send, normed_one))
     received = swap(send)
+    received, norm_turned = lax.optimization_barrier((received, norm_source.T))
     middle = (
         tokens.astype(F32) + nt(own_rows(attended), out_turned) + received.astype(F32)
     ).astype(BF)
@@ -1063,14 +1068,7 @@
         (middle, middle_other), (cotangent, cot_other), ffn_row, second, hidden_width
     )
     down_grad, up_grad, ffn_gain_grad, gate_whole, grad_middle, block_own, block_send = ffn_scatter(
-        devices,
-        normed_two,
-        (cotangent, cot_other),
-        ffn_grads,
-        parts,
-        gain_part,
-        middle,
-        second,
+        devices, cot_turned, normed_two, ffn_grads, cotangent, middle, parts, gain_part, second
     )
     gate_grad = lax.psum_scatter(gate_whole, "dp", scatter_dimension=0, tiled=True).astype(F32)
     grad_middle = grad_middle.reshape(length, d)
@@ -1083,7 +1081,7 @@
         query_grad, key_grad, value_grad, output_grad, attn_gain_grad, token_grad, block_out,
     ) = attention_scatter(
         devices,
-        normed_one,
+        norm_turned,
         grad_middle,
         rows_all,
         attn_row,
@@ -1095,8 +1093,8 @@
     )
     gain_rows = d // devices // 2
 
-    def gain_piece(columns):
-        return lax.dynamic_slice_in_dim(columns[:, 0], mine * gain_rows, gain_rows, 0)
+    def gain_piece(columns, side):
+        return lax.dynamic_slice_in_dim(columns[:, 0], side * gain_rows, gain_rows, 0)
 
     return (
         block_out,
@@ -1108,8 +1106,8 @@
         gate_grad,
         up_grad,
         down_grad.T,
-        gain_piece(attn_gain_grad),
-        gain_piece(ffn_gain_grad),
+        gain_piece(attn_gain_grad, mine) + swap(gain_piece(attn_gain_grad, 1 - mine)),
+        gain_piece(ffn_gain_grad, mine),
     )
 
 

time: 538 us -> 519 us (0.965)
  Pallas kernels: 338 us -> 312 us
  waiting for transfers between devices: 139 us -> 126 us
  local copies, waits for them, and re-layouts: 22.2 us -> 32.3 us
    pallas_call x1, Pallas kernels: 111 us -> 92.2 us  [attention_scatter(): pl.pallas_call(functools.partial(attention_scatter_kernel, scatter, per),...]
    ppermute x4 -> x5, waiting for transfers between devices: 127 us -> 120 us  [swap(): return lax.ppermute(x, 'tensor', [(0, 1), (1, 0)])]
    pallas_call x1, Pallas kernels: 105 us -> 98.4 us  [ffn_scatter(): pl.pallas_call(functools.partial(ffn_scatter_kernel, scatter, per), grid=...]
    all_gather x2, waiting for transfers between devices: 11.9 us -> 5.9 us  [gather(): return lax.all_gather(shard, 'dp', axis=0, tiled=True)]
    unnamed x46 -> x57, local copies, waits for them, and re-layouts: 10.9 us -> 15.9 us
  transfers between devices with their start and end apart: 7 -> 8, of which waited for: 5 -> 5; matrix products, arithmetic and copies ran while one was open for 5% -> 8% of each run, Pallas kernels for 34% -> 32%
where the time goes in v5:
time: 519 us; the launch traced here: 518 us
  Pallas kernels  312 us (60%)
  waiting for transfers between devices  126 us (24%)
  local copies, waits for them, and re-layouts  32.3 us (6%)
  matrix products  14.2 us (3%)
  between operations  14.1 us (3%)
  other arithmetic  12.9 us (2%)
  starting transfers between devices  7.22 us (1%)
    ppermute x5, waiting for transfers between devices, swap(): return lax.ppermute(x, 'tensor', [(0, 1), (1, 0)])  120 us
    pallas_call x1, Pallas kernels, ffn_scatter(): pl.pallas_call(functools.partial(ffn_scatter_kernel, scatter, per), grid=...  98.4 us
    pallas_call x1, Pallas kernels, attention_scatter(): pl.pallas_call(functools.partial(attention_scatter_kernel, scatter, per),...  92.2 us
    pallas_call x1, Pallas kernels, ffn(): pl.pallas_call(ffn_kernel, grid=(2, steps), in_specs=[resident((rows, d))...  49.7 us
    pallas_call x1, Pallas kernels, attend_back(): pl.pallas_call(functools.partial(attend_back_kernel, block, seg_rows), gr...  34 us
    pallas_call x1, Pallas kernels, attend(): pl.pallas_call(functools.partial(attend_kernel, block, seg_rows), grid=(g...  21.5 us
    unnamed x57, local copies, waits for them, and re-layouts  15.9 us
    pallas_call x1, Pallas kernels, project(): pl.pallas_call(functools.partial(project_kernel, parts), grid=(3 * parts,...  15.8 us
  transfers between devices with their start and end apart: 8, of which 5 were waited for; matrix products, arithmetic and copies ran while one was open for 8% of the time, Pallas kernels for 32%

profile of v5, /device:TPU:0, one launch (start us, length us, event | category | flops | bytes accessed | tf_op | source)
XLA Modules:
  0.0 518.1 jit_solution(13492459330422935280)
XLA Ops:
  7.2 2.0 pad_maximum_fusion.2
  9.3 2.4 pad_maximum_fusion.1
  12.5 3.0 collective-permute-start.1
  18.5 2.6 copy.55.cos_ref
  22.2 2.7 copy.56.sin_ref
  26.5 57.2 %collective-permute-done = bf16[512,1536]{1,0:T(8,128)(2,1)} collective-permute-done((bf16[512,1536]{1,0:T(8,128)(2,1)}, bf16[512,1536]{1,0:T(8,128)(2,1)}, u32[]{:S(2)}, u32[]{:S(2)}) %collective-permute-start) | collective-permute-done | bytes 1572896 | tf_op jit(solution)/shard_map/ppermute | solution.py:995
  87.0 2.2 pad_maximum_fusion.refs_0_
  89.1 5.9 %all-gather.3.cloned.1.call-done.w_ref.refs_3_ = bf16[1536,3072]{1,0:T(8,128)(2,1)} async-done(((bf16[96,3072]{1,0:T(8,128)(2,1)}), bf16[1536,3072]{1,0:T(8,128)(2,1)}) %all-gather.3.cloned.1.call-update) | async-done | bytes 9437200 | tf_op jit(solution)/shard_map/all_gather | solution.py:1033
  97.5 15.8 %project.1 = (bf16[1024,2304]{1,0:T(8,128)(2,1)}, bf16[1024,1536]{1,0:T(8,128)(2,1)S(1)}) custom-call(bf16[1024,1536]{1,0:T(8,128)(2,1)} %copy-done.9, f32[1,1536]{1,0:T(1,128)S(1)} %broadcast_in_dim.17.gain_ref.refs_1_, f32[1024,256]{1,0:T(8,128)S(1)} %copy-done, f32[1024,256]{1,0:T(8,128)S(1)} %copy-done.2, ...), custom_call_target="tpu_custom_call" | custom-call | flops 7247757312 | bytes 13369344 | tf_op jit(solution)/shard_map/project/pallas_call | solution.py:120
  113.3 21.5 %attend.1 = (bf16[1024,768]{1,0:T(8,128)(2,1)S(1)}, f32[6,2,1024]{2,1,0:T(2,128)S(1)}) custom-call(bf16[1024,2304]{1,0:T(8,128)(2,1)} %get-tuple-element.41.q_ref.k_ref.v_ref, bf16[1024,2304]{1,0:T(8,128)(2,1)} %get-tuple-element.41.q_ref.k_ref.v_ref, bf16[1024,2304]{1,0:T(8,128)(2,1)} %get-tuple-element.41.q_ref.k_ref.v_ref, ...), custom_call_target="tpu_custom_call" | custom-call | flops 6442450944 | bytes 6291456 | tf_op jit(solution)/shard_map/attend/pallas_call | solution.py:199
  134.8 4.9 convolution_convert_fusion
  141.2 2.9 copy.59
  144.1 3.9 convolution_add_fusion
  148.0 28.5 %collective-permute-done.2 = bf16[512,1536]{1,0:T(8,128)(2,1)} collective-permute-done((bf16[512,1536]{1,0:T(8,128)(2,1)}, bf16[512,1536]{1,0:T(8,128)(2,1)}, u32[]{:S(2)}, u32[]{:S(2)}) %collective-permute-start.2) | collective-permute-done | bytes 1572896 | tf_op jit(solution)/shard_map/ppermute | solution.py:995
  176.6 2.2 add_convert_fusion.x_own.refs_8_
  182.5 32.1 %collective-permute-done.3.x_other = bf16[512,1536]{1,0:T(8,128)(2,1)} collective-permute-done((bf16[512,1536]{1,0:T(8,128)(2,1)S(1)}, bf16[512,1536]{1,0:T(8,128)(2,1)}, u32[]{:S(2)}, u32[]{:S(2)}) %collective-permute-start.3) | collective-permute-done | bytes 1572896 | tf_op jit(solution)/shard_map/ppermute | solution.py:995
  214.6 49.7 %ffn.1 = (bf16[2,3,512,2048]{3,2,1,0:T(8,128)(2,1)}, bf16[2,512,1536]{2,1,0:T(8,128)(2,1)}, bf16[2,512,1536]{2,1,0:T(8,128)(2,1)}, f32[8,1536]{1,0:T(8,128)}) custom-call(bf16[512,1536]{1,0:T(8,128)(2,1)} %copy-done.13, bf16[512,1536]{1,0:T(8,128)(2,1)} %collective-permute-done.3.x_other, bf16[512,1536]{1,0:T(8,128)(2,1)} %refs_7_.1, ...), custom_call_target="tpu_custom_call" | custom-call | flops 32212254720 | bytes 62914560 | tf_op jit(solution)/shard_map/ffn/pallas_call | solution.py:396
  264.4 98.4 %ffn_scatter.1 = (f32[96,2048]{1,0:T(8,128)}, f32[96,2048]{1,0:T(8,128)}, f32[96,256]{1,0:T(8,128)}, bf16[1536,2048]{1,0:T(8,128)(2,1)}, bf16[2,512,1536]{2,1,0:...) custom-call(bf16[1536,1024]{1,0:T(8,128)(2,1)} %pad_maximum_fusion.refs_0_, ...), custom_call_target="tpu_custom_call" | custom-call | flops 25769803776 | bytes 15728640 | tf_op jit(solution)/shard_map/ffn_scatter/pallas_call | solution.py:760
  364.4 5.3 %fusion.4.do_ref = bf16[1024,768]{1,0:T(8,128)(2,1)S(1)} fusion(bf16[1024,1536]{1,0:T(8,128)(2,1)} %bitcast.34, bf16[1536,3072]{1,0:T(8,128)(2,1)} %all-gather.3.cloned.1.call-done.w_ref.refs_3_), kind=kOutput, calls=%fused_computation.8 | convolution fusion | flops 2416705536 | bytes 7077888 | tf_op jit(solution)/shard_map/dot_general | solution.py:33
  369.7 34.0 %attend_back.1.refs_2_ = bf16[3,1024,768]{2,1,0:T(8,128)(2,1)} custom-call(bf16[1024,2304]{1,0:T(8,128)(2,1)} %get-tuple-element.41.q_ref.k_ref.v_ref, bf16[1024,2304]{1,0:T(8,128)(2,1)} %get-tuple-element.41.q_ref.k_ref.v_ref, bf16[1024,2304]{1,0:T(8,128)(2,1)} %get-tuple-element.41.q_ref.k_ref.v_ref, bf16[1024,768]{1,0:T(8,128)(2,1)S(1)} %copy-done.6, ...), custom_call_target="tpu_custom_call" | custom-call | flops 16106127360 | bytes 12582912 | tf_op jit(solution)/shard_map/attend_back/pallas_call | solution.py:287
  403.8 92.2 %attention_scatter.1 = (f32[96,768]{1,0:T(8,128)}, f32[96,768]{1,0:T(8,128)}, f32[96,768]{1,0:T(8,128)}, f32[96,768]{1,0:T(8,128)}, f32[96,256]{1,0:T(8,128)}, /...) custom-call(bf16[1536,1024]{1,0:T(8,128)(2,1)} %bitcast.28, f32[1,1536]{1,0:T(1,128)} %copy-done.4, ...), custom_call_target="tpu_custom_call" | custom-call | flops 16911433728 | bytes 31457280 | tf_op jit(solution)/shard_map/attention_scatter/pallas_call | solution.py:956
  498.6 2.0 collective-permute-done.4
  501.1 1.9 convert_element_type.88
  503.1 2.7 copy.73
  (111 shorter events, 27.9 us)
Async XLA Ops:
  7.2 87.9 %all-gather.3.cloned.1.call-start = ((), (), s32[]{:S(2)}) async-start(), calls=%async_computation.1 | async-start | bytes 10027008 | tf_op jit(solution)/shard_map/all_gather | solution.py:1033
  9.2 2.6 copy-start.10
  9.2 205.4 %all-gather.5.cloned.1.call-start = ((), (), s32[]{:S(2)}) async-start(), calls=%async_computation.2 | async-start | bytes 20054016 | tf_op jit(solution)/shard_map/all_gather | solution.py:1033
  11.7 3.9 copy-start.23
  11.7 5.0 copy-start.21
  11.7 489.4 %reduce-scatter.2.cloned.1.call-start = ((), (), s32[]{:S(2)}) async-start(), calls=%async_computation.3 | async-start | bytes 6684672 | tf_op jit(solution)/shard_map/reduce_scatter | solution.py:1073
  12.5 72.8 %collective-permute-start.1 = (bf16[512,1536]{0,1:T(8,128)(2,1)S(1)}, bf16[512,1536]{0,1:T(8,128)(2,1)S(1)}, u32[]{:S(2)}, u32[]{:S(2)}) collective-permute-start(bf16[512,1536]{0,1:T(8,128)(2,1)S(1)} %copy.53), channel_id=1, source_target_pairs={{0,1},{1,0},{2,3},{3,2},{4,5},{5,4},{6,7},{7,6},{8,9},{9,8},{10,11... | collective-permute-start | bytes 4718600 | tf_op jit(solution)/shard_map/ppermute | solution.py:995
  15.5 68.2 %collective-permute-start = (bf16[512,1536]{1,0:T(8,128)(2,1)}, bf16[512,1536]{1,0:T(8,128)(2,1)}, u32[]{:S(2)}, u32[]{:S(2)}) collective-permute-start(bf16[512,1536]{1,0:T(8,128)(2,1)} %param.12), channel_id=1, source_target_pairs={{0,1},{1,0},{2,3},{3,2},{4,5},{5,4},{6,7},{7,6},{8,9},{9,8},{10,11... | collective-permute-start | bytes 4718600 | tf_op jit(solution)/shard_map/ppermute | solution.py:995
  16.7 78.3 %copy-start.4 = (f32[1,1536]{1,0:T(1,128)}, f32[1,1536]{1,0:T(1,128)S(1)}, u32[]{:S(2)}) copy-start(f32[1,1536]{1,0:T(1,128)S(1)} %broadcast_in_dim.17.gain_ref.refs_1_) | copy-start | bytes 18436
  87.0 2.2 copy-start.7
  134.8 5.0 copy-start.5
  139.7 36.8 %collective-permute-start.2 = (bf16[512,1536]{1,0:T(8,128)(2,1)}, bf16[512,1536]{1,0:T(8,128)(2,1)}, u32[]{:S(2)}, u32[]{:S(2)}) collective-permute-start(bf16[512,1536]{1,0:T(8,128)(2,1)} %convolution_convert_fusion), channel_id=1, source_target_pairs={{0,1},{1,0},{2,3},{3,2},{4,5},{5,4},{6,7},{7,6},{8,9},{9,8},{10,11... | collective-permute-start | bytes 4718600 | tf_op jit(solution)/shard_map/ppermute | solution.py:995
  176.6 3.8 copy-start.22
  176.6 4.4 copy-start.8
  178.8 35.8 %copy-start.13 = (bf16[512,1536]{1,0:T(8,128)(2,1)}, bf16[512,1536]{1,0:T(8,128)(2,1)S(1)}, u32[]{:S(2)}) copy-start(bf16[512,1536]{1,0:T(8,128)(2,1)S(1)} %add_convert_fusion.x_own.refs_8_) | copy-start | bytes 4718596
  178.8 35.8 %collective-permute-start.3 = (bf16[512,1536]{1,0:T(8,128)(2,1)S(1)}, bf16[512,1536]{1,0:T(8,128)(2,1)}, u32[]{:S(2)}, u32[]{:S(2)}) collective-permute-start(bf16[512,1536]{1,0:T(8,128)(2,1)S(1)} %add_convert_fusion.x_own.refs_8_), channel_id=1, source_target_pairs={{0,1},{1,0},{2,3},{3,2},{4,5},{5,4},{6,7},{7,6},{8,9},{9,8},{10,11... | collective-permute-start | bytes 4718600 | tf_op jit(solution)/shard_map/ppermute | solution.py:995
  364.4 5.3 %copy-start.6 = (bf16[1024,768]{1,0:T(8,128)(2,1)S(1)}, bf16[1024,768]{1,0:T(8,128)(2,1)}, u32[]{:S(2)}) copy-start(bf16[1024,768]{1,0:T(8,128)(2,1)} %copy-done.5) | copy-start | bytes 4718596
  496.0 9.8 %copy-start.11 = (bf16[512,1536]{1,0:T(8,128)(2,1)S(1)}, bf16[512,1536]{1,0:T(8,128)(2,1)}, u32[]{:S(2)}) copy-start(bf16[512,1536]{1,0:T(8,128)(2,1)} %get-tuple-element.88) | copy-start | bytes 4718596
  497.0 3.6 collective-permute-start.4
  505.7 1.9 copy-start.18
  505.7 2.6 copy-start.17
  505.7 3.3 copy-start.16
  505.7 4.0 copy-start.15
  506.9 3.8 copy-start.14
  (8 other events, 11.0 us)
Sparse Core Ops, SparseCore 0:
  10.9 84.1 all-gather.2
  96.6 97.0 all-gather.4
  362.9 98.8 reduce-scatter.1

commit v6 on v5

--- a/solution.py
+++ b/solution.py
@@ -48,22 +48,24 @@
         reach = jnp.minimum(eye + up, 1)
     depths = jnp.sum(reach, axis=1) - 1
     bias = jnp.where(reach.T > 0, 0.0, MASKED).astype(F32)
-    bias = jnp.repeat(bias, seg_rows, axis=1)
-    rows = jnp.arange(segs * seg_rows, dtype=jnp.int32)
-    positions = jnp.repeat(depths * seg_rows, seg_rows) + rows % seg_rows
-    return bias, positions.astype(F32)
-
-
-def turn_tables(positions, width):
-    half = HD // 2
-    rates = jnp.exp(jnp.arange(half, dtype=F32) * (-2.0 * math.log(10000.0) / HD))
-    angles = positions[:, None] * rates[None, :]
-    cosine, sine = jnp.cos(angles), jnp.sin(angles)
-    heads = width // HD
-    return (
-        jnp.tile(jnp.concatenate([cosine, cosine], axis=1), (1, heads)),
-        jnp.tile(jnp.concatenate([-sine, sine], axis=1), (1, heads)),
-    )
+    return jnp.repeat(bias, seg_rows, axis=1), depths
+
+
+def turn_tables(depths_ref, cos_ref, sin_ref):
+    segs = depths_ref.shape[0]
+    seg_rows = 2 * cos_ref.shape[1] // segs
+    shape = (seg_rows, LANES)
+    lane = lax.broadcasted_iota(jnp.int32, shape, 1) % HD
+    row = lax.broadcasted_iota(jnp.int32, shape, 0)
+    rates = jnp.exp((lane % (HD // 2)).astype(F32) * (-2.0 * math.log(10000.0) / HD))
+    sign = jnp.where(lane < HD // 2, -1.0, 1.0).astype(F32)
+
+    @pl.loop(0, segs)
+    def _(seg):
+        angles = (depths_ref[seg] * seg_rows + row).astype(F32) * rates
+        span = pl.ds(seg % (segs // 2) * seg_rows, seg_rows)
+        cos_ref[seg // (segs // 2), span, :] = jnp.cos(angles)
+        sin_ref[seg // (segs // 2), span, :] = jnp.sin(angles) * sign
 
 
 def turn(x, cosine, sine):
@@ -88,57 +90,6 @@
         span = pl.ds(i * chunk, chunk)
         x = x_ref[span, :].astype(F32)
         normed_ref[span, :] = (x * inverse_rms(x) * gain_ref[...]).astype(BF)
-
-
-def project_kernel(parts, x_ref, gain_ref, cos_ref, sin_ref, w_ref, out_ref, normed_ref):
-    j = pl.program_id(0)
-    rows = x_ref.shape[0]
-    chunk = 256
-
-    @pl.when(j == 0)
-    def _():
-        norm_rows(x_ref, gain_ref, normed_ref)
-
-    @pl.when(j < 2 * parts)
-    def _():
-        scale = jnp.where(j < parts, 1.0 / math.sqrt(HD), 1.0).astype(BF)
-        for r in range(0, rows, chunk):
-            pre = nn(normed_ref[r : r + chunk, :], w_ref[...])
-            rotated = turn(pre, cos_ref[r : r + chunk, :], sin_ref[r : r + chunk, :])
-            out_ref[r : r + chunk, :] = rotated.astype(BF) * scale
-
-    @pl.when(j >= 2 * parts)
-    def _():
-        for r in range(0, rows, chunk):
-            out_ref[r : r + chunk, :] = nn(normed_ref[r : r + chunk, :], w_ref[...]).astype(BF)
-
-
-def project(x, gain, cosine, sine, w, width):
-    rows, d = x.shape
-    parts = width // COLS
-    whole = lambda j: (0, 0)
-    return pl.pallas_call(
-        functools.partial(project_kernel, parts),
-        grid=(3 * parts,),
-        in_specs=[
-            pl.BlockSpec((rows, d), whole),
-            pl.BlockSpec((1, d), whole),
-            pl.BlockSpec((rows, COLS), whole),
-            pl.BlockSpec((rows, COLS), whole),
-            pl.BlockSpec((d, COLS), lambda j: (0, j)),
-        ],
-        out_specs=[
-            pl.BlockSpec((rows, COLS), lambda j: (0, j)),
-            pl.BlockSpec((rows, d), whole),
-        ],
-        out_shape=[
-            jax.ShapeDtypeStruct((rows, 3 * width), BF),
-            jax.ShapeDtypeStruct((rows, d), BF),
-        ],
-        compiler_params=settings(),
-        cost_estimate=cost(6 * rows * d * width, 2 * (2 * rows * d + 3 * d * width)),
-        name="project",
-    )(x, gain, cosine, sine, w)
 
 
 def mask_block(block, seg_rows, bias_ref, m, u):
@@ -558,10 +509,31 @@
 
 
 def turn_piece(turned_ref, left, start, row):
+    cols = pl.ds(pl.multiple_of(start + row, 256), 256)
+
     @pl.loop(0, left.shape[1] // 256)
     def _(i):
         span = pl.ds(pl.multiple_of(i * 256, 256), 256)
-        turned_ref[span, start + row : start + row + 256] = left[row : row + 256, span].T
+        turned_ref[span, cols] = left[row : row + 256, span].T
+
+
+def turn_kernel(first_ref, second_ref, out_ref):
+    start = 0
+    for left in (first_ref, second_ref):
+        for row in range(0, left.shape[0], 256):
+            turn_piece(out_ref, left, start, row)
+        start += left.shape[0]
+
+
+def turn_pair(first, second):
+    rows, d = first.shape
+    return pl.pallas_call(
+        turn_kernel,
+        out_shape=jax.ShapeDtypeStruct((d, 2 * rows), first.dtype),
+        compiler_params=pltpu.CompilerParams(vmem_limit_bytes=32 * 1024 * 1024),
+        cost_estimate=cost(0, 8 * rows * d),
+        name="turn_pair",
+    )(first, second)
 
 
 def emit_into(outs, per, block, value):
@@ -991,6 +963,247 @@
     )(norm_turned, gain, grads, w, attended, gm, x, block_own, block_send)
 
 
+class Gather:
+    def __init__(self, devices, rows, count):
+        self.devices, self.rows, self.count = devices, rows, count
+        self.stages = devices.bit_length() - 1
+        self.lags = [2] * (self.stages - 1) + [1]
+        self.starts = [sum(self.lags[:t]) for t in range(self.stages + 1)]
+        self.steps = count + self.starts[-1]
+
+    def scratch(self):
+        return [
+            pltpu.VMEM((self.count, self.devices, self.rows, COLS), BF),
+            pltpu.SemaphoreType.DMA((self.stages, self.count, 2)),
+            pltpu.SemaphoreType.DMA((self.count,)),
+        ]
+
+    def bind(self, refs):
+        self.held, self.sems, self.load_sems = refs
+        self.me, self.side = lax.axis_index("dp"), lax.axis_index("tensor")
+
+    def late(self, block):
+        return (block % 4) // 3 if self.stages >= 4 else 0 * block
+
+    def place(self, device, block):
+        late = self.late(block)
+        total = 0
+        for t in range(self.stages):
+            bit = (device // (1 << (self.stages - 1 - t))) % 2
+            if t in (1, 2) and self.stages >= 4:
+                total = total + bit * ((1 << t) * (1 - late) + (1 << (3 - t)) * late)
+            else:
+                total = total + bit * (1 << t)
+        return total
+
+    def partner_at(self, t):
+        weight = 1 << (self.stages - 1 - t)
+        return self.me + (1 - 2 * ((self.me // weight) % 2)) * weight
+
+    def partner(self, t, block):
+        if t not in (1, 2) or self.stages < 4:
+            return self.partner_at(t)
+        late = self.late(block)
+        return self.partner_at(t) * (1 - late) + self.partner_at(3 - t) * late
+
+    def barrier(self):
+        arrived = pltpu.get_barrier_semaphore()
+        for t in range(self.stages):
+            pl.semaphore_signal(
+                arrived, inc=1, device_id=(self.partner_at(t), self.side), device_id_type=MESH
+            )
+        pl.semaphore_signal(
+            arrived, inc=1, device_id=(self.me, 1 - self.side), device_id_type=MESH
+        )
+        pl.semaphore_wait(arrived, self.stages + 1)
+
+    def load(self, shard, column, block):
+        return pltpu.make_async_copy(
+            shard.at[:, pl.ds(column, COLS)],
+            self.held.at[block, self.place(self.me, block)],
+            self.load_sems.at[block],
+        )
+
+    def load_all(self, shards):
+        block = 0
+        for shard in shards:
+            for column in range(0, shard.shape[1], COLS):
+                self.load(shard, column, jnp.int32(block)).start()
+                block += 1
+
+    def copy(self, t, block):
+        size = 1 << t
+        first = self.place(self.me, block) // size * size
+        run = self.held.at[block, pl.ds(first, size)]
+        return remote(run, run, self.sems.at[t, block], (self.partner(t, block), self.side))
+
+    def advance(self, step, shards):
+        for t in range(self.stages, -1, -1):
+            block = step - self.starts[t]
+
+            @pl.when((block >= 0) & (block < self.count))
+            def _():
+                if t > 0:
+                    self.copy(t - 1, block).wait()
+                else:
+                    self.load(shards[0], 0, block).wait()
+                if t < self.stages:
+                    self.copy(t, block).start()
+
+
+def gather_project_kernel(gather, per, *refs):
+    shards, (tokens, cot, gain_ref, depths_ref) = refs[:4], refs[4:8]
+    w_hbm, qkv_ref, turned_ref, rows_hbm, cot_other, cos_ref, sin_ref, done_ref = refs[8:16]
+    w_ref, rows_ref, normed_ref, x_sems, row_sems, w_sems = refs[16:22]
+    gather.bind(refs[22:])
+    step = pl.program_id(0)
+    side = gather.side
+    across = (gather.me, 1 - side)
+    lead = gather.starts[-1]
+    others = lead + gather.count // 2 - 1
+    kinds = 3 * per
+
+    def token_copy():
+        return remote(tokens, rows_ref.at[side], x_sems.at[0], across)
+
+    def cot_copy():
+        return remote(cot, cot_other, x_sems.at[1], across)
+
+    def token_load():
+        return pltpu.make_async_copy(tokens, rows_ref.at[side], row_sems.at[0])
+
+    def rows_store():
+        return pltpu.make_async_copy(rows_ref, rows_hbm, row_sems.at[1])
+
+    def w_store(block):
+        cols = pl.ds(pl.multiple_of(block * COLS, COLS), COLS)
+        return pltpu.make_async_copy(w_ref.at[:, cols], w_hbm.at[:, cols], w_sems.at[block])
+
+    @pl.when(step == 0)
+    def _():
+        token_load().start()
+        gather.load_all(shards)
+        gather.barrier()
+        token_copy().start()
+        cot_copy().start()
+
+    gather.advance(step, shards)
+
+    @pl.when(step == 1)
+    def _():
+        token_load().wait()
+        norm_rows(rows_ref.at[side], gain_ref, normed_ref.at[side])
+        turn_tables(depths_ref, cos_ref, sin_ref)
+
+    for nth, row in enumerate(range(0, rows_ref.shape[1], 256)):
+
+        @pl.when(step == 2 + nth)
+        def _():
+            turn_piece(turned_ref, normed_ref.at[side], side * rows_ref.shape[1], row)
+
+        @pl.when(step == others + 1 + nth)
+        def _():
+            turn_piece(turned_ref, normed_ref.at[1 - side], (1 - side) * rows_ref.shape[1], row)
+
+    @pl.when(step == others)
+    def _():
+        token_copy().wait()
+        rows_store().start()
+        norm_rows(rows_ref.at[1 - side], gain_ref, normed_ref.at[1 - side])
+
+    @pl.when(step >= lead)
+    def _():
+        block = step - lead
+        cols = pl.ds(pl.multiple_of(block * COLS, COLS), COLS)
+        for device in range(gather.devices):
+            rows = slice(device * gather.rows, (device + 1) * gather.rows)
+            w_ref[rows, cols] = gather.held[block, gather.place(device, block)]
+        w_store(block).start()
+
+    @pl.loop(0, 3)
+    def _(task):
+        mine = jnp.where(task == 0, 1, 0)
+        half = side * mine + (1 - side) * (1 - mine)
+        block = (step - lead) * mine + (2 * (step - others) + task - 1) * (1 - mine)
+        cols = pl.ds(pl.multiple_of(block * COLS, COLS), COLS)
+        chunk = 256
+
+        @pl.when((block >= 0) & (block < 2 * per))
+        def _():
+            scale = jnp.where(block < per, 1.0 / math.sqrt(HD), 1.0).astype(BF)
+            for r in range(0, qkv_ref.shape[1], chunk):
+                span = slice(r, r + chunk)
+                pre = nn(normed_ref[half, span, :], w_ref[:, cols])
+                cosine = jnp.concatenate([cos_ref[half, span, :]] * (COLS // LANES), axis=1)
+                sine = jnp.concatenate([sin_ref[half, span, :]] * (COLS // LANES), axis=1)
+                turned = turn(pre, cosine, sine)
+                qkv_ref[half, span, cols] = turned.astype(BF) * scale
+
+        @pl.when((block >= 2 * per) & (block < kinds))
+        def _():
+            for r in range(0, qkv_ref.shape[1], chunk):
+                span = slice(r, r + chunk)
+                qkv_ref[half, span, cols] = nn(normed_ref[half, span, :], w_ref[:, cols]).astype(BF)
+
+    @pl.when(step == gather.steps - 1)
+    def _():
+        done_ref[...] = gain_ref[...]
+        cot_copy().wait()
+        rows_store().wait()
+
+        @pl.loop(0, gather.count)
+        def _(block):
+            w_store(block).wait()
+
+
+def gather_project(devices, shards, tokens, cot, gain, depths):
+    half, d = tokens.shape
+    rows, width = shards[0].shape
+    total = len(shards) * width
+    per = width // COLS
+    gather = Gather(devices, rows, total // COLS)
+    count = gather.count
+    assert rows * devices == d and count // 2 - 1 + (3 * per + 1) // 2 <= count
+    left_there = pl.BlockSpec(memory_space=pl.ANY)
+    return pl.pallas_call(
+        functools.partial(gather_project_kernel, gather, per),
+        grid=(gather.steps,),
+        in_specs=[left_there] * 6 + [resident((1, d)), pl.BlockSpec(memory_space=pltpu.SMEM)],
+        out_specs=[
+            left_there,
+            resident((2, half, 3 * width)),
+            resident((d, 2 * half)),
+            left_there,
+            left_there,
+            resident((2, half, LANES)),
+            resident((2, half, LANES)),
+            resident((1, d)),
+        ],
+        out_shape=[
+            jax.ShapeDtypeStruct((d, total), BF),
+            jax.ShapeDtypeStruct((2, half, 3 * width), BF),
+            jax.ShapeDtypeStruct((d, 2 * half), BF),
+            jax.ShapeDtypeStruct((2, half, d), BF),
+            jax.ShapeDtypeStruct((half, d), BF),
+            jax.ShapeDtypeStruct((2, half, LANES), F32),
+            jax.ShapeDtypeStruct((2, half, LANES), F32),
+            jax.ShapeDtypeStruct((1, d), F32),
+        ],
+        scratch_shapes=[
+            pltpu.VMEM((d, total), BF),
+            pltpu.VMEM((2, half, d), BF),
+            pltpu.VMEM((2, half, d), BF),
+            pltpu.SemaphoreType.DMA((2, 2)),
+            pltpu.SemaphoreType.DMA((2,)),
+            pltpu.SemaphoreType.DMA((count,)),
+        ]
+        + gather.scratch(),
+        compiler_params=remote_settings(2),
+        cost_estimate=cost(12 * half * d * width, 2 * d * total),
+        name="gather_project",
+    )(*shards, tokens, cot, gain, depths)
+
+
 def swap(x):
     return lax.ppermute(x, "tensor", [(0, 1), (1, 0)])
 
@@ -1018,11 +1231,6 @@
     own_start = mine * half
     other_start = (1 - mine) * half
 
-    def place(own, other):
-        full = jnp.zeros((length, own.shape[1]), own.dtype)
-        full = lax.dynamic_update_slice(full, own, (own_start, 0))
-        return lax.dynamic_update_slice(full, other, (other_start, 0))
-
     def own_rows(full):
         return lax.dynamic_slice_in_dim(full, own_start, half, 0)
 
@@ -1035,30 +1243,31 @@
     attn_row = attn_gain[None, :]
     ffn_row = ffn_gain[None, :]
 
-    first = gather(
-        jnp.concatenate([query_weight, key_weight, value_weight, output_weight.T], axis=1)
-    )
-    second = gather(jnp.concatenate([gate_weight, up_weight, down_weight.T], axis=1))
     devices = lax.axis_size("dp")
-
-    bias, positions = tree_tables(parents[0], seg_rows)
-    cosine, sine = turn_tables(positions, COLS)
-    cot_other = swap(cotangent)
-    rows_all, cot_other, cot_turned = lax.optimization_barrier(
-        (
-            place(tokens, swap(tokens)),
-            cot_other,
-            jnp.concatenate([cotangent.T, cot_other.T], axis=1),
-        )
-    )
-
-    qkv, normed_one = project(rows_all, attn_row, cosine, sine, first, width)
+    bias, depths = tree_tables(parents[0], seg_rows)
+
+    first, qkv, norm_turned, rows_all, cot_other, cosine, sine, attn_row = gather_project(
+        devices,
+        (query_weight, key_weight, value_weight, output_weight.T),
+        tokens,
+        cotangent,
+        attn_row,
+        depths,
+    )
+    second_shard, attn_row = lax.optimization_barrier(
+        (jnp.concatenate([gate_weight, up_weight, down_weight.T], axis=1), attn_row)
+    )
+    second = gather(second_shard)
+    qkv = qkv.reshape(length, 3 * width)
+    rows_all = rows_all.reshape(length, d)
+    cosine, sine = cosine.reshape(length, LANES), sine.reshape(length, LANES)
+
     attended, lse = attend(qkv, bias, width, seg_rows)
     out_turned = first[:, 3 * width :]
     send = nt(other_rows(attended), out_turned).astype(BF)
-    send, norm_source = lax.optimization_barrier((send, normed_one))
+    send, cot_source = lax.optimization_barrier((send, cot_other))
     received = swap(send)
-    received, norm_turned = lax.optimization_barrier((received, norm_source.T))
+    received, cot_turned = lax.optimization_barrier((received, turn_pair(cotangent, cot_source)))
     middle = (
         tokens.astype(F32) + nt(own_rows(attended), out_turned) + received.astype(F32)
     ).astype(BF)
@@ -1075,7 +1284,7 @@
 
     grad_attended = nn(grad_middle, out_turned).astype(BF)
     grads = attend_back(
-        qkv, attended, grad_attended, lse, bias, cosine[:, :LANES], sine[:, :LANES], seg_rows
+        qkv, attended, grad_attended, lse, bias, cosine, sine, seg_rows
     )
     (
         query_grad, key_grad, value_grad, output_grad, attn_gain_grad, token_grad, block_out,

time: 519 us -> 498 us (0.960)
  Pallas kernels: 312 us -> 378 us
  waiting for transfers between devices: 126 us -> 62.6 us
  local copies, waits for them, and re-layouts: 32.3 us -> 18.1 us
    pallas_call x1 -> x2, Pallas kernels: 15.8 us -> 81.2 us  [the longest x1 79.1 us: gather_project(): pl.pallas_call(functools.partial(gather_project_kernel, gather, per), gri...]
    ppermute x5 -> x3, waiting for transfers between devices: 120 us -> 62.6 us  [swap(): return lax.ppermute(x, 'tensor', [(0, 1), (1, 0)])]
    another operation x4 -> x0, local copies, waits for them, and re-layouts: 7.44 us -> none  [the longest x2 3.75 us: turn_tables(): jnp.tile(jnp.concatenate([-sine, sine], axis=1), (1, heads))]
    all_gather x2 -> x1, waiting for transfers between devices: 5.9 us -> 0.01 us  [gather(): return lax.all_gather(shard, 'dp', axis=0, tiled=True)]
    unnamed x57 -> x46, local copies, waits for them, and re-layouts: 15.9 us -> 14.3 us
  transfers between devices with their start and end apart: 8 -> 5, of which waited for: 5 -> 3; matrix products, arithmetic and copies ran while one was open for 8% -> 4% of each run, Pallas kernels for 32% -> 30%
where the time goes in v6:
time: 498 us
  Pallas kernels  378 us (76%)
  waiting for transfers between devices  62.6 us (13%)
  local copies, waits for them, and re-layouts  18.1 us (4%)
  between operations  14.3 us (3%)
  matrix products  13.1 us (3%)
  other arithmetic  8.99 us (2%)
    pallas_call x1, Pallas kernels, ffn_scatter(): pl.pallas_call(functools.partial(ffn_scatter_kernel, scatter, per), grid=...  99.3 us
    pallas_call x1, Pallas kernels, attention_scatter(): pl.pallas_call(functools.partial(attention_scatter_kernel, scatter, per),...  92.9 us
    pallas_call x1, Pallas kernels, gather_project(): pl.pallas_call(functools.partial(gather_project_kernel, gather, per), gri...  79.1 us
    ppermute x3, waiting for transfers between devices, swap(): return lax.ppermute(x, 'tensor', [(0, 1), (1, 0)])  62.6 us
    pallas_call x1, Pallas kernels, ffn(): pl.pallas_call(ffn_kernel, grid=(2, steps), in_specs=[resident((rows, d))...  49.5 us
    pallas_call x1, Pallas kernels, attend_back(): pl.pallas_call(functools.partial(attend_back_kernel, block, seg_rows), gr...  33.8 us
    pallas_call x1, Pallas kernels, attend(): pl.pallas_call(functools.partial(attend_kernel, block, seg_rows), grid=(g...  21.5 us
    unnamed x46, local copies, waits for them, and re-layouts  14.3 us
  transfers between devices with their start and end apart: 5, of which 3 were waited for; matrix products, arithmetic and copies ran while one was open for 4% of the time, Pallas kernels for 30%

profile of v6, /device:TPU:0, one launch (start us, length us, event | category | flops | bytes accessed | tf_op | source)
XLA Modules:
  0.0 497.6 jit_solution(13463553457542495159)
XLA Ops:
  7.2 1.3 broadcast_in_dim.12.refs_6_
  10.7 2.3 pad_maximum_fusion
  13.0 79.1 %gather_project.1 = (bf16[1536,3072]{1,0:T(8,128)(2,1)}, bf16[2,512,2304]{2,1,0:T(8,128)(2,1)}, bf16[1536,1024]{1,0:T(8,128)(2,1)}, bf16[2,512,1536]{2,1,0:T(8,1...) custom-call(bf16[96,768]{1,0:T(8,128)(2,1)} %refs_0_.1, ...), custom_call_target="tpu_custom_call" | custom-call | flops 7247757312 | bytes 9437184 | tf_op jit(solution)/shard_map/gather_project/pallas_call | solution.py:1168
  92.6 21.5 %attend.1 = (bf16[1024,768]{1,0:T(8,128)(2,1)S(1)}, f32[6,2,1024]{2,1,0:T(2,128)S(1)}) custom-call(bf16[1024,2304]{1,0:T(8,128)(2,1)} %bitcast.28, bf16[1024,2304]{1,0:T(8,128)(2,1)} %bitcast.29, bf16[1024,2304]{1,0:T(8,128)(2,1)} %bitcast.30, f32[8,1024]{1,0:T(8,128)S(1)} %broadcast_bitcast_fusion.bias_ref), custom_call_target="tpu_custom_call" | custom-call | flops 6442450944 | bytes 6291456 | tf_op jit(solution)/shard_map/attend/pallas_call | solution.py:150
  114.1 4.8 convolution_convert_fusion
  119.5 2.2 turn_pair.1.refs_0_
  121.7 1.6 copy-done
  123.3 3.9 convolution_add_fusion
  127.2 27.4 %collective-permute-done = bf16[512,1536]{1,0:T(8,128)(2,1)} collective-permute-done((bf16[512,1536]{1,0:T(8,128)(2,1)}, bf16[512,1536]{1,0:T(8,128)(2,1)}, u32[]{:S(2)}, u32[]{:S(2)}) %collective-permute-start) | collective-permute-done | bytes 1572896 | tf_op jit(solution)/shard_map/ppermute | solution.py:1208
  154.6 2.1 add_convert_fusion.x_own.refs_8_
  156.7 1.1 copy-done.8
  158.9 33.2 %collective-permute-done.1.x_other = bf16[512,1536]{1,0:T(8,128)(2,1)S(1)} collective-permute-done((bf16[512,1536]{1,0:T(8,128)(2,1)S(1)}, bf16[512,1536]{1,0:T(8,128)(2,1)S(1)}, u32[]{:S(2)}, u32[]{:S(2)}) %collective-permute-start.1) | collective-permute-done | bytes 1572896 | tf_op jit(solution)/shard_map/ppermute | solution.py:1208
  192.1 1.2 copy-done.17
  193.3 49.5 %ffn.1 = (bf16[2,3,512,2048]{3,2,1,0:T(8,128)(2,1)}, bf16[2,512,1536]{2,1,0:T(8,128)(2,1)}, bf16[2,512,1536]{2,1,0:T(8,128)(2,1)}, f32[8,1536]{1,0:T(8,128)}) custom-call(bf16[512,1536]{1,0:T(8,128)(2,1)} %copy-done.8, bf16[512,1536]{1,0:T(8,128)(2,1)} %copy-done.17, bf16[512,1536]{1,0:T(8,128)(2,1)} %refs_7_.1, ...), custom_call_target="tpu_custom_call" | custom-call | flops 32212254720 | bytes 62914560 | tf_op jit(solution)/shard_map/ffn/pallas_call | solution.py:347
  242.8 99.3 %ffn_scatter.1 = (f32[96,2048]{1,0:T(8,128)}, f32[96,2048]{1,0:T(8,128)}, f32[96,256]{1,0:T(8,128)}, bf16[1536,2048]{1,0:T(8,128)(2,1)}, bf16[2,512,1536]{2,1,0:...) custom-call(bf16[1536,1024]{1,0:T(8,128)(2,1)} %copy-done, ...), custom_call_target="tpu_custom_call" | custom-call | flops 25769803776 | bytes 15728640 | tf_op jit(solution)/shard_map/ffn_scatter/pallas_call | solution.py:732
  343.0 1.1 copy-done.18
  344.1 4.4 fusion.4.do_ref
  348.5 33.8 %attend_back.1.refs_2_ = bf16[3,1024,768]{2,1,0:T(8,128)(2,1)} custom-call(bf16[1024,2304]{1,0:T(8,128)(2,1)} %bitcast.31, bf16[1024,2304]{1,0:T(8,128)(2,1)} %bitcast.32, bf16[1024,2304]{1,0:T(8,128)(2,1)} %bitcast.33, bf16[1024,768]{1,0:T(8,128)(2,1)S(1)} %copy-done.6, bf16[1024,768]{1,0:T(8,128)(2,1)S(1)} %fusion.4.do_ref, ...), custom_call_target="tpu_custom_call" | custom-call | flops 16106127360 | bytes 12582912 | tf_op jit(solution)/shard_map/attend_back/pallas_call | solution.py:238
  382.3 92.9 %attention_scatter.1 = (f32[96,768]{1,0:T(8,128)}, f32[96,768]{1,0:T(8,128)}, f32[96,768]{1,0:T(8,128)}, f32[96,768]{1,0:T(8,128)}, f32[96,256]{1,0:T(8,128)}, /...) custom-call(bf16[1536,1024]{1,0:T(8,128)(2,1)} %get-tuple-element.45.refs_0_, f32[1,1536]{1,0:T(1,128)} %get-tuple-element.47.refs_1_, ...), custom_call_target="tpu_custom_call" | custom-call | flops 16911433728 | bytes 31457280 | tf_op jit(solution)/shard_map/attention_scatter/pallas_call | solution.py:928
  475.2 0.9 slice.11
  477.8 2.1 collective-permute-done.2
  480.4 1.9 convert_element_type.80
  482.3 2.7 copy.51
  485.0 1.1 copy.52
  (76 shorter events, 12.0 us)
Async XLA Ops:
  7.2 184.9 %all-gather.2.cloned.1.call-start = ((), (), s32[]{:S(2)}) async-start(), calls=%async_computation.1 | async-start | bytes 20054016 | tf_op jit(solution)/shard_map/all_gather | solution.py:1241
  92.1 388.3 %reduce-scatter.2.cloned.1.call-start = ((), (), s32[]{:S(2)}) async-start(), calls=%async_computation.2 | async-start | bytes 6684672 | tf_op jit(solution)/shard_map/reduce_scatter | solution.py:1282
  114.1 4.9 copy-start.5
  114.1 5.4 %copy-start.1 = (bf16[512,1536]{1,0:T(8,128)(2,1)S(1)}, bf16[512,1536]{1,0:T(8,128)(2,1)}, u32[]{:S(2)}) copy-start(bf16[512,1536]{1,0:T(8,128)(2,1)} %refs_7_.1) | copy-start | bytes 4718596
  114.1 5.4 %copy-start.2 = (bf16[512,1536]{1,0:T(8,128)(2,1)S(1)}, bf16[512,1536]{1,0:T(8,128)(2,1)}, u32[]{:S(2)}) copy-start(bf16[512,1536]{1,0:T(8,128)(2,1)} %get-tuple-element.53.second_ref.cot_other) | copy-start | bytes 4718596
  119.0 35.6 %collective-permute-start = (bf16[512,1536]{1,0:T(8,128)(2,1)}, bf16[512,1536]{1,0:T(8,128)(2,1)}, u32[]{:S(2)}, u32[]{:S(2)}) collective-permute-start(bf16[512,1536]{1,0:T(8,128)(2,1)} %convolution_convert_fusion), channel_id=1, source_target_pairs={{0,1},{1,0},{2,3},{3,2},{4,5},{5,4},{6,7},{7,6},{8,9},{9,8},{10,11... | collective-permute-start | bytes 4718600 | tf_op jit(solution)/shard_map/ppermute | solution.py:1208
  121.7 1.6 copy-start
  127.2 31.1 %copy-start.16 = (f32[1536]{0:T(1024)S(1)}, f32[1536]{0:T(1024)}, u32[]{:S(2)}) copy-start(f32[1536]{0:T(1024)} %param.15) | copy-start | bytes 18436
  156.7 1.1 copy-start.8
  157.8 34.3 %collective-permute-start.1 = (bf16[512,1536]{1,0:T(8,128)(2,1)S(1)}, bf16[512,1536]{1,0:T(8,128)(2,1)S(1)}, u32[]{:S(2)}, u32[]{:S(2)}) collective-permute-start(bf16[512,1536]{1,0:T(8,128)(2,1)S(1)} %add_convert_fusion.x_own.refs_8_), channel_id=1, source_target_pairs={{0,1},{1,0},{2,3},{3,2},{4,5},{5,4},{6,7},{7,6},{8,9},{9,8},{10,11... | collective-permute-start | bytes 4718600 | tf_op jit(solution)/shard_map/ppermute | solution.py:1208
  192.1 1.2 copy-start.17
  342.1 0.9 copy-start.15
  342.1 1.9 copy-start.18
  344.1 4.4 copy-start.3
  344.1 4.4 copy-start.4
  344.1 4.4 copy-start.6
  475.2 9.8 %copy-start.7 = (bf16[512,1536]{1,0:T(8,128)(2,1)S(1)}, bf16[512,1536]{1,0:T(8,128)(2,1)}, u32[]{:S(2)}) copy-start(bf16[512,1536]{1,0:T(8,128)(2,1)} %get-tuple-element.95) | copy-start | bytes 4718596
  476.3 3.6 collective-permute-start.2
  485.0 1.2 copy-start.14
  485.0 1.9 copy-start.13
  485.0 2.6 copy-start.12
  485.0 3.3 copy-start.11
  485.0 4.0 copy-start.10
  486.2 3.8 copy-start.9
Sparse Core Ops, SparseCore 0:
  92.2 98.2 all-gather.1
  342.3 98.9 reduce-scatter.1

commit v7 on v6

--- a/solution.py
+++ b/solution.py
@@ -293,19 +293,31 @@
     normed_ref,
     part_ref,
     gain_part_ref,
+    got_hbm,
     cot_ref,
     acc_ref,
+    part_send,
+    part_sems,
 ):
     h, j = pl.program_id(0), pl.program_id(1)
     chunk = 256
+    across = (lax.axis_index("dp"), 1 - lax.axis_index("tensor"))
+    quarter = part_send.shape[0] // QUARTERS
+
+    def part_copy(r):
+        span = pl.ds(r * quarter, quarter)
+        return remote(part_send.at[span], got_hbm.at[span], part_sems.at[r], across)
 
     @pl.when((h == 0) & (j == 0))
     def _():
+        arrived = pltpu.get_barrier_semaphore()
+        pl.semaphore_signal(arrived, inc=1, device_id=across, device_id_type=MESH)
+        pl.semaphore_wait(arrived, 1)
         gain_part_ref[...] = jnp.zeros_like(gain_part_ref)
 
-    for side, (x_ref, c_ref) in enumerate(((x_own, cot_own), (x_other, cot_other))):
-
-        @pl.when((h == side) & (j == 0))
+    for turn_at, (x_ref, c_ref) in enumerate(((x_other, cot_other), (x_own, cot_own))):
+
+        @pl.when((h == turn_at) & (j == 0))
         def _():
             norm_rows(x_ref, gain_ref, normed_ref)
             cot_ref[...] = c_ref[...]
@@ -328,11 +340,18 @@
         grads_ref[1, span, :] = grad_up
         acc_ref[span, :] += nt(grad_gate, wg_ref[...]) + nt(grad_up, wu_ref[...])
 
-    for side, x_ref in enumerate((x_own, x_other)):
-
-        @pl.when((h == side) & (j == pl.num_programs(1) - 1))
+    for turn_at, x_ref in enumerate((x_other, x_own)):
+
+        @pl.when((h == turn_at) & (j == pl.num_programs(1) - 1))
         def _():
             back_rows(acc_ref, x_ref, gain_ref, gain_part_ref, part_ref)
+            if turn_at == 0:
+                part_send[...] = part_ref[...]
+                for r in range(EARLY):
+                    part_copy(r).start()
+            else:
+                for r in range(EARLY):
+                    part_copy(r).wait()
 
 
 def resident(shape):
@@ -343,7 +362,7 @@
 def ffn(xs, cots, gain, w, hidden_width, cols=512):
     rows, d = xs[0].shape
     steps = hidden_width // cols
-    per_half = lambda h, j: (h, 0, 0)
+    per_half = lambda h, j: (1 - h, 0, 0)
     return pl.pallas_call(
         ffn_kernel,
         grid=(2, steps),
@@ -355,21 +374,26 @@
             pl.BlockSpec((d, cols), lambda h, j: (0, 2 * steps + j)),
         ],
         out_specs=[
-            pl.BlockSpec((None, 3, rows, cols), lambda h, j: (h, 0, 0, j)),
+            pl.BlockSpec((None, 3, rows, cols), lambda h, j: (1 - h, 0, 0, j)),
             pl.BlockSpec((None, rows, d), per_half),
             pl.BlockSpec((None, rows, d), per_half),
             pl.BlockSpec((8, d), lambda h, j: (0, 0)),
+            pl.BlockSpec(memory_space=pl.ANY),
         ],
         out_shape=[
             jax.ShapeDtypeStruct((2, 3, rows, hidden_width), BF),
             jax.ShapeDtypeStruct((2, rows, d), BF),
             jax.ShapeDtypeStruct((2, rows, d), BF),
             jax.ShapeDtypeStruct((8, d), F32),
-        ],
-        scratch_shapes=[pltpu.VMEM((rows, d), BF), pltpu.VMEM((rows, d), F32)],
-        compiler_params=pltpu.CompilerParams(
-            dimension_semantics=("arbitrary", "arbitrary"), vmem_limit_bytes=56 * 1024 * 1024
-        ),
+            jax.ShapeDtypeStruct((rows, d), BF),
+        ],
+        scratch_shapes=[
+            pltpu.VMEM((rows, d), BF),
+            pltpu.VMEM((rows, d), F32),
+            pltpu.VMEM((rows, d), BF),
+            pltpu.SemaphoreType.DMA((EARLY, 2)),
+        ],
+        compiler_params=remote_settings(3, axes=2),
         cost_estimate=cost(
             20 * rows * d * hidden_width,
             12 * d * hidden_width + 16 * rows * d + 12 * rows * hidden_width,
@@ -381,13 +405,16 @@
 
 MESH = pl.DeviceIdType.MESH
 QUARTERS = 4
+EARLY = 3
+UP_SENT = 8
+GAIN_ROWS = 16
 
 
 class Scatter:
     def __init__(self, devices, rows, count):
         self.devices, self.rows, self.count = devices, rows, count
         self.stages = devices.bit_length() - 1
-        self.lags = [min(s + 1, 2) for s in range(self.stages)]
+        self.lags = [1] + [3] * (self.stages - 1)
         self.slots = [2 * lag for lag in self.lags]
         if self.stages >= 3:
             self.slots[1] = self.slots[2] = 8
@@ -438,14 +465,18 @@
         )
         pl.semaphore_wait(arrived, self.stages + 1)
 
-    def copy(self, s, block):
+    def copy(self, s, block, gain=False):
         slot = block % self.slots[s]
         bit, partner = self.turned(s, block)
+        src, dst = self.held[s].at[slot, 1 - bit], self.got[s].at[slot]
+        if gain:
+            src, dst = src.at[:, pl.ds(0, GAIN_ROWS)], dst.at[:, pl.ds(0, GAIN_ROWS)]
+        sems = self.sent_sem[s].at[slot], self.got_sem[s].at[slot]
         return pltpu.make_async_remote_copy(
-            src_ref=self.held[s].at[slot, 1 - bit],
-            dst_ref=self.got[s].at[slot],
-            send_sem=self.sent_sem[s].at[slot],
-            recv_sem=self.got_sem[s].at[slot],
+            src_ref=src,
+            dst_ref=dst,
+            send_sem=sems[0],
+            recv_sem=sems[1],
             device_id=(partner, self.side),
             device_id_type=MESH,
         )
@@ -453,30 +484,37 @@
     def advance(self, step, emit):
         for s in range(self.stages, 0, -1):
             block = step - self.starts[s]
-
-            @pl.when((block >= 0) & (block < self.count))
-            def _():
-                slot = block % self.slots[s - 1]
-                self.copy(s - 1, block).wait()
-                keep, _ = self.turned(s - 1, block)
-                held, got = self.held[s - 1], self.got[s - 1]
-                if s == self.stages:
-                    emit(block, held[slot, keep, 0].astype(F32) + got[slot, 0].astype(F32))
-                else:
-                    later = block % self.slots[s]
-                    late = self.late(block)
-
-                    def add(k, carry):
-                        total = held[slot, keep, k] + got[slot, k]
-                        bit, rest = k % 2, k // 2
-                        if s == 1 and self.stages >= 3:
-                            bit = bit * (1 - late) + (k // 2) % 2 * late
-                            rest = rest * (1 - late) + (k // 4 * 2 + k % 2) * late
-                        self.held[s][later, bit, rest] = total
-                        return carry
-
-                    lax.fori_loop(0, self.devices >> s, add, 0)
-                    self.copy(s, block).start()
+            last = self.count - 1
+            for gain in (False, True):
+
+                @pl.when((block == last) if gain else (block >= 0) & (block < last))
+                def _():
+                    self.receive(s, block, gain, emit)
+
+    def receive(self, s, block, gain, emit):
+        slot = block % self.slots[s - 1]
+        self.copy(s - 1, block, gain).wait()
+        keep, _ = self.turned(s - 1, block)
+        held, got = self.held[s - 1], self.got[s - 1]
+        rows = slice(0, GAIN_ROWS if gain else self.rows)
+        if s == self.stages:
+            total = held[slot, keep, 0, rows].astype(F32) + got[slot, 0, rows].astype(F32)
+            emit(block, total, gain)
+            return
+        later = block % self.slots[s]
+        late = self.late(block)
+
+        def add(k, carry):
+            total = held[slot, keep, k, rows] + got[slot, k, rows]
+            bit, rest = k % 2, k // 2
+            if s == 1 and self.stages >= 3:
+                bit = bit * (1 - late) + (k // 2) % 2 * late
+                rest = rest * (1 - late) + (k // 4 * 2 + k % 2) * late
+            self.held[s][later, bit, rest, rows] = total
+            return carry
+
+        lax.fori_loop(0, self.devices >> s, add, 0)
+        self.copy(s, block, gain).start()
 
     def multiply(self, block, turned_ref, rights):
         slot = block % self.slots[0]
@@ -500,12 +538,12 @@
 
     def put_gain(self, block, row):
         slot = block % self.slots[0]
-        column = jnp.broadcast_to(row, (LANES, row.shape[1])).T.astype(BF)
+        empty = jnp.zeros((1, COLS - self.rows), F32)
         for k in range(self.devices):
-            rows = column[k * self.rows : (k + 1) * self.rows, :]
-            wide = jnp.concatenate([rows] * (COLS // LANES), axis=1)
-            self.held[0][slot, k % 2, k // 2] = wide
-        self.copy(0, block).start()
+            piece = jnp.concatenate([row[:, k * self.rows : (k + 1) * self.rows], empty], axis=1)
+            piece = jnp.broadcast_to(piece, (GAIN_ROWS, COLS)).astype(BF)
+            self.held[0][slot, k % 2, k // 2, :GAIN_ROWS] = piece
+        self.copy(0, block, True).start()
 
 
 def turn_piece(turned_ref, left, start, row):
@@ -536,25 +574,33 @@
     )(first, second)
 
 
-def emit_into(outs, per, block, value):
-    for kind, out in enumerate(outs):
-
-        @pl.when((block >= kind * per) & (block < (kind + 1) * per))
+def emit_into(outs, counts, block, value, gain):
+    if gain:
+        outs[-1][...] = value
+        return
+    first = 0
+    for out, count in zip(outs, counts):
+
+        @pl.when((block >= first) & (block < first + count))
         def _():
             out[...] = value
 
-
-def emit_specs(scatter, kinds, per, width):
-    lead = scatter.starts[-1]
+        first += count
+
+
+def emit_specs(scatter, counts):
+    first = scatter.starts[-1]
     specs, shapes = [], []
-    for kind in range(kinds + 1):
-        most, size = (per - 1, width) if kind < kinds else (0, COLS)
-
-        def where(j, first=lead + kind * per, most=most):
+    for count in counts:
+
+        def where(j, first=first, most=count - 1):
             return (0, jnp.clip(j - first, 0, most))
 
         specs.append(pl.BlockSpec((scatter.rows, COLS), where))
-        shapes.append(jax.ShapeDtypeStruct((scatter.rows, size), F32))
+        shapes.append(jax.ShapeDtypeStruct((scatter.rows, count * COLS), F32))
+        first += count
+    specs.append(pl.BlockSpec((GAIN_ROWS, COLS), lambda j: (0, 0)))
+    shapes.append(jax.ShapeDtypeStruct((GAIN_ROWS, COLS), F32))
     return specs, shapes
 
 
@@ -569,32 +615,36 @@
     )
 
 
-def ffn_scatter_kernel(scatter, per, *refs):
+def ffn_scatter_kernel(scatter, per, sent, unsent, *refs):
     (
-        cot_turned, norm_own, norm_other, right_own, right_other, gate_own, gate_other,
-        cot_hbm, middle_hbm, parts_hbm, gain_ref, wd_ref,
-    ) = refs[:12]
-    outs = refs[12:15]
-    gate_ref, gm_ref, block_own, block_send = refs[15:19]
+        cot_turned, norm_own, norm_other, right_own, right_other, whole_own, whole_other,
+        cot_hbm, middle_hbm, parts_hbm, got_hbm, gain_ref, wd_ref, wo_ref,
+    ) = refs[:14]
+    outs = refs[14:17]
+    whole_ref, gm_ref, grad_attended, block_out_ref = refs[17:21]
     (
-        norm_turned, cot_own, middle_own, part_own, got_part, gm_own, gain_got, acc_other,
-        gain_sems, part_sems, gm_sems, local_sems,
-    ) = refs[19:31]
-    scatter.bind(refs[31:])
+        norm_turned, cot_own, middle_own, part_own, got_part, gm_own, gm_got, gain_got, acc_own,
+        acc_other, block_send, block_got, gain_sems, part_sems, gm_sems, block_sems, local_sems,
+    ) = refs[21:38]
+    scatter.bind(refs[38:])
     step = pl.program_id(0)
     side = scatter.side
     across = (scatter.me, 1 - side)
     half = part_own.shape[0]
     quarter = half // QUARTERS
     row_chunk = 128
-
-    def part_copy(r):
-        span = pl.ds(r * quarter, quarter)
-        return remote(parts_hbm.at[1, span], got_part.at[span], part_sems.at[r], across)
+    early = pl.ds(0, EARLY * quarter)
+    rest = pl.ds(EARLY * quarter, half - EARLY * quarter)
+
+    def part_copy():
+        return remote(parts_hbm.at[1, rest], got_part.at[rest], part_sems, across)
 
     def gm_copy(r):
         span = pl.ds(r * quarter, quarter)
-        return remote(gm_own.at[span], gm_ref.at[side, span], gm_sems.at[r], across)
+        return remote(gm_own.at[span], gm_got.at[span], gm_sems.at[r], across)
+
+    def block_copy():
+        return remote(block_send, block_got, block_sems, across)
 
     def gain_copy():
         return remote(gain_ref, gain_got, gain_sems, across)
@@ -603,21 +653,23 @@
         pltpu.make_async_copy(cot_hbm, cot_own, local_sems.at[0]),
         pltpu.make_async_copy(parts_hbm.at[0], part_own, local_sems.at[1]),
         pltpu.make_async_copy(middle_hbm, middle_own, local_sems.at[2]),
+        pltpu.make_async_copy(got_hbm.at[early], got_part.at[early], local_sems.at[3]),
     ]
 
-    def gm_keep():
-        return pltpu.make_async_copy(gm_own, gm_ref.at[side], local_sems.at[3])
+    keeps = [
+        pltpu.make_async_copy(gm_own, gm_ref.at[side], local_sems.at[4]),
+        pltpu.make_async_copy(gm_got, gm_ref.at[1 - side], local_sems.at[5]),
+    ]
 
     @pl.when(step == 0)
     def _():
         for load in loads:
             load.start()
         scatter.barrier()
-        for r in range(QUARTERS):
-            part_copy(r).start()
+        part_copy().start()
         gain_copy().start()
 
-    scatter.advance(step, functools.partial(emit_into, outs, per))
+    scatter.advance(step, functools.partial(emit_into, outs, (per, sent - per)))
 
     @pl.when(step < per)
     def _():
@@ -625,14 +677,23 @@
 
         @pl.when(step == 0)
         def _():
-            block_own[...] = jnp.zeros_like(block_own)
+            acc_own[...] = jnp.zeros_like(acc_own)
             acc_other[...] = jnp.zeros_like(acc_other)
 
         @pl.loop(0, half // 256)
         def _(i):
             span = pl.ds(i * 256, 256)
-            block_own[span, :] += nt(right_own[span, :], wd_ref[...])
+            acc_own[span, :] += nt(right_own[span, :], wd_ref[...])
             acc_other[span, :] += nt(right_other[span, :], wd_ref[...])
+
+    @pl.when(step == per)
+    def _():
+        @pl.loop(0, half // row_chunk)
+        def _(i):
+            span = pl.ds(i * row_chunk, row_chunk)
+            block_send[span, :] = acc_other[span, :].astype(BF)
+
+        block_copy().start()
 
     pieces = [(norm_own, 0, r) for r in range(0, half, 256)]
     pieces += [(norm_other, half, r) for r in range(0, half, 256)]
@@ -642,30 +703,34 @@
         def _():
             turn_piece(norm_turned, left, start, row)
 
-    @pl.when((step >= per) & (step < 2 * per))
+    @pl.when((step >= per) & (step < sent))
     def _():
         scatter.multiply(step, norm_turned, (right_own, right_other))
-        rows = gate_ref.shape[0] // 4
+
+    @pl.when(step == sent)
+    def _():
+        gain_copy().wait()
+        scatter.put_gain(step, gain_ref[0:1, :] + gain_got[0:1, :])
+
+    @pl.when((step >= per) & (step < per + unsent))
+    def _():
+        rows = whole_ref.shape[0] // 4
 
         @pl.loop(0, 4)
         def _(i):
             span = pl.ds(i * rows, rows)
-            total = nn(norm_turned[span, :half], gate_own[...])
-            gate_ref[span, :] = (total + nn(norm_turned[span, half:], gate_other[...])).astype(BF)
-
-    @pl.when(step == 2 * per)
-    def _():
-        gain_copy().wait()
-        scatter.put_gain(step, gain_ref[0:1, :] + gain_got[0:1, :])
+            total = nn(norm_turned[span, :half], whole_own[...])
+            whole_ref[span, :] = (total + nn(norm_turned[span, half:], whole_other[...])).astype(BF)
 
     for r in range(QUARTERS):
 
-        @pl.when(step == 3 + 2 * r)
+        @pl.when(step == 1 + r + (1 if r >= EARLY else 0))
         def _():
             if r == 0:
                 for load in loads:
                     load.wait()
-            part_copy(r).wait()
+            if r == EARLY:
+                part_copy().wait()
 
             @pl.loop(r * quarter // row_chunk, (r + 1) * quarter // row_chunk)
             def _(i):
@@ -674,63 +739,87 @@
                 gm_own[span, :] = (total + got_part[span, :].astype(F32)).astype(BF)
 
             gm_copy(r).start()
-            if r == QUARTERS - 1:
-                gm_keep().start()
-
-    @pl.when(step == 2 * per + 1)
-    def _():
+
+    @pl.when(step == sent + 1)
+    def _():
+        for r in range(QUARTERS):
+            gm_copy(r).wait()
+        for keep in keeps:
+            keep.start()
+
+    width = grad_attended.shape[2]
+    for nth in range(width // COLS):
+
+        @pl.when(step == sent + 2 + nth)
+        def _():
+            cols = slice(nth * COLS, (nth + 1) * COLS)
+            grad_attended[side, :, cols] = nn(gm_own[...], wo_ref[...]).astype(BF)
+            grad_attended[1 - side, :, cols] = nn(gm_got[...], wo_ref[...]).astype(BF)
+
+    @pl.when(step == scatter.steps - 1)
+    def _():
+        block_copy().wait()
+
         @pl.loop(0, half // row_chunk)
         def _(i):
             span = pl.ds(i * row_chunk, row_chunk)
-            block_own[span, :] += middle_own[span, :].astype(F32)
-            block_send[span, :] = acc_other[span, :].astype(BF)
-
-    @pl.when(step == scatter.steps - 1)
-    def _():
-        for r in range(QUARTERS):
-            gm_copy(r).wait()
-        gm_keep().wait()
-
-
-def remote_settings(identity, mib=60):
+            total = middle_own[span, :].astype(F32) + acc_own[span, :]
+            block_out_ref[span, :] = (total + block_got[span, :].astype(F32)).astype(BF)
+
+        for keep in keeps:
+            keep.wait()
+
+
+def remote_settings(identity, mib=60, axes=1):
     return pltpu.CompilerParams(
-        dimension_semantics=("arbitrary",),
+        dimension_semantics=("arbitrary",) * axes,
         vmem_limit_bytes=mib * 1024 * 1024,
         collective_id=identity,
         has_side_effects=True,
     )
 
 
-def ffn_scatter(devices, cot_turned, normed, grads, cot, middle, parts, gain_part, w):
+def ffn_scatter(
+    devices, cot_turned, normed, grads, cot, middle, parts, got, gain_part, w, w_attention, heads
+):
     half, d = middle.shape
     width = grads.shape[3]
     per = width // COLS
-    scatter = Scatter(devices, d // devices, 2 * per + 1)
-    assert 2 * per > 3 + 2 * QUARTERS and scatter.rows * devices == d and per >= 2 * half // 256
+    up_sent = per * UP_SENT // 8
+    sent = per + up_sent
+    left = 2 * per - up_sent
+    head_blocks = heads // COLS
+    scatter = Scatter(devices, d // devices, sent + 1)
+    assert scatter.rows * devices == d and per >= 2 * half // 256 and per > QUARTERS + 1
+    assert scatter.steps >= max(per + left, sent + 2 + head_blocks) and COLS >= scatter.rows >= GAIN_ROWS
 
     def right(side):
         def where(j):
-            c = jnp.minimum(j, 2 * per - 1)
+            c = jnp.minimum(j, sent - 1)
             return (side, 2 - c // per, 0, c % per)
 
         return pl.BlockSpec((None, None, half, COLS), where)
 
-    def gate_block(j):
-        return jnp.clip(j - per, 0, per - 1)
-
-    def gate(side):
-        return pl.BlockSpec((None, None, half, COLS), lambda j: (side, 0, 0, gate_block(j)))
+    def whole_block(j):
+        return jnp.clip(j - per, 0, left - 1)
+
+    def left_whole(side):
+        def where(j):
+            c = whole_block(j)
+            kind = c // per
+            return (side, kind, 0, (c + kind * up_sent) % per)
+
+        return pl.BlockSpec((None, None, half, COLS), where)
 
     def rows_of(side):
         return pl.BlockSpec(
             (None, half, d), lambda j: (side, 0, 0), pipeline_mode=pl.Buffered(1)
         )
 
-    specs, shapes = emit_specs(scatter, 2, per, width)
-    whole = lambda j: (0, 0)
+    specs, shapes = emit_specs(scatter, (per, sent - per))
     left_there = pl.BlockSpec(memory_space=pl.ANY)
     return pl.pallas_call(
-        functools.partial(ffn_scatter_kernel, scatter, per),
+        functools.partial(ffn_scatter_kernel, scatter, per, sent, left),
         grid=(scatter.steps,),
         in_specs=[
             resident((d, 2 * half)),
@@ -738,26 +827,31 @@
             rows_of(1),
             right(0),
             right(1),
-            gate(0),
-            gate(1),
+            left_whole(0),
+            left_whole(1),
+            left_there,
             left_there,
             left_there,
             left_there,
             resident((8, d)),
             pl.BlockSpec((d, COLS), lambda j: (0, 2 * per + jnp.minimum(j, per - 1))),
+            pl.BlockSpec(
+                (d, COLS),
+                lambda j: (0, 3 * head_blocks + jnp.clip(j - sent - 2, 0, head_blocks - 1)),
+            ),
         ],
         out_specs=specs
         + [
-            pl.BlockSpec((d, COLS), lambda j: (0, gate_block(j))),
+            pl.BlockSpec((d, COLS), lambda j: (0, whole_block(j))),
             left_there,
-            pl.BlockSpec((half, d), whole),
-            pl.BlockSpec((half, d), whole),
+            resident((2, half, heads)),
+            resident((half, d)),
         ],
         out_shape=shapes
         + [
-            jax.ShapeDtypeStruct((d, width), BF),
+            jax.ShapeDtypeStruct((d, left * COLS), BF),
             jax.ShapeDtypeStruct((2, half, d), BF),
-            jax.ShapeDtypeStruct((half, d), F32),
+            jax.ShapeDtypeStruct((2, half, heads), BF),
             jax.ShapeDtypeStruct((half, d), BF),
         ],
         scratch_shapes=[
@@ -767,33 +861,37 @@
             pltpu.VMEM((half, d), BF),
             pltpu.VMEM((half, d), BF),
             pltpu.VMEM((half, d), BF),
+            pltpu.VMEM((half, d), BF),
             pltpu.VMEM((8, d), F32),
             pltpu.VMEM((half, d), F32),
+            pltpu.VMEM((half, d), F32),
+            pltpu.VMEM((half, d), BF),
+            pltpu.VMEM((half, d), BF),
+            pltpu.SemaphoreType.DMA((2,)),
             pltpu.SemaphoreType.DMA((2,)),
             pltpu.SemaphoreType.DMA((QUARTERS, 2)),
-            pltpu.SemaphoreType.DMA((QUARTERS, 2)),
-            pltpu.SemaphoreType.DMA((4,)),
+            pltpu.SemaphoreType.DMA((2,)),
+            pltpu.SemaphoreType.DMA((6,)),
         ]
         + scatter.scratch(),
         compiler_params=remote_settings(0),
         cost_estimate=cost(16 * half * d * per * COLS, 20 * half * d),
         name="ffn_scatter",
     )(
-        cot_turned, normed, normed, grads, grads, grads, grads, cot, middle, parts, gain_part, w,
+        cot_turned, normed, normed, grads, grads, grads, grads, cot, middle, parts, got,
+        gain_part, w, w_attention,
     )
 
 
 def attention_scatter_kernel(scatter, per, *refs):
     (
-        norm_turned, gain_ref, right_ref, w_ref, attended_ref, gm_hbm, x_hbm, block_hbm, block_send,
-    ) = refs[:9]
-    outs = refs[9:14]
-    token_grad_ref, block_out_ref = refs[14:16]
+        norm_turned, gain_ref, right_ref, kind_ref, w_ref, attended_ref, gm_hbm, x_hbm,
+    ) = refs[:8]
+    outs, token_grad_ref = refs[8:13], refs[13]
     (
-        gm_turned, gm_ref, x_ref, block_own, acc_ref, part_send, part_got, block_got,
-        gain_part, part_sems, block_sems, local_sems,
-    ) = refs[16:28]
-    scatter.bind(refs[28:])
+        gm_turned, gm_ref, x_ref, acc_ref, part_send, part_got, gain_part, part_sems, local_sems,
+    ) = refs[14:23]
+    scatter.bind(refs[23:])
     step = pl.program_id(0)
     side = scatter.side
     across = (scatter.me, 1 - side)
@@ -808,13 +906,9 @@
         span = pl.ds(r * quarter, quarter)
         return remote(part_send.at[span], part_got.at[span], part_sems.at[r], across)
 
-    def block_copy():
-        return remote(block_send, block_got, block_sems, across)
-
     loads = [
         pltpu.make_async_copy(x_hbm, x_ref, local_sems.at[0]),
         pltpu.make_async_copy(gm_hbm, gm_ref, local_sems.at[1]),
-        pltpu.make_async_copy(block_hbm, block_own, local_sems.at[2]),
     ]
 
     def back(row):
@@ -828,9 +922,8 @@
         for load in loads:
             load.start()
         scatter.barrier()
-        block_copy().start()
-
-    scatter.advance(step, functools.partial(emit_into, outs, per))
+
+    scatter.advance(step, functools.partial(emit_into, outs, (per,) * 4))
 
     @pl.when(step == 0)
     def _():
@@ -841,10 +934,12 @@
     def _():
         scatter.multiply(step, norm_turned, (right_ref,))
 
+    @pl.when(step < 3)
+    def _():
         @pl.loop(0, length // 256)
         def _(i):
             span = pl.ds(i * 256, 256)
-            acc_ref[span, :] += nt(right_ref[span, :], w_ref[...])
+            acc_ref[span, :] += nt(kind_ref[span, :], w_ref[...])
 
     @pl.when(step == 1)
     def _():
@@ -863,7 +958,7 @@
 
     for r in range(QUARTERS):
 
-        @pl.when(step == kinds + min(r, per - 1))
+        @pl.when(step == 3 + r)
         def _():
             @pl.loop(r * quarter // chunk, (r + 1) * quarter // chunk)
             def _(i):
@@ -879,16 +974,6 @@
     @pl.when(step == 4 * per)
     def _():
         scatter.put_gain(step, gain_part[0:1, :])
-
-    @pl.when(step == 4 * per + 1)
-    def _():
-        block_copy().wait()
-
-        @pl.loop(0, half // chunk)
-        def _(i):
-            span = pl.ds(i * chunk, chunk)
-            total = block_own[span, :] + block_got[span, :].astype(F32)
-            block_out_ref[span, :] = total.astype(BF)
 
     for r in range(QUARTERS):
 
@@ -903,9 +988,7 @@
                 token_grad_ref[span, :] = (total + part_got[span, :].astype(F32)).astype(BF)
 
 
-def attention_scatter(
-    devices, norm_turned, gm, x, gain, grads, attended, block_own, block_send, w
-):
+def attention_scatter(devices, norm_turned, gm, x, gain, grads, attended, w):
     length, d = gm.shape
     half = length // 2
     width = grads.shape[2]
@@ -922,8 +1005,7 @@
     def attended_map(j):
         return (0, jnp.clip(j - kinds, 0, per - 1))
 
-    specs, shapes = emit_specs(scatter, 4, per, width)
-    whole = lambda j: (0, 0)
+    specs, shapes = emit_specs(scatter, (per,) * 4)
     left_there = pl.BlockSpec(memory_space=pl.ANY)
     return pl.pallas_call(
         functools.partial(attention_scatter_kernel, scatter, per),
@@ -932,35 +1014,30 @@
             resident((d, length)),
             resident((1, d)),
             pl.BlockSpec((None, length, COLS), grads_map),
-            pl.BlockSpec((d, COLS), lambda j: (0, jnp.minimum(j, kinds - 1))),
+            pl.BlockSpec((None, length, width), lambda j: (jnp.minimum(j, 2), 0, 0)),
+            pl.BlockSpec((d, width), lambda j: (0, jnp.minimum(j, 2))),
             pl.BlockSpec((length, COLS), attended_map),
             left_there,
             left_there,
-            left_there,
-            left_there,
-        ],
-        out_specs=specs + [pl.BlockSpec((half, d), whole), pl.BlockSpec((half, d), whole)],
-        out_shape=shapes
-        + [jax.ShapeDtypeStruct((half, d), BF), jax.ShapeDtypeStruct((half, d), BF)],
+        ],
+        out_specs=specs + [resident((half, d))],
+        out_shape=shapes + [jax.ShapeDtypeStruct((half, d), BF)],
         scratch_shapes=[
             pltpu.VMEM((d, length), BF),
             pltpu.VMEM((length, d), BF),
             pltpu.VMEM((length, d), BF),
-            pltpu.VMEM((half, d), F32),
             pltpu.VMEM((length, d), F32),
-            pltpu.VMEM((half, d), BF),
             pltpu.VMEM((half, d), BF),
             pltpu.VMEM((half, d), BF),
             pltpu.VMEM((8, d), F32),
             pltpu.SemaphoreType.DMA((QUARTERS, 2)),
             pltpu.SemaphoreType.DMA((2,)),
-            pltpu.SemaphoreType.DMA((3,)),
         ]
         + scatter.scratch(),
         compiler_params=remote_settings(1),
         cost_estimate=cost(14 * length * d * per * COLS, 20 * length * d),
         name="attention_scatter",
-    )(norm_turned, gain, grads, w, attended, gm, x, block_own, block_send)
+    )(norm_turned, gain, grads, grads, w, attended, gm, x)
 
 
 class Gather:
@@ -1052,10 +1129,10 @@
 
 
 def gather_project_kernel(gather, per, *refs):
-    shards, (tokens, cot, gain_ref, depths_ref) = refs[:4], refs[4:8]
-    w_hbm, qkv_ref, turned_ref, rows_hbm, cot_other, cos_ref, sin_ref, done_ref = refs[8:16]
-    w_ref, rows_ref, normed_ref, x_sems, row_sems, w_sems = refs[16:22]
-    gather.bind(refs[22:])
+    shards, (tokens, cot, gain_ref, depths_ref), later = refs[:4], refs[4:8], refs[8:11]
+    w_hbm, qkv_ref, turned_ref, rows_hbm, cot_other, cos_ref, sin_ref, joined = refs[11:19]
+    w_ref, rows_ref, normed_ref, x_sems, row_sems, w_sems, join_sems = refs[19:26]
+    gather.bind(refs[26:])
     step = pl.program_id(0)
     side = gather.side
     across = (gather.me, 1 - side)
@@ -1078,6 +1155,18 @@
     def w_store(block):
         cols = pl.ds(pl.multiple_of(block * COLS, COLS), COLS)
         return pltpu.make_async_copy(w_ref.at[:, cols], w_hbm.at[:, cols], w_sems.at[block])
+
+    def joins():
+        column = 0
+        for nth, shard in enumerate(later):
+            span = pl.ds(column, shard.shape[1])
+            yield pltpu.make_async_copy(shard, joined.at[:, span], join_sems.at[nth])
+            column += shard.shape[1]
+
+    @pl.when(step == 1)
+    def _():
+        for join in joins():
+            join.start()
 
     @pl.when(step == 0)
     def _():
@@ -1147,7 +1236,8 @@
 
     @pl.when(step == gather.steps - 1)
     def _():
-        done_ref[...] = gain_ref[...]
+        for join in joins():
+            join.wait()
         cot_copy().wait()
         rows_store().wait()
 
@@ -1156,7 +1246,7 @@
             w_store(block).wait()
 
 
-def gather_project(devices, shards, tokens, cot, gain, depths):
+def gather_project(devices, shards, tokens, cot, gain, depths, later):
     half, d = tokens.shape
     rows, width = shards[0].shape
     total = len(shards) * width
@@ -1168,7 +1258,9 @@
     return pl.pallas_call(
         functools.partial(gather_project_kernel, gather, per),
         grid=(gather.steps,),
-        in_specs=[left_there] * 6 + [resident((1, d)), pl.BlockSpec(memory_space=pltpu.SMEM)],
+        in_specs=[left_there] * 6
+        + [resident((1, d)), pl.BlockSpec(memory_space=pltpu.SMEM)]
+        + [left_there] * len(later),
         out_specs=[
             left_there,
             resident((2, half, 3 * width)),
@@ -1177,7 +1269,7 @@
             left_there,
             resident((2, half, LANES)),
             resident((2, half, LANES)),
-            resident((1, d)),
+            left_there,
         ],
         out_shape=[
             jax.ShapeDtypeStruct((d, total), BF),
@@ -1187,7 +1279,7 @@
             jax.ShapeDtypeStruct((half, d), BF),
             jax.ShapeDtypeStruct((2, half, LANES), F32),
             jax.ShapeDtypeStruct((2, half, LANES), F32),
-            jax.ShapeDtypeStruct((1, d), F32),
+            jax.ShapeDtypeStruct((rows, sum(shard.shape[1] for shard in later)), BF),
         ],
         scratch_shapes=[
             pltpu.VMEM((d, total), BF),
@@ -1196,12 +1288,13 @@
             pltpu.SemaphoreType.DMA((2, 2)),
             pltpu.SemaphoreType.DMA((2,)),
             pltpu.SemaphoreType.DMA((count,)),
+            pltpu.SemaphoreType.DMA((len(later),)),
         ]
         + gather.scratch(),
         compiler_params=remote_settings(2),
         cost_estimate=cost(12 * half * d * width, 2 * d * total),
         name="gather_project",
-    )(*shards, tokens, cot, gain, depths)
+    )(*shards, tokens, cot, gain, depths, *later)
 
 
 def swap(x):
@@ -1246,16 +1339,14 @@
     devices = lax.axis_size("dp")
     bias, depths = tree_tables(parents[0], seg_rows)
 
-    first, qkv, norm_turned, rows_all, cot_other, cosine, sine, attn_row = gather_project(
+    first, qkv, norm_turned, rows_all, cot_other, cosine, sine, second_shard = gather_project(
         devices,
         (query_weight, key_weight, value_weight, output_weight.T),
         tokens,
         cotangent,
         attn_row,
         depths,
-    )
-    second_shard, attn_row = lax.optimization_barrier(
-        (jnp.concatenate([gate_weight, up_weight, down_weight.T], axis=1), attn_row)
+        (gate_weight, up_weight, down_weight.T),
     )
     second = gather(second_shard)
     qkv = qkv.reshape(length, 3 * width)
@@ -1273,37 +1364,38 @@
     ).astype(BF)
     middle_other = swap(middle)
 
-    ffn_grads, normed_two, parts, gain_part = ffn(
+    ffn_grads, normed_two, parts, gain_part, got_part = ffn(
         (middle, middle_other), (cotangent, cot_other), ffn_row, second, hidden_width
     )
-    down_grad, up_grad, ffn_gain_grad, gate_whole, grad_middle, block_own, block_send = ffn_scatter(
-        devices, cot_turned, normed_two, ffn_grads, cotangent, middle, parts, gain_part, second
+    down_grad, up_first, ffn_gain_grad, whole, grad_middle, grad_attended, block_out = ffn_scatter(
+        devices,
+        cot_turned,
+        normed_two,
+        ffn_grads,
+        cotangent,
+        middle,
+        parts,
+        got_part,
+        gain_part,
+        second,
+        first,
+        width,
     )
-    gate_grad = lax.psum_scatter(gate_whole, "dp", scatter_dimension=0, tiled=True).astype(F32)
+    whole = lax.psum_scatter(whole, "dp", scatter_dimension=0, tiled=True).astype(F32)
+    gate_grad = whole[:, :hidden_width]
+    up_grad = jnp.concatenate([up_first, whole[:, hidden_width:]], axis=1)
     grad_middle = grad_middle.reshape(length, d)
-
-    grad_attended = nn(grad_middle, out_turned).astype(BF)
-    grads = attend_back(
-        qkv, attended, grad_attended, lse, bias, cosine, sine, seg_rows
-    )
+    grad_attended = grad_attended.reshape(length, width)
+    grads = attend_back(qkv, attended, grad_attended, lse, bias, cosine, sine, seg_rows)
     (
-        query_grad, key_grad, value_grad, output_grad, attn_gain_grad, token_grad, block_out,
+        query_grad, key_grad, value_grad, output_grad, attn_gain_grad, token_grad,
     ) = attention_scatter(
-        devices,
-        norm_turned,
-        grad_middle,
-        rows_all,
-        attn_row,
-        grads,
-        attended,
-        block_own,
-        block_send,
-        first,
+        devices, norm_turned, grad_middle, rows_all, attn_row, grads, attended, first
     )
     gain_rows = d // devices // 2
 
     def gain_piece(columns, side):
-        return lax.dynamic_slice_in_dim(columns[:, 0], side * gain_rows, gain_rows, 0)
+        return lax.dynamic_slice_in_dim(columns[0], side * gain_rows, gain_rows, 0)
 
     return (
         block_out,

time: 498 us -> 488 us (0.980)
    pallas_call x1, Pallas kernels: 49.5 us -> 54.9 us  [ffn(): pl.pallas_call(ffn_kernel, grid=(2, steps), in_specs=[resident((rows, d))...]
  transfers between devices with their start and end apart: 5 -> 5, of which waited for: 3 -> 3; matrix products, arithmetic and copies ran while one was open for 4% -> 3% of each run, Pallas kernels for 30% -> 30%
where the time goes in v7:
time: 488 us; the launch traced here: 487 us
  Pallas kernels  375 us (77%)
  waiting for transfers between devices  62.1 us (13%)
  local copies, waits for them, and re-layouts  17.2 us (4%)
  between operations  14.3 us (3%)
  matrix products  8.68 us (2%)
  other arithmetic  6.73 us (1%)
    pallas_call x1, Pallas kernels, ffn_scatter(): pl.pallas_call(functools.partial(ffn_scatter_kernel, scatter, per, sent,...  94.6 us
    pallas_call x1, Pallas kernels, attention_scatter(): pl.pallas_call(functools.partial(attention_scatter_kernel, scatter, per),...  89.4 us
    pallas_call x1, Pallas kernels, gather_project(): pl.pallas_call(functools.partial(gather_project_kernel, gather, per), gri...  79.1 us
    ppermute x3, waiting for transfers between devices, swap(): return lax.ppermute(x, 'tensor', [(0, 1), (1, 0)])  62 us
    pallas_call x1, Pallas kernels, ffn(): pl.pallas_call(ffn_kernel, grid=(2, steps), in_specs=[resident((rows, d))...  54.9 us
    pallas_call x1, Pallas kernels, attend_back(): pl.pallas_call(functools.partial(attend_back_kernel, block, seg_rows), gr...  33.7 us
    pallas_call x1, Pallas kernels, attend(): pl.pallas_call(functools.partial(attend_kernel, block, seg_rows), grid=(g...  21.5 us
    unnamed x46, local copies, waits for them, and re-layouts  12.9 us
  transfers between devices with their start and end apart: 5, of which 3 were waited for; matrix products, arithmetic and copies ran while one was open for 3% of the time, Pallas kernels for 30%

profile of v7, /device:TPU:0, one launch (start us, length us, event | category | flops | bytes accessed | tf_op | source)
XLA Modules:
  0.0 487.2 jit_solution(965941471003869006)
XLA Ops:
  7.2 1.3 broadcast_in_dim.12.refs_6_.refs_1_
  10.7 79.1 %gather_project.1 = (bf16[1536,3072]{1,0:T(8,128)(2,1)}, bf16[2,512,2304]{2,1,0:T(8,128)(2,1)}, bf16[1536,1024]{1,0:T(8,128)(2,1)}, bf16[2,512,1536]{2,1,0:T(8,1...) custom-call(bf16[96,768]{1,0:T(8,128)(2,1)} %refs_0_.1, ...), custom_call_target="tpu_custom_call" | custom-call | flops 7247757312 | bytes 9437184 | tf_op jit(solution)/shard_map/gather_project/pallas_call | solution.py:1258
  90.3 21.5 %attend.1 = (bf16[1024,768]{1,0:T(8,128)(2,1)S(1)}, f32[6,2,1024]{2,1,0:T(2,128)S(1)}) custom-call(bf16[1024,2304]{1,0:T(8,128)(2,1)} %bitcast.38, bf16[1024,2304]{1,0:T(8,128)(2,1)} %bitcast.39, bf16[1024,2304]{1,0:T(8,128)(2,1)} %bitcast.40, f32[8,1024]{1,0:T(8,128)S(1)} %broadcast_bitcast_fusion.bias_ref), custom_call_target="tpu_custom_call" | custom-call | flops 6442450944 | bytes 6291456 | tf_op jit(solution)/shard_map/attend/pallas_call | solution.py:150
  111.8 4.8 convolution_convert_fusion
  117.3 2.2 turn_pair.1.refs_0_
  119.4 1.8 copy-done
  121.2 3.8 convolution_add_fusion
  125.0 27.2 %collective-permute-done = bf16[512,1536]{1,0:T(8,128)(2,1)} collective-permute-done((bf16[512,1536]{1,0:T(8,128)(2,1)}, bf16[512,1536]{1,0:T(8,128)(2,1)}, u32[]{:S(2)}, u32[]{:S(2)}) %collective-permute-start) | collective-permute-done | bytes 1572896 | tf_op jit(solution)/shard_map/ppermute | solution.py:1301
  152.3 2.1 add_convert_fusion.x_own.refs_8_
  155.6 33.2 %collective-permute-done.1.x_other = bf16[512,1536]{1,0:T(8,128)(2,1)S(1)} collective-permute-done((bf16[512,1536]{1,0:T(8,128)(2,1)S(1)}, bf16[512,1536]{1,0:T(8,128)(2,1)S(1)}, u32[]{:S(2)}, u32[]{:S(2)}) %collective-permute-start.1) | collective-permute-done | bytes 1572896 | tf_op jit(solution)/shard_map/ppermute | solution.py:1301
  188.7 1.2 copy-done.18
  189.9 54.9 %ffn.1 = (bf16[2,3,512,2048]{3,2,1,0:T(8,128)(2,1)}, bf16[2,512,1536]{2,1,0:T(8,128)(2,1)}, bf16[2,512,1536]{2,1,0:T(8,128)(2,1)}, f32[8,1536]{1,0:T(8,128)}, bf16[512,1536]{1,0:T(8,128)(2,1)}) custom-call(bf16[512,1536]{1,0:T(8,128)(2,1)} %copy-done.8, bf16[512,1536]{1,0:T(8,128)(2,1)} %copy-done.18, bf16[512,1536]{1,0:T(8,128)(2,1)} %refs_7_.1, ...), custom_call_target="tpu_custom_call" | custom-call | flops 32212254720 | bytes 62914560 | tf_op jit(solution)/shard_map/ffn/pallas_call | solution.py:366
  244.9 94.6 %ffn_scatter.1 = (f32[96,2048]{1,0:T(8,128)}, f32[96,2048]{1,0:T(8,128)}, f32[16,256]{1,0:T(8,128)}, bf16[1536,2048]{1,0:T(8,128)(2,1)}, bf16[2,512,1536]{2,1,0:...) custom-call(bf16[1536,1024]{1,0:T(8,128)(2,1)} %copy-done, ...), custom_call_target="tpu_custom_call" | custom-call | flops 25769803776 | bytes 15728640 | tf_op jit(solution)/shard_map/ffn_scatter/pallas_call | solution.py:821
  339.5 1.3 copy-done.3
  341.1 1.4 copy-done.7
  342.6 33.7 %attend_back.1.refs_2_.refs_3_ = bf16[3,1024,768]{2,1,0:T(8,128)(2,1)} custom-call(bf16[1024,2304]{1,0:T(8,128)(2,1)} %bitcast.41, bf16[1024,2304]{1,0:T(8,128)(2,1)} %bitcast.42, bf16[1024,2304]{1,0:T(8,128)(2,1)} %bitcast.43, bf16[1024,768]{1,0:T(8,128)(2,1)S(1)} %copy-done.7, bf16[1024,768]{1,0:T(8,128)(2,1)S(1)} %bitcast.29, ...), custom_call_target="tpu_custom_call" | custom-call | flops 16106127360 | bytes 12582912 | tf_op jit(solution)/shard_map/attend_back/pallas_call | solution.py:238
  376.3 89.4 %attention_scatter.1 = (f32[96,768]{1,0:T(8,128)}, f32[96,768]{1,0:T(8,128)}, f32[96,768]{1,0:T(8,128)}, f32[96,768]{1,0:T(8,128)}, f32[16,256]{1,0:T(8,128)}, /*index=5*/bf16[512,1536]{1,0:T(8,128)(2,1)}) custom-call(bf16[1536,1024]{1,0:T(8,128)(2,1)} %get-tuple-element.58.refs_0_, f32[1,1536]{1,0:T(1,128)} %broadcast_in_dim.12.refs_6_.refs_1_, ...), custom_call_target="tpu_custom_call" | custom-call | flops 16911433728 | bytes 31457280 | tf_op jit(solution)/shard_map/attention_scatter/pallas_call | solution.py:1010
  467.3 1.3 collective-permute-start.2
  469.2 1.6 collective-permute-done.2
  471.4 1.9 convert_element_type.76
  473.4 1.1 copy.42
  474.6 1.1 copy.43
  478.6 0.9 copy.48
  479.5 0.9 copy.49
  (74 shorter events, 10.3 us)
Async XLA Ops:
  7.2 181.6 %all-gather.2.cloned.1.call-start = ((), (), s32[]{:S(2)}) async-start(), calls=%async_computation.1 | async-start | bytes 20054016 | tf_op jit(solution)/shard_map/all_gather | solution.py:1334
  89.8 381.6 %reduce-scatter.2.cloned.1.call-start = ((), (), s32[]{:S(2)}) async-start(), calls=%async_computation.2 | async-start | bytes 6684672 | tf_op jit(solution)/shard_map/reduce_scatter | solution.py:1384
  111.8 4.9 %copy-start.6 = (bf16[1024,768]{1,0:T(8,128)(2,1)}, bf16[1024,768]{1,0:T(8,128)(2,1)S(1)}, u32[]{:S(2)}) copy-start(bf16[1024,768]{1,0:T(8,128)(2,1)S(1)} %get-tuple-element.44.o_ref.refs_5_) | copy-start | bytes 4718596
  111.8 5.4 %copy-start.1 = (bf16[512,1536]{1,0:T(8,128)(2,1)S(1)}, bf16[512,1536]{1,0:T(8,128)(2,1)}, u32[]{:S(2)}) copy-start(bf16[512,1536]{1,0:T(8,128)(2,1)} %refs_7_.1) | copy-start | bytes 4718596
  111.8 5.4 %copy-start.2 = (bf16[512,1536]{1,0:T(8,128)(2,1)S(1)}, bf16[512,1536]{1,0:T(8,128)(2,1)}, u32[]{:S(2)}) copy-start(bf16[512,1536]{1,0:T(8,128)(2,1)} %get-tuple-element.48.second_ref.cot_other) | copy-start | bytes 4718596
  116.7 35.6 %collective-permute-start = (bf16[512,1536]{1,0:T(8,128)(2,1)}, bf16[512,1536]{1,0:T(8,128)(2,1)}, u32[]{:S(2)}, u32[]{:S(2)}) collective-permute-start(bf16[512,1536]{1,0:T(8,128)(2,1)} %convolution_convert_fusion), channel_id=1, source_target_pairs={{0,1},{1,0},{2,3},{3,2},{4,5},{5,4},{6,7},{7,6},{8,9},{9,8},{10,11... | collective-permute-start | bytes 4718600 | tf_op jit(solution)/shard_map/ppermute | solution.py:1301
  119.4 1.8 copy-start
  125.0 30.0 %copy-start.17 = (f32[1536]{0:T(1024)S(1)}, f32[1536]{0:T(1024)}, u32[]{:S(2)}) copy-start(f32[1536]{0:T(1024)} %param.15) | copy-start | bytes 18436
  154.4 34.4 %copy-start.8 = (bf16[512,1536]{1,0:T(8,128)(2,1)}, bf16[512,1536]{1,0:T(8,128)(2,1)S(1)}, u32[]{:S(2)}) copy-start(bf16[512,1536]{1,0:T(8,128)(2,1)S(1)} %add_convert_fusion.x_own.refs_8_) | copy-start | bytes 4718596
  154.4 34.3 %collective-permute-start.1 = (bf16[512,1536]{1,0:T(8,128)(2,1)S(1)}, bf16[512,1536]{1,0:T(8,128)(2,1)S(1)}, u32[]{:S(2)}, u32[]{:S(2)}) collective-permute-start(bf16[512,1536]{1,0:T(8,128)(2,1)S(1)} %add_convert_fusion.x_own.refs_8_), channel_id=1, source_target_pairs={{0,1},{1,0},{2,3},{3,2},{4,5},{5,4},{6,7},{7,6},{8,9},{9,8},{10,11... | collective-permute-start | bytes 4718600 | tf_op jit(solution)/shard_map/ppermute | solution.py:1301
  188.7 1.2 copy-start.18
  339.5 1.4 copy-start.3
  339.5 1.5 copy-start.4
  339.5 1.7 copy-start.5
  341.1 1.4 copy-start.7
  376.2 97.1 %copy-start.9 = (bf16[512,1536]{1,0:T(8,128)(2,1)S(1)}, bf16[512,1536]{1,0:T(8,128)(2,1)}, u32[]{:S(2)}) copy-start(bf16[512,1536]{1,0:T(8,128)(2,1)} %get-tuple-element.88) | copy-start | bytes 4718596
  465.7 8.8 %copy-start.10 = (bf16[512,1536]{1,0:T(8,128)(2,1)S(1)}, bf16[512,1536]{1,0:T(8,128)(2,1)}, u32[]{:S(2)}) copy-start(bf16[512,1536]{1,0:T(8,128)(2,1)} %get-tuple-element.89) | copy-start | bytes 4718596
  467.3 3.5 collective-permute-start.2
  474.5 1.2 copy-start.16
  474.5 1.9 copy-start.15
  474.5 2.6 copy-start.14
  474.5 3.3 copy-start.13
  474.5 4.0 copy-start.12
  475.7 3.8 copy-start.11
Sparse Core Ops, SparseCore 0:
  89.9 98.2 all-gather.1
  339.6 94.8 reduce-scatter.1

commit v8 on v7

--- a/solution.py
+++ b/solution.py
@@ -170,28 +170,16 @@
     )(qkv, qkv, qkv, bias)
 
 
-def attend_back_kernel(
-    block,
-    seg_rows,
-    q_ref,
-    k_ref,
-    v_ref,
-    o_ref,
-    do_ref,
-    lse_ref,
-    bias_ref,
-    cos_ref,
-    sin_ref,
-    out_ref,
-    dk_ref,
-    dv_ref,
+def attend_back_pair(
+    blocks, finish, block, seg_rows, lanes_out, q_ref, k_ref, v_ref, o_ref, do_ref, lse_ref, bias_ref, cos_ref,
+    sin_ref, out_ref, dk_ref, dv_ref,
 ):
     length = q_ref.shape[0]
     heads = q_ref.shape[1] // HD
     k_turned = k_ref[...].T
     product = (do_ref[...].astype(F32) * o_ref[...].astype(F32)).T
     deltas = [product[h * HD : (h + 1) * HD].sum(axis=0, keepdims=True) for h in range(heads)]
-    for m in range(length // block):
+    for m in blocks:
         cols = slice(m * block, (m + 1) * block)
         grads = []
         for h in range(heads):
@@ -219,46 +207,14 @@
                 acc = acc + nn(k_turned[lanes, keys], ds)
             grads.append(acc)
         dq = jnp.concatenate(grads, axis=0).T * (1.0 / math.sqrt(HD))
-        out_ref[0, cols, :] = turn(dq, cos_ref[cols, :], -sin_ref[cols, :]).astype(BF)
-    for m in range(length // block):
+        out_ref[0, cols, lanes_out] = turn(dq, cos_ref[cols, :], -sin_ref[cols, :]).astype(BF)
+    for m in range(length // block if finish else 0):
         cols = slice(m * block, (m + 1) * block)
         dk = jnp.concatenate([dk_ref[h, cols, :] for h in range(heads)], axis=1)
-        out_ref[1, cols, :] = turn(dk, cos_ref[cols, :], -sin_ref[cols, :]).astype(BF)
-        out_ref[2, cols, :] = jnp.concatenate(
+        out_ref[1, cols, lanes_out] = turn(dk, cos_ref[cols, :], -sin_ref[cols, :]).astype(BF)
+        out_ref[2, cols, lanes_out] = jnp.concatenate(
             [dv_ref[h, cols, :] for h in range(heads)], axis=1
         ).astype(BF)
-
-
-def attend_back(qkv, attended, grad_attended, lse, bias, cosine, sine, seg_rows):
-    length, width = attended.shape
-    groups = width // LANES
-    heads = LANES // HD
-    block = 2 * seg_rows
-    live = length * length // 2
-    return pl.pallas_call(
-        functools.partial(attend_back_kernel, block, seg_rows),
-        grid=(groups,),
-        in_specs=[
-            pl.BlockSpec((length, LANES), lambda i: (0, i)),
-            pl.BlockSpec((length, LANES), lambda i: (0, groups + i)),
-            pl.BlockSpec((length, LANES), lambda i: (0, 2 * groups + i)),
-            pl.BlockSpec((length, LANES), lambda i: (0, i)),
-            pl.BlockSpec((length, LANES), lambda i: (0, i)),
-            pl.BlockSpec((1, heads, length), lambda i: (i, 0, 0)),
-            pl.BlockSpec(bias.shape, lambda i: (0, 0)),
-            pl.BlockSpec((length, LANES), lambda i: (0, 0)),
-            pl.BlockSpec((length, LANES), lambda i: (0, 0)),
-        ],
-        out_specs=pl.BlockSpec((3, length, LANES), lambda i: (0, 0, i)),
-        out_shape=jax.ShapeDtypeStruct((3, length, width), BF),
-        scratch_shapes=[
-            pltpu.VMEM((heads, length, HD), F32),
-            pltpu.VMEM((heads, length, HD), F32),
-        ],
-        compiler_params=settings(),
-        cost_estimate=cost(40 * live * width, 16 * length * width, live * width // HD),
-        name="attend_back",
-    )(qkv, qkv, qkv, attended, grad_attended, lse, bias, cosine, sine)
 
 
 def rms_back(grad, x, gain):
@@ -406,7 +362,7 @@
 MESH = pl.DeviceIdType.MESH
 QUARTERS = 4
 EARLY = 3
-UP_SENT = 8
+UP_SENT = 6
 GAIN_ROWS = 16
 
 
@@ -536,6 +492,22 @@
         lax.fori_loop(0, pieces, piece, 0)
         self.copy(0, block).start()
 
+    def enter(self, block, ref):
+        slot = block % self.slots[0]
+        pieces = 4
+        size = self.devices // pieces
+
+        def piece(i, carry):
+            rows = ref[pl.ds(i * size * self.rows, size * self.rows), :]
+            for r in range(size):
+                self.held[0][slot, r % 2, i * (size // 2) + r // 2] = rows[
+                    r * self.rows : (r + 1) * self.rows
+                ]
+            return carry
+
+        lax.fori_loop(0, pieces, piece, 0)
+        self.copy(0, block).start()
+
     def put_gain(self, block, row):
         slot = block % self.slots[0]
         empty = jnp.zeros((1, COLS - self.rows), F32)
@@ -621,12 +593,12 @@
         cot_hbm, middle_hbm, parts_hbm, got_hbm, gain_ref, wd_ref, wo_ref,
     ) = refs[:14]
     outs = refs[14:17]
-    whole_ref, gm_ref, grad_attended, block_out_ref = refs[17:21]
+    whole_ref, gm_ref, grad_attended, block_out_ref, gm_turned = refs[17:22]
     (
         norm_turned, cot_own, middle_own, part_own, got_part, gm_own, gm_got, gain_got, acc_own,
         acc_other, block_send, block_got, gain_sems, part_sems, gm_sems, block_sems, local_sems,
-    ) = refs[21:38]
-    scatter.bind(refs[38:])
+    ) = refs[22:39]
+    scatter.bind(refs[39:])
     step = pl.program_id(0)
     side = scatter.side
     across = (scatter.me, 1 - side)
@@ -755,6 +727,14 @@
             cols = slice(nth * COLS, (nth + 1) * COLS)
             grad_attended[side, :, cols] = nn(gm_own[...], wo_ref[...]).astype(BF)
             grad_attended[1 - side, :, cols] = nn(gm_got[...], wo_ref[...]).astype(BF)
+
+    pieces = [(gm_own, side, r) for r in range(0, half, 256)]
+    pieces += [(gm_got, 1 - side, r) for r in range(0, half, 256)]
+    for nth, (left, at, row) in enumerate(pieces):
+
+        @pl.when(step == sent + 2 + width // COLS + nth)
+        def _():
+            turn_piece(gm_turned, left, at * half, row)
 
     @pl.when(step == scatter.steps - 1)
     def _():
@@ -791,7 +771,8 @@
     head_blocks = heads // COLS
     scatter = Scatter(devices, d // devices, sent + 1)
     assert scatter.rows * devices == d and per >= 2 * half // 256 and per > QUARTERS + 1
-    assert scatter.steps >= max(per + left, sent + 2 + head_blocks) and COLS >= scatter.rows >= GAIN_ROWS
+    assert scatter.steps >= max(per + left, sent + 2 + head_blocks + 2 * half // 256)
+    assert COLS >= scatter.rows >= GAIN_ROWS
 
     def right(side):
         def where(j):
@@ -846,6 +827,7 @@
             left_there,
             resident((2, half, heads)),
             resident((half, d)),
+            resident((d, 2 * half)),
         ],
         out_shape=shapes
         + [
@@ -853,6 +835,7 @@
             jax.ShapeDtypeStruct((2, half, d), BF),
             jax.ShapeDtypeStruct((2, half, heads), BF),
             jax.ShapeDtypeStruct((half, d), BF),
+            jax.ShapeDtypeStruct((d, 2 * half), BF),
         ],
         scratch_shapes=[
             pltpu.VMEM((d, 2 * half), BF),
@@ -883,15 +866,18 @@
     )
 
 
-def attention_scatter_kernel(scatter, per, *refs):
+def attention_scatter_kernel(scatter, per, early, block, seg_rows, *refs):
     (
-        norm_turned, gain_ref, right_ref, kind_ref, w_ref, attended_ref, gm_hbm, x_hbm,
-    ) = refs[:8]
-    outs, token_grad_ref = refs[8:13], refs[13]
+        norm_turned, gm_turned, gain_ref, q_ref, k_ref, v_ref, o_ref, do_ref, lse_ref, bias_ref,
+        cos_ref, sin_ref, attended_ref, w_ref, whole_ref, gm_hbm, x_hbm,
+    ) = refs[:17]
+    outs, token_grad_ref = refs[17 : 22 + len(early)], refs[22 + len(early)]
+    refs = refs[23 + len(early) :]
     (
-        gm_turned, gm_ref, x_ref, acc_ref, part_send, part_got, gain_part, part_sems, local_sems,
-    ) = refs[14:23]
-    scatter.bind(refs[23:])
+        grads_ref, dk_ref, dv_ref, gm_own, x_ref, acc_ref, part_send, part_got, gain_part,
+        part_sems, local_sems,
+    ) = refs[:11]
+    scatter.bind(refs[11:])
     step = pl.program_id(0)
     side = scatter.side
     across = (scatter.me, 1 - side)
@@ -899,8 +885,10 @@
     half = length // 2
     quarter = half // QUARTERS
     chunk = 128
-    kinds = 3 * per
+    groups = grads_ref.shape[2] // LANES
     own, other = side * half, (1 - side) * half
+    before = sum(early)
+    turns = 2 * groups
 
     def part_copy(r):
         span = pl.ds(r * quarter, quarter)
@@ -908,7 +896,7 @@
 
     loads = [
         pltpu.make_async_copy(x_hbm, x_ref, local_sems.at[0]),
-        pltpu.make_async_copy(gm_hbm, gm_ref, local_sems.at[1]),
+        pltpu.make_async_copy(gm_hbm.at[side], gm_own, local_sems.at[1]),
     ]
 
     def back(row):
@@ -917,48 +905,83 @@
         gain_part[...] += jnp.broadcast_to(piece, gain_part.shape)
         return part
 
+    def emit(column, value, gain):
+        if gain:
+            outs[4][...] = value
+            return
+        first = 0
+        for out, count in zip(outs[5:], early):
+
+            @pl.when((column >= first) & (column < first + count))
+            def _():
+                out[...] = value
+
+            first += count
+
+        @pl.when((column >= before) & (column < before + per))
+        def _():
+            outs[3][...] = value
+
+        for kind in range(3):
+
+            @pl.when((column >= before + per) & ((column - before - per) % 3 == kind))
+            def _():
+                outs[kind][...] = value
+
     @pl.when(step == 0)
     def _():
         for load in loads:
             load.start()
         scatter.barrier()
 
-    scatter.advance(step, functools.partial(emit_into, outs, (per,) * 4))
-
-    @pl.when(step == 0)
-    def _():
+    scatter.advance(step, emit)
+
+    @pl.when(step < before)
+    def _():
+        scatter.enter(step, whole_ref)
+
+    @pl.when((step >= before) & (step < before + per))
+    def _():
+        scatter.multiply(step, gm_turned, (attended_ref,))
+
+    @pl.when((step >= before + per) & (step < before + 4 * per))
+    def _():
+        column = step - before - per
+        cols = pl.ds(pl.multiple_of(column // 3 * COLS, COLS), COLS)
+        scatter.multiply(step, norm_turned, (grads_ref.at[column % 3, :, cols],))
+
+    count = length // block
+    split = count - count // 4
+    for odd in range(2):
+
+        @pl.when((step < turns) & (step % 2 == odd))
+        def _():
+            lanes = pl.ds(pl.multiple_of(step // 2 * LANES, LANES), LANES)
+            blocks = range(split, count) if odd else range(split)
+            attend_back_pair(
+                blocks, odd == 1, block, seg_rows, lanes, q_ref, k_ref, v_ref, o_ref, do_ref,
+                lse_ref, bias_ref, cos_ref, sin_ref, grads_ref, dk_ref, dv_ref,
+            )
+
+    @pl.when(step == 1)
+    def _():
+        for load in loads:
+            load.wait()
         acc_ref[...] = jnp.zeros_like(acc_ref)
         gain_part[...] = jnp.zeros_like(gain_part)
 
-    @pl.when(step < kinds)
-    def _():
-        scatter.multiply(step, norm_turned, (right_ref,))
-
-    @pl.when(step < 3)
-    def _():
+    @pl.when((step >= turns) & (step < turns + 3))
+    def _():
+        kind = step - turns
+
         @pl.loop(0, length // 256)
         def _(i):
             span = pl.ds(i * 256, 256)
-            acc_ref[span, :] += nt(kind_ref[span, :], w_ref[...])
-
-    @pl.when(step == 1)
-    def _():
-        for load in loads:
-            load.wait()
-
-    for nth, row in enumerate(range(0, length, 256)):
-
-        @pl.when(step == kinds - length // 256 + nth)
-        def _():
-            turn_piece(gm_turned, gm_ref, 0, row)
-
-    @pl.when((step >= kinds) & (step < 4 * per))
-    def _():
-        scatter.multiply(step, gm_turned, (attended_ref,))
+            acc_ref[span, :] += nt(grads_ref[kind, span, :], w_ref[...])
 
     for r in range(QUARTERS):
 
-        @pl.when(step == 3 + r)
+        @pl.when(step == turns + 3 + r // 2)
         def _():
             @pl.loop(r * quarter // chunk, (r + 1) * quarter // chunk)
             def _(i):
@@ -966,12 +989,15 @@
 
             part_copy(r).start()
 
+        @pl.when(step == turns + 5 + r // 2)
+        def _():
             @pl.loop(r * quarter // chunk, (r + 1) * quarter // chunk)
             def _(i):
                 span = pl.ds(own + i * chunk, chunk)
-                acc_ref[span, :] = back(own + i * chunk) + gm_ref[span, :].astype(F32)
-
-    @pl.when(step == 4 * per)
+                kept = gm_own[pl.ds(i * chunk, chunk), :].astype(F32)
+                acc_ref[span, :] = back(own + i * chunk) + kept
+
+    @pl.when(step == before + 4 * per)
     def _():
         scatter.put_gain(step, gain_part[0:1, :])
 
@@ -988,43 +1014,70 @@
                 token_grad_ref[span, :] = (total + part_got[span, :].astype(F32)).astype(BF)
 
 
-def attention_scatter(devices, norm_turned, gm, x, gain, grads, attended, w):
-    length, d = gm.shape
-    half = length // 2
-    width = grads.shape[2]
+def attention_scatter(
+    devices, norm_turned, gm_turned, gm, x, gain, qkv, attended, grad_attended, lse, bias, cosine,
+    sine, w, whole, early, seg_rows,
+):
+    length, width = attended.shape
+    half, d = gm.shape[1:]
     per = width // COLS
-    kinds = 3 * per
-    scatter = Scatter(devices, d // devices, 4 * per + 1)
-    assert kinds >= length // 256 and scatter.rows * devices == d
-    assert scatter.starts[-1] > QUARTERS
-
-    def grads_map(j):
-        c = jnp.minimum(j, kinds - 1)
-        return (c // per, 0, c % per)
-
-    def attended_map(j):
-        return (0, jnp.clip(j - kinds, 0, per - 1))
-
-    specs, shapes = emit_specs(scatter, (per,) * 4)
+    groups = width // LANES
+    heads = LANES // HD
+    before = sum(early)
+    scatter = Scatter(devices, d // devices, before + 4 * per + 1)
+    lead = scatter.starts[-1]
+    assert groups == 2 * per and 2 * groups + 7 <= before + 4 * per and lead > QUARTERS
+    assert scatter.rows * devices == d and whole.shape[1] == before * COLS
+
+    def group(j):
+        return jnp.minimum(j // 2, groups - 1)
+
+    def lanes_of(kind):
+        return pl.BlockSpec((length, LANES), lambda j: (0, kind * groups + group(j)))
+
+    specs, shapes = [], []
+    for kind in range(4):
+        first = lead + before + (per + kind if kind < 3 else 0)
+        stride = 3 if kind < 3 else 1
+
+        def where(j, first=first, stride=stride):
+            return (0, jnp.clip(jnp.maximum(j - first, 0) // stride, 0, per - 1))
+
+        specs.append(pl.BlockSpec((scatter.rows, COLS), where))
+        shapes.append(jax.ShapeDtypeStruct((scatter.rows, width), F32))
+    more_specs, more_shapes = emit_specs(scatter, early)
+    specs += more_specs[-1:] + more_specs[:-1]
+    shapes += more_shapes[-1:] + more_shapes[:-1]
     left_there = pl.BlockSpec(memory_space=pl.ANY)
     return pl.pallas_call(
-        functools.partial(attention_scatter_kernel, scatter, per),
+        functools.partial(attention_scatter_kernel, scatter, per, early, 2 * seg_rows, seg_rows),
         grid=(scatter.steps,),
         in_specs=[
             resident((d, length)),
+            resident((d, length)),
             resident((1, d)),
-            pl.BlockSpec((None, length, COLS), grads_map),
-            pl.BlockSpec((None, length, width), lambda j: (jnp.minimum(j, 2), 0, 0)),
-            pl.BlockSpec((d, width), lambda j: (0, jnp.minimum(j, 2))),
-            pl.BlockSpec((length, COLS), attended_map),
+            lanes_of(0),
+            lanes_of(1),
+            lanes_of(2),
+            lanes_of(0),
+            lanes_of(0),
+            pl.BlockSpec((1, heads, length), lambda j: (group(j), 0, 0)),
+            resident(bias.shape),
+            resident((length, LANES)),
+            resident((length, LANES)),
+            pl.BlockSpec((length, COLS), lambda j: (0, jnp.clip(j - before, 0, per - 1))),
+            pl.BlockSpec((d, width), lambda j: (0, jnp.clip(j - 2 * groups, 0, 2))),
+            pl.BlockSpec((d, COLS), lambda j: (0, jnp.minimum(j, before - 1))),
             left_there,
             left_there,
         ],
         out_specs=specs + [resident((half, d))],
         out_shape=shapes + [jax.ShapeDtypeStruct((half, d), BF)],
         scratch_shapes=[
-            pltpu.VMEM((d, length), BF),
-            pltpu.VMEM((length, d), BF),
+            pltpu.VMEM((3, length, width), BF),
+            pltpu.VMEM((heads, length, HD), F32),
+            pltpu.VMEM((heads, length, HD), F32),
+            pltpu.VMEM((half, d), BF),
             pltpu.VMEM((length, d), BF),
             pltpu.VMEM((length, d), F32),
             pltpu.VMEM((half, d), BF),
@@ -1035,9 +1088,16 @@
         ]
         + scatter.scratch(),
         compiler_params=remote_settings(1),
-        cost_estimate=cost(14 * length * d * per * COLS, 20 * length * d),
+        cost_estimate=cost(
+            14 * length * d * width + 20 * length * length * width,
+            20 * length * d,
+            length * length * width // HD,
+        ),
         name="attention_scatter",
-    )(norm_turned, gain, grads, grads, w, attended, gm, x)
+    )(
+        norm_turned, gm_turned, gain, qkv, qkv, qkv, attended, grad_attended, lse, bias, cosine,
+        sine, attended, w, whole, gm, x,
+    )
 
 
 class Gather:
@@ -1367,7 +1427,9 @@
     ffn_grads, normed_two, parts, gain_part, got_part = ffn(
         (middle, middle_other), (cotangent, cot_other), ffn_row, second, hidden_width
     )
-    down_grad, up_first, ffn_gain_grad, whole, grad_middle, grad_attended, block_out = ffn_scatter(
+    (
+        down_grad, up_first, ffn_gain_grad, whole, grad_middle, grad_attended, block_out, gm_turned,
+    ) = ffn_scatter(
         devices,
         cot_turned,
         normed_two,
@@ -1381,17 +1443,31 @@
         first,
         width,
     )
-    whole = lax.psum_scatter(whole, "dp", scatter_dimension=0, tiled=True).astype(F32)
-    gate_grad = whole[:, :hidden_width]
-    up_grad = jnp.concatenate([up_first, whole[:, hidden_width:]], axis=1)
-    grad_middle = grad_middle.reshape(length, d)
-    grad_attended = grad_attended.reshape(length, width)
-    grads = attend_back(qkv, attended, grad_attended, lse, bias, cosine, sine, seg_rows)
+    blocks = hidden_width // COLS
+    rest = whole.shape[1] // COLS - blocks
     (
-        query_grad, key_grad, value_grad, output_grad, attn_gain_grad, token_grad,
+        query_grad, key_grad, value_grad, output_grad, attn_gain_grad, gate_grad, *up_rest,
+        token_grad,
     ) = attention_scatter(
-        devices, norm_turned, grad_middle, rows_all, attn_row, grads, attended, first
+        devices,
+        norm_turned,
+        gm_turned,
+        grad_middle,
+        rows_all,
+        attn_row,
+        qkv,
+        attended,
+        grad_attended.reshape(length, width),
+        lse,
+        bias,
+        cosine,
+        sine,
+        first,
+        whole,
+        (blocks, rest) if rest else (blocks,),
+        seg_rows,
     )
+    up_grad = jnp.concatenate([up_first, *up_rest], axis=1)
     gain_rows = d // devices // 2
 
     def gain_piece(columns, side):

time: 488 us -> 473 us (0.969)
  Pallas kernels: 375 us -> 366 us
    pallas_call x1, Pallas kernels: 94.6 us -> 89 us  [ffn_scatter(): pl.pallas_call(functools.partial(ffn_scatter_kernel, scatter, per, sent,...]
    pallas_call x2 -> x1, Pallas kernels: 123 us -> 119 us  [attention_scatter(): pl.pallas_call(functools.partial(attention_scatter_kernel, scatter, per,...]
    unnamed x46 -> x44, local copies, waits for them, and re-layouts: 12.9 us -> 9.8 us
  transfers between devices with their start and end apart: 5 -> 4, of which waited for: 3 -> 3; matrix products, arithmetic and copies ran while one was open for 3% -> 3% of each run, Pallas kernels for 30% -> 5%
where the time goes in v8:
time: 473 us
  Pallas kernels  366 us (77%)
  waiting for transfers between devices  60.8 us (13%)
  between operations  14.3 us (3%)
  local copies, waits for them, and re-layouts  14.1 us (3%)
  matrix products  8.72 us (2%)
  other arithmetic  6.79 us (1%)
    pallas_call x1, Pallas kernels, attention_scatter(): pl.pallas_call(functools.partial(attention_scatter_kernel, scatter, per,...  119 us
    pallas_call x1, Pallas kernels, ffn_scatter(): pl.pallas_call(functools.partial(ffn_scatter_kernel, scatter, per, sent,...  89 us
    pallas_call x1, Pallas kernels, gather_project(): pl.pallas_call(functools.partial(gather_project_kernel, gather, per), gri...  79.1 us
    ppermute x3, waiting for transfers between devices, swap(): return lax.ppermute(x, 'tensor', [(0, 1), (1, 0)])  60.8 us
    pallas_call x1, Pallas kernels, ffn(): pl.pallas_call(ffn_kernel, grid=(2, steps), in_specs=[resident((rows, d))...  55.2 us
    pallas_call x1, Pallas kernels, attend(): pl.pallas_call(functools.partial(attend_kernel, block, seg_rows), grid=(g...  21.5 us
    unnamed x44, local copies, waits for them, and re-layouts  9.8 us
  transfers between devices with their start and end apart: 4, of which 3 were waited for; matrix products, arithmetic and copies ran while one was open for 3% of the time, Pallas kernels for 5%

profile of v8, /device:TPU:0, one launch (start us, length us, event | category | flops | bytes accessed | tf_op | source)
XLA Modules:
  0.0 472.7 jit_solution(12363828774207045151)
XLA Ops:
  7.2 1.3 broadcast_in_dim.12.refs_6_.refs_2_
  8.5 0.7 fusion.15
  10.7 79.1 %gather_project.1 = (bf16[1536,3072]{1,0:T(8,128)(2,1)}, bf16[2,512,2304]{2,1,0:T(8,128)(2,1)}, bf16[1536,1024]{1,0:T(8,128)(2,1)}, bf16[2,512,1536]{2,1,0:T(8,1...) custom-call(bf16[96,768]{1,0:T(8,128)(2,1)} %refs_0_.1, ...), custom_call_target="tpu_custom_call" | custom-call | flops 7247757312 | bytes 9437184 | tf_op jit(solution)/shard_map/gather_project/pallas_call | solution.py:1318
  90.0 21.5 %attend.1 = (bf16[1024,768]{1,0:T(8,128)(2,1)S(1)}, f32[6,2,1024]{2,1,0:T(2,128)S(1)}) custom-call(bf16[1024,2304]{1,0:T(8,128)(2,1)} %bitcast.34, bf16[1024,2304]{1,0:T(8,128)(2,1)} %bitcast.35, bf16[1024,2304]{1,0:T(8,128)(2,1)} %bitcast.36, f32[8,1024]{1,0:T(8,128)S(1)} %broadcast_bitcast_fusion.bias_ref.refs_9_), custom_call_target="tpu_custom_call" | custom-call | flops 6442450944 | bytes 6291456 | tf_op jit(solution)/shard_map/attend/pallas_call | solution.py:150
  111.6 4.9 %convolution_convert_fusion = bf16[512,1536]{1,0:T(8,128)(2,1)} fusion(bf16[1536,3072]{1,0:T(8,128)(2,1)} %get-tuple-element.48.refs_13_, bf16[1024,768]{1,0:T(8,128)(2,1)S(1)} %get-tuple-element.47.refs_6_.refs_12_, s32[]{:T(128)S(6)} %select_n.18), kind=kOutput, calls=%fused_computation.2 | convolution fusion | flops 1208745984 | bytes 4718596 | tf_op jit(solution)/shard_map/dot_general | solution.py:37
  117.0 2.2 turn_pair.1.refs_0_
  119.2 1.6 copy-done
  120.8 3.9 convolution_add_fusion
  124.7 27.4 %collective-permute-done = bf16[512,1536]{1,0:T(8,128)(2,1)} collective-permute-done((bf16[512,1536]{1,0:T(8,128)(2,1)}, bf16[512,1536]{1,0:T(8,128)(2,1)}, u32[]{:S(2)}, u32[]{:S(2)}) %collective-permute-start) | collective-permute-done | bytes 1572896 | tf_op jit(solution)/shard_map/ppermute | solution.py:1361
  152.1 2.1 add_convert_fusion.x_own.refs_8_
  155.3 33.2 %collective-permute-done.1.x_other = bf16[512,1536]{1,0:T(8,128)(2,1)S(1)} collective-permute-done((bf16[512,1536]{1,0:T(8,128)(2,1)S(1)}, bf16[512,1536]{1,0:T(8,128)(2,1)S(1)}, u32[]{:S(2)}, u32[]{:S(2)}) %collective-permute-start.1) | collective-permute-done | bytes 1572896 | tf_op jit(solution)/shard_map/ppermute | solution.py:1361
  188.5 1.2 copy-done.17
  189.7 55.2 %ffn.1 = (bf16[2,3,512,2048]{3,2,1,0:T(8,128)(2,1)}, bf16[2,512,1536]{2,1,0:T(8,128)(2,1)}, bf16[2,512,1536]{2,1,0:T(8,128)(2,1)}, f32[8,1536]{1,0:T(8,128)}, bf16[512,1536]{1,0:T(8,128)(2,1)}) custom-call(bf16[512,1536]{1,0:T(8,128)(2,1)} %copy-done.6, bf16[512,1536]{1,0:T(8,128)(2,1)} %copy-done.17, bf16[512,1536]{1,0:T(8,128)(2,1)} %refs_7_.1, ...), custom_call_target="tpu_custom_call" | custom-call | flops 32212254720 | bytes 62914560 | tf_op jit(solution)/shard_map/ffn/pallas_call | solution.py:322
  244.9 89.0 %ffn_scatter.1 = (f32[96,2048]{1,0:T(8,128)}, f32[96,1536]{1,0:T(8,128)}, f32[16,256]{1,0:T(8,128)}, bf16[1536,2560]{1,0:T(8,128)(2,1)}, bf16[2,512,1536]{2,1,0:...) custom-call(bf16[1536,1024]{1,0:T(8,128)(2,1)} %copy-done, ...), custom_call_target="tpu_custom_call" | custom-call | flops 25769803776 | bytes 15728640 | tf_op jit(solution)/shard_map/ffn_scatter/pallas_call | solution.py:802
  333.9 119.2 %attention_scatter.1 = (f32[96,768]{1,0:T(8,128)}, f32[96,768]{1,0:T(8,128)}, f32[96,768]{1,0:T(8,128)}, f32[96,768]{1,0:T(8,128)}, f32[16,256]{1,0:T(8,128)}, /...) custom-call(bf16[1536,1024]{1,0:T(8,128)(2,1)} %get-tuple-element.61.refs_0_, ...), custom_call_target="tpu_custom_call" | custom-call | flops 33017561088 | bytes 31457280 | tf_op jit(solution)/shard_map/attention_scatter/pallas_call | solution.py:1052
  453.2 0.8 slice.11
  456.1 2.0 pad_maximum_fusion
  458.9 1.1 copy.42
  460.1 1.1 copy.43
  461.2 0.7 copy.44
  462.7 0.7 copy.46
  463.4 0.7 copy.47
  464.1 0.9 copy.48
  465.0 0.9 copy.49
  (68 shorter events, 7.1 us)
Async XLA Ops:
  7.2 181.3 %all-gather.2.cloned.1.call-start = ((), (), s32[]{:S(2)}) async-start(), calls=%async_computation | async-start | bytes 20054016 | tf_op jit(solution)/shard_map/all_gather | solution.py:1394
  90.0 21.5 %copy-start.3 = (f32[8,1024]{1,0:T(8,128)}, f32[8,1024]{1,0:T(8,128)S(1)}, u32[]{:S(2)}) copy-start(f32[8,1024]{1,0:T(8,128)S(1)} %broadcast_bitcast_fusion.bias_ref.refs_9_) | copy-start | bytes 98308
  111.6 4.9 %copy-start.4 = (bf16[1024,768]{1,0:T(8,128)(2,1)}, bf16[1024,768]{1,0:T(8,128)(2,1)S(1)}, u32[]{:S(2)}) copy-start(bf16[1024,768]{1,0:T(8,128)(2,1)S(1)} %get-tuple-element.47.refs_6_.refs_12_) | copy-start | bytes 4718596
  111.6 4.9 %copy-start.5 = (f32[6,2,1024]{2,1,0:T(2,128)}, f32[6,2,1024]{2,1,0:T(2,128)S(1)}, u32[]{:S(2)}) copy-start(f32[6,2,1024]{2,1,0:T(2,128)S(1)} %get-tuple-element.64.refs_8_) | copy-start | bytes 147460
  111.6 5.5 %copy-start.1 = (bf16[512,1536]{1,0:T(8,128)(2,1)S(1)}, bf16[512,1536]{1,0:T(8,128)(2,1)}, u32[]{:S(2)}) copy-start(bf16[512,1536]{1,0:T(8,128)(2,1)} %refs_7_.1) | copy-start | bytes 4718596
  111.6 5.4 %copy-start.2 = (bf16[512,1536]{1,0:T(8,128)(2,1)S(1)}, bf16[512,1536]{1,0:T(8,128)(2,1)}, u32[]{:S(2)}) copy-start(bf16[512,1536]{1,0:T(8,128)(2,1)} %get-tuple-element.51.second_ref.cot_other) | copy-start | bytes 4718596
  116.5 35.6 %collective-permute-start = (bf16[512,1536]{1,0:T(8,128)(2,1)}, bf16[512,1536]{1,0:T(8,128)(2,1)}, u32[]{:S(2)}, u32[]{:S(2)}) collective-permute-start(bf16[512,1536]{1,0:T(8,128)(2,1)} %convolution_convert_fusion), channel_id=1, source_target_pairs={{0,1},{1,0},{2,3},{3,2},{4,5},{5,4},{6,7},{7,6},{8,9},{9,8},{10,11... | collective-permute-start | bytes 4718600 | tf_op jit(solution)/shard_map/ppermute | solution.py:1361
  119.2 1.6 copy-start
  124.7 30.0 %copy-start.16 = (f32[1536]{0:T(1024)S(1)}, f32[1536]{0:T(1024)}, u32[]{:S(2)}) copy-start(f32[1536]{0:T(1024)} %param.15) | copy-start | bytes 18436
  154.2 34.3 %copy-start.6 = (bf16[512,1536]{1,0:T(8,128)(2,1)}, bf16[512,1536]{1,0:T(8,128)(2,1)S(1)}, u32[]{:S(2)}) copy-start(bf16[512,1536]{1,0:T(8,128)(2,1)S(1)} %add_convert_fusion.x_own.refs_8_) | copy-start | bytes 4718596
  154.2 34.3 %collective-permute-start.1 = (bf16[512,1536]{1,0:T(8,128)(2,1)S(1)}, bf16[512,1536]{1,0:T(8,128)(2,1)S(1)}, u32[]{:S(2)}, u32[]{:S(2)}) collective-permute-start(bf16[512,1536]{1,0:T(8,128)(2,1)S(1)} %add_convert_fusion.x_own.refs_8_), channel_id=1, source_target_pairs={{0,1},{1,0},{2,3},{3,2},{4,5},{5,4},{6,7},{7,6},{8,9},{9,8},{10,11... | collective-permute-start | bytes 4718600 | tf_op jit(solution)/shard_map/ppermute | solution.py:1361
  188.5 1.2 copy-start.17
  333.9 122.1 %copy-start.11 = (f32[96,1536]{1,0:T(8,128)S(1)}, f32[96,1536]{1,0:T(8,128)}, u32[]{:S(2)}) copy-start(f32[96,1536]{1,0:T(8,128)} %get-tuple-element.76) | copy-start | bytes 1769476
  453.2 5.7 %copy-start.7 = (bf16[512,1536]{1,0:T(8,128)(2,1)S(1)}, bf16[512,1536]{1,0:T(8,128)(2,1)}, u32[]{:S(2)}) copy-start(bf16[512,1536]{1,0:T(8,128)(2,1)} %get-tuple-element.94) | copy-start | bytes 4718596
  454.8 3.5 collective-permute-start.2
  456.1 4.0 copy-start.8
  460.0 1.2 copy-start.15
  460.0 1.9 copy-start.14
  460.0 2.6 copy-start.13
  460.1 3.3 copy-start.12
  460.1 4.0 copy-start.10
  461.2 3.8 copy-start.9
Sparse Core Ops, SparseCore 0:
  89.9 98.1 all-gather.1

commit v9 on v8

--- a/solution.py
+++ b/solution.py
@@ -1190,9 +1190,9 @@
 
 def gather_project_kernel(gather, per, *refs):
     shards, (tokens, cot, gain_ref, depths_ref), later = refs[:4], refs[4:8], refs[8:11]
-    w_hbm, qkv_ref, turned_ref, rows_hbm, cot_other, cos_ref, sin_ref, joined = refs[11:19]
-    w_ref, rows_ref, normed_ref, x_sems, row_sems, w_sems, join_sems = refs[19:26]
-    gather.bind(refs[26:])
+    w_hbm, qkv_ref, turned_ref, rows_hbm, cot_other, cot_rest, cos_ref, sin_ref, joined = refs[11:20]
+    w_ref, rows_ref, normed_ref, x_sems, row_sems, w_sems, join_sems = refs[20:27]
+    gather.bind(refs[27:])
     step = pl.program_id(0)
     side = gather.side
     across = (gather.me, 1 - side)
@@ -1204,7 +1204,8 @@
         return remote(tokens, rows_ref.at[side], x_sems.at[0], across)
 
     def cot_copy():
-        return remote(cot, cot_other, x_sems.at[1], across)
+        rows = pl.ds(0, cot_other.shape[0])
+        return remote(cot.at[rows], cot_other, x_sems.at[1], across)
 
     def token_load():
         return pltpu.make_async_copy(tokens, rows_ref.at[side], row_sems.at[0])
@@ -1222,6 +1223,8 @@
             span = pl.ds(column, shard.shape[1])
             yield pltpu.make_async_copy(shard, joined.at[:, span], join_sems.at[nth])
             column += shard.shape[1]
+        rows = pl.ds(cot_other.shape[0], cot_rest.shape[0])
+        yield pltpu.make_async_copy(cot.at[rows], cot_rest, join_sems.at[len(later)])
 
     @pl.when(step == 1)
     def _():
@@ -1306,7 +1309,7 @@
             w_store(block).wait()
 
 
-def gather_project(devices, shards, tokens, cot, gain, depths, later):
+def gather_project(devices, shards, tokens, cot, cot_rows, gain, depths, later):
     half, d = tokens.shape
     rows, width = shards[0].shape
     total = len(shards) * width
@@ -1327,6 +1330,7 @@
             resident((d, 2 * half)),
             left_there,
             left_there,
+            left_there,
             resident((2, half, LANES)),
             resident((2, half, LANES)),
             left_there,
@@ -1336,7 +1340,8 @@
             jax.ShapeDtypeStruct((2, half, 3 * width), BF),
             jax.ShapeDtypeStruct((d, 2 * half), BF),
             jax.ShapeDtypeStruct((2, half, d), BF),
-            jax.ShapeDtypeStruct((half, d), BF),
+            jax.ShapeDtypeStruct((cot_rows, d), BF),
+            jax.ShapeDtypeStruct((half - cot_rows, d), BF),
             jax.ShapeDtypeStruct((2, half, LANES), F32),
             jax.ShapeDtypeStruct((2, half, LANES), F32),
             jax.ShapeDtypeStruct((rows, sum(shard.shape[1] for shard in later)), BF),
@@ -1348,13 +1353,39 @@
             pltpu.SemaphoreType.DMA((2, 2)),
             pltpu.SemaphoreType.DMA((2,)),
             pltpu.SemaphoreType.DMA((count,)),
-            pltpu.SemaphoreType.DMA((len(later),)),
+            pltpu.SemaphoreType.DMA((len(later) + 1,)),
         ]
         + gather.scratch(),
         compiler_params=remote_settings(2),
         cost_estimate=cost(12 * half * d * width, 2 * d * total),
         name="gather_project",
     )(*shards, tokens, cot, gain, depths, *later)
+
+
+def project_out_kernel(half_ref, attended_ref, w_ref, out_ref):
+    out_ref[...] = nt(attended_ref[...], w_ref[...]).astype(BF)
+
+
+def project_out(attended, w, half, cols=512):
+    _, rows, width = attended.shape
+    d = w.shape[0]
+    part = w.shape[1] // width - 1
+    return pl.pallas_call(
+        project_out_kernel,
+        grid_spec=pltpu.PrefetchScalarGridSpec(
+            num_scalar_prefetch=1,
+            grid=(d // cols,),
+            in_specs=[
+                pl.BlockSpec((None, rows, width), lambda j, half_ref: (half_ref[0], 0, 0)),
+                pl.BlockSpec((cols, width), lambda j, half_ref: (j, part)),
+            ],
+            out_specs=pl.BlockSpec((rows, cols), lambda j, half_ref: (0, j)),
+        ),
+        out_shape=jax.ShapeDtypeStruct((rows, d), BF),
+        compiler_params=settings(32),
+        cost_estimate=cost(2 * rows * d * width, 2 * d * (width + rows)),
+        name="project_out",
+    )(half.reshape(1), attended, w)
 
 
 def swap(x):
@@ -1382,14 +1413,10 @@
     seg_rows = length // parents.shape[1]
     mine = lax.axis_index("tensor")
     own_start = mine * half
-    other_start = (1 - mine) * half
 
     def own_rows(full):
         return lax.dynamic_slice_in_dim(full, own_start, half, 0)
 
-    def other_rows(full):
-        return lax.dynamic_slice_in_dim(full, other_start, half, 0)
-
     def gather(shard):
         return lax.all_gather(shard, "dp", axis=0, tiled=True)
 
@@ -1399,26 +1426,30 @@
     devices = lax.axis_size("dp")
     bias, depths = tree_tables(parents[0], seg_rows)
 
-    first, qkv, norm_turned, rows_all, cot_other, cosine, sine, second_shard = gather_project(
+    cut = half // 2
+    first, qkv, norm_turned, rows_all, cot_first, cot_rest, cosine, sine, second_shard = gather_project(
         devices,
         (query_weight, key_weight, value_weight, output_weight.T),
         tokens,
         cotangent,
+        cut,
         attn_row,
         depths,
         (gate_weight, up_weight, down_weight.T),
     )
     second = gather(second_shard)
+    cot_rest = swap(cot_rest)
     qkv = qkv.reshape(length, 3 * width)
     rows_all = rows_all.reshape(length, d)
     cosine, sine = cosine.reshape(length, LANES), sine.reshape(length, LANES)
 
     attended, lse = attend(qkv, bias, width, seg_rows)
     out_turned = first[:, 3 * width :]
-    send = nt(other_rows(attended), out_turned).astype(BF)
-    send, cot_source = lax.optimization_barrier((send, cot_other))
+    send = project_out(attended.reshape(2, half, width), first, 1 - mine)
+    send, cot_first, cot_rest = lax.optimization_barrier((send, cot_first, cot_rest))
+    cot_other = jnp.concatenate([cot_first, cot_rest], axis=0)
     received = swap(send)
-    received, cot_turned = lax.optimization_barrier((received, turn_pair(cotangent, cot_source)))
+    received, cot_turned = lax.optimization_barrier((received, turn_pair(cotangent, cot_other)))
     middle = (
         tokens.astype(F32) + nt(own_rows(attended), out_turned) + received.astype(F32)
     ).astype(BF)

time: 473 us -> 468 us (0.989)
  matrix products: 8.72 us -> 3.74 us
    pallas_call x1, Pallas kernels: 79.1 us -> 72.7 us  [gather_project(): pl.pallas_call(functools.partial(gather_project_kernel, gather, per), gri...]
    dot_general x2 -> x1, matrix products: 8.72 us -> 3.74 us  [nt(): lax.dot_general(a, b, (((1,), (1,)), ((), ())), preferred_element_type=F32)]
    ppermute x3 -> x4, waiting for transfers between devices: 60.8 us -> 62.7 us  [swap(): return lax.ppermute(x, 'tensor', [(0, 1), (1, 0)])]
    unnamed x44 -> x53, local copies, waits for them, and re-layouts: 9.8 us -> 10.4 us
  transfers between devices with their start and end apart: 4 -> 5, of which waited for: 3 -> 2; matrix products, arithmetic and copies ran while one was open for 3% -> 2% of each run, Pallas kernels for 5% -> 6%
where the time goes in v9:
time: 468 us
  Pallas kernels  362 us (77%)
  waiting for transfers between devices  62.7 us (13%)
  local copies, waits for them, and re-layouts  14.7 us (3%)
  between operations  14.4 us (3%)
  other arithmetic  6.46 us (1%)
    pallas_call x1, Pallas kernels, attention_scatter(): pl.pallas_call(functools.partial(attention_scatter_kernel, scatter, per,...  120 us
    pallas_call x1, Pallas kernels, ffn_scatter(): pl.pallas_call(functools.partial(ffn_scatter_kernel, scatter, per, sent,...  87.7 us
    pallas_call x1, Pallas kernels, gather_project(): pl.pallas_call(functools.partial(gather_project_kernel, gather, per), gri...  72.7 us
    ppermute x4, waiting for transfers between devices, swap(): return lax.ppermute(x, 'tensor', [(0, 1), (1, 0)])  62.7 us
    pallas_call x1, Pallas kernels, ffn(): pl.pallas_call(ffn_kernel, grid=(2, steps), in_specs=[resident((rows, d))...  54.3 us
    pallas_call x1, Pallas kernels, attend(): pl.pallas_call(functools.partial(attend_kernel, block, seg_rows), grid=(g...  21.7 us
    unnamed x53, local copies, waits for them, and re-layouts  10.4 us
  transfers between devices with their start and end apart: 5, of which 2 were waited for; matrix products, arithmetic and copies ran while one was open for 2% of the time, Pallas kernels for 6%

profile of v9, /device:TPU:0, one launch (start us, length us, event | category | flops | bytes accessed | tf_op | source)
XLA Modules:
  0.0 467.7 jit_solution(9148367524310367890)
XLA Ops:
  7.2 1.3 broadcast_in_dim.12.refs_6_.refs_2_
  8.5 0.7 fusion.13
  10.7 72.7 %gather_project.1 = (bf16[1536,3072]{1,0:T(8,128)(2,1)}, bf16[2,512,2304]{2,1,0:T(8,128)(2,1)}, bf16[1536,1024]{1,0:T(8,128)(2,1)}, bf16[2,512,1536]{2,1,0:T(8,1...) custom-call(bf16[96,768]{1,0:T(8,128)(2,1)} %refs_0_.1, ...), custom_call_target="tpu_custom_call" | custom-call | flops 7247757312 | bytes 9437184 | tf_op jit(solution)/shard_map/gather_project/pallas_call | solution.py:1321
  83.5 1.6 collective-permute-start
  85.3 21.7 %attend.1 = (bf16[1024,768]{1,0:T(8,128)(2,1)S(1)}, f32[6,2,1024]{2,1,0:T(2,128)S(1)}) custom-call(bf16[1024,2304]{1,0:T(8,128)(2,1)} %bitcast.39, bf16[1024,2304]{1,0:T(8,128)(2,1)} %bitcast.40, bf16[1024,2304]{1,0:T(8,128)(2,1)} %bitcast.41, f32[8,1024]{1,0:T(8,128)S(1)} %broadcast_bitcast_fusion.bias_ref.refs_9_), custom_call_target="tpu_custom_call" | custom-call | flops 6442450944 | bytes 6291456 | tf_op jit(solution)/shard_map/attend/pallas_call | solution.py:150
  107.0 2.9 project_out.1
  110.5 3.7 convolution_add_fusion
  114.4 1.4 copy-done.1
  115.7 2.2 turn_pair.1.refs_0_
  117.9 28.5 %collective-permute-done.1 = bf16[512,1536]{1,0:T(8,128)(2,1)} collective-permute-done((bf16[512,1536]{1,0:T(8,128)(2,1)}, bf16[512,1536]{1,0:T(8,128)(2,1)}, u32[]{:S(2)}, u32[]{:S(2)}) %collective-permute-start.1) | collective-permute-done | bytes 1572896 | tf_op jit(solution)/shard_map/ppermute | solution.py:1392
  146.4 1.9 add_convert_fusion.x_own.refs_8_
  149.5 34.2 %collective-permute-done.2.x_other = bf16[512,1536]{1,0:T(8,128)(2,1)S(1)} collective-permute-done((bf16[512,1536]{1,0:T(8,128)(2,1)S(1)}, bf16[512,1536]{1,0:T(8,128)(2,1)S(1)}, u32[]{:S(2)}, u32[]{:S(2)}) %collective-permute-start.2) | collective-permute-done | bytes 1572896 | tf_op jit(solution)/shard_map/ppermute | solution.py:1392
  183.7 1.1 copy-done.18
  184.8 54.3 %ffn.1 = (bf16[2,3,512,2048]{3,2,1,0:T(8,128)(2,1)}, bf16[2,512,1536]{2,1,0:T(8,128)(2,1)}, bf16[2,512,1536]{2,1,0:T(8,128)(2,1)}, f32[8,1536]{1,0:T(8,128)}, bf16[512,1536]{1,0:T(8,128)(2,1)}) custom-call(bf16[512,1536]{1,0:T(8,128)(2,1)} %copy-done.6, bf16[512,1536]{1,0:T(8,128)(2,1)} %copy-done.18, bf16[512,1536]{1,0:T(8,128)(2,1)} %refs_7_.1, ...), custom_call_target="tpu_custom_call" | custom-call | flops 32212254720 | bytes 62914560 | tf_op jit(solution)/shard_map/ffn/pallas_call | solution.py:322
  239.2 87.7 %ffn_scatter.1 = (f32[96,2048]{1,0:T(8,128)}, f32[96,1536]{1,0:T(8,128)}, f32[16,256]{1,0:T(8,128)}, bf16[1536,2560]{1,0:T(8,128)(2,1)}, bf16[2,512,1536]{2,1,0:...) custom-call(bf16[1536,1024]{1,0:T(8,128)(2,1)} %copy-done, ...), custom_call_target="tpu_custom_call" | custom-call | flops 25769803776 | bytes 15728640 | tf_op jit(solution)/shard_map/ffn_scatter/pallas_call | solution.py:802
  326.9 120.1 %attention_scatter.1 = (f32[96,768]{1,0:T(8,128)}, f32[96,768]{1,0:T(8,128)}, f32[96,768]{1,0:T(8,128)}, f32[96,768]{1,0:T(8,128)}, f32[16,256]{1,0:T(8,128)}, /...) custom-call(bf16[1536,1024]{1,0:T(8,128)(2,1)} %get-tuple-element.65.refs_0_, ...), custom_call_target="tpu_custom_call" | custom-call | flops 33017561088 | bytes 31457280 | tf_op jit(solution)/shard_map/attention_scatter/pallas_call | solution.py:1052
  447.1 0.8 slice.11
  448.6 1.5 collective-permute-start.3
  450.7 1.9 pad_maximum_fusion
  453.1 1.1 copy.43
  454.3 0.8 copy-done.8
  455.1 1.1 copy.44
  459.1 0.9 copy.49
  460.0 0.9 copy.50
  (81 shorter events, 8.3 us)
Async XLA Ops:
  7.2 176.5 %all-gather.2.cloned.1.call-start = ((), (), s32[]{:S(2)}) async-start(), calls=%async_computation | async-start | bytes 20054016 | tf_op jit(solution)/shard_map/all_gather | solution.py:1421
  83.5 26.5 %collective-permute-start = (bf16[256,1536]{1,0:T(8,128)(2,1)}, bf16[256,1536]{1,0:T(8,128)(2,1)S(1)}, u32[]{:S(2)}, u32[]{:S(2)}) collective-permute-start(bf16[256,1536]{1,0:T(8,128)(2,1)} %get-tuple-element.52), channel_id=1, source_target_pairs={{0,1},{1,0},{2,3},{3,2},{4,5},{5,4},{6,7},{7,6},{8,9},{9,8},{10,11... | collective-permute-start | bytes 2359304 | tf_op jit(solution)/shard_map/ppermute | solution.py:1392
  85.3 21.7 %copy-start.4 = (f32[8,1024]{1,0:T(8,128)}, f32[8,1024]{1,0:T(8,128)S(1)}, u32[]{:S(2)}) copy-start(f32[8,1024]{1,0:T(8,128)S(1)} %broadcast_bitcast_fusion.bias_ref.refs_9_) | copy-start | bytes 98308
  85.3 21.7 %slice-start = ((s8[9437184]{0:T(1024)(128)(4,1)}), s8[4194304]{0:T(1024)(128)(4,1)S(1)}, s32[]{:S(2)}) async-start(s8[9437184]{0:T(1024)(128)(4,1)} %bitcast.30), calls=%async_computation.1 | async-start | bytes 8388608
  85.3 21.7 %slice-start.1 = ((s8[9437184]{0:T(1024)(128)(4,1)}), s8[4194304]{0:T(1024)(128)(4,1)S(1)}, s32[]{:S(2)}) async-start(s8[9437184]{0:T(1024)(128)(4,1)} %bitcast.30), calls=%async_computation.2 | async-start | bytes 8388608
  85.3 21.7 %slice-start.2 = ((s8[9437184]{0:T(1024)(128)(4,1)}), s8[1048576]{0:T(1024)(128)(4,1)S(1)}, s32[]{:S(2)}) async-start(s8[9437184]{0:T(1024)(128)(4,1)} %bitcast.30), calls=%async_computation.3 | async-start | bytes 2097152
  106.9 3.0 copy-start.5
  107.0 3.5 copy-start.3
  109.9 36.5 %collective-permute-start.1 = (bf16[512,1536]{1,0:T(8,128)(2,1)}, bf16[512,1536]{1,0:T(8,128)(2,1)}, u32[]{:S(2)}, u32[]{:S(2)}) collective-permute-start(bf16[512,1536]{1,0:T(8,128)(2,1)} %project_out.1), channel_id=1, source_target_pairs={{0,1},{1,0},{2,3},{3,2},{4,5},{5,4},{6,7},{7,6},{8,9},{9,8},{10,11... | collective-permute-start | bytes 4718600 | tf_op jit(solution)/shard_map/ppermute | solution.py:1392
  110.5 3.8 copy-start.10
  115.7 2.2 copy-start.2
  117.9 30.4 %copy-start = (bf16[1536,1024]{1,0:T(8,128)(2,1)}, bf16[1536,1024]{1,0:T(8,128)(2,1)S(1)}, u32[]{:S(2)}) copy-start(bf16[1536,1024]{1,0:T(8,128)(2,1)S(1)} %turn_pair.1.refs_0_) | copy-start | bytes 9437188
  117.9 31.0 %copy-start.17 = (f32[1536]{0:T(1024)S(1)}, f32[1536]{0:T(1024)}, u32[]{:S(2)}) copy-start(f32[1536]{0:T(1024)} %param.15) | copy-start | bytes 18436
  148.3 35.4 %copy-start.6 = (bf16[512,1536]{1,0:T(8,128)(2,1)}, bf16[512,1536]{1,0:T(8,128)(2,1)S(1)}, u32[]{:S(2)}) copy-start(bf16[512,1536]{1,0:T(8,128)(2,1)S(1)} %add_convert_fusion.x_own.refs_8_) | copy-start | bytes 4718596
  148.4 35.3 %collective-permute-start.2 = (bf16[512,1536]{1,0:T(8,128)(2,1)S(1)}, bf16[512,1536]{1,0:T(8,128)(2,1)S(1)}, u32[]{:S(2)}, u32[]{:S(2)}) collective-permute-start(bf16[512,1536]{1,0:T(8,128)(2,1)S(1)} %add_convert_fusion.x_own.refs_8_), channel_id=1, source_target_pairs={{0,1},{1,0},{2,3},{3,2},{4,5},{5,4},{6,7},{7,6},{8,9},{9,8},{10,11... | collective-permute-start | bytes 4718600 | tf_op jit(solution)/shard_map/ppermute | solution.py:1392
  326.9 123.8 %copy-start.12 = (f32[96,1536]{1,0:T(8,128)S(1)}, f32[96,1536]{1,0:T(8,128)}, u32[]{:S(2)}) copy-start(f32[96,1536]{1,0:T(8,128)} %get-tuple-element.80) | copy-start | bytes 1769476
  447.0 6.1 %copy-start.7 = (bf16[512,1536]{1,0:T(8,128)(2,1)S(1)}, bf16[512,1536]{1,0:T(8,128)(2,1)}, u32[]{:S(2)}) copy-start(bf16[512,1536]{1,0:T(8,128)(2,1)} %get-tuple-element.98) | copy-start | bytes 4718596
  448.6 3.9 collective-permute-start.3
  453.1 2.0 copy-start.8
  455.1 1.9 copy-start.15
  455.1 2.6 copy-start.14
  456.3 2.2 copy-start.13
  456.3 2.9 copy-start.11
  457.0 3.0 copy-start.9
  (3 other events, 3.8 us)
Sparse Core Ops, SparseCore 0:
  83.6 98.6 all-gather.1

commit v10 on v9

--- a/solution.py
+++ b/solution.py
@@ -362,7 +362,7 @@
 MESH = pl.DeviceIdType.MESH
 QUARTERS = 4
 EARLY = 3
-UP_SENT = 6
+UP_SENT = 7
 GAIN_ROWS = 16
 
 
@@ -1322,7 +1322,7 @@
         functools.partial(gather_project_kernel, gather, per),
         grid=(gather.steps,),
         in_specs=[left_there] * 6
-        + [resident((1, d)), pl.BlockSpec(memory_space=pltpu.SMEM)]
+        + [resident((d,)), pl.BlockSpec(memory_space=pltpu.SMEM)]
         + [left_there] * len(later),
         out_specs=[
             left_there,
@@ -1433,7 +1433,7 @@
         tokens,
         cotangent,
         cut,
-        attn_row,
+        attn_gain,
         depths,
         (gate_weight, up_weight, down_weight.T),
     )

time: 468 us -> 466 us (level)
    unnamed x53 -> x55, local copies, waits for them, and re-layouts: 10.4 us -> 10.4 us
where the time goes in v10:
time: 466 us
  Pallas kernels  361 us (77%)
  waiting for transfers between devices  62.1 us (13%)
  between operations  14.4 us (3%)
  local copies, waits for them, and re-layouts  14 us (3%)
  other arithmetic  6.45 us (1%)
    pallas_call x1, Pallas kernels, attention_scatter(): pl.pallas_call(functools.partial(attention_scatter_kernel, scatter, per,...  118 us
    pallas_call x1, Pallas kernels, ffn_scatter(): pl.pallas_call(functools.partial(ffn_scatter_kernel, scatter, per, sent,...  89 us
    pallas_call x1, Pallas kernels, gather_project(): pl.pallas_call(functools.partial(gather_project_kernel, gather, per), gri...  72.8 us
    ppermute x4, waiting for transfers between devices, swap(): return lax.ppermute(x, 'tensor', [(0, 1), (1, 0)])  62.1 us
    pallas_call x1, Pallas kernels, ffn(): pl.pallas_call(ffn_kernel, grid=(2, steps), in_specs=[resident((rows, d))...  54.4 us
    pallas_call x1, Pallas kernels, attend(): pl.pallas_call(functools.partial(attend_kernel, block, seg_rows), grid=(g...  21.7 us
    unnamed x55, local copies, waits for them, and re-layouts  10.4 us
  transfers between devices with their start and end apart: 5, of which 2 were waited for; matrix products, arithmetic and copies ran while one was open for 2% of the time, Pallas kernels for 6%

profile of v10, /device:TPU:0, one launch (start us, length us, event | category | flops | bytes accessed | tf_op | source)
XLA Modules:
  0.0 466.0 jit_solution(3925137171538686967)
XLA Ops:
  7.2 0.7 fusion.13
  9.4 72.8 %gather_project.1 = (bf16[1536,3072]{1,0:T(8,128)(2,1)}, bf16[2,512,2304]{2,1,0:T(8,128)(2,1)}, bf16[1536,1024]{1,0:T(8,128)(2,1)}, bf16[2,512,1536]{2,1,0:T(8,1...) custom-call(bf16[96,768]{1,0:T(8,128)(2,1)} %refs_0_.1, ...), custom_call_target="tpu_custom_call" | custom-call | flops 7247757312 | bytes 9437184 | tf_op jit(solution)/shard_map/gather_project/pallas_call | solution.py:1321
  82.2 1.6 collective-permute-start
  84.0 21.7 %attend.1 = (bf16[1024,768]{1,0:T(8,128)(2,1)S(1)}, f32[6,2,1024]{2,1,0:T(2,128)S(1)}) custom-call(bf16[1024,2304]{1,0:T(8,128)(2,1)} %bitcast.39, bf16[1024,2304]{1,0:T(8,128)(2,1)} %bitcast.40, bf16[1024,2304]{1,0:T(8,128)(2,1)} %bitcast.41, f32[8,1024]{1,0:T(8,128)S(1)} %broadcast_bitcast_fusion.bias_ref.refs_9_), custom_call_target="tpu_custom_call" | custom-call | flops 6442450944 | bytes 6291456 | tf_op jit(solution)/shard_map/attend/pallas_call | solution.py:150
  105.7 2.9 project_out.1
  109.2 3.7 convolution_add_fusion
  113.1 1.4 copy-done.1
  114.5 2.2 turn_pair.1.refs_0_
  116.7 28.5 %collective-permute-done.1 = bf16[512,1536]{1,0:T(8,128)(2,1)} collective-permute-done((bf16[512,1536]{1,0:T(8,128)(2,1)}, bf16[512,1536]{1,0:T(8,128)(2,1)}, u32[]{:S(2)}, u32[]{:S(2)}) %collective-permute-start.1) | collective-permute-done | bytes 1572896 | tf_op jit(solution)/shard_map/ppermute | solution.py:1392
  145.1 1.9 add_convert_fusion.x_own.refs_8_
  148.8 33.6 %collective-permute-done.2.x_other = bf16[512,1536]{1,0:T(8,128)(2,1)S(1)} collective-permute-done((bf16[512,1536]{1,0:T(8,128)(2,1)S(1)}, bf16[512,1536]{1,0:T(8,128)(2,1)S(1)}, u32[]{:S(2)}, u32[]{:S(2)}) %collective-permute-start.2) | collective-permute-done | bytes 1572896 | tf_op jit(solution)/shard_map/ppermute | solution.py:1392
  182.4 1.1 copy-done.19
  183.6 54.4 %ffn.1 = (bf16[2,3,512,2048]{3,2,1,0:T(8,128)(2,1)}, bf16[2,512,1536]{2,1,0:T(8,128)(2,1)}, bf16[2,512,1536]{2,1,0:T(8,128)(2,1)}, f32[8,1536]{1,0:T(8,128)}, bf16[512,1536]{1,0:T(8,128)(2,1)}) custom-call(bf16[512,1536]{1,0:T(8,128)(2,1)} %copy-done.6, bf16[512,1536]{1,0:T(8,128)(2,1)} %copy-done.19, bf16[512,1536]{1,0:T(8,128)(2,1)} %refs_7_.1, ...), custom_call_target="tpu_custom_call" | custom-call | flops 32212254720 | bytes 62914560 | tf_op jit(solution)/shard_map/ffn/pallas_call | solution.py:322
  238.0 89.0 %ffn_scatter.1 = (f32[96,2048]{1,0:T(8,128)}, f32[96,1792]{1,0:T(8,128)}, f32[16,256]{1,0:T(8,128)}, bf16[1536,2304]{1,0:T(8,128)(2,1)}, bf16[2,512,1536]{2,1,0:...) custom-call(bf16[1536,1024]{1,0:T(8,128)(2,1)} %copy-done, ...), custom_call_target="tpu_custom_call" | custom-call | flops 25769803776 | bytes 15728640 | tf_op jit(solution)/shard_map/ffn_scatter/pallas_call | solution.py:802
  327.0 118.2 %attention_scatter.1 = (f32[96,768]{1,0:T(8,128)}, f32[96,768]{1,0:T(8,128)}, f32[96,768]{1,0:T(8,128)}, f32[96,768]{1,0:T(8,128)}, f32[16,256]{1,0:T(8,128)}, /...) custom-call(bf16[1536,1024]{1,0:T(8,128)(2,1)} %get-tuple-element.65.refs_0_, ...), custom_call_target="tpu_custom_call" | custom-call | flops 33017561088 | bytes 31457280 | tf_op jit(solution)/shard_map/attention_scatter/pallas_call | solution.py:1052
  445.3 0.8 slice.11
  446.2 1.5 collective-permute-start.3
  448.4 1.8 pad_maximum_fusion
  451.4 1.1 copy.43
  452.5 0.8 copy-done.8
  453.4 1.1 copy.44
  455.2 0.7 copy.46
  457.4 0.9 copy.49
  458.3 0.9 copy.50
  (83 shorter events, 8.2 us)
Async XLA Ops:
  7.2 175.3 %all-gather.2.cloned.1.call-start = ((), (), s32[]{:S(2)}) async-start(), calls=%async_computation | async-start | bytes 20054016 | tf_op jit(solution)/shard_map/all_gather | solution.py:1421
  82.2 26.5 %collective-permute-start = (bf16[256,1536]{1,0:T(8,128)(2,1)}, bf16[256,1536]{1,0:T(8,128)(2,1)S(1)}, u32[]{:S(2)}, u32[]{:S(2)}) collective-permute-start(bf16[256,1536]{1,0:T(8,128)(2,1)} %get-tuple-element.52), channel_id=1, source_target_pairs={{0,1},{1,0},{2,3},{3,2},{4,5},{5,4},{6,7},{7,6},{8,9},{9,8},{10,11... | collective-permute-start | bytes 2359304 | tf_op jit(solution)/shard_map/ppermute | solution.py:1392
  84.0 21.7 %copy-start.4 = (f32[8,1024]{1,0:T(8,128)}, f32[8,1024]{1,0:T(8,128)S(1)}, u32[]{:S(2)}) copy-start(f32[8,1024]{1,0:T(8,128)S(1)} %broadcast_bitcast_fusion.bias_ref.refs_9_) | copy-start | bytes 98308
  84.0 21.7 %slice-start = ((s8[9437184]{0:T(1024)(128)(4,1)}), s8[4194304]{0:T(1024)(128)(4,1)S(1)}, s32[]{:S(2)}) async-start(s8[9437184]{0:T(1024)(128)(4,1)} %bitcast.30), calls=%async_computation.1 | async-start | bytes 8388608
  84.0 21.7 %slice-start.1 = ((s8[9437184]{0:T(1024)(128)(4,1)}), s8[4194304]{0:T(1024)(128)(4,1)S(1)}, s32[]{:S(2)}) async-start(s8[9437184]{0:T(1024)(128)(4,1)} %bitcast.30), calls=%async_computation.2 | async-start | bytes 8388608
  84.0 21.7 %slice-start.2 = ((s8[9437184]{0:T(1024)(128)(4,1)}), s8[1048576]{0:T(1024)(128)(4,1)S(1)}, s32[]{:S(2)}) async-start(s8[9437184]{0:T(1024)(128)(4,1)} %bitcast.30), calls=%async_computation.3 | async-start | bytes 2097152
  105.7 3.0 copy-start.5
  105.7 3.5 copy-start.3
  108.7 36.5 %collective-permute-start.1 = (bf16[512,1536]{1,0:T(8,128)(2,1)}, bf16[512,1536]{1,0:T(8,128)(2,1)}, u32[]{:S(2)}, u32[]{:S(2)}) collective-permute-start(bf16[512,1536]{1,0:T(8,128)(2,1)} %project_out.1), channel_id=1, source_target_pairs={{0,1},{1,0},{2,3},{3,2},{4,5},{5,4},{6,7},{7,6},{8,9},{9,8},{10,11... | collective-permute-start | bytes 4718600 | tf_op jit(solution)/shard_map/ppermute | solution.py:1392
  109.2 3.8 copy-start.10
  114.5 2.2 copy-start.2
  116.6 30.4 %copy-start = (bf16[1536,1024]{1,0:T(8,128)(2,1)}, bf16[1536,1024]{1,0:T(8,128)(2,1)S(1)}, u32[]{:S(2)}) copy-start(bf16[1536,1024]{1,0:T(8,128)(2,1)S(1)} %turn_pair.1.refs_0_) | copy-start | bytes 9437188
  116.6 31.0 %copy-start.17 = (f32[1536]{0:T(1024)S(1)}, f32[1536]{0:T(1024)}, u32[]{:S(2)}) copy-start(f32[1536]{0:T(1024)} %refs_6_.1) | copy-start | bytes 18436
  116.7 31.6 %copy-start.18 = (f32[1536]{0:T(1024)S(1)}, f32[1536]{0:T(1024)}, u32[]{:S(2)}) copy-start(f32[1536]{0:T(1024)} %param.15) | copy-start | bytes 18436
  147.1 35.4 %copy-start.6 = (bf16[512,1536]{1,0:T(8,128)(2,1)}, bf16[512,1536]{1,0:T(8,128)(2,1)S(1)}, u32[]{:S(2)}) copy-start(bf16[512,1536]{1,0:T(8,128)(2,1)S(1)} %add_convert_fusion.x_own.refs_8_) | copy-start | bytes 4718596
  147.1 35.3 %collective-permute-start.2 = (bf16[512,1536]{1,0:T(8,128)(2,1)S(1)}, bf16[512,1536]{1,0:T(8,128)(2,1)S(1)}, u32[]{:S(2)}, u32[]{:S(2)}) collective-permute-start(bf16[512,1536]{1,0:T(8,128)(2,1)S(1)} %add_convert_fusion.x_own.refs_8_), channel_id=1, source_target_pairs={{0,1},{1,0},{2,3},{3,2},{4,5},{5,4},{6,7},{7,6},{8,9},{9,8},{10,11... | collective-permute-start | bytes 4718600 | tf_op jit(solution)/shard_map/ppermute | solution.py:1392
  327.0 121.4 %copy-start.12 = (f32[96,1792]{1,0:T(8,128)S(1)}, f32[96,1792]{1,0:T(8,128)}, u32[]{:S(2)}) copy-start(f32[96,1792]{1,0:T(8,128)} %get-tuple-element.80) | copy-start | bytes 2064388
  445.3 6.1 %copy-start.7 = (bf16[512,1536]{1,0:T(8,128)(2,1)S(1)}, bf16[512,1536]{1,0:T(8,128)(2,1)}, u32[]{:S(2)}) copy-start(bf16[512,1536]{1,0:T(8,128)(2,1)} %get-tuple-element.98) | copy-start | bytes 4718596
  446.2 4.6 collective-permute-start.3
  451.4 2.0 copy-start.8
  453.4 2.6 copy-start.14
  454.5 2.2 copy-start.13
  454.5 2.9 copy-start.11
  455.2 3.0 copy-start.9
  (4 other events, 5.7 us)
Sparse Core Ops, SparseCore 0:
  82.3 98.6 all-gather.1

commit v11 on v10

--- a/solution.py
+++ b/solution.py
@@ -1104,7 +1104,7 @@
     def __init__(self, devices, rows, count):
         self.devices, self.rows, self.count = devices, rows, count
         self.stages = devices.bit_length() - 1
-        self.lags = [2] * (self.stages - 1) + [1]
+        self.lags = [2] + [3] * (self.stages - 2) + [1]
         self.starts = [sum(self.lags[:t]) for t in range(self.stages + 1)]
         self.steps = count + self.starts[-1]
 

time: 466 us -> 463 us (level)
  no operation moved by 1% of the time
where the time goes in v11:
time: 463 us; the launch traced here: 462 us
  Pallas kernels  358 us (77%)
  waiting for transfers between devices  62.1 us (13%)
  between operations  14.4 us (3%)
  local copies, waits for them, and re-layouts  14 us (3%)
  other arithmetic  6.42 us (1%)
    pallas_call x1, Pallas kernels, attention_scatter(): pl.pallas_call(functools.partial(attention_scatter_kernel, scatter, per,...  118 us
    pallas_call x1, Pallas kernels, ffn_scatter(): pl.pallas_call(functools.partial(ffn_scatter_kernel, scatter, per, sent,...  87.9 us
    pallas_call x1, Pallas kernels, gather_project(): pl.pallas_call(functools.partial(gather_project_kernel, gather, per), gri...  71 us
    ppermute x4, waiting for transfers between devices, swap(): return lax.ppermute(x, 'tensor', [(0, 1), (1, 0)])  62.1 us
    pallas_call x1, Pallas kernels, ffn(): pl.pallas_call(ffn_kernel, grid=(2, steps), in_specs=[resident((rows, d))...  54.4 us
    pallas_call x1, Pallas kernels, attend(): pl.pallas_call(functools.partial(attend_kernel, block, seg_rows), grid=(g...  21.7 us
    unnamed x55, local copies, waits for them, and re-layouts  10.3 us
  transfers between devices with their start and end apart: 5, of which 2 were waited for; matrix products, arithmetic and copies ran while one was open for 2% of the time, Pallas kernels for 6%

profile of v11, /device:TPU:0, one launch (start us, length us, event | category | flops | bytes accessed | tf_op | source)
XLA Modules:
  0.0 462.3 jit_solution(5159346151880118203)
XLA Ops:
  7.2 0.7 fusion.13
  9.4 71.0 %gather_project.1 = (bf16[1536,3072]{1,0:T(8,128)(2,1)}, bf16[2,512,2304]{2,1,0:T(8,128)(2,1)}, bf16[1536,1024]{1,0:T(8,128)(2,1)}, bf16[2,512,1536]{2,1,0:T(8,1...) custom-call(bf16[96,768]{1,0:T(8,128)(2,1)} %refs_0_.1, ...), custom_call_target="tpu_custom_call" | custom-call | flops 7247757312 | bytes 9437184 | tf_op jit(solution)/shard_map/gather_project/pallas_call | solution.py:1321
  80.4 1.6 collective-permute-start
  82.3 21.7 %attend.1 = (bf16[1024,768]{1,0:T(8,128)(2,1)S(1)}, f32[6,2,1024]{2,1,0:T(2,128)S(1)}) custom-call(bf16[1024,2304]{1,0:T(8,128)(2,1)} %bitcast.39, bf16[1024,2304]{1,0:T(8,128)(2,1)} %bitcast.40, bf16[1024,2304]{1,0:T(8,128)(2,1)} %bitcast.41, f32[8,1024]{1,0:T(8,128)S(1)} %broadcast_bitcast_fusion.bias_ref.refs_9_), custom_call_target="tpu_custom_call" | custom-call | flops 6442450944 | bytes 6291456 | tf_op jit(solution)/shard_map/attend/pallas_call | solution.py:150
  104.0 2.9 project_out.1
  107.5 3.7 convolution_add_fusion
  111.3 1.3 copy-done.1
  112.7 2.2 turn_pair.1.refs_0_
  114.9 28.5 %collective-permute-done.1 = bf16[512,1536]{1,0:T(8,128)(2,1)} collective-permute-done((bf16[512,1536]{1,0:T(8,128)(2,1)}, bf16[512,1536]{1,0:T(8,128)(2,1)}, u32[]{:S(2)}, u32[]{:S(2)}) %collective-permute-start.1) | collective-permute-done | bytes 1572896 | tf_op jit(solution)/shard_map/ppermute | solution.py:1392
  143.4 1.9 add_convert_fusion.x_own.refs_8_
  147.1 33.6 %collective-permute-done.2.x_other = bf16[512,1536]{1,0:T(8,128)(2,1)S(1)} collective-permute-done((bf16[512,1536]{1,0:T(8,128)(2,1)S(1)}, bf16[512,1536]{1,0:T(8,128)(2,1)S(1)}, u32[]{:S(2)}, u32[]{:S(2)}) %collective-permute-start.2) | collective-permute-done | bytes 1572896 | tf_op jit(solution)/shard_map/ppermute | solution.py:1392
  180.7 1.1 copy-done.19
  181.8 54.4 %ffn.1 = (bf16[2,3,512,2048]{3,2,1,0:T(8,128)(2,1)}, bf16[2,512,1536]{2,1,0:T(8,128)(2,1)}, bf16[2,512,1536]{2,1,0:T(8,128)(2,1)}, f32[8,1536]{1,0:T(8,128)}, bf16[512,1536]{1,0:T(8,128)(2,1)}) custom-call(bf16[512,1536]{1,0:T(8,128)(2,1)} %copy-done.6, bf16[512,1536]{1,0:T(8,128)(2,1)} %copy-done.19, bf16[512,1536]{1,0:T(8,128)(2,1)} %refs_7_.1, ...), custom_call_target="tpu_custom_call" | custom-call | flops 32212254720 | bytes 62914560 | tf_op jit(solution)/shard_map/ffn/pallas_call | solution.py:322
  236.2 87.9 %ffn_scatter.1 = (f32[96,2048]{1,0:T(8,128)}, f32[96,1792]{1,0:T(8,128)}, f32[16,256]{1,0:T(8,128)}, bf16[1536,2304]{1,0:T(8,128)(2,1)}, bf16[2,512,1536]{2,1,0:...) custom-call(bf16[1536,1024]{1,0:T(8,128)(2,1)} %copy-done, ...), custom_call_target="tpu_custom_call" | custom-call | flops 25769803776 | bytes 15728640 | tf_op jit(solution)/shard_map/ffn_scatter/pallas_call | solution.py:802
  324.2 118.4 %attention_scatter.1 = (f32[96,768]{1,0:T(8,128)}, f32[96,768]{1,0:T(8,128)}, f32[96,768]{1,0:T(8,128)}, f32[96,768]{1,0:T(8,128)}, f32[16,256]{1,0:T(8,128)}, /...) custom-call(bf16[1536,1024]{1,0:T(8,128)(2,1)} %get-tuple-element.65.refs_0_, ...), custom_call_target="tpu_custom_call" | custom-call | flops 33017561088 | bytes 31457280 | tf_op jit(solution)/shard_map/attention_scatter/pallas_call | solution.py:1052
  442.6 0.8 slice.11
  444.7 1.8 pad_maximum_fusion
  447.7 1.1 copy.43
  448.8 0.8 copy-done.8
  449.7 1.1 copy.44
  450.8 0.7 copy.45
  453.0 0.7 copy.48
  453.7 0.9 copy.49
  454.6 0.9 copy.50
  (83 shorter events, 8.1 us)
Async XLA Ops:
  7.2 173.5 %all-gather.2.cloned.1.call-start = ((), (), s32[]{:S(2)}) async-start(), calls=%async_computation | async-start | bytes 20054016 | tf_op jit(solution)/shard_map/all_gather | solution.py:1421
  80.4 26.5 %collective-permute-start = (bf16[256,1536]{1,0:T(8,128)(2,1)}, bf16[256,1536]{1,0:T(8,128)(2,1)S(1)}, u32[]{:S(2)}, u32[]{:S(2)}) collective-permute-start(bf16[256,1536]{1,0:T(8,128)(2,1)} %get-tuple-element.52), channel_id=1, source_target_pairs={{0,1},{1,0},{2,3},{3,2},{4,5},{5,4},{6,7},{7,6},{8,9},{9,8},{10,11... | collective-permute-start | bytes 2359304 | tf_op jit(solution)/shard_map/ppermute | solution.py:1392
  82.2 21.7 %copy-start.4 = (f32[8,1024]{1,0:T(8,128)}, f32[8,1024]{1,0:T(8,128)S(1)}, u32[]{:S(2)}) copy-start(f32[8,1024]{1,0:T(8,128)S(1)} %broadcast_bitcast_fusion.bias_ref.refs_9_) | copy-start | bytes 98308
  82.2 21.7 %slice-start = ((s8[9437184]{0:T(1024)(128)(4,1)}), s8[4194304]{0:T(1024)(128)(4,1)S(1)}, s32[]{:S(2)}) async-start(s8[9437184]{0:T(1024)(128)(4,1)} %bitcast.30), calls=%async_computation.1 | async-start | bytes 8388608
  82.2 21.7 %slice-start.1 = ((s8[9437184]{0:T(1024)(128)(4,1)}), s8[4194304]{0:T(1024)(128)(4,1)S(1)}, s32[]{:S(2)}) async-start(s8[9437184]{0:T(1024)(128)(4,1)} %bitcast.30), calls=%async_computation.2 | async-start | bytes 8388608
  82.2 21.7 %slice-start.2 = ((s8[9437184]{0:T(1024)(128)(4,1)}), s8[1048576]{0:T(1024)(128)(4,1)S(1)}, s32[]{:S(2)}) async-start(s8[9437184]{0:T(1024)(128)(4,1)} %bitcast.30), calls=%async_computation.3 | async-start | bytes 2097152
  103.9 3.0 copy-start.5
  103.9 3.5 copy-start.3
  106.9 36.5 %collective-permute-start.1 = (bf16[512,1536]{1,0:T(8,128)(2,1)}, bf16[512,1536]{1,0:T(8,128)(2,1)}, u32[]{:S(2)}, u32[]{:S(2)}) collective-permute-start(bf16[512,1536]{1,0:T(8,128)(2,1)} %project_out.1), channel_id=1, source_target_pairs={{0,1},{1,0},{2,3},{3,2},{4,5},{5,4},{6,7},{7,6},{8,9},{9,8},{10,11... | collective-permute-start | bytes 4718600 | tf_op jit(solution)/shard_map/ppermute | solution.py:1392
  107.4 3.8 copy-start.10
  112.7 2.2 copy-start.2
  114.8 30.5 %copy-start = (bf16[1536,1024]{1,0:T(8,128)(2,1)}, bf16[1536,1024]{1,0:T(8,128)(2,1)S(1)}, u32[]{:S(2)}) copy-start(bf16[1536,1024]{1,0:T(8,128)(2,1)S(1)} %turn_pair.1.refs_0_) | copy-start | bytes 9437188
  114.8 31.1 %copy-start.17 = (f32[1536]{0:T(1024)S(1)}, f32[1536]{0:T(1024)}, u32[]{:S(2)}) copy-start(f32[1536]{0:T(1024)} %refs_6_.1) | copy-start | bytes 18436
  114.9 31.7 %copy-start.18 = (f32[1536]{0:T(1024)S(1)}, f32[1536]{0:T(1024)}, u32[]{:S(2)}) copy-start(f32[1536]{0:T(1024)} %param.15) | copy-start | bytes 18436
  145.3 35.4 %copy-start.6 = (bf16[512,1536]{1,0:T(8,128)(2,1)}, bf16[512,1536]{1,0:T(8,128)(2,1)S(1)}, u32[]{:S(2)}) copy-start(bf16[512,1536]{1,0:T(8,128)(2,1)S(1)} %add_convert_fusion.x_own.refs_8_) | copy-start | bytes 4718596
  145.3 35.4 %collective-permute-start.2 = (bf16[512,1536]{1,0:T(8,128)(2,1)S(1)}, bf16[512,1536]{1,0:T(8,128)(2,1)S(1)}, u32[]{:S(2)}, u32[]{:S(2)}) collective-permute-start(bf16[512,1536]{1,0:T(8,128)(2,1)S(1)} %add_convert_fusion.x_own.refs_8_), channel_id=1, source_target_pairs={{0,1},{1,0},{2,3},{3,2},{4,5},{5,4},{6,7},{7,6},{8,9},{9,8},{10,11... | collective-permute-start | bytes 4718600 | tf_op jit(solution)/shard_map/ppermute | solution.py:1392
  324.2 120.5 %copy-start.12 = (f32[96,1792]{1,0:T(8,128)S(1)}, f32[96,1792]{1,0:T(8,128)}, u32[]{:S(2)}) copy-start(f32[96,1792]{1,0:T(8,128)} %get-tuple-element.80) | copy-start | bytes 2064388
  442.6 5.1 %copy-start.7 = (bf16[512,1536]{1,0:T(8,128)(2,1)S(1)}, bf16[512,1536]{1,0:T(8,128)(2,1)}, u32[]{:S(2)}) copy-start(bf16[512,1536]{1,0:T(8,128)(2,1)} %get-tuple-element.98) | copy-start | bytes 4718596
  443.5 3.6 collective-permute-start.3
  447.7 2.0 copy-start.8
  449.7 2.6 copy-start.14
  450.8 2.2 copy-start.13
  450.8 2.9 copy-start.11
  451.6 3.0 copy-start.9
  (4 other events, 5.6 us)
Sparse Core Ops, SparseCore 0:
  80.5 97.5 all-gather.1
